TPU v7x, 128 devices: a whole 4x4x4 slice. The times are simulated.
128 devices in a mesh: row: 8 (over z, x_hi), col: 16 (over x_lo, y, core).
Axes of the slice: x: 4 (x_hi: 2, x_lo: 2; x = x_hi * 2 + x_lo), y: 4, z: 4, core: 2. Of those that a mesh axis runs over, the one named last changes fastest.
Arguments:
- tile_blocks: bfloat16 [8, 16, 384, 128, 128], P('row', 'col'), may hold values from -0.109375 to 0.109375
- tile_rows: int32 [8, 16, 384], P('row', 'col'), may hold values from 0 to 127, as said below
- tile_cols: int32 [8, 16, 384], P('row', 'col'), may hold values from 0 to 63, as said below
- tile_count: int32 [8, 16], P('row', 'col'), may hold values from 48 to 384, as said below
- vectors: float32 [16, 131072], P(None, ('row', 'col')), may hold values from -8 to 8
- hvectors: float32 [16, 131072], P(None, ('row', 'col')), may hold values from -20 to 20
- previous: float32 [16, 131072], P(None, ('row', 'col')), may hold values from -6 to 6
- hprevious: float32 [16, 131072], P(None, ('row', 'col')), may hold values from -6 to 6
Outputs:
- orthonormal: float32 [48, 131072], P(None, ('row', 'col'))
- orthonormal_image: float32 [48, 131072], P(None, ('row', 'col'))
- projected: float32 [48, 48], replicated
Inputs may be any that keep to these rules, and one draw needn't show every extreme that they name: `tile_rows`: both ends occur in every draw. `tile_cols`: both ends occur in every draw. `tile_count`: one process cell holds exactly 384 live slots in every draw; every other cell holds between 48 and 192.
All inputs are finite; a program needn't handle non-finite values.
Results may differ from a plain program's by a relative error of at most 0.0003.
Values sent between devices are 32-bit elements; how exact they have to be, the bound alone decides.
No kernel may reach another device: no remote copies, remote signals or barrier semaphores. Data moves between devices by JAX's collectives and lax.ppermute only.
A program may use at most 64 MiB of HBM per device.

v0:
```python
import math

import jax
import jax.numpy as jnp
from jax import lax
from jax.sharding import PartitionSpec as P

EPSILON = 1e-06
HIGHEST_PRECISION = lax.Precision.HIGHEST


def dense_product(first, second):
    return jnp.dot(first, second, preferred_element_type=jnp.float32, precision=HIGHEST_PRECISION)


def hamiltonian(tile_blocks, tile_rows, tile_cols, tile_count, operand):
    tile_stack = tile_blocks[0, 0]
    row_ids = tile_rows[0, 0]
    col_ids = tile_cols[0, 0]
    slot_count = tile_stack.shape[0]
    tile_width = tile_stack.shape[-1]
    members = operand.shape[0]
    live_mask = lax.iota(jnp.int32, slot_count) < tile_count[0, 0]
    row_range = lax.all_gather(operand, "col", axis=1, tiled=True)
    col_range = lax.all_gather(operand, "row", axis=1, tiled=True)
    row_blocks = row_range.reshape(members, -1, tile_width)
    col_blocks = col_range.reshape(members, -1, tile_width)
    block_size = math.gcd(slot_count, 64)
    block_count = slot_count // block_size

    def slot_block(counter):
        start = counter * block_size
        tile_part = lax.dynamic_slice_in_dim(tile_stack, start, block_size, 0).astype(jnp.float32)
        row_part = lax.dynamic_slice_in_dim(row_ids, start, block_size, 0)
        col_part = lax.dynamic_slice_in_dim(col_ids, start, block_size, 0)
        live_part = lax.dynamic_slice_in_dim(live_mask, start, block_size, 0)[None, :, None]
        return (tile_part, row_part, col_part, live_part)

    def forward_product(tile_part, col_part):
        inputs = jnp.take(col_blocks, col_part, axis=1)
        return jnp.einsum("tij,mtj->mti", tile_part, inputs, precision=HIGHEST_PRECISION)

    def backward_product(tile_part, row_part):
        inputs = jnp.take(row_blocks, row_part, axis=1)
        return jnp.einsum("tij,mti->mtj", tile_part, inputs, precision=HIGHEST_PRECISION)

    def forward(counter, totals):
        tile_part, row_part, col_part, live_part = slot_block(counter)
        product = forward_product(tile_part, col_part)
        return totals.at[:, row_part, :].add(jnp.where(live_part, product, 0.0))

    def backward(counter, totals):
        tile_part, row_part, col_part, live_part = slot_block(counter)
        product = backward_product(tile_part, row_part)
        return totals.at[:, col_part, :].add(jnp.where(live_part, product, 0.0))

    zero_rows = jnp.zeros(row_blocks.shape, jnp.float32)
    zero_cols = jnp.zeros(col_blocks.shape, jnp.float32)
    row_totals = lax.fori_loop(0, block_count, forward, zero_rows)
    col_totals = lax.fori_loop(0, block_count, backward, zero_cols)
    applied = lax.psum_scatter(
        row_totals.reshape(members, -1), "col", scatter_dimension=1, tiled=True
    )
    applied = applied + lax.psum_scatter(
        col_totals.reshape(members, -1), "row", scatter_dimension=1, tiled=True
    )
    return applied


def on_device(
    tile_blocks, tile_rows, tile_cols, tile_count, vectors, hvectors, previous, hprevious
):
    total_rows = vectors.shape[1] * lax.axis_size("row") * lax.axis_size("col")
    rayleigh_top, rayleigh_bottom = lax.psum(
        (jnp.sum(vectors * hvectors, axis=1), jnp.sum(vectors * vectors, axis=1)), ("row", "col")
    )
    ritz_values = rayleigh_top / (rayleigh_bottom + EPSILON)
    residual = hvectors - ritz_values[:, None] * vectors
    residual_image = hamiltonian(tile_blocks, tile_rows, tile_cols, tile_count, residual)
    basis_rows = jnp.concatenate([vectors, residual, previous], axis=0)
    image_rows = jnp.concatenate([hvectors, residual_image, hprevious], axis=0)
    gram_matrix, mixed_matrix = lax.psum(
        (dense_product(basis_rows, basis_rows.T), dense_product(basis_rows, image_rows.T)),
        ("row", "col"),
    )
    factor = jnp.linalg.cholesky(gram_matrix)
    row_scale = math.sqrt(total_rows)
    orthonormal = row_scale * lax.linalg.triangular_solve(
        factor, basis_rows, left_side=True, lower=True
    )
    orthonormal_image = row_scale * lax.linalg.triangular_solve(
        factor, image_rows, left_side=True, lower=True
    )
    half_done = lax.linalg.triangular_solve(factor, mixed_matrix, left_side=True, lower=True)
    projected = lax.linalg.triangular_solve(
        factor, half_done, left_side=False, lower=True, transpose_a=True
    )
    return (orthonormal, orthonormal_image, projected)


def solution(mesh):
    in_specs = (
        P("row", "col", None, None, None),
        P("row", "col", None),
        P("row", "col", None),
        P("row", "col"),
        P(None, ("row", "col")),
        P(None, ("row", "col")),
        P(None, ("row", "col")),
        P(None, ("row", "col")),
    )
    out_specs = (P(None, ("row", "col")), P(None, ("row", "col")), P())
    return jax.shard_map(
        on_device, mesh=mesh, in_specs=in_specs, out_specs=out_specs, check_vma=False
    )
```

profile of v0, /device:TPU:1, one launch (start us, length us, event | category | flops | bytes accessed | tf_op | source)
XLA Modules:
  0.0 387.4 jit_solution(8466629798709150425)
XLA Ops:
  7.2 1.0 multiply_reduce_fusion
  8.2 68.7 %all-reduce.1 = (f32[16]{0:T(128)S(1)}, f32[16]{0:T(128)S(1)}) all-reduce(f32[16]{0:T(128)S(1)} %get-tuple-element.269, f32[16]{0:T(128)S(1)} %get-tuple-element.268), channel_id=1, replica_groups=mesh['row'=8,'col'=16] {'row','col'}, use_global_device_ids=true, to_apply=%region_1.0 | all-reduce | flops 32 | bytes 256 | tf_op jit(solution)/shard_map/psum | solution.py:74
  76.9 1.6 multiply_subtract_fusion
  78.5 31.3 %all_gather.6 = f32[16,8192]{1,0:T(8,128)S(1)} all-gather(f32[16,1024]{1,0:T(8,128)} %multiply_subtract_fusion), channel_id=1, replica_groups=mesh['row'=8,'col'=16] {'row'}, dimensions={1}, use_global_device_ids=true | all-gather | bytes 589824 | tf_op jit(solution)/shard_map/all_gather | solution.py:25
  109.9 0.7 reduce.6
  110.6 0.7 reduce.7
  112.0 52.6 %while.26 = (s32[]{:T(128)}, f32[16,128,128]{2,0,1:T(8,128)S(1)}, s32[384]{0:T(512)S(1)}, pred[384]{0:T(512)(128)(4,1)S(1)}, s32[384]{0:T(512)S(1)}, /*index=5*/...) while((s32[]{:T(128)}, f32[16,128,128]{2,0,1:T(8,128)S(1)}, ...), condition=%wide.region_9.11_spmd, body=%wide.region_7.10_spmd.sunk | while | flops 201721408 | bytes 5773547 | solution.py:59
  112.1 0.6 gather_fusion
  112.9 5.0 %fusion.50 = f32[64,16,128]{2,1,0:T(8,128)S(1)} fusion(bf16[384,128,128]{2,1,0:T(8,128)(2,1)} %get-tuple-element.428, s32[]{:T(128)S(6)} %select_n.125, f32[64,16,128]{2,1,0:T(8,128)S(1)} %gather_fusion, pred[64]{0:T(512)(128)(4,1)S(1)} %get-tuple-element.390, pred[64]{0:T(512)(128)(4,1)S(1)} %dynamic_slice.78), kind=kOutput, calls=%fused_computation.6.clone.1 | convolution fusion | flops 201588736 | bytes 3145860 | tf_op jit(solution)/shard_map/while/body/eval_jaxpr/tij,mtj->mti/dot_general | solution.py:41
  117.8 0.1 compare_select_fusion.8
  117.9 2.9 scatter_fusion
  120.9 0.6 gather_fusion
  121.6 5.0 %fusion.50 = f32[64,16,128]{2,1,0:T(8,128)S(1)} fusion(bf16[384,128,128]{2,1,0:T(8,128)(2,1)} %get-tuple-element.428, s32[]{:T(128)S(6)} %select_n.125, f32[64,16,128]{2,1,0:T(8,128)S(1)} %gather_fusion, pred[64]{0:T(512)(128)(4,1)S(1)} %get-tuple-element.390, pred[64]{0:T(512)(128)(4,1)S(1)} %dynamic_slice.78), kind=kOutput, calls=%fused_computation.6.clone.1 | convolution fusion | flops 201588736 | bytes 3145860 | tf_op jit(solution)/shard_map/while/body/eval_jaxpr/tij,mtj->mti/dot_general | solution.py:41
  126.7 2.9 scatter_fusion
  129.7 0.6 gather_fusion
  130.4 5.0 %fusion.50 = f32[64,16,128]{2,1,0:T(8,128)S(1)} fusion(bf16[384,128,128]{2,1,0:T(8,128)(2,1)} %get-tuple-element.428, s32[]{:T(128)S(6)} %select_n.125, f32[64,16,128]{2,1,0:T(8,128)S(1)} %gather_fusion, pred[64]{0:T(512)(128)(4,1)S(1)} %get-tuple-element.390, pred[64]{0:T(512)(128)(4,1)S(1)} %dynamic_slice.78), kind=kOutput, calls=%fused_computation.6.clone.1 | convolution fusion | flops 201588736 | bytes 3145860 | tf_op jit(solution)/shard_map/while/body/eval_jaxpr/tij,mtj->mti/dot_general | solution.py:41
  135.4 0.1 compare_select_fusion.8
  135.5 2.9 scatter_fusion
  138.5 0.6 gather_fusion
  139.2 5.0 %fusion.50 = f32[64,16,128]{2,1,0:T(8,128)S(1)} fusion(bf16[384,128,128]{2,1,0:T(8,128)(2,1)} %get-tuple-element.428, s32[]{:T(128)S(6)} %select_n.125, f32[64,16,128]{2,1,0:T(8,128)S(1)} %gather_fusion, pred[64]{0:T(512)(128)(4,1)S(1)} %get-tuple-element.390, pred[64]{0:T(512)(128)(4,1)S(1)} %dynamic_slice.78), kind=kOutput, calls=%fused_computation.6.clone.1 | convolution fusion | flops 201588736 | bytes 3145860 | tf_op jit(solution)/shard_map/while/body/eval_jaxpr/tij,mtj->mti/dot_general | solution.py:41
  144.2 2.9 scatter_fusion
  147.2 0.6 gather_fusion
  147.9 5.0 %fusion.50 = f32[64,16,128]{2,1,0:T(8,128)S(1)} fusion(bf16[384,128,128]{2,1,0:T(8,128)(2,1)} %get-tuple-element.428, s32[]{:T(128)S(6)} %select_n.125, f32[64,16,128]{2,1,0:T(8,128)S(1)} %gather_fusion, pred[64]{0:T(512)(128)(4,1)S(1)} %get-tuple-element.390, pred[64]{0:T(512)(128)(4,1)S(1)} %dynamic_slice.78), kind=kOutput, calls=%fused_computation.6.clone.1 | convolution fusion | flops 201588736 | bytes 3145860 | tf_op jit(solution)/shard_map/while/body/eval_jaxpr/tij,mtj->mti/dot_general | solution.py:41
  152.9 0.1 compare_select_fusion.8
  153.0 2.9 scatter_fusion
  156.0 0.6 gather_fusion
  156.7 5.0 %fusion.50 = f32[64,16,128]{2,1,0:T(8,128)S(1)} fusion(bf16[384,128,128]{2,1,0:T(8,128)(2,1)} %get-tuple-element.428, s32[]{:T(128)S(6)} %select_n.125, f32[64,16,128]{2,1,0:T(8,128)S(1)} %gather_fusion, pred[64]{0:T(512)(128)(4,1)S(1)} %get-tuple-element.390, pred[64]{0:T(512)(128)(4,1)S(1)} %dynamic_slice.78), kind=kOutput, calls=%fused_computation.6.clone.1 | convolution fusion | flops 201588736 | bytes 3145860 | tf_op jit(solution)/shard_map/while/body/eval_jaxpr/tij,mtj->mti/dot_general | solution.py:41
  161.8 2.9 scatter_fusion
  164.7 1.1 copy_bitcast_fusion
  165.8 1.3 copy_bitcast_fusion.1
  167.2 43.1 %while.27 = (s32[]{:T(128)}, f32[16,64,128]{2,0,1:T(8,128)S(1)}, s32[384]{0:T(512)S(1)}, pred[384]{0:T(512)(128)(4,1)S(1)}, s32[384]{0:T(512)S(1)}, /*index=5*/f...) while((s32[]{:T(128)}, f32[16,64,128]{2,0,1:T(8,128)S(1)}, ...), condition=%wide.region_13.15_spmd, body=%wide.region_11.14_spmd.sunk | while | flops 201721408 | bytes 5773547 | solution.py:60
  167.3 0.6 gather_fusion.1
  168.1 3.4 fusion.53
  171.5 2.9 scatter_fusion.1
  174.5 0.6 gather_fusion.1
  175.2 3.4 fusion.53
  178.7 2.9 scatter_fusion.1
  181.7 0.6 gather_fusion.1
  182.4 3.4 fusion.53
  185.9 2.9 scatter_fusion.1
  188.9 0.6 gather_fusion.1
  189.6 3.4 fusion.53
  193.1 2.9 scatter_fusion.1
  196.1 0.6 gather_fusion.1
  196.8 3.4 fusion.53
  200.3 2.9 scatter_fusion.1
  203.3 0.6 gather_fusion.1
  204.0 3.4 fusion.53
  207.5 2.9 scatter_fusion.1
  210.4 0.9 copy_bitcast_fusion.2
  211.3 0.3 fusion.23
  211.6 14.0 %reduce-scatter.3.cloned.1.call-done = f32[16,1024]{1,0:T(8,128)} async-done(((f32[16,16384]{1,0:T(8,128)}), f32[16,1024]{1,0:T(8,128)}) %reduce-scatter.3.cloned.1.call-update) | async-done | bytes 65552 | tf_op jit(solution)/shard_map/reduce_scatter | solution.py:61
  225.6 74.9 %reduce-scatter.5.cloned.1.call-done = f32[16,1024]{1,0:T(8,128)} async-done(((f32[16,8192]{1,0:T(8,128)}), f32[16,1024]{1,0:T(8,128)}) %reduce-scatter.5.cloned.1.call-update) | async-done | bytes 65552 | tf_op jit(solution)/shard_map/reduce_scatter | solution.py:64
  300.4 0.9 add.136
  301.3 0.3 fusion.22
  301.7 66.6 %all-reduce = (f32[48,48]{0,1:T(8,128)S(1)}, f32[48,48]{1,0:T(8,128)S(1)}) all-reduce(f32[48,48]{0,1:T(8,128)S(1)} %fusion.23, f32[48,48]{1,0:T(8,128)S(1)} %fusion.22), channel_id=1, replica_groups=mesh['row'=8,'col'=16] {'row','col'}, use_global_device_ids=true, to_apply=%region_4.5 | all-reduce | flops 4608 | bytes 36864 | tf_op jit(solution)/shard_map/psum | solution.py:82
  368.3 4.4 %cholesky.18 = f32[48,48]{1,0:T(8,128)S(1)} custom-call(f32[48,48]{1,0:T(8,128)S(1)} %fusion.31), custom_call_target="Cholesky" | custom-call | tf_op jit(solution)/shard_map/jit(cholesky)/cholesky | solution.py:86
  372.8 0.6 compare_reduce_fusion
  373.4 0.7 fusion.24
  374.1 3.7 custom-call.13
  377.7 1.1 convolution_multiply_fusion
  378.8 1.0 convolution_multiply_fusion.1
  379.8 0.2 fusion.27
  380.1 0.8 fusion.25
  (70 shorter events, 3.2 us)
Async XLA Ops:
  7.2 158.6 %all-gather.2.cloned.1.call-start = ((), (), s32[]{:S(2)}) async-start(), calls=%async_computation.3 | async-start | bytes 1114112 | tf_op jit(solution)/shard_map/all_gather | solution.py:24
  78.5 147.1 %reduce-scatter.3.cloned.1.call-start = ((), (), s32[]{:S(2)}) async-start(), calls=%async_computation.2 | async-start | bytes 1114112 | tf_op jit(solution)/shard_map/reduce_scatter | solution.py:61
  165.7 134.7 %reduce-scatter.5.cloned.1.call-start = ((), (), s32[]{:S(2)}) async-start(), calls=%async_computation.4 | async-start | bytes 589824 | tf_op jit(solution)/shard_map/reduce_scatter | solution.py:64
  167.2 44.1 %copy-start = (f32[16,1024]{1,0:T(8,128)S(1)}, f32[16,1024]{1,0:T(8,128)}, u32[]{:S(2)}) copy-start(f32[16,1024]{1,0:T(8,128)} %multiply_subtract_fusion) | copy-start | bytes 196612
  167.2 44.1 %copy-start.2 = (f32[16,1024]{1,0:T(8,128)S(1)}, f32[16,1024]{1,0:T(8,128)}, u32[]{:S(2)}) copy-start(f32[16,1024]{1,0:T(8,128)} %param.18) | copy-start | bytes 196612
  167.2 44.1 %copy-start.4 = (f32[16,1024]{1,0:T(8,128)S(1)}, f32[16,1024]{1,0:T(8,128)}, u32[]{:S(2)}) copy-start(f32[16,1024]{1,0:T(8,128)} %param.20) | copy-start | bytes 196612
  167.2 134.1 %copy-start.1 = (f32[16,1024]{1,0:T(8,128)S(1)}, f32[16,1024]{1,0:T(8,128)}, u32[]{:S(2)}) copy-start(f32[16,1024]{1,0:T(8,128)} %param.19) | copy-start | bytes 196612
  167.2 134.1 %copy-start.3 = (f32[16,1024]{1,0:T(8,128)S(1)}, f32[16,1024]{1,0:T(8,128)}, u32[]{:S(2)}) copy-start(f32[16,1024]{1,0:T(8,128)} %param.21) | copy-start | bytes 196612
Sparse Core Ops, SparseCore 0:
  78.6 29.4 all-gather.1
  165.9 59.6 reduce-scatter.2
  229.5 70.8 reduce-scatter.4
where the time goes:
time: 388 us; the launch traced here: 387 us
  blocking collectives  167 us (43%)
  waiting for transfers between devices  88.9 us (23%)
  matrix products  53.9 us (14%)
  other arithmetic  50.7 us (13%)
  between operations  14.6 us (4%)
  local copies, waits for them, and re-layouts  12 us (3%)
    reduce_scatter x1, waiting for transfers between devices, hamiltonian(): lax.psum_scatter(col_totals.reshape(members, -1), 'row', scatter_dimensio...  74.9 us
    psum x1, blocking collectives, on_device(): lax.psum((jnp.sum(vectors * hvectors, axis=1), jnp.sum(vectors * vectors,...  68.7 us
    psum x1, blocking collectives, on_device(): lax.psum((dense_product(basis_rows, basis_rows.T), dense_product(basis_ro...  66.6 us
    all_gather x1, blocking collectives, hamiltonian(): col_range = lax.all_gather(operand, 'row', axis=1, tiled=True)  31.3 us
    dot_general x6, matrix products, forward_product(): jnp.einsum('tij,mtj->mti', tile_part, inputs, precision=HIGHEST_PRECISION)  29.9 us
    dot_general x6, matrix products, backward_product(): jnp.einsum('tij,mti->mtj', tile_part, inputs, precision=HIGHEST_PRECISION)  20.4 us
    scatter-add x6, other arithmetic, backward(): return totals.at[:, col_part, :].add(jnp.where(live_part, product, 0.0))  17.2 us
    scatter-add x6, other arithmetic, forward(): return totals.at[:, row_part, :].add(jnp.where(live_part, product, 0.0))  17.2 us
  transfers between devices with their start and end apart: 3, of which 2 were waited for; matrix products, arithmetic and copies ran while one was open for 26% of the time, Pallas kernels for 0%

commit v1 on v0

v1 whole, which is shorter than its diff:
```python
import functools
import math

import jax
import jax.numpy as jnp
from jax import lax
from jax.experimental import pallas as pl
from jax.experimental.pallas import tpu as pltpu
from jax.sharding import PartitionSpec as P

EPSILON = 1e-06
HIGHEST_PRECISION = lax.Precision.HIGHEST
LANES = 128
VMEM_BYTES = 48 << 20
NT = (((1,), (1,)), ((), ()))
NN = (((1,), (0,)), ((), ()))


def exact_dot(first, second, dims):
    return lax.dot_general(
        first, second, dims, precision=HIGHEST_PRECISION, preferred_element_type=jnp.float32
    )


def call(kernel, out_shapes, name):
    return pl.pallas_call(
        kernel,
        out_shape=[jax.ShapeDtypeStruct(shape, jnp.float32) for shape in out_shapes],
        compiler_params=pltpu.CompilerParams(vmem_limit_bytes=VMEM_BYTES),
        name=name,
    )


def block(array, index):
    return array[:, index * LANES : (index + 1) * LANES]


def rayleigh_kernel(vectors_ref, hvectors_ref, slots_ref):
    vectors = vectors_ref[...]
    hvectors = hvectors_ref[...]
    members = vectors.shape[0]
    top = jnp.sum(vectors * hvectors, axis=1, keepdims=True)
    bottom = jnp.sum(vectors * vectors, axis=1, keepdims=True)
    lane = lax.broadcasted_iota(jnp.int32, (members, LANES), 1)
    line = lax.broadcasted_iota(jnp.int32, (members, LANES), 0)
    spread = jnp.where(lane == line, top, 0.0) + jnp.where(lane == line + members, bottom, 0.0)
    sums = jnp.sum(spread, axis=0, keepdims=True)
    slots_ref[...] = jnp.broadcast_to(sums, slots_ref.shape)


def residual_kernel(
    sums_ref, vectors_ref, hvectors_ref, previous_ref, hprevious_ref, residual_ref, slots_ref
):
    vectors = vectors_ref[...]
    hvectors = hvectors_ref[...]
    previous = previous_ref[...]
    hprevious = hprevious_ref[...]
    members = vectors.shape[0]
    sums = jnp.sum(sums_ref[...], axis=0, keepdims=True)
    lane = lax.broadcasted_iota(jnp.int32, (members, LANES), 1)
    line = lax.broadcasted_iota(jnp.int32, (members, LANES), 0)
    top = jnp.sum(jnp.where(lane == line, sums, 0.0), axis=1, keepdims=True)
    bottom = jnp.sum(jnp.where(lane == line + members, sums, 0.0), axis=1, keepdims=True)
    residual = hvectors - (top / (bottom + EPSILON)) * vectors
    residual_ref[...] = residual
    blocks = vectors.shape[1] // LANES
    for index in range(blocks):
        part = block(residual, index)
        for slot in range(slots_ref.shape[0]):
            slots_ref[slot, index] = part
    basis = jnp.concatenate([vectors, residual, previous], axis=0)
    gram = exact_dot(basis, basis, NT)
    early = exact_dot(jnp.concatenate([hvectors, hprevious], axis=0), basis, NT)
    pad = jnp.zeros((members, LANES - 3 * members), jnp.float32)
    extra = [
        gram[:members],
        gram[members : 2 * members],
        gram[2 * members :],
        early[:members],
        early[members:],
    ]
    for index, part in enumerate(pack_rows(extra, pad)):
        for slot in range(slots_ref.shape[0]):
            slots_ref[slot, blocks + index] = part


def pack_rows(parts, pad):
    members = pad.shape[0]
    first, second, third, fourth, fifth = parts
    pieces = [fifth[:, i * members : (i + 1) * members] for i in range(3)]
    zero = jnp.zeros((members, members), jnp.float32)
    return [
        jnp.concatenate([first, second, pieces[0], pieces[1]], axis=1),
        jnp.concatenate([third, fourth, pieces[2], zero], axis=1),
    ]


def unpack_rows(one, two, members):
    wide = 3 * members
    fifth = jnp.concatenate([one[:, 2 * wide :], two[:, 2 * wide : 2 * wide + members]], axis=1)
    return [one[:, :wide], one[:, wide : 2 * wide], two[:, :wide], two[:, wide : 2 * wide], fifth]


def relay_kernel(received_ref, residual_ref, slots_ref):
    residual = residual_ref[...]
    blocks = residual.shape[1] // LANES
    for index in range(blocks):
        part = block(residual, index)
        for slot in range(slots_ref.shape[0]):
            slots_ref[slot, index] = part
    for index in range(blocks, slots_ref.shape[1]):
        part = received_ref[0, index]
        for peer in range(1, received_ref.shape[0]):
            part = part + received_ref[peer, index]
        for slot in range(slots_ref.shape[0]):
            slots_ref[slot, index] = part


def factor_kernel(received_ref, inverse_ref, early_ref):
    extras = []
    for index in range(received_ref.shape[1] - 2, received_ref.shape[1]):
        part = received_ref[0, index]
        for peer in range(1, received_ref.shape[0]):
            part = part + received_ref[peer, index]
        extras.append(part)
    members = extras[0].shape[0]
    order = 3 * members
    first, second, third, fourth, fifth = unpack_rows(*extras, members)
    early_ref[...] = jnp.concatenate([fourth, fifth], axis=0)
    gram = jnp.concatenate([first, second, third], axis=0)
    line = lax.broadcasted_iota(jnp.int32, (order, order), 0)
    lane = lax.broadcasted_iota(jnp.int32, (order, order), 1)
    work = jnp.concatenate([gram, jnp.where(line == lane, 1.0, 0.0)], axis=1)
    rows = lax.broadcasted_iota(jnp.int32, (order, 1), 0)
    for step in range(order):
        pivot = work[step : step + 1, step : step + 1]
        scale = lax.rsqrt(pivot)
        scale = scale * (1.5 - 0.5 * pivot * scale * scale)
        lead = work[step : step + 1, :] * scale
        column = work[:, step : step + 1] * scale
        work = jnp.where(rows == step, lead, jnp.where(rows > step, work - column * lead, work))
    inverse_ref[...] = work[:, order:]


def orthonormal_kernel(inverse_ref, first_ref, second_ref, third_ref, out_ref, *, row_scale):
    rows = jnp.concatenate([first_ref[...], second_ref[...], third_ref[...]], axis=0)
    out_ref[...] = exact_dot(inverse_ref[...] * row_scale, rows, NN)


def image_kernel(
    row_parts_ref, col_parts_ref, vectors_ref, residual_ref, previous_ref, image_ref, slots_ref
):
    for index in range(row_parts_ref.shape[1]):
        part = row_parts_ref[0, index]
        for peer in range(1, row_parts_ref.shape[0]):
            part = part + row_parts_ref[peer, index]
        other = col_parts_ref[0, index]
        for peer in range(1, col_parts_ref.shape[0]):
            other = other + col_parts_ref[peer, index]
        image_ref[:, index * LANES : (index + 1) * LANES] = part + other
    basis = jnp.concatenate([vectors_ref[...], residual_ref[...], previous_ref[...]], axis=0)
    late = exact_dot(image_ref[...], basis, NT)
    half = late.shape[0] // 2
    pad = jnp.zeros((half, LANES // 2 - late.shape[1]), jnp.float32)
    packed = jnp.concatenate([late[:half], pad, late[half:], pad], axis=1)
    slots_ref[...] = jnp.broadcast_to(packed[None], slots_ref.shape)


def projected_kernel(received_ref, inverse_ref, early_ref, projected_ref):
    packed = jnp.sum(received_ref[...], axis=0)
    early = early_ref[...]
    members = early.shape[0] // 2
    wide = early.shape[1]
    half = LANES // 2
    late = jnp.concatenate([packed[:, :wide], packed[:, half : half + wide]], axis=0)
    mixed_t = jnp.concatenate([early[:members], late, early[members:]], axis=0)
    inverse = inverse_ref[...]
    half_done = exact_dot(inverse, mixed_t, NT)
    projected_ref[...] = exact_dot(half_done, inverse, NT)


def tile_kernel(
    count_ref, source_ref, target_ref, tiles_ref, x_ref, out_ref, split_ref, *, transpose, unroll
):
    step = pl.program_id(0)
    batch, _, _ = tiles_ref.shape
    live = count_ref[0, 0]
    start = step * batch
    members = x_ref.shape[2]

    @pl.when(step == 0)
    def _():
        out_ref[...] = jnp.zeros_like(out_ref)
        per_peer = split_ref.shape[0] // x_ref.shape[0]

        def split(peer, carry):
            for index in range(per_peer):
                value = x_ref[peer, index]
                high = value.astype(jnp.bfloat16)
                low = (value - high.astype(jnp.float32)).astype(jnp.bfloat16)
                split_ref[peer * per_peer + index] = jnp.concatenate([high, low], axis=0)
            return carry

        lax.fori_loop(0, x_ref.shape[0], split, 0)

    @pl.when(start < live)
    def _():
        def group(counter, carry):
            base = counter * unroll
            products = []
            for offset in range(unroll):
                slot = start + base + offset
                product = lax.dot_general(
                    split_ref[source_ref[0, 0, slot]],
                    tiles_ref[base + offset],
                    NT if transpose else NN,
                    preferred_element_type=jnp.float32,
                )
                product = product[:members] + product[members:]
                products.append(jnp.where(slot < live, product, 0.0))
            for offset in range(unroll):
                target = target_ref[0, 0, start + base + offset]
                out_ref[target] = out_ref[target] + products[offset]
            return carry

        groups = jnp.minimum((live - start + unroll - 1) // unroll, batch // unroll)
        lax.fori_loop(0, groups, group, 0)


def tile_products(count, source, target, tiles, received, sources, targets, transpose):
    slots = tiles.shape[0]
    batch = math.gcd(slots, 96)
    unroll = math.gcd(batch, 24)
    members = received.shape[2]
    return pl.pallas_call(
        functools.partial(tile_kernel, transpose=transpose, unroll=unroll),
        out_shape=jax.ShapeDtypeStruct((targets, members, LANES), jnp.float32),
        grid_spec=pltpu.PrefetchScalarGridSpec(
            num_scalar_prefetch=3,
            grid=(slots // batch,),
            in_specs=[
                pl.BlockSpec(
                    (batch,) + tiles.shape[1:],
                    lambda i, count, source, target: (
                        jnp.minimum(i, (count[0, 0] - 1) // batch),
                        0,
                        0,
                    ),
                ),
                pl.BlockSpec(
                    received.shape,
                    lambda i, count, source, target: (0, 0, 0, 0),
                    pipeline_mode=pl.Buffered(1),
                ),
            ],
            out_specs=pl.BlockSpec(
                (targets, members, LANES),
                lambda i, count, source, target: (0, 0, 0),
                pipeline_mode=pl.Buffered(1),
            ),
            scratch_shapes=[pltpu.VMEM((sources, 2 * members, LANES), jnp.bfloat16)],
        ),
        compiler_params=pltpu.CompilerParams(vmem_limit_bytes=VMEM_BYTES),
        name="forward_tiles" if transpose else "backward_tiles",
    )(count, source, target, tiles, received)


def exchange(slots, axes):
    return lax.all_to_all(slots, axes, 0, 0, tiled=True)


def on_device(
    tile_blocks, tile_rows, tile_cols, tile_count, vectors, hvectors, previous, hprevious
):
    n_row = lax.axis_size("row")
    n_col = lax.axis_size("col")
    everyone = ("row", "col")
    members, piece = vectors.shape
    blocks = piece // LANES
    order = 3 * members
    row_scale = math.sqrt(piece * n_row * n_col)
    tiles = tile_blocks[0, 0]

    (sums,) = call(rayleigh_kernel, [(n_row * n_col, LANES)], "rayleigh")(vectors, hvectors)
    sums = exchange(sums, everyone)
    slot = (blocks + 2, members, LANES)
    residual, slots = call(residual_kernel, [(members, piece), (n_row,) + slot], "residual")(
        sums, vectors, hvectors, previous, hprevious
    )
    col_range = exchange(slots, "row")
    (slots,) = call(relay_kernel, [(n_col,) + slot], "relay")(col_range, residual)
    row_range = exchange(slots, "col")
    row_totals = tile_products(
        tile_count, tile_cols, tile_rows, tiles, col_range, n_row * blocks, n_col * blocks, True
    )
    row_parts = exchange(row_totals.reshape(n_col, blocks, members, LANES), "col")
    col_totals = tile_products(
        tile_count, tile_rows, tile_cols, tiles, row_range, n_col * blocks, n_row * blocks, False
    )
    col_parts = exchange(col_totals.reshape(n_row, blocks, members, LANES), "row")
    inverse, early = call(factor_kernel, [(order, order), (2 * members, order)], "factor")(row_range)
    scaled = functools.partial(orthonormal_kernel, row_scale=row_scale)
    (orthonormal,) = call(scaled, [(order, piece)], "orthonormal")(
        inverse, vectors, residual, previous
    )
    image, slots = call(
        image_kernel, [(members, piece), (n_row * n_col, members // 2, LANES)], "image"
    )(row_parts, col_parts, vectors, residual, previous)
    late = exchange(slots, everyone)
    (orthonormal_image,) = call(scaled, [(order, piece)], "orthonormal_image")(
        inverse, hvectors, image, hprevious
    )
    (projected,) = call(projected_kernel, [(order, order)], "projected")(late, inverse, early)
    return (orthonormal, orthonormal_image, projected)


def solution(mesh):
    in_specs = (
        P("row", "col", None, None, None),
        P("row", "col", None),
        P("row", "col", None),
        P("row", "col"),
        P(None, ("row", "col")),
        P(None, ("row", "col")),
        P(None, ("row", "col")),
        P(None, ("row", "col")),
    )
    out_specs = (P(None, ("row", "col")), P(None, ("row", "col")), P())
    return jax.shard_map(
        on_device, mesh=mesh, in_specs=in_specs, out_specs=out_specs, check_vma=False
    )
```

time: 388 us -> 122 us (0.31)
  blocking collectives: 167 us -> 48.5 us
  waiting for transfers between devices: 88.9 us -> 27.5 us
  matrix products: 53.9 us -> 0 us
  other arithmetic: 50.7 us -> 0 us
  Pallas kernels: 0 us -> 24.4 us
  starting transfers between devices: 0.12 us -> 15.8 us
  between operations: 14.6 us -> 1.36 us
  local copies, waits for them, and re-layouts: 12 us -> 3.38 us
    psum x2 -> x0, blocking collectives: 135 us -> none  [the longest x1 68.7 us: on_device(): lax.psum((jnp.sum(vectors * hvectors, axis=1), jnp.sum(vectors * vectors,...]
    reduce_scatter x2 -> x0, waiting for transfers between devices: 88.9 us -> none  [the longest x1 74.9 us: hamiltonian(): lax.psum_scatter(col_totals.reshape(members, -1), 'row', scatter_dimensio...]
    dot_general x14 -> x0, matrix products: 50.9 us -> none  [the longest x6 29.9 us: forward_product(): jnp.einsum('tij,mtj->mti', tile_part, inputs, precision=HIGHEST_PRECISION)]
    all_to_all x0 -> x3, blocking collectives: none -> 48.5 us  [exchange(): return lax.all_to_all(slots, axes, 0, 0, tiled=True)]
    scatter-add x12 -> x0, other arithmetic: 34.4 us -> none  [the longest x6 17.2 us: backward(): return totals.at[:, col_part, :].add(jnp.where(live_part, product, 0.0))]
    all_gather x1 -> x0, blocking collectives: 31.3 us -> none  [hamiltonian(): col_range = lax.all_gather(operand, 'row', axis=1, tiled=True)]
    all_to_all x0 -> x3, waiting for transfers between devices: none -> 27.5 us  [exchange(): return lax.all_to_all(slots, axes, 0, 0, tiled=True)]
    pallas_call x0 -> x10, Pallas kernels: none -> 24.4 us  [the longest x2 13.5 us: tile_products(): pl.pallas_call(functools.partial(tile_kernel, transpose=transpose, unroll...]
  transfers between devices with their start and end apart: 3 -> 3, of which waited for: 2 -> 3; matrix products, arithmetic and copies ran while one was open for 26% -> 0% of each run, Pallas kernels for 0% -> 17%
where the time goes in v1:
time: 122 us; the launch traced here: 121 us
  blocking collectives  48.5 us (40%)
  waiting for transfers between devices  27.5 us (23%)
  Pallas kernels  24.4 us (20%)
  starting transfers between devices  15.8 us (13%)
  local copies, waits for them, and re-layouts  3.38 us (3%)
  between operations  1.36 us (1%)
    all_to_all x3, blocking collectives, exchange(): return lax.all_to_all(slots, axes, 0, 0, tiled=True)  48.5 us
    all_to_all x3, waiting for transfers between devices, exchange(): return lax.all_to_all(slots, axes, 0, 0, tiled=True)  27.5 us
    all_to_all x3, starting transfers between devices, exchange(): return lax.all_to_all(slots, axes, 0, 0, tiled=True)  15.8 us
    pallas_call x2, Pallas kernels, tile_products(): pl.pallas_call(functools.partial(tile_kernel, transpose=transpose, unroll...  13.5 us
    pallas_call x1, Pallas kernels, on_device(): call(factor_kernel, [(order, order), (2 * members, order)], 'factor')  4.48 us
    unnamed x20, local copies, waits for them, and re-layouts  3.38 us
  transfers between devices with their start and end apart: 3, of which 3 were waited for; matrix products, arithmetic and copies ran while one was open for 0% of the time, Pallas kernels for 17%

profile of v1, /device:TPU:1, one launch (start us, length us, event | category | flops | bytes accessed | tf_op | source)
XLA Modules:
  0.0 120.9 jit_solution(7868135385087935384)
XLA Ops:
  0.6 0.0 copy-start
  0.6 0.8 copy-done
  1.5 0.0 copy-start.4
  1.5 0.8 copy-done.4
  2.3 0.1 rayleigh.1
  2.4 20.9 %all_to_all.36 = f32[128,1,128]{2,1,0:T(1,128)S(1)} all-to-all(f32[128,1,128]{2,1,0:T(1,128)S(1)} %bitcast.9), channel_id=1, replica_groups=mesh['row'=8,'col'=16] {'row','col'}, dimensions={0} | all-to-all | bytes 131072 | tf_op jit(solution)/shard_map/all_to_all | solution.py:269
  23.3 0.0 copy-start.2
  23.3 0.8 copy-done.2
  24.2 0.0 copy-start.6
  24.2 0.8 copy-done.6
  25.0 0.7 residual.1
  25.7 14.7 %all_to_all.37.received_ref.x_ref = f32[8,10,16,128]{3,2,1,0:T(8,128)S(1)} all-to-all(f32[8,10,16,128]{3,2,1,0:T(8,128)S(1)} %get-tuple-element.9), channel_id=1, replica_groups=mesh['row'=8,'col'=16] {'row'}, dimensions={0} | all-to-all | bytes 1310720 | tf_op jit(solution)/shard_map/all_to_all | solution.py:269
  40.4 1.2 %relay.1 = f32[16,10,16,128]{3,2,1,0:T(8,128)} custom-call(f32[8,10,16,128]{3,2,1,0:T(8,128)S(1)} %all_to_all.37.received_ref.x_ref, f32[16,1024]{1,0:T(8,128)S(1)} %get-tuple-element.10.residual_ref.second_ref), custom_call_target="tpu_custom_call" | custom-call | tf_op jit(solution)/shard_map/relay/pallas_call | solution.py:291
  41.6 0.0 copy-start.8
  41.6 0.0 copy-start.9
  41.6 5.5 %all-to-all-start.2 = ((f32[16,10,16,128]{3,2,1,0:T(8,128)}), f32[16,10,16,128]{3,2,1,0:T(8,128)S(1)}, u32[]{:S(2)}, u32[]{:S(2)}) async-start(f32[16,10,16,128]{3,2,1,0:T(8,128)} %relay.1), calls=%async_computation.2 | async-start | bytes 2621440 | tf_op jit(solution)/shard_map/all_to_all | solution.py:269
  47.8 0.0 copy-done.8
  47.8 0.0 copy-done.9
  47.8 8.0 %forward_tiles.1 = f32[128,16,128]{2,1,0:T(8,128)} custom-call(s32[1,1]{1,0:T(1,128)S(6)} %copy.12.count_ref, s32[1,1,384]{2,1,0:T(1,128)S(1)} %copy-done.8, s32[1,1,384]{2,1,0:T(1,128)S(1)} %copy-done.9, bf16[384,128,128]{2,1,0:T(8,128)(2,1)} %bitcast.10, f32[8,10,16,128]{3,2,1,0:T(8,128)S(1)} %all_to_all.37.received_ref.x_ref), custom_call_target="tpu_custom_call" | custom-call | tf_op jit(solution)/shard_map/forward_tiles/pallas_call | solution.py:235
  55.8 10.1 %all-to-all-done.2.received_ref.x_ref = f32[16,10,16,128]{3,2,1,0:T(8,128)S(1)} async-done(((f32[16,10,16,128]{3,2,1,0:T(8,128)}), f32[16,10,16,128]{3,2,1,0:T(8,128)S(1)}, u32[]{:S(2)}, u32[]{:S(2)}) %all-to-all-start.2) | async-done | bytes 1310752 | tf_op jit(solution)/shard_map/all_to_all | solution.py:269
  65.9 4.3 %all-to-all-start.3 = ((f32[16,8,16,128]{3,2,1,0:T(8,128)}), f32[16,8,16,128]{3,2,1,0:T(8,128)S(1)}, u32[]{:S(2)}, u32[]{:S(2)}) async-start(f32[16,8,16,128]{3,2,1,0:T(8,128)} %bitcast.4), calls=%async_computation.3 | async-start | bytes 2097152 | tf_op jit(solution)/shard_map/all_to_all | solution.py:269
  70.2 0.0 copy-start.1
  70.2 0.0 copy-start.3
  70.2 5.5 %backward_tiles.1 = f32[64,16,128]{2,1,0:T(8,128)S(1)} custom-call(s32[1,1]{1,0:T(1,128)S(6)} %copy.12.count_ref, s32[1,1,384]{2,1,0:T(1,128)S(1)} %copy-done.9, s32[1,1,384]{2,1,0:T(1,128)S(1)} %copy-done.8, bf16[384,128,128]{2,1,0:T(8,128)(2,1)} %bitcast.11, f32[16,10,16,128]{3,2,1,0:T(8,128)S(1)} %all-to-all-done.2.received_ref.x_ref), custom_call_target="tpu_custom_call" | custom-call | tf_op jit(solution)/shard_map/backward_tiles/pallas_call | solution.py:235
  75.8 10.3 %all-to-all-done.3.row_parts_ref = f32[16,8,16,128]{3,2,1,0:T(8,128)S(1)} async-done(((f32[16,8,16,128]{3,2,1,0:T(8,128)}), f32[16,8,16,128]{3,2,1,0:T(8,128)S(1)}, u32[]{:S(2)}, u32[]{:S(2)}) %all-to-all-start.3) | async-done | bytes 1048608 | tf_op jit(solution)/shard_map/all_to_all | solution.py:269
  86.1 12.9 %all_to_all.38.col_parts_ref = f32[8,8,16,128]{3,2,1,0:T(8,128)S(1)} all-to-all(f32[8,8,16,128]{3,2,1,0:T(8,128)S(1)} %bitcast.7), channel_id=1, replica_groups=mesh['row'=8,'col'=16] {'row'}, dimensions={0} | all-to-all | bytes 1048576 | tf_op jit(solution)/shard_map/all_to_all | solution.py:269
  99.0 0.0 copy-done.1
  99.0 0.0 copy-done.3
  99.0 1.2 %image.1 = (f32[16,1024]{1,0:T(8,128)S(1)}, f32[128,8,128]{2,1,0:T(8,128)}) custom-call(f32[16,8,16,128]{3,2,1,0:T(8,128)S(1)} %all-to-all-done.3.row_parts_ref, f32[8,8,16,128]{3,2,1,0:T(8,128)S(1)} %all_to_all.38.col_parts_ref, f32[16,1024]{1,0:T(8,128)S(1)} %copy-done.1, f32[16,1024]{1,0:T(8,128)S(1)} %get-tuple-element.10.residual_ref.second_ref, ...), custom_call_target="tpu_custom_call" | custom-call | tf_op jit(solution)/shard_map/image/pallas_call | solution.py:306
  100.3 0.0 copy-start.5
  100.3 0.0 copy-start.7
  100.3 5.9 %all-to-all-start.5 = ((f32[128,8,128]{2,1,0:T(8,128)}), f32[128,8,128]{2,1,0:T(8,128)S(1)}, u32[]{:S(2)}, u32[]{:S(2)}) async-start(f32[128,8,128]{2,1,0:T(8,128)} %get-tuple-element.13), calls=%async_computation.5 | async-start | bytes 1048576 | tf_op jit(solution)/shard_map/all_to_all | solution.py:269
  106.2 4.5 %factor.1 = (f32[48,48]{1,0:T(8,128)S(1)}, f32[32,48]{1,0:T(8,128)S(1)}) custom-call(f32[16,10,16,128]{3,2,1,0:T(8,128)S(1)} %all-to-all-done.2.received_ref.x_ref), custom_call_target="tpu_custom_call" | custom-call | tf_op jit(solution)/shard_map/factor/pallas_call | solution.py:301
  110.7 1.0 orthonormal.1
  111.7 0.0 copy-done.5
  111.7 0.0 copy-done.7
  111.7 1.0 orthonormal_image.1
  112.7 7.0 %all-to-all-done.5.received_ref = f32[128,8,128]{2,1,0:T(8,128)S(1)} async-done(((f32[128,8,128]{2,1,0:T(8,128)}), f32[128,8,128]{2,1,0:T(8,128)S(1)}, u32[]{:S(2)}, u32[]{:S(2)}) %all-to-all-start.5) | async-done | bytes 524320 | tf_op jit(solution)/shard_map/all_to_all | solution.py:269
  119.7 1.2 projected.1
Async XLA Ops:
  0.6 0.8 copy-start
  1.5 0.8 copy-start.4
  23.3 0.8 copy-start.2
  24.2 0.8 copy-start.6
  41.6 6.2 %copy-start.8 = (s32[1,1,384]{2,1,0:T(1,128)S(1)}, s32[1,1,384]{2,1,0:T(1,128)}, u32[]{:S(2)}) copy-start(s32[1,1,384]{2,1,0:T(1,128)} %target_ref.3) | copy-start | bytes 4612
  41.6 6.2 %copy-start.9 = (s32[1,1,384]{2,1,0:T(1,128)S(1)}, s32[1,1,384]{2,1,0:T(1,128)}, u32[]{:S(2)}) copy-start(s32[1,1,384]{2,1,0:T(1,128)} %source_ref.3) | copy-start | bytes 4612
  41.6 24.3 %all-to-all-start.2 = ((f32[16,10,16,128]{3,2,1,0:T(8,128)}), f32[16,10,16,128]{3,2,1,0:T(8,128)S(1)}, u32[]{:S(2)}, u32[]{:S(2)}) async-start(f32[16,10,16,128]{3,2,1,0:T(8,128)} %relay.1), calls=%async_computation.2 | async-start | bytes 2621440 | tf_op jit(solution)/shard_map/all_to_all | solution.py:269
  65.9 20.2 %all-to-all-start.3 = ((f32[16,8,16,128]{3,2,1,0:T(8,128)}), f32[16,8,16,128]{3,2,1,0:T(8,128)S(1)}, u32[]{:S(2)}, u32[]{:S(2)}) async-start(f32[16,8,16,128]{3,2,1,0:T(8,128)} %bitcast.4), calls=%async_computation.3 | async-start | bytes 2097152 | tf_op jit(solution)/shard_map/all_to_all | solution.py:269
  70.2 28.8 %copy-start.1 = (f32[16,1024]{1,0:T(8,128)S(1)}, f32[16,1024]{1,0:T(8,128)}, u32[]{:S(2)}) copy-start(f32[16,1024]{1,0:T(8,128)} %vectors_ref.5) | copy-start | bytes 196612
  70.2 28.8 %copy-start.3 = (f32[16,1024]{1,0:T(8,128)S(1)}, f32[16,1024]{1,0:T(8,128)}, u32[]{:S(2)}) copy-start(f32[16,1024]{1,0:T(8,128)} %previous_ref.3) | copy-start | bytes 196612
  100.3 11.4 %copy-start.5 = (f32[16,1024]{1,0:T(8,128)S(1)}, f32[16,1024]{1,0:T(8,128)}, u32[]{:S(2)}) copy-start(f32[16,1024]{1,0:T(8,128)} %first_ref.3) | copy-start | bytes 196612
  100.3 11.4 %copy-start.7 = (f32[16,1024]{1,0:T(8,128)S(1)}, f32[16,1024]{1,0:T(8,128)}, u32[]{:S(2)}) copy-start(f32[16,1024]{1,0:T(8,128)} %third_ref.3) | copy-start | bytes 196612
  100.3 19.4 %all-to-all-start.5 = ((f32[128,8,128]{2,1,0:T(8,128)}), f32[128,8,128]{2,1,0:T(8,128)S(1)}, u32[]{:S(2)}, u32[]{:S(2)}) async-start(f32[128,8,128]{2,1,0:T(8,128)} %get-tuple-element.13), calls=%async_computation.5 | async-start | bytes 1048576 | tf_op jit(solution)/shard_map/all_to_all | solution.py:269

commit v2 on v1

v2 whole, which is shorter than its diff:
```python
import functools
import math

import jax
import jax.numpy as jnp
from jax import lax
from jax.experimental import pallas as pl
from jax.experimental.pallas import tpu as pltpu
from jax.sharding import PartitionSpec as P

EPSILON = 1e-06
HIGHEST_PRECISION = lax.Precision.HIGHEST
LANES = 128
VMEM_BYTES = 48 << 20
NT = (((1,), (1,)), ((), ()))
NN = (((1,), (0,)), ((), ()))


def exact_dot(first, second, dims):
    return lax.dot_general(
        first, second, dims, precision=HIGHEST_PRECISION, preferred_element_type=jnp.float32
    )


def call(kernel, out_shapes, name):
    return pl.pallas_call(
        kernel,
        out_shape=[jax.ShapeDtypeStruct(shape, jnp.float32) for shape in out_shapes],
        compiler_params=pltpu.CompilerParams(vmem_limit_bytes=VMEM_BYTES),
        name=name,
    )


def block(array, index):
    return array[:, index * LANES : (index + 1) * LANES]


def here():
    row = lax.axis_index("row")
    col = lax.axis_index("col")
    return (lax.rem(row, 2), col // (lax.axis_size("col") // 2), lax.rem(col, 2))


def stage_kernel(
    rows_ref, vectors_hbm, hvectors_hbm, previous_hbm, slots_ref, stack_ref, rows_out_ref, arrived
):
    copies = [
        pltpu.make_async_copy(source, stack_ref.at[index], arrived.at[index])
        for index, source in enumerate((vectors_hbm, hvectors_hbm, previous_hbm))
    ]
    for copy in copies:
        copy.start()
    rows = rows_ref[...]
    core = lax.rem(lax.axis_index("col"), 2)
    lines = lax.axis_size("col") // 4
    blocks = stack_ref.shape[2] // LANES
    index, peer = rows % blocks, rows // blocks
    other = jnp.where(peer % 2 == core, 0, 1)
    line = (peer // 2) % lines
    half = peer // (2 * lines)
    rows_out_ref[...] = ((other * lines + line) * 2 + half) * blocks + index
    for copy in copies[:2]:
        copy.wait()
    vectors = stack_ref[0]
    hvectors = stack_ref[1]
    members = vectors.shape[0]
    top = jnp.sum(vectors * hvectors, axis=1, keepdims=True)
    bottom = jnp.sum(vectors * vectors, axis=1, keepdims=True)
    lane = lax.broadcasted_iota(jnp.int32, (members, LANES), 1)
    line = lax.broadcasted_iota(jnp.int32, (members, LANES), 0)
    spread = jnp.where(lane == line, top, 0.0) + jnp.where(lane == line + members, bottom, 0.0)
    sums = jnp.sum(spread, axis=0, keepdims=True)
    slots_ref[...] = jnp.broadcast_to(sums, slots_ref.shape)
    copies[2].wait()


def residual_kernel(
    sums_ref, stack_ref, lo_ref, hi_ref, hprevious_ref, residuals_ref, y_slots_ref, z_slots_ref
):
    x_hi, x_lo, _ = here()
    members = stack_ref.shape[1]
    sums = jnp.sum(sums_ref[...], axis=0, keepdims=True)
    lane = lax.broadcasted_iota(jnp.int32, (members, LANES), 1)
    line = lax.broadcasted_iota(jnp.int32, (members, LANES), 0)
    top = jnp.sum(jnp.where(lane == line, sums, 0.0), axis=1, keepdims=True)
    bottom = jnp.sum(jnp.where(lane == line + members, sums, 0.0), axis=1, keepdims=True)
    ritz_values = top / (bottom + EPSILON)
    residual = stack_ref[1] - ritz_values * stack_ref[0]
    lo_residual = lo_ref[1] - ritz_values * lo_ref[0]
    hi_residual = hi_ref[1] - ritz_values * hi_ref[0]
    residuals_ref[0] = residual
    residuals_ref[1] = lo_residual
    residuals_ref[2] = hi_residual
    blocks = residual.shape[1] // LANES
    for index in range(blocks):
        mine = block(residual, index)
        for slot in range(y_slots_ref.shape[0]):
            y_slots_ref[slot, x_lo * blocks + index] = mine
            y_slots_ref[slot, (1 - x_lo) * blocks + index] = block(lo_residual, index)
        for slot in range(z_slots_ref.shape[0]):
            z_slots_ref[slot, x_hi * blocks + index] = mine
            z_slots_ref[slot, (1 - x_hi) * blocks + index] = block(hi_residual, index)
    hvectors = stack_ref[1]
    basis = jnp.concatenate([stack_ref[0], residual, stack_ref[2]], axis=0)
    gram = exact_dot(basis, basis, NT)
    early = exact_dot(jnp.concatenate([hvectors, hprevious_ref[...]], axis=0), basis, NT)
    extra = [
        gram[:members],
        gram[members : 2 * members],
        gram[2 * members :],
        early[:members],
        early[members:],
    ]
    for index, part in enumerate(pack_rows(extra)):
        for slot in range(y_slots_ref.shape[0]):
            y_slots_ref[slot, 2 * blocks + index] = part


def pack_rows(parts):
    first, second, third, fourth, fifth = parts
    members = first.shape[0]
    pieces = [fifth[:, i * members : (i + 1) * members] for i in range(3)]
    zero = jnp.zeros((members, members), jnp.float32)
    return [
        jnp.concatenate([first, second, pieces[0], pieces[1]], axis=1),
        jnp.concatenate([third, fourth, pieces[2], zero], axis=1),
    ]


def unpack_rows(one, two):
    members = one.shape[0]
    wide = 3 * members
    fifth = jnp.concatenate([one[:, 2 * wide :], two[:, 2 * wide : 2 * wide + members]], axis=1)
    return [one[:, :wide], one[:, wide : 2 * wide], two[:, :wide], two[:, wide : 2 * wide], fifth]


def factor_kernel(sums_ref, far_ref, inverse_ref, early_ref):
    extras = [sums_ref[index] + far_ref[index] for index in range(2)]
    members = extras[0].shape[0]
    order = 3 * members
    first, second, third, fourth, fifth = unpack_rows(*extras)
    early_ref[...] = jnp.concatenate([fourth, fifth], axis=0)
    gram = jnp.concatenate([first, second, third], axis=0)
    line = lax.broadcasted_iota(jnp.int32, (order, order), 0)
    lane = lax.broadcasted_iota(jnp.int32, (order, order), 1)
    work = jnp.concatenate([gram, jnp.where(line == lane, 1.0, 0.0)], axis=1)
    rows = lax.broadcasted_iota(jnp.int32, (order, 1), 0)
    for step in range(order):
        pivot = work[step : step + 1, step : step + 1]
        scale = lax.rsqrt(pivot)
        scale = scale * (1.5 - 0.5 * pivot * scale * scale)
        lead = work[step : step + 1, :] * scale
        column = work[:, step : step + 1] * scale
        work = jnp.where(rows == step, lead, jnp.where(rows > step, work - column * lead, work))
    inverse_ref[...] = work[:, order:]


def orthonormal_kernel(inverse_ref, stack_ref, residuals_ref, out_ref, *, row_scale):
    rows = jnp.concatenate([stack_ref[0], residuals_ref[0], stack_ref[2]], axis=0)
    out_ref[...] = exact_dot(inverse_ref[...] * row_scale, rows, NN)


def orthonormal_image_kernel(
    inverse_ref, stack_ref, image_ref, lo_ref, hi_ref, hprevious_ref, out_ref, *, row_scale
):
    image = image_ref[...] + lo_ref[...] + hi_ref[...]
    rows = jnp.concatenate([stack_ref[1], image, hprevious_ref[...]], axis=0)
    out_ref[...] = exact_dot(inverse_ref[...] * row_scale, rows, NN)


def sum_peers(parts_ref, index):
    part = parts_ref[0, index]
    for peer in range(1, parts_ref.shape[0]):
        part = part + parts_ref[peer, index]
    return part


def image_kernel(
    y_parts_ref,
    z_parts_ref,
    stack_ref,
    lo_ref,
    hi_ref,
    residuals_ref,
    image_ref,
    to_lo_ref,
    to_hi_ref,
    slots_ref,
):
    x_hi, x_lo, _ = here()
    blocks = image_ref.shape[1] // LANES
    for index in range(blocks):
        lanes = slice(index * LANES, (index + 1) * LANES)
        image_ref[:, lanes] = sum_peers(y_parts_ref, x_lo * blocks + index) + sum_peers(
            z_parts_ref, x_hi * blocks + index
        )
        to_lo_ref[:, lanes] = sum_peers(y_parts_ref, (1 - x_lo) * blocks + index)
        to_hi_ref[:, lanes] = sum_peers(z_parts_ref, (1 - x_hi) * blocks + index)
    late = None
    for rows, parts, place in ((image_ref, stack_ref, 0), (to_lo_ref, lo_ref, 1), (to_hi_ref, hi_ref, 2)):
        basis = jnp.concatenate([parts[0], residuals_ref[place], parts[2]], axis=0)
        product = exact_dot(rows[...], basis, NT)
        late = product if late is None else late + product
    half = late.shape[0] // 2
    pad = jnp.zeros((half, LANES // 2 - late.shape[1]), jnp.float32)
    packed = jnp.concatenate([late[:half], pad, late[half:], pad], axis=1)
    slots_ref[...] = jnp.broadcast_to(packed[None], slots_ref.shape)


def projected_kernel(received_ref, inverse_ref, early_ref, projected_ref):
    packed = jnp.sum(received_ref[...], axis=0)
    early = early_ref[...]
    members = early.shape[0] // 2
    wide = early.shape[1]
    half = LANES // 2
    late = jnp.concatenate([packed[:, :wide], packed[:, half : half + wide]], axis=0)
    mixed_t = jnp.concatenate([early[:members], late, early[members:]], axis=0)
    inverse = inverse_ref[...]
    half_done = exact_dot(inverse, mixed_t, NT)
    projected_ref[...] = exact_dot(half_done, inverse, NT)


def split_blocks(x_ref, split_ref, start, per_peer):
    def split(peer, carry):
        for index in range(per_peer):
            value = x_ref[peer, index]
            high = value.astype(jnp.bfloat16)
            low = (value - high.astype(jnp.float32)).astype(jnp.bfloat16)
            split_ref[start + peer * per_peer + index] = jnp.concatenate([high, low], axis=0)
        return carry

    lax.fori_loop(0, x_ref.shape[0], split, 0)


def tile_groups(count_ref, tiles_ref, split_ref, out_ref, source_of, target_of, dims, unroll):
    batch = tiles_ref.shape[0]
    live = count_ref[0, 0]
    start = pl.program_id(0) * batch
    members = split_ref.shape[1] // 2

    @pl.when(start < live)
    def _():
        def group(counter, carry):
            base = counter * unroll
            products = []
            for offset in range(unroll):
                slot = start + base + offset
                product = lax.dot_general(
                    split_ref[source_of(slot)],
                    tiles_ref[base + offset],
                    dims,
                    preferred_element_type=jnp.float32,
                )
                product = product[:members] + product[members:]
                products.append(jnp.where(slot < live, product, 0.0))
            for offset in range(unroll):
                target = target_of(start + base + offset)
                out_ref[target] = out_ref[target] + products[offset]
            return carry

        groups = jnp.minimum((live - start + unroll - 1) // unroll, batch // unroll)
        lax.fori_loop(0, groups, group, 0)


def backward_kernel(
    count_ref, rows_ref, cols_ref, tiles_ref, own_ref, other_ref, out_ref, split_ref, *, unroll
):
    peers, width = own_ref.shape[:2]
    per_peer = split_ref.shape[0] // (2 * peers)

    @pl.when(pl.program_id(0) == 0)
    def _():
        out_ref[...] = jnp.zeros_like(out_ref)
        split_blocks(own_ref, split_ref, 0, per_peer)
        split_blocks(other_ref, split_ref, peers * per_peer, per_peer)
        for index in range(per_peer, width):
            part = sum_peers(own_ref, index) + sum_peers(other_ref, index)
            for start in range(0, out_ref.shape[0], width):
                out_ref[start + index] = part

    tile_groups(
        count_ref,
        tiles_ref,
        split_ref,
        out_ref,
        lambda slot: rows_ref[0, 0, slot],
        lambda slot: cols_ref[0, 0, slot] + (width - per_peer) * (cols_ref[0, 0, slot] // per_peer),
        NN,
        unroll,
    )


def forward_kernel(
    count_ref,
    rows_ref,
    cols_ref,
    tiles_ref,
    x_ref,
    own_ref,
    other_ref,
    split_ref,
    totals_ref,
    *,
    unroll,
):
    peers, width = x_ref.shape[:2]

    @pl.when(pl.program_id(0) == 0)
    def _():
        totals_ref[...] = jnp.zeros_like(totals_ref)
        split_blocks(x_ref, split_ref, 0, width)

    tile_groups(
        count_ref,
        tiles_ref,
        split_ref,
        totals_ref,
        lambda slot: cols_ref[0, 0, slot],
        lambda slot: rows_ref[0, 0, slot],
        NT,
        unroll,
    )

    @pl.when(pl.program_id(0) == pl.num_programs(0) - 1)
    def _():
        half = totals_ref.shape[0] // 2
        own_ref[...] = totals_ref[:half]
        other_ref[...] = totals_ref[half:]


def tile_call(kernel, count, rows, cols, tiles, arrays, out_shapes, scratch, name):
    slots = tiles.shape[0]
    batch = math.gcd(slots, 96)
    unroll = math.gcd(batch, 24)

    def whole(shape):
        return pl.BlockSpec(
            shape, lambda i, count, rows, cols: (0,) * len(shape), pipeline_mode=pl.Buffered(1)
        )

    def tile_index(i, count, rows, cols):
        return (jnp.minimum(i, (count[0, 0] - 1) // batch), 0, 0)

    return pl.pallas_call(
        functools.partial(kernel, unroll=unroll),
        out_shape=[jax.ShapeDtypeStruct(shape, jnp.float32) for shape in out_shapes],
        grid_spec=pltpu.PrefetchScalarGridSpec(
            num_scalar_prefetch=3,
            grid=(slots // batch,),
            in_specs=[pl.BlockSpec((batch,) + tiles.shape[1:], tile_index)]
            + [whole(array.shape) for array in arrays],
            out_specs=[whole(shape) for shape in out_shapes],
            scratch_shapes=scratch,
        ),
        compiler_params=pltpu.CompilerParams(vmem_limit_bytes=VMEM_BYTES),
        name=name,
    )(count, rows, cols, tiles, *arrays)


def exchange(slots, axes, groups=None):
    return lax.all_to_all(slots, axes, 0, 0, axis_index_groups=groups, tiled=True)


def swap(array, axis, distance):
    return lax.ppermute(array, axis, [(i, i ^ distance) for i in range(lax.axis_size(axis))])


def on_device(
    tile_blocks, tile_rows, tile_cols, tile_count, vectors, hvectors, previous, hprevious
):
    n_row = lax.axis_size("row")
    n_col = lax.axis_size("col")
    everyone = ("row", "col")
    y_lines = n_col // 4
    z_lines = n_row // 2
    y_groups = [[x * n_col // 2 + y * 2 + core for y in range(y_lines)] for x in (0, 1) for core in (0, 1)]
    z_groups = [[z * 2 + x for z in range(z_lines)] for x in (0, 1)]
    members, piece = vectors.shape
    blocks = piece // LANES
    order = 3 * members
    row_scale = math.sqrt(piece * n_row * n_col)
    tiles = tile_blocks[0, 0]
    f32 = jnp.float32

    any_spec = pl.BlockSpec(memory_space=pl.ANY)
    vmem_spec = pl.BlockSpec(memory_space=pltpu.VMEM)
    sums, stack, rows = pl.pallas_call(
        stage_kernel,
        out_shape=[
            jax.ShapeDtypeStruct((n_row * n_col, LANES), f32),
            jax.ShapeDtypeStruct((3, members, piece), f32),
            jax.ShapeDtypeStruct(tile_rows.shape, jnp.int32),
        ],
        in_specs=[vmem_spec, any_spec, any_spec, any_spec],
        out_specs=[vmem_spec] * 3,
        scratch_shapes=[pltpu.SemaphoreType.DMA((3,))],
        name="stage",
    )(tile_rows, vectors, hvectors, previous)
    lo_stack = swap(stack, "col", n_col // 2)
    hi_stack = swap(stack, "row", 1)
    sums = exchange(sums, everyone)
    pair = 2 * blocks
    residuals, y_slots, z_slots = call(
        residual_kernel,
        [
            (3, members, piece),
            (y_lines, pair + 2, members, LANES),
            (z_lines, pair, members, LANES),
        ],
        "residual",
    )(sums, stack, lo_stack, hi_stack, hprevious)
    own_range = exchange(y_slots, "col", y_groups)
    other_range = swap(own_range, "col", 1)
    col_range = exchange(z_slots, "row", z_groups)
    (col_totals,) = tile_call(
        backward_kernel,
        tile_count,
        rows,
        tile_cols,
        tiles,
        (own_range, other_range),
        [(z_lines * (pair + 2), members, LANES)],
        [pltpu.VMEM((2 * y_lines * pair, 2 * members, LANES), jnp.bfloat16)],
        "backward_tiles",
    )
    z_parts = exchange(col_totals.reshape(z_lines, pair + 2, members, LANES), "row", z_groups)
    half = (y_lines * pair, members, LANES)
    own_totals, other_totals = tile_call(
        forward_kernel,
        tile_count,
        rows,
        tile_cols,
        tiles,
        (col_range,),
        [half, half],
        [
            pltpu.VMEM((z_lines * pair, 2 * members, LANES), jnp.bfloat16),
            pltpu.VMEM((2 * y_lines * pair, members, LANES), f32),
        ],
        "forward_tiles",
    )
    totals = own_totals + swap(other_totals, "col", 1)
    y_parts = exchange(totals.reshape(y_lines, pair, members, LANES), "col", y_groups)
    gram_sums = jnp.sum(z_parts[:, pair:], axis=0)
    gram_sums = gram_sums + swap(gram_sums, "col", n_col // 2)
    gram_far = swap(gram_sums, "row", 1)
    image, to_lo, to_hi, slots = call(
        image_kernel,
        [(members, piece)] * 3 + [(n_row * n_col, members // 2, LANES)],
        "image",
    )(y_parts, z_parts, stack, lo_stack, hi_stack, residuals)
    late = exchange(slots, everyone)
    from_lo = swap(to_lo, "col", n_col // 2)
    from_hi = swap(to_hi, "row", 1)
    inverse, early = call(factor_kernel, [(order, order), (2 * members, order)], "factor")(
        gram_sums, gram_far
    )
    (orthonormal,) = call(
        functools.partial(orthonormal_kernel, row_scale=row_scale), [(order, piece)], "orthonormal"
    )(inverse, stack, residuals)
    (orthonormal_image,) = call(
        functools.partial(orthonormal_image_kernel, row_scale=row_scale),
        [(order, piece)],
        "orthonormal_image",
    )(inverse, stack, image, from_lo, from_hi, hprevious)
    (projected,) = call(projected_kernel, [(order, order)], "projected")(late, inverse, early)
    return (orthonormal, orthonormal_image, projected)


def solution(mesh):
    in_specs = (
        P("row", "col", None, None, None),
        P("row", "col", None),
        P("row", "col", None),
        P("row", "col"),
        P(None, ("row", "col")),
        P(None, ("row", "col")),
        P(None, ("row", "col")),
        P(None, ("row", "col")),
    )
    out_specs = (P(None, ("row", "col")), P(None, ("row", "col")), P())
    return jax.shard_map(
        on_device, mesh=mesh, in_specs=in_specs, out_specs=out_specs, check_vma=False
    )
```

time: 122 us -> 117 us (0.959)
  waiting for transfers between devices: 27.5 us -> 12.6 us
  starting transfers between devices: 15.8 us -> 29.9 us
  blocking collectives: 48.5 us -> 42.3 us
  Pallas kernels: 24.4 us -> 26.4 us
    all_to_all x3, waiting for transfers between devices: 27.5 us -> 3.39 us  [exchange(): lax.all_to_all(slots, axes, 0, 0, axis_index_groups=groups, tiled=True)]
    ppermute x0 -> x8, starting transfers between devices: none -> 11.4 us  [swap(): lax.ppermute(array, axis, [(i, i ^ distance) for i in range(lax.axis_size...]
    ppermute x0 -> x8, waiting for transfers between devices: none -> 9.26 us  [swap(): lax.ppermute(array, axis, [(i, i ^ distance) for i in range(lax.axis_size...]
    all_to_all x3, blocking collectives: 48.5 us -> 42.3 us  [exchange(): lax.all_to_all(slots, axes, 0, 0, axis_index_groups=groups, tiled=True)]
    all_to_all x3, starting transfers between devices: 15.8 us -> 18.4 us  [exchange(): lax.all_to_all(slots, axes, 0, 0, axis_index_groups=groups, tiled=True)]
    pallas_call x8 -> x7, Pallas kernels: 18.7 us -> 20.8 us  [the longest x2 13.4 us: tile_call(): pl.pallas_call(functools.partial(kernel, unroll=unroll), out_shape=[jax.S...]
    unnamed x20 -> x16, local copies, waits for them, and re-layouts: 3.38 us -> 3.14 us
  transfers between devices with their start and end apart: 3 -> 11, of which waited for: 3 -> 4; matrix products, arithmetic and copies ran while one was open for 0% -> 1% of each run, Pallas kernels for 17% -> 17%
where the time goes in v2:
time: 117 us
  blocking collectives  42.3 us (36%)
  starting transfers between devices  29.9 us (26%)
  Pallas kernels  26.4 us (23%)
  waiting for transfers between devices  12.6 us (11%)
  local copies, waits for them, and re-layouts  3.14 us (3%)
  between operations  1.38 us (1%)
    all_to_all x3, blocking collectives, exchange(): lax.all_to_all(slots, axes, 0, 0, axis_index_groups=groups, tiled=True)  42.3 us
    all_to_all x3, starting transfers between devices, exchange(): lax.all_to_all(slots, axes, 0, 0, axis_index_groups=groups, tiled=True)  18.4 us
    pallas_call x2, Pallas kernels, tile_call(): pl.pallas_call(functools.partial(kernel, unroll=unroll), out_shape=[jax.S...  13.4 us
    ppermute x8, starting transfers between devices, swap(): lax.ppermute(array, axis, [(i, i ^ distance) for i in range(lax.axis_size...  11.4 us
    ppermute x8, waiting for transfers between devices, swap(): lax.ppermute(array, axis, [(i, i ^ distance) for i in range(lax.axis_size...  9.26 us
    pallas_call x1, Pallas kernels, on_device(): call(factor_kernel, [(order, order), (2 * members, order)], 'factor')  4.48 us
    all_to_all x3, waiting for transfers between devices, exchange(): lax.all_to_all(slots, axes, 0, 0, axis_index_groups=groups, tiled=True)  3.39 us
    unnamed x16, local copies, waits for them, and re-layouts  3.14 us
  transfers between devices with their start and end apart: 11, of which 4 were waited for; matrix products, arithmetic and copies ran while one was open for 1% of the time, Pallas kernels for 17%

profile of v2, /device:TPU:1, one launch (start us, length us, event | category | flops | bytes accessed | tf_op | source)
XLA Modules:
  0.0 116.7 jit_solution(1283606511997255947)
XLA Ops:
  0.6 0.0 copy-start.5
  0.6 2.4 %stage.1 = (f32[128,128]{1,0:T(8,128)}, f32[3,16,1024]{2,1,0:T(8,128)}, s32[1,1,384]{2,1,0:T(1,128)}) custom-call(s32[1,1,384]{2,1,0:T(1,128)} %rows_ref.1, f32[16,1024]{1,0:T(8,128)} %vectors_hbm.1, f32[16,1024]{1,0:T(8,128)} %hvectors_hbm.1, f32[16,1024]{1,0:T(8,128)} %previous_hbm.1), custom_call_target="tpu_custom_call" | custom-call | tf_op jit(solution)/shard_map/stage/pallas_call | solution.py:387
  3.0 0.0 copy-start.7
  3.0 3.7 %collective-permute-start.1 = (f32[3,16,1024]{2,1,0:T(8,128)}, f32[3,16,1024]{2,1,0:T(8,128)S(1)}, u32[]{:S(2)}, u32[]{:S(2)}) collective-permute-start(f32[3,16,1024]{2,1,0:T(8,128)} %get-tuple-element.19.stack_ref), channel_id=1, source_target_pairs={{0,16},{16,0},{32,48},{48,32},{64,80},{80,64},{96,112},{112,96},{1... | collective-permute-start | bytes 589832 | tf_op jit(solution)/shard_map/ppermute | solution.py:365
  6.7 0.3 collective-permute-start
  7.0 19.8 %all_to_all.36 = f32[128,1,128]{2,1,0:T(1,128)S(1)} all-to-all(f32[128,1,128]{2,1,0:T(1,128)} %bitcast.11), channel_id=1, replica_groups=mesh['row'=8,'col'=16] {'row','col'}, dimensions={0} | all-to-all | bytes 131072 | tf_op jit(solution)/shard_map/all_to_all | solution.py:361
  26.8 0.0 collective-permute-done.1.hi_ref
  26.8 0.0 collective-permute-done.lo_ref
  26.8 0.0 copy-start
  26.8 0.9 copy-done
  27.7 0.0 copy-start.2
  27.7 0.8 copy-done.2
  28.5 1.5 %residual.1 = (f32[3,16,1024]{2,1,0:T(8,128)S(1)}, f32[4,18,16,128]{3,2,1,0:T(8,128)}, f32[4,16,16,128]{3,2,1,0:T(8,128)S(1)}) custom-call(f32[128,128]{1,0:T(8,128)S(1)} %bitcast.8, f32[3,16,1024]{2,1,0:T(8,128)S(1)} %copy-done, f32[3,16,1024]{2,1,0:T(8,128)S(1)} %collective-permute-done.lo_ref, f32[3,16,1024]{2,1,0:T(8,128)S(1)} %collective-permute-done.1.hi_ref, ...), custom_call_target="tpu_custom_call" | custom-call | tf_op jit(solution)/shard_map/residual/pallas_call | solution.py:403
  30.0 10.9 %all_to_all.37.x_ref = f32[4,16,16,128]{3,2,1,0:T(8,128)S(1)} all-to-all(f32[4,16,16,128]{3,2,1,0:T(8,128)S(1)} %get-tuple-element.23), channel_id=1, replica_groups={{0,32,64,96},{16,48,80,112},{1,33,65,97},{17,49,81,113},{2,34,66,98},{1..., dimensions={0} | all-to-all | bytes 1048576 | tf_op jit(solution)/shard_map/all_to_all | solution.py:361
  40.9 3.5 %all-to-all-start.1 = ((f32[4,18,16,128]{3,2,1,0:T(8,128)}), f32[4,18,16,128]{3,2,1,0:T(8,128)S(1)}, u32[]{:S(2)}, u32[]{:S(2)}) async-start(f32[4,18,16,128]{3,2,1,0:T(8,128)} %get-tuple-element.20), calls=%async_computation.1 | async-start | bytes 1179648 | tf_op jit(solution)/shard_map/all_to_all | solution.py:361
  45.1 0.0 copy-start.4
  45.1 0.7 copy-done.4
  45.7 0.0 copy-start.6
  45.7 0.7 copy-done.6
  46.4 0.0 copy-start.1
  46.4 7.9 %forward_tiles.1 = (f32[64,16,128]{2,1,0:T(8,128)S(1)}, f32[64,16,128]{2,1,0:T(8,128)}) custom-call(s32[1,1]{1,0:T(1,128)S(6)} %copy.12.count_ref, s32[1,1,384]{2,1,0:T(1,128)S(1)} %copy-done.6, s32[1,1,384]{2,1,0:T(1,128)S(1)} %copy-done.4, bf16[384,128,128]{2,1,0:T(8,128)(2,1)} %bitcast.9, f32[4,16,16,128]{3,2,1,0:T(8,128)S(1)} %all_to_all.37.x_ref), custom_call_target="tpu_custom_call" | custom-call | tf_op jit(solution)/shard_map/forward_tiles/pallas_call | solution.py:344
  54.3 0.0 copy-start.3
  54.3 0.0 collective-permute-start.5
  54.3 0.0 all-to-all-done.1.own_ref
  54.3 1.2 %collective-permute-start.2 = (f32[4,18,16,128]{3,2,1,0:T(8,128)S(1)}, f32[4,18,16,128]{3,2,1,0:T(8,128)S(1)}, u32[]{:S(2)}, u32[]{:S(2)}) collective-permute-start(f32[4,18,16,128]{3,2,1,0:T(8,128)S(1)} %all-to-all-done.1.own_ref), channel_id=1, source_target_pairs={{0,1},{1,0},{2,3},{3,2},{4,5},{5,4},{6,7},{7,6},{8,9},{9,8},{10,11... | collective-permute-start | bytes 1769480 | tf_op jit(solution)/shard_map/ppermute | solution.py:365
  55.5 0.9 collective-permute-done.5
  56.4 0.9 add.7
  57.3 4.5 %all-to-all-start.4 = ((f32[4,16,16,128]{3,2,1,0:T(8,128)}), f32[4,16,16,128]{3,2,1,0:T(8,128)S(1)}, u32[]{:S(2)}, u32[]{:S(2)}) async-start(f32[4,16,16,128]{3,2,1,0:T(8,128)} %bitcast.5), calls=%async_computation.4 | async-start | bytes 1048576 | tf_op jit(solution)/shard_map/all_to_all | solution.py:361
  61.8 0.0 collective-permute-done.2.other_ref
  61.8 0.0 copy-done.5
  61.8 0.0 copy-done.7
  61.8 5.5 %backward_tiles.1 = f32[72,16,128]{2,1,0:T(8,128)S(1)} custom-call(s32[1,1]{1,0:T(1,128)S(6)} %copy.12.count_ref, s32[1,1,384]{2,1,0:T(1,128)S(1)} %copy-done.7, s32[1,1,384]{2,1,0:T(1,128)S(1)} %copy-done.5, bf16[384,128,128]{2,1,0:T(8,128)(2,1)} %bitcast.10, f32[4,18,16,128]{3,2,1,0:T(8,128)S(1)} %all-to-all-done.1.own_ref, ...), custom_call_target="tpu_custom_call" | custom-call | tf_op jit(solution)/shard_map/backward_tiles/pallas_call | solution.py:344
  67.3 3.4 %all-to-all-done.4.y_parts_ref = f32[4,16,16,128]{3,2,1,0:T(8,128)S(1)} async-done(((f32[4,16,16,128]{3,2,1,0:T(8,128)}), f32[4,16,16,128]{3,2,1,0:T(8,128)S(1)}, u32[]{:S(2)}, u32[]{:S(2)}) %all-to-all-start.4) | async-done | bytes 524320 | tf_op jit(solution)/shard_map/all_to_all | solution.py:361
  70.7 11.7 %all_to_all.38.z_parts_ref = f32[4,18,16,128]{3,2,1,0:T(8,128)S(1)} all-to-all(f32[4,18,16,128]{3,2,1,0:T(8,128)S(1)} %bitcast.7), channel_id=1, replica_groups={{0,32,64,96},{16,48,80,112},{1,33,65,97},{17,49,81,113},{2,34,66,98},{1..., dimensions={0} | all-to-all | bytes 1179648 | tf_op jit(solution)/shard_map/all_to_all | solution.py:361
  82.3 0.0 copy-done.1
  82.3 1.5 %image.1 = (f32[16,1024]{1,0:T(8,128)S(1)}, f32[16,1024]{1,0:T(8,128)S(1)}, f32[16,1024]{1,0:T(8,128)S(1)}, f32[128,8,128]{2,1,0:T(8,128)}) custom-call(f32[4,16,16,128]{3,2,1,0:T(8,128)S(1)} %all-to-all-done.4.y_parts_ref, f32[4,18,16,128]{3,2,1,0:T(8,128)S(1)} %all_to_all.38.z_parts_ref, f32[3,16,1024]{2,1,0:T(8,128)S(1)} %copy-done.1, ...), custom_call_target="tpu_custom_call" | custom-call | tf_op jit(solution)/shard_map/image/pallas_call | solution.py:447
  83.8 10.5 %all-to-all-start.5 = ((f32[128,8,128]{2,1,0:T(8,128)}), f32[128,8,128]{2,1,0:T(8,128)S(1)}, u32[]{:S(2)}, u32[]{:S(2)}) async-start(f32[128,8,128]{2,1,0:T(8,128)} %get-tuple-element.29), calls=%async_computation.5 | async-start | bytes 1048576 | tf_op jit(solution)/shard_map/all_to_all | solution.py:361
  94.4 1.5 %collective-permute-start.6 = (f32[16,1024]{1,0:T(8,128)S(1)}, f32[16,1024]{1,0:T(8,128)S(1)}, u32[]{:S(2)}, u32[]{:S(2)}) collective-permute-start(f32[16,1024]{1,0:T(8,128)S(1)} %get-tuple-element.27), channel_id=1, source_target_pairs={{0,8},{1,9},{2,10},{3,11},{4,12},{5,13},{6,14},{7,15},{8,0},{9,1},... | collective-permute-start | bytes 196616 | tf_op jit(solution)/shard_map/ppermute | solution.py:365
  95.8 2.4 %collective-permute-start.7 = (f32[16,1024]{1,0:T(8,128)S(1)}, f32[16,1024]{1,0:T(8,128)S(1)}, u32[]{:S(2)}, u32[]{:S(2)}) collective-permute-start(f32[16,1024]{1,0:T(8,128)S(1)} %get-tuple-element.28), channel_id=1, source_target_pairs={{0,16},{16,0},{32,48},{48,32},{64,80},{80,64},{96,112},{112,96},{1... | collective-permute-start | bytes 196616 | tf_op jit(solution)/shard_map/ppermute | solution.py:365
  98.2 0.0 collective-permute-start.3
  98.2 6.4 %collective-permute-done.3 = f32[2,16,128]{2,1,0:T(8,128)S(1)} collective-permute-done((f32[2,16,128]{2,1,0:T(8,128)S(1)}, f32[2,16,128]{2,1,0:T(8,128)S(1)}, u32[]{:S(2)}, u32[]{:S(2)}) %collective-permute-start.3) | collective-permute-done | bytes 16416 | tf_op jit(solution)/shard_map/ppermute | solution.py:365
  104.6 2.4 %collective-permute-start.4 = (f32[2,16,128]{2,1,0:T(8,128)S(1)}, f32[2,16,128]{2,1,0:T(8,128)S(1)}, u32[]{:S(2)}, u32[]{:S(2)}) collective-permute-start(f32[2,16,128]{2,1,0:T(8,128)S(1)} %add.6.sums_ref), channel_id=1, source_target_pairs={{0,16},{16,0},{32,48},{48,32},{64,80},{80,64},{96,112},{112,96},{1... | collective-permute-start | bytes 49160 | tf_op jit(solution)/shard_map/ppermute | solution.py:365
  107.0 1.9 %collective-permute-done.4.far_ref = f32[2,16,128]{2,1,0:T(8,128)S(1)} collective-permute-done((f32[2,16,128]{2,1,0:T(8,128)S(1)}, f32[2,16,128]{2,1,0:T(8,128)S(1)}, u32[]{:S(2)}, u32[]{:S(2)}) %collective-permute-start.4) | collective-permute-done | bytes 16416 | tf_op jit(solution)/shard_map/ppermute | solution.py:365
  109.0 4.5 %factor.1 = (f32[48,48]{1,0:T(8,128)S(1)}, f32[32,48]{1,0:T(8,128)S(1)}) custom-call(f32[2,16,128]{2,1,0:T(8,128)S(1)} %add.6.sums_ref, f32[2,16,128]{2,1,0:T(8,128)S(1)} %collective-permute-done.4.far_ref), custom_call_target="tpu_custom_call" | custom-call | tf_op jit(solution)/shard_map/factor/pallas_call | solution.py:455
  113.5 1.0 orthonormal.1
  114.5 0.0 collective-permute-done.6.lo_ref
  114.5 0.0 collective-permute-done.7.hi_ref
  114.5 0.0 copy-done.3
  114.5 1.0 orthonormal_image.1
  115.5 0.0 all-to-all-done.5.received_ref
  115.5 1.2 %projected.1 = f32[48,48]{1,0:T(8,128)} custom-call(f32[128,8,128]{2,1,0:T(8,128)S(1)} %all-to-all-done.5.received_ref, f32[48,48]{1,0:T(8,128)S(1)} %get-tuple-element.21.inverse_ref, f32[32,48]{1,0:T(8,128)S(1)} %get-tuple-element.30.early_ref), custom_call_target="tpu_custom_call" | custom-call | tf_op jit(solution)/shard_map/projected/pallas_call | solution.py:466
  (2 shorter events, 0.0 us)
Async XLA Ops:
  0.6 61.1 %copy-start.5 = (s32[1,1,384]{2,1,0:T(1,128)S(1)}, s32[1,1,384]{2,1,0:T(1,128)}, u32[]{:S(2)}) copy-start(s32[1,1,384]{2,1,0:T(1,128)} %cols_ref.3) | copy-start | bytes 4612
  3.0 58.7 %copy-start.7 = (s32[1,1,384]{2,1,0:T(1,128)S(1)}, s32[1,1,384]{2,1,0:T(1,128)}, u32[]{:S(2)}) copy-start(s32[1,1,384]{2,1,0:T(1,128)} %get-tuple-element.17.rows_ref) | copy-start | bytes 4612
  3.0 23.7 %collective-permute-start.1 = (f32[3,16,1024]{2,1,0:T(8,128)}, f32[3,16,1024]{2,1,0:T(8,128)S(1)}, u32[]{:S(2)}, u32[]{:S(2)}) collective-permute-start(f32[3,16,1024]{2,1,0:T(8,128)} %get-tuple-element.19.stack_ref), channel_id=1, source_target_pairs={{0,16},{16,0},{32,48},{48,32},{64,80},{80,64},{96,112},{112,96},{1... | collective-permute-start | bytes 589832 | tf_op jit(solution)/shard_map/ppermute | solution.py:365
  6.7 20.1 %collective-permute-start = (f32[3,16,1024]{2,1,0:T(8,128)}, f32[3,16,1024]{2,1,0:T(8,128)S(1)}, u32[]{:S(2)}, u32[]{:S(2)}) collective-permute-start(f32[3,16,1024]{2,1,0:T(8,128)} %get-tuple-element.19.stack_ref), channel_id=1, source_target_pairs={{0,8},{1,9},{2,10},{3,11},{4,12},{5,13},{6,14},{7,15},{8,0},{9,1},... | collective-permute-start | bytes 589832 | tf_op jit(solution)/shard_map/ppermute | solution.py:365
  26.8 0.9 copy-start
  27.7 0.8 copy-start.2
  40.9 13.4 %all-to-all-start.1 = ((f32[4,18,16,128]{3,2,1,0:T(8,128)}), f32[4,18,16,128]{3,2,1,0:T(8,128)S(1)}, u32[]{:S(2)}, u32[]{:S(2)}) async-start(f32[4,18,16,128]{3,2,1,0:T(8,128)} %get-tuple-element.20), calls=%async_computation.1 | async-start | bytes 1179648 | tf_op jit(solution)/shard_map/all_to_all | solution.py:361
  45.1 0.7 copy-start.4
  45.7 0.7 copy-start.6
  46.4 35.9 %copy-start.1 = (f32[3,16,1024]{2,1,0:T(8,128)S(1)}, f32[3,16,1024]{2,1,0:T(8,128)}, u32[]{:S(2)}) copy-start(f32[3,16,1024]{2,1,0:T(8,128)} %get-tuple-element.19.stack_ref) | copy-start | bytes 589828
  54.3 60.2 %copy-start.3 = (f32[16,1024]{1,0:T(8,128)S(1)}, f32[16,1024]{1,0:T(8,128)}, u32[]{:S(2)}) copy-start(f32[16,1024]{1,0:T(8,128)} %hprevious_ref.3) | copy-start | bytes 196612
  54.3 2.1 %collective-permute-start.5 = (f32[64,16,128]{2,1,0:T(8,128)}, f32[64,16,128]{2,1,0:T(8,128)S(1)}, u32[]{:S(2)}, u32[]{:S(2)}) collective-permute-start(f32[64,16,128]{2,1,0:T(8,128)} %get-tuple-element.25), channel_id=1, source_target_pairs={{0,1},{1,0},{2,3},{3,2},{4,5},{5,4},{6,7},{7,6},{8,9},{9,8},{10,11... | collective-permute-start | bytes 1572872 | tf_op jit(solution)/shard_map/ppermute | solution.py:365
  54.3 7.4 %collective-permute-start.2 = (f32[4,18,16,128]{3,2,1,0:T(8,128)S(1)}, f32[4,18,16,128]{3,2,1,0:T(8,128)S(1)}, u32[]{:S(2)}, u32[]{:S(2)}) collective-permute-start(f32[4,18,16,128]{3,2,1,0:T(8,128)S(1)} %all-to-all-done.1.own_ref), channel_id=1, source_target_pairs={{0,1},{1,0},{2,3},{3,2},{4,5},{5,4},{6,7},{7,6},{8,9},{9,8},{10,11... | collective-permute-start | bytes 1769480 | tf_op jit(solution)/shard_map/ppermute | solution.py:365
  57.3 13.4 %all-to-all-start.4 = ((f32[4,16,16,128]{3,2,1,0:T(8,128)}), f32[4,16,16,128]{3,2,1,0:T(8,128)S(1)}, u32[]{:S(2)}, u32[]{:S(2)}) async-start(f32[4,16,16,128]{3,2,1,0:T(8,128)} %bitcast.5), calls=%async_computation.4 | async-start | bytes 1048576 | tf_op jit(solution)/shard_map/all_to_all | solution.py:361
  83.8 31.6 %all-to-all-start.5 = ((f32[128,8,128]{2,1,0:T(8,128)}), f32[128,8,128]{2,1,0:T(8,128)S(1)}, u32[]{:S(2)}, u32[]{:S(2)}) async-start(f32[128,8,128]{2,1,0:T(8,128)} %get-tuple-element.29), calls=%async_computation.5 | async-start | bytes 1048576 | tf_op jit(solution)/shard_map/all_to_all | solution.py:361
  94.4 20.1 %collective-permute-start.6 = (f32[16,1024]{1,0:T(8,128)S(1)}, f32[16,1024]{1,0:T(8,128)S(1)}, u32[]{:S(2)}, u32[]{:S(2)}) collective-permute-start(f32[16,1024]{1,0:T(8,128)S(1)} %get-tuple-element.27), channel_id=1, source_target_pairs={{0,8},{1,9},{2,10},{3,11},{4,12},{5,13},{6,14},{7,15},{8,0},{9,1},... | collective-permute-start | bytes 196616 | tf_op jit(solution)/shard_map/ppermute | solution.py:365
  95.8 18.6 %collective-permute-start.7 = (f32[16,1024]{1,0:T(8,128)S(1)}, f32[16,1024]{1,0:T(8,128)S(1)}, u32[]{:S(2)}, u32[]{:S(2)}) collective-permute-start(f32[16,1024]{1,0:T(8,128)S(1)} %get-tuple-element.28), channel_id=1, source_target_pairs={{0,16},{16,0},{32,48},{48,32},{64,80},{80,64},{96,112},{112,96},{1... | collective-permute-start | bytes 196616 | tf_op jit(solution)/shard_map/ppermute | solution.py:365
  98.2 6.4 %collective-permute-start.3 = (f32[2,16,128]{2,1,0:T(8,128)S(1)}, f32[2,16,128]{2,1,0:T(8,128)S(1)}, u32[]{:S(2)}, u32[]{:S(2)}) collective-permute-start(f32[2,16,128]{2,1,0:T(8,128)S(1)} %slice_reduce_fusion), channel_id=1, source_target_pairs={{0,8},{1,9},{2,10},{3,11},{4,12},{5,13},{6,14},{7,15},{8,0},{9,1},... | collective-permute-start | bytes 49160 | tf_op jit(solution)/shard_map/ppermute | solution.py:365
  104.6 4.3 %collective-permute-start.4 = (f32[2,16,128]{2,1,0:T(8,128)S(1)}, f32[2,16,128]{2,1,0:T(8,128)S(1)}, u32[]{:S(2)}, u32[]{:S(2)}) collective-permute-start(f32[2,16,128]{2,1,0:T(8,128)S(1)} %add.6.sums_ref), channel_id=1, source_target_pairs={{0,16},{16,0},{32,48},{48,32},{64,80},{80,64},{96,112},{112,96},{1... | collective-permute-start | bytes 49160 | tf_op jit(solution)/shard_map/ppermute | solution.py:365

commit v3 on v2

--- a/solution.py
+++ b/solution.py
@@ -12,6 +12,7 @@
 HIGHEST_PRECISION = lax.Precision.HIGHEST
 LANES = 128
 VMEM_BYTES = 48 << 20
+STAGE_BYTES = 60 << 20
 NT = (((1,), (1,)), ((), ()))
 NN = (((1,), (0,)), ((), ()))
 
@@ -35,31 +36,14 @@
     return array[:, index * LANES : (index + 1) * LANES]
 
 
-def here():
-    row = lax.axis_index("row")
-    col = lax.axis_index("col")
-    return (lax.rem(row, 2), col // (lax.axis_size("col") // 2), lax.rem(col, 2))
-
-
-def stage_kernel(
-    rows_ref, vectors_hbm, hvectors_hbm, previous_hbm, slots_ref, stack_ref, rows_out_ref, arrived
-):
+def stage_kernel(vectors_hbm, hvectors_hbm, slots_ref, stack_ref, arrived):
     copies = [
         pltpu.make_async_copy(source, stack_ref.at[index], arrived.at[index])
-        for index, source in enumerate((vectors_hbm, hvectors_hbm, previous_hbm))
+        for index, source in enumerate((vectors_hbm, hvectors_hbm))
     ]
     for copy in copies:
         copy.start()
-    rows = rows_ref[...]
-    core = lax.rem(lax.axis_index("col"), 2)
-    lines = lax.axis_size("col") // 4
-    blocks = stack_ref.shape[2] // LANES
-    index, peer = rows % blocks, rows // blocks
-    other = jnp.where(peer % 2 == core, 0, 1)
-    line = (peer // 2) % lines
-    half = peer // (2 * lines)
-    rows_out_ref[...] = ((other * lines + line) * 2 + half) * blocks + index
-    for copy in copies[:2]:
+    for copy in copies:
         copy.wait()
     vectors = stack_ref[0]
     hvectors = stack_ref[1]
@@ -71,13 +55,57 @@
     spread = jnp.where(lane == line, top, 0.0) + jnp.where(lane == line + members, bottom, 0.0)
     sums = jnp.sum(spread, axis=0, keepdims=True)
     slots_ref[...] = jnp.broadcast_to(sums, slots_ref.shape)
-    copies[2].wait()
+
+
+def prepare_kernel(
+    rows_ref,
+    stack_hbm,
+    previous_hbm,
+    hprevious_hbm,
+    rows_out_ref,
+    stack_ref,
+    previous_ref,
+    hprevious_ref,
+    arrived,
+):
+    copies = [
+        pltpu.make_async_copy(source, target, arrived.at[index])
+        for index, (source, target) in enumerate(
+            (
+                (stack_hbm, stack_ref),
+                (previous_hbm, previous_ref),
+                (hprevious_hbm, hprevious_ref),
+            )
+        )
+    ]
+    for copy in copies:
+        copy.start()
+    rows = rows_ref[...]
+    core = lax.rem(lax.axis_index("col"), 2)
+    chips = lax.axis_size("col") // 2
+    blocks = previous_ref.shape[1] // LANES
+    index, peer = rows % blocks, rows // blocks
+    other = jnp.where(peer % 2 == core, 0, 1)
+    rows_out_ref[...] = (other * chips + peer // 2) * blocks + index
+    for copy in copies:
+        copy.wait()
 
 
 def residual_kernel(
-    sums_ref, stack_ref, lo_ref, hi_ref, hprevious_ref, residuals_ref, y_slots_ref, z_slots_ref
-):
-    x_hi, x_lo, _ = here()
+    sums_ref,
+    stack_ref,
+    previous_ref,
+    hprevious_ref,
+    far_hbm,
+    residuals_ref,
+    col_slots_ref,
+    row_slots_ref,
+    far_ref,
+    arrived,
+):
+    fetch = pltpu.make_async_copy(far_hbm, far_ref, arrived)
+    fetch.start()
+    x_hi = lax.rem(lax.axis_index("row"), 2)
     members = stack_ref.shape[1]
     sums = jnp.sum(sums_ref[...], axis=0, keepdims=True)
     lane = lax.broadcasted_iota(jnp.int32, (members, LANES), 1)
@@ -85,23 +113,17 @@
     top = jnp.sum(jnp.where(lane == line, sums, 0.0), axis=1, keepdims=True)
     bottom = jnp.sum(jnp.where(lane == line + members, sums, 0.0), axis=1, keepdims=True)
     ritz_values = top / (bottom + EPSILON)
-    residual = stack_ref[1] - ritz_values * stack_ref[0]
-    lo_residual = lo_ref[1] - ritz_values * lo_ref[0]
-    hi_residual = hi_ref[1] - ritz_values * hi_ref[0]
+    hvectors = stack_ref[1]
+    residual = hvectors - ritz_values * stack_ref[0]
     residuals_ref[0] = residual
-    residuals_ref[1] = lo_residual
-    residuals_ref[2] = hi_residual
     blocks = residual.shape[1] // LANES
     for index in range(blocks):
         mine = block(residual, index)
-        for slot in range(y_slots_ref.shape[0]):
-            y_slots_ref[slot, x_lo * blocks + index] = mine
-            y_slots_ref[slot, (1 - x_lo) * blocks + index] = block(lo_residual, index)
-        for slot in range(z_slots_ref.shape[0]):
-            z_slots_ref[slot, x_hi * blocks + index] = mine
-            z_slots_ref[slot, (1 - x_hi) * blocks + index] = block(hi_residual, index)
-    hvectors = stack_ref[1]
-    basis = jnp.concatenate([stack_ref[0], residual, stack_ref[2]], axis=0)
+        for slot in range(col_slots_ref.shape[0]):
+            col_slots_ref[slot, index] = mine
+        for slot in range(row_slots_ref.shape[0]):
+            row_slots_ref[slot, x_hi * blocks + index] = mine
+    basis = jnp.concatenate([stack_ref[0], residual, previous_ref[...]], axis=0)
     gram = exact_dot(basis, basis, NT)
     early = exact_dot(jnp.concatenate([hvectors, hprevious_ref[...]], axis=0), basis, NT)
     extra = [
@@ -112,8 +134,14 @@
         early[members:],
     ]
     for index, part in enumerate(pack_rows(extra)):
-        for slot in range(y_slots_ref.shape[0]):
-            y_slots_ref[slot, 2 * blocks + index] = part
+        for slot in range(col_slots_ref.shape[0]):
+            col_slots_ref[slot, blocks + index] = part
+    fetch.wait()
+    far_residual = far_ref[1] - ritz_values * far_ref[0]
+    residuals_ref[1] = far_residual
+    for index in range(blocks):
+        for slot in range(row_slots_ref.shape[0]):
+            row_slots_ref[slot, (1 - x_hi) * blocks + index] = block(far_residual, index)
 
 
 def pack_rows(parts):
@@ -155,15 +183,17 @@
     inverse_ref[...] = work[:, order:]
 
 
-def orthonormal_kernel(inverse_ref, stack_ref, residuals_ref, out_ref, *, row_scale):
-    rows = jnp.concatenate([stack_ref[0], residuals_ref[0], stack_ref[2]], axis=0)
+def orthonormal_kernel(
+    inverse_ref, stack_ref, residuals_ref, previous_ref, out_ref, *, row_scale
+):
+    rows = jnp.concatenate([stack_ref[0], residuals_ref[0], previous_ref[...]], axis=0)
     out_ref[...] = exact_dot(inverse_ref[...] * row_scale, rows, NN)
 
 
 def orthonormal_image_kernel(
-    inverse_ref, stack_ref, image_ref, lo_ref, hi_ref, hprevious_ref, out_ref, *, row_scale
-):
-    image = image_ref[...] + lo_ref[...] + hi_ref[...]
+    inverse_ref, stack_ref, image_ref, far_ref, hprevious_ref, out_ref, *, row_scale
+):
+    image = image_ref[...] + far_ref[...]
     rows = jnp.concatenate([stack_ref[1], image, hprevious_ref[...]], axis=0)
     out_ref[...] = exact_dot(inverse_ref[...] * row_scale, rows, NN)
 
@@ -176,31 +206,29 @@
 
 
 def image_kernel(
-    y_parts_ref,
-    z_parts_ref,
+    col_parts_ref,
+    row_parts_ref,
     stack_ref,
-    lo_ref,
-    hi_ref,
+    previous_ref,
+    far_ref,
+    far_previous_ref,
     residuals_ref,
     image_ref,
-    to_lo_ref,
-    to_hi_ref,
+    to_far_ref,
     slots_ref,
 ):
-    x_hi, x_lo, _ = here()
+    x_hi = lax.rem(lax.axis_index("row"), 2)
     blocks = image_ref.shape[1] // LANES
     for index in range(blocks):
         lanes = slice(index * LANES, (index + 1) * LANES)
-        image_ref[:, lanes] = sum_peers(y_parts_ref, x_lo * blocks + index) + sum_peers(
-            z_parts_ref, x_hi * blocks + index
+        image_ref[:, lanes] = sum_peers(col_parts_ref, index) + sum_peers(
+            row_parts_ref, x_hi * blocks + index
         )
-        to_lo_ref[:, lanes] = sum_peers(y_parts_ref, (1 - x_lo) * blocks + index)
-        to_hi_ref[:, lanes] = sum_peers(z_parts_ref, (1 - x_hi) * blocks + index)
-    late = None
-    for rows, parts, place in ((image_ref, stack_ref, 0), (to_lo_ref, lo_ref, 1), (to_hi_ref, hi_ref, 2)):
-        basis = jnp.concatenate([parts[0], residuals_ref[place], parts[2]], axis=0)
-        product = exact_dot(rows[...], basis, NT)
-        late = product if late is None else late + product
+        to_far_ref[:, lanes] = sum_peers(row_parts_ref, (1 - x_hi) * blocks + index)
+    basis = jnp.concatenate([stack_ref[0], residuals_ref[0], previous_ref[...]], axis=0)
+    late = exact_dot(image_ref[...], basis, NT)
+    basis = jnp.concatenate([far_ref[0], residuals_ref[1], far_previous_ref[...]], axis=0)
+    late = late + exact_dot(to_far_ref[...], basis, NT)
     half = late.shape[0] // 2
     pad = jnp.zeros((half, LANES // 2 - late.shape[1]), jnp.float32)
     packed = jnp.concatenate([late[:half], pad, late[half:], pad], axis=1)
@@ -267,15 +295,17 @@
 ):
     peers, width = own_ref.shape[:2]
     per_peer = split_ref.shape[0] // (2 * peers)
+    extra = width - per_peer
+    pair = 2 * per_peer
 
     @pl.when(pl.program_id(0) == 0)
     def _():
         out_ref[...] = jnp.zeros_like(out_ref)
         split_blocks(own_ref, split_ref, 0, per_peer)
         split_blocks(other_ref, split_ref, peers * per_peer, per_peer)
-        for index in range(per_peer, width):
-            part = sum_peers(own_ref, index) + sum_peers(other_ref, index)
-            for start in range(0, out_ref.shape[0], width):
+        for index in range(extra):
+            part = sum_peers(own_ref, per_peer + index) + sum_peers(other_ref, per_peer + index)
+            for start in range(pair, out_ref.shape[0], pair + extra):
                 out_ref[start + index] = part
 
     tile_groups(
@@ -284,7 +314,7 @@
         split_ref,
         out_ref,
         lambda slot: rows_ref[0, 0, slot],
-        lambda slot: cols_ref[0, 0, slot] + (width - per_peer) * (cols_ref[0, 0, slot] // per_peer),
+        lambda slot: cols_ref[0, 0, slot] + extra * (cols_ref[0, 0, slot] // pair),
         NN,
         unroll,
     )
@@ -371,47 +401,74 @@
     n_row = lax.axis_size("row")
     n_col = lax.axis_size("col")
     everyone = ("row", "col")
-    y_lines = n_col // 4
-    z_lines = n_row // 2
-    y_groups = [[x * n_col // 2 + y * 2 + core for y in range(y_lines)] for x in (0, 1) for core in (0, 1)]
-    z_groups = [[z * 2 + x for z in range(z_lines)] for x in (0, 1)]
+    chips = n_col // 2
+    lines = n_row // 2
+    core_groups = [[2 * chip + core for chip in range(chips)] for core in (0, 1)]
+    z_groups = [[2 * line + x for line in range(lines)] for x in (0, 1)]
     members, piece = vectors.shape
     blocks = piece // LANES
+    pair = 2 * blocks
     order = 3 * members
     row_scale = math.sqrt(piece * n_row * n_col)
     tiles = tile_blocks[0, 0]
     f32 = jnp.float32
 
-    any_spec = pl.BlockSpec(memory_space=pl.ANY)
+    hbm_spec = pl.BlockSpec(memory_space=pl.ANY)
     vmem_spec = pl.BlockSpec(memory_space=pltpu.VMEM)
-    sums, stack, rows = pl.pallas_call(
+    params = pltpu.CompilerParams(vmem_limit_bytes=VMEM_BYTES)
+    sums, stack = pl.pallas_call(
         stage_kernel,
         out_shape=[
             jax.ShapeDtypeStruct((n_row * n_col, LANES), f32),
-            jax.ShapeDtypeStruct((3, members, piece), f32),
+            jax.ShapeDtypeStruct((2, members, piece), f32),
+        ],
+        in_specs=[hbm_spec, hbm_spec],
+        out_specs=[vmem_spec] * 2,
+        scratch_shapes=[pltpu.SemaphoreType.DMA((2,))],
+        compiler_params=pltpu.CompilerParams(vmem_limit_bytes=STAGE_BYTES),
+        name="stage",
+    )(vectors, hvectors)
+    far_stack = swap(stack, "row", 1)
+    rows, stack, previous, hprevious = pl.pallas_call(
+        prepare_kernel,
+        out_shape=[
             jax.ShapeDtypeStruct(tile_rows.shape, jnp.int32),
+            jax.ShapeDtypeStruct(stack.shape, f32),
+            jax.ShapeDtypeStruct(previous.shape, f32),
+            jax.ShapeDtypeStruct(hprevious.shape, f32),
         ],
-        in_specs=[vmem_spec, any_spec, any_spec, any_spec],
-        out_specs=[vmem_spec] * 3,
+        in_specs=[vmem_spec, hbm_spec, hbm_spec, hbm_spec],
+        out_specs=[vmem_spec] * 4,
         scratch_shapes=[pltpu.SemaphoreType.DMA((3,))],
-        name="stage",
-    )(tile_rows, vectors, hvectors, previous)
-    lo_stack = swap(stack, "col", n_col // 2)
-    hi_stack = swap(stack, "row", 1)
+        compiler_params=params,
+        name="prepare",
+    )(tile_rows, stack, previous, hprevious)
     sums = exchange(sums, everyone)
-    pair = 2 * blocks
-    residuals, y_slots, z_slots = call(
+    sums, rows, stack, previous, hprevious = lax.optimization_barrier(
+        (sums, rows, stack, previous, hprevious)
+    )
+    far_previous = swap(previous, "row", 1)
+    residuals, col_slots, row_slots, far_stack = pl.pallas_call(
         residual_kernel,
-        [
-            (3, members, piece),
-            (y_lines, pair + 2, members, LANES),
-            (z_lines, pair, members, LANES),
+        out_shape=[
+            jax.ShapeDtypeStruct(shape, f32)
+            for shape in (
+                (2, members, piece),
+                (chips, blocks + 2, members, LANES),
+                (lines, pair, members, LANES),
+                (2, members, piece),
+            )
         ],
-        "residual",
-    )(sums, stack, lo_stack, hi_stack, hprevious)
-    own_range = exchange(y_slots, "col", y_groups)
+        in_specs=[vmem_spec] * 4 + [hbm_spec],
+        out_specs=[vmem_spec] * 4,
+        scratch_shapes=[pltpu.SemaphoreType.DMA(())],
+        compiler_params=params,
+        name="residual",
+    )(sums, stack, previous, hprevious, far_stack)
+    own_range = exchange(col_slots, "col", core_groups)
+    own_range, row_slots = lax.optimization_barrier((own_range, row_slots))
     other_range = swap(own_range, "col", 1)
-    col_range = exchange(z_slots, "row", z_groups)
+    col_range = exchange(row_slots, "row", z_groups)
     (col_totals,) = tile_call(
         backward_kernel,
         tile_count,
@@ -419,12 +476,13 @@
         tile_cols,
         tiles,
         (own_range, other_range),
-        [(z_lines * (pair + 2), members, LANES)],
-        [pltpu.VMEM((2 * y_lines * pair, 2 * members, LANES), jnp.bfloat16)],
+        [(lines * (pair + 2), members, LANES)],
+        [pltpu.VMEM((n_col * blocks, 2 * members, LANES), jnp.bfloat16)],
         "backward_tiles",
     )
-    z_parts = exchange(col_totals.reshape(z_lines, pair + 2, members, LANES), "row", z_groups)
-    half = (y_lines * pair, members, LANES)
+    col_totals, col_range = lax.optimization_barrier((col_totals, col_range))
+    row_parts = exchange(col_totals.reshape(lines, pair + 2, members, LANES), "row", z_groups)
+    half = (chips * blocks, members, LANES)
     own_totals, other_totals = tile_call(
         forward_kernel,
         tile_count,
@@ -434,35 +492,37 @@
         (col_range,),
         [half, half],
         [
-            pltpu.VMEM((z_lines * pair, 2 * members, LANES), jnp.bfloat16),
-            pltpu.VMEM((2 * y_lines * pair, members, LANES), f32),
+            pltpu.VMEM((lines * pair, 2 * members, LANES), jnp.bfloat16),
+            pltpu.VMEM((n_col * blocks, members, LANES), f32),
         ],
         "forward_tiles",
     )
+    row_parts, own_totals, other_totals = lax.optimization_barrier(
+        (row_parts, own_totals, other_totals)
+    )
     totals = own_totals + swap(other_totals, "col", 1)
-    y_parts = exchange(totals.reshape(y_lines, pair, members, LANES), "col", y_groups)
-    gram_sums = jnp.sum(z_parts[:, pair:], axis=0)
-    gram_sums = gram_sums + swap(gram_sums, "col", n_col // 2)
+    col_parts = exchange(totals.reshape(chips, blocks, members, LANES), "col", core_groups)
+    gram_sums = jnp.sum(row_parts[:, pair:], axis=0)
     gram_far = swap(gram_sums, "row", 1)
-    image, to_lo, to_hi, slots = call(
-        image_kernel,
-        [(members, piece)] * 3 + [(n_row * n_col, members // 2, LANES)],
-        "image",
-    )(y_parts, z_parts, stack, lo_stack, hi_stack, residuals)
-    late = exchange(slots, everyone)
-    from_lo = swap(to_lo, "col", n_col // 2)
-    from_hi = swap(to_hi, "row", 1)
     inverse, early = call(factor_kernel, [(order, order), (2 * members, order)], "factor")(
         gram_sums, gram_far
     )
     (orthonormal,) = call(
         functools.partial(orthonormal_kernel, row_scale=row_scale), [(order, piece)], "orthonormal"
-    )(inverse, stack, residuals)
+    )(inverse, stack, residuals, previous)
+    col_parts, inverse, orthonormal = lax.optimization_barrier((col_parts, inverse, orthonormal))
+    image, to_far, slots = call(
+        image_kernel,
+        [(members, piece)] * 2 + [(n_row * n_col, members // 2, LANES)],
+        "image",
+    )(col_parts, row_parts, stack, previous, far_stack, far_previous, residuals)
+    late = exchange(slots, everyone)
+    from_far = swap(to_far, "row", 1)
     (orthonormal_image,) = call(
         functools.partial(orthonormal_image_kernel, row_scale=row_scale),
         [(order, piece)],
         "orthonormal_image",
-    )(inverse, stack, image, from_lo, from_hi, hprevious)
+    )(inverse, stack, image, from_far, hprevious)
     (projected,) = call(projected_kernel, [(order, order)], "projected")(late, inverse, early)
     return (orthonormal, orthonormal_image, projected)
 

time: 117 us -> 117 us (level)
  blocking collectives: 42.3 us -> 12.9 us
  waiting for transfers between devices: 12.6 us -> 29.8 us
  starting transfers between devices: 29.9 us -> 44.2 us
  Pallas kernels: 26.4 us -> 24.5 us
    all_to_all x3 -> x1, blocking collectives: 42.3 us -> 12.9 us  [exchange(): lax.all_to_all(slots, axes, 0, 0, axis_index_groups=groups, tiled=True)]
    all_to_all x3 -> x5, starting transfers between devices: 18.4 us -> 30.8 us  [exchange(): lax.all_to_all(slots, axes, 0, 0, axis_index_groups=groups, tiled=True)]
    all_to_all x3 -> x5, waiting for transfers between devices: 3.39 us -> 14.3 us  [exchange(): lax.all_to_all(slots, axes, 0, 0, axis_index_groups=groups, tiled=True)]
    ppermute x8 -> x6, waiting for transfers between devices: 9.26 us -> 15.5 us  [swap(): lax.ppermute(array, axis, [(i, i ^ distance) for i in range(lax.axis_size...]
    ppermute x8 -> x6, starting transfers between devices: 11.4 us -> 13.4 us  [swap(): lax.ppermute(array, axis, [(i, i ^ distance) for i in range(lax.axis_size...]
    pallas_call x2, Pallas kernels: 13.4 us -> 11.8 us  [tile_call(): pl.pallas_call(functools.partial(kernel, unroll=unroll), out_shape=[jax.S...]
    unnamed x16 -> x12, local copies, waits for them, and re-layouts: 3.14 us -> 3.94 us
    pallas_call x2 -> x3, Pallas kernels: 3 us -> 3.41 us  [the longest x1 1.68 us: on_device(): pl.pallas_call(residual_kernel, out_shape=[jax.ShapeDtypeStruct(shape, f3...]
  transfers between devices with their start and end apart: 11 -> 11, of which waited for: 4 -> 7; matrix products, arithmetic and copies ran while one was open for 1% -> 0% of each run, Pallas kernels for 17% -> 16%
where the time goes in v3:
time: 117 us; the launch traced here: 118 us
  starting transfers between devices  44.2 us (38%)
  waiting for transfers between devices  29.8 us (25%)
  Pallas kernels  24.5 us (21%)
  blocking collectives  12.9 us (11%)
  local copies, waits for them, and re-layouts  3.94 us (3%)
  between operations  1.41 us (1%)
    all_to_all x5, starting transfers between devices, exchange(): lax.all_to_all(slots, axes, 0, 0, axis_index_groups=groups, tiled=True)  30.8 us
    ppermute x6, waiting for transfers between devices, swap(): lax.ppermute(array, axis, [(i, i ^ distance) for i in range(lax.axis_size...  15.5 us
    all_to_all x5, waiting for transfers between devices, exchange(): lax.all_to_all(slots, axes, 0, 0, axis_index_groups=groups, tiled=True)  14.3 us
    ppermute x6, starting transfers between devices, swap(): lax.ppermute(array, axis, [(i, i ^ distance) for i in range(lax.axis_size...  13.4 us
    all_to_all x1, blocking collectives, exchange(): lax.all_to_all(slots, axes, 0, 0, axis_index_groups=groups, tiled=True)  12.9 us
    pallas_call x2, Pallas kernels, tile_call(): pl.pallas_call(functools.partial(kernel, unroll=unroll), out_shape=[jax.S...  11.8 us
    pallas_call x1, Pallas kernels, on_device(): call(factor_kernel, [(order, order), (2 * members, order)], 'factor')  4.48 us
    unnamed x12, local copies, waits for them, and re-layouts  3.94 us
  transfers between devices with their start and end apart: 11, of which 7 were waited for; matrix products, arithmetic and copies ran while one was open for 0% of the time, Pallas kernels for 16%

profile of v3, /device:TPU:1, one launch (start us, length us, event | category | flops | bytes accessed | tf_op | source)
XLA Modules:
  0.0 117.5 jit_solution(3276697662714408463)
XLA Ops:
  0.6 0.0 copy-start.4
  0.6 1.6 %stage.1 = (f32[128,128]{1,0:T(8,128)}, f32[2,16,1024]{2,1,0:T(8,128)}) custom-call(f32[16,1024]{1,0:T(8,128)} %vectors_hbm.1, f32[16,1024]{1,0:T(8,128)} %hvectors_hbm.1), custom_call_target="tpu_custom_call" | custom-call | tf_op jit(solution)/shard_map/stage/pallas_call | solution.py:419
  2.3 3.7 %collective-permute-start = (f32[2,16,1024]{2,1,0:T(8,128)}, f32[2,16,1024]{2,1,0:T(8,128)S(1)}, u32[]{:S(2)}, u32[]{:S(2)}) collective-permute-start(f32[2,16,1024]{2,1,0:T(8,128)} %get-tuple-element.36.stack_hbm), channel_id=1, source_target_pairs={{0,16},{16,0},{32,48},{48,32},{64,80},{80,64},{96,112},{112,96},{1... | collective-permute-start | bytes 393224 | tf_op jit(solution)/shard_map/ppermute | solution.py:395
  5.9 9.1 %all-to-all-start = ((f32[128,1,128]{2,1,0:T(1,128)}), f32[128,1,128]{2,1,0:T(1,128)S(1)}, u32[]{:S(2)}, u32[]{:S(2)}) async-start(f32[128,1,128]{2,1,0:T(1,128)} %bitcast.10), calls=%async_computation | async-start | bytes 131072 | tf_op jit(solution)/shard_map/all_to_all | solution.py:391
  15.0 0.0 copy-start
  15.0 0.9 copy-done
  15.9 0.0 copy-start.1
  15.9 0.8 copy-done.1
  16.7 0.0 copy-start.2
  16.7 0.8 copy-done.2
  17.6 0.0 copy-start.5
  17.6 0.7 copy-done.5
  18.3 0.4 prepare.1
  18.6 5.9 %all-to-all-done = f32[128,1,128]{2,1,0:T(1,128)S(1)} async-done(((f32[128,1,128]{2,1,0:T(1,128)}), f32[128,1,128]{2,1,0:T(1,128)S(1)}, u32[]{:S(2)}, u32[]{:S(2)}) %all-to-all-start) | async-done | bytes 65568 | tf_op jit(solution)/shard_map/all_to_all | solution.py:391
  24.5 0.0 collective-permute-done.far_hbm
  24.5 1.7 %residual.1 = (f32[2,16,1024]{2,1,0:T(8,128)S(1)}, f32[8,10,16,128]{3,2,1,0:T(8,128)S(1)}, f32[4,16,16,128]{3,2,1,0:T(8,128)}, f32[2,16,1024]{2,1,0:T(8,128)S(1)}) custom-call(f32[128,128]{1,0:T(8,128)S(1)} %bitcast.7, f32[2,16,1024]{2,1,0:T(8,128)S(1)} %get-tuple-element.43.stack_ref, f32[16,1024]{1,0:T(8,128)S(1)} %get-tuple-element.44.previous_ref, ...), custom_call_target="tpu_custom_call" | custom-call | tf_op jit(solution)/shard_map/residual/pallas_call | solution.py:451
  26.2 12.9 %all_to_all.37.own_ref = f32[8,10,16,128]{3,2,1,0:T(8,128)S(1)} all-to-all(f32[8,10,16,128]{3,2,1,0:T(8,128)S(1)} %get-tuple-element.46), channel_id=1, replica_groups={{0,2,4,6,8,10,12,14},{1,3,5,7,9,11,13,15},{16,18,20,22,24,26,28,30},{17..., dimensions={0} | all-to-all | bytes 1310720 | tf_op jit(solution)/shard_map/all_to_all | solution.py:391
  39.1 2.0 %collective-permute-start.1 = (f32[8,10,16,128]{3,2,1,0:T(8,128)S(1)}, f32[8,10,16,128]{3,2,1,0:T(8,128)S(1)}, u32[]{:S(2)}, u32[]{:S(2)}) collective-permute-start(f32[8,10,16,128]{3,2,1,0:T(8,128)S(1)} %all_to_all.37.own_ref), channel_id=1, source_target_pairs={{0,1},{1,0},{2,3},{3,2},{4,5},{5,4},{6,7},{7,6},{8,9},{9,8},{10,11... | collective-permute-start | bytes 1966088 | tf_op jit(solution)/shard_map/ppermute | solution.py:395
  41.1 3.5 %all-to-all-start.2 = ((f32[4,16,16,128]{3,2,1,0:T(8,128)}), f32[4,16,16,128]{3,2,1,0:T(8,128)S(1)}, u32[]{:S(2)}, u32[]{:S(2)}) async-start(f32[4,16,16,128]{3,2,1,0:T(8,128)} %get-tuple-element.49), calls=%async_computation.2 | async-start | bytes 1048576 | tf_op jit(solution)/shard_map/all_to_all | solution.py:391
  45.2 0.0 collective-permute-done.1.other_ref
  45.2 0.0 copy-start.3
  45.3 0.7 copy-done.3
  45.9 5.7 %backward_tiles.1 = f32[72,16,128]{2,1,0:T(8,128)} custom-call(s32[1,1]{1,0:T(1,128)S(6)} %copy.12.count_ref, s32[1,1,384]{2,1,0:T(1,128)S(1)} %get-tuple-element.41.rows_ref, s32[1,1,384]{2,1,0:T(1,128)S(1)} %copy-done.3, bf16[384,128,128]{2,1,0:T(8,128)(2,1)} %bitcast.8, f32[8,10,16,128]{3,2,1,0:T(8,128)S(1)} %all_to_all.37.own_ref, ...), custom_call_target="tpu_custom_call" | custom-call | tf_op jit(solution)/shard_map/backward_tiles/pallas_call | solution.py:374
  51.7 2.5 %all-to-all-done.2.x_ref = f32[4,16,16,128]{3,2,1,0:T(8,128)S(1)} async-done(((f32[4,16,16,128]{3,2,1,0:T(8,128)}), f32[4,16,16,128]{3,2,1,0:T(8,128)S(1)}, u32[]{:S(2)}, u32[]{:S(2)}) %all-to-all-start.2) | async-done | bytes 524320 | tf_op jit(solution)/shard_map/all_to_all | solution.py:391
  54.2 3.5 %all-to-all-start.3 = ((f32[4,18,16,128]{3,2,1,0:T(8,128)}), f32[4,18,16,128]{3,2,1,0:T(8,128)S(1)}, u32[]{:S(2)}, u32[]{:S(2)}) async-start(f32[4,18,16,128]{3,2,1,0:T(8,128)} %bitcast.4), calls=%async_computation.3 | async-start | bytes 1179648 | tf_op jit(solution)/shard_map/all_to_all | solution.py:391
  57.7 0.0 copy-done.4
  57.7 6.0 %forward_tiles.1 = (f32[64,16,128]{2,1,0:T(8,128)S(1)}, f32[64,16,128]{2,1,0:T(8,128)S(1)}) custom-call(s32[1,1]{1,0:T(1,128)S(6)} %copy.12.count_ref, s32[1,1,384]{2,1,0:T(1,128)S(1)} %get-tuple-element.41.rows_ref, s32[1,1,384]{2,1,0:T(1,128)S(1)} %copy-done.4, bf16[384,128,128]{2,1,0:T(8,128)(2,1)} %bitcast.9, f32[4,16,16,128]{3,2,1,0:T(8,128)S(1)} %all-to-all-done.2.x_ref), custom_call_target="tpu_custom_call" | custom-call | tf_op jit(solution)/shard_map/forward_tiles/pallas_call | solution.py:374
  63.7 3.4 %all-to-all-done.3.row_parts_ref = f32[4,18,16,128]{3,2,1,0:T(8,128)S(1)} async-done(((f32[4,18,16,128]{3,2,1,0:T(8,128)}), f32[4,18,16,128]{3,2,1,0:T(8,128)S(1)}, u32[]{:S(2)}, u32[]{:S(2)}) %all-to-all-start.3) | async-done | bytes 589856 | tf_op jit(solution)/shard_map/all_to_all | solution.py:391
  67.1 1.7 %collective-permute-start.2 = (f32[64,16,128]{2,1,0:T(8,128)S(1)}, f32[64,16,128]{2,1,0:T(8,128)S(1)}, u32[]{:S(2)}, u32[]{:S(2)}) collective-permute-start(f32[64,16,128]{2,1,0:T(8,128)S(1)} %get-tuple-element.55), channel_id=1, source_target_pairs={{0,1},{1,0},{2,3},{3,2},{4,5},{5,4},{6,7},{7,6},{8,9},{9,8},{10,11... | collective-permute-start | bytes 1572872 | tf_op jit(solution)/shard_map/ppermute | solution.py:395
  68.8 1.5 %collective-permute-done.2 = f32[64,16,128]{2,1,0:T(8,128)S(1)} collective-permute-done((f32[64,16,128]{2,1,0:T(8,128)S(1)}, f32[64,16,128]{2,1,0:T(8,128)S(1)}, u32[]{:S(2)}, u32[]{:S(2)}) %collective-permute-start.2) | collective-permute-done | bytes 524320 | tf_op jit(solution)/shard_map/ppermute | solution.py:395
  70.3 0.9 add.3
  71.2 3.5 %all-to-all-start.4 = ((f32[8,8,16,128]{3,2,1,0:T(8,128)}), f32[8,8,16,128]{3,2,1,0:T(8,128)S(1)}, u32[]{:S(2)}, u32[]{:S(2)}) async-start(f32[8,8,16,128]{3,2,1,0:T(8,128)} %bitcast.5), calls=%async_computation.4 | async-start | bytes 1048576 | tf_op jit(solution)/shard_map/all_to_all | solution.py:391
  74.7 1.7 %collective-permute-start.4 = (f32[16,1024]{1,0:T(8,128)S(1)}, f32[16,1024]{1,0:T(8,128)S(1)}, u32[]{:S(2)}, u32[]{:S(2)}) collective-permute-start(f32[16,1024]{1,0:T(8,128)S(1)} %get-tuple-element.44.previous_ref), channel_id=1, source_target_pairs={{0,16},{16,0},{32,48},{48,32},{64,80},{80,64},{96,112},{112,96},{1... | collective-permute-start | bytes 196616 | tf_op jit(solution)/shard_map/ppermute | solution.py:395
  76.4 1.3 %collective-permute-start.3 = (f32[2,16,128]{2,1,0:T(8,128)S(1)}, f32[2,16,128]{2,1,0:T(8,128)S(1)}, u32[]{:S(2)}, u32[]{:S(2)}) collective-permute-start(f32[2,16,128]{2,1,0:T(8,128)S(1)} %slice_reduce_fusion.sums_ref), channel_id=1, source_target_pairs={{0,16},{16,0},{32,48},{48,32},{64,80},{80,64},{96,112},{112,96},{1... | collective-permute-start | bytes 49160 | tf_op jit(solution)/shard_map/ppermute | solution.py:395
  77.8 6.9 %collective-permute-done.3.far_ref = f32[2,16,128]{2,1,0:T(8,128)S(1)} collective-permute-done((f32[2,16,128]{2,1,0:T(8,128)S(1)}, f32[2,16,128]{2,1,0:T(8,128)S(1)}, u32[]{:S(2)}, u32[]{:S(2)}) %collective-permute-start.3) | collective-permute-done | bytes 16416 | tf_op jit(solution)/shard_map/ppermute | solution.py:395
  84.6 4.5 %factor.1 = (f32[48,48]{1,0:T(8,128)S(1)}, f32[32,48]{1,0:T(8,128)S(1)}) custom-call(f32[2,16,128]{2,1,0:T(8,128)S(1)} %slice_reduce_fusion.sums_ref, f32[2,16,128]{2,1,0:T(8,128)S(1)} %collective-permute-done.3.far_ref), custom_call_target="tpu_custom_call" | custom-call | tf_op jit(solution)/shard_map/factor/pallas_call | solution.py:507
  89.1 1.0 orthonormal.1
  90.1 0.0 all-to-all-done.4.col_parts_ref
  90.1 0.0 collective-permute-done.4.far_previous_ref
  90.1 1.4 %image.1 = (f32[16,1024]{1,0:T(8,128)S(1)}, f32[16,1024]{1,0:T(8,128)S(1)}, f32[128,8,128]{2,1,0:T(8,128)}) custom-call(f32[8,8,16,128]{3,2,1,0:T(8,128)S(1)} %all-to-all-done.4.col_parts_ref, f32[4,18,16,128]{3,2,1,0:T(8,128)S(1)} %all-to-all-done.3.row_parts_ref, f32[2,16,1024]{2,1,0:T(8,128)S(1)} %get-tuple-element.43.stack_ref, ...), custom_call_target="tpu_custom_call" | custom-call | tf_op jit(solution)/shard_map/image/pallas_call | solution.py:514
  91.5 11.3 %all-to-all-start.5 = ((f32[128,8,128]{2,1,0:T(8,128)}), f32[128,8,128]{2,1,0:T(8,128)S(1)}, u32[]{:S(2)}, u32[]{:S(2)}) async-start(f32[128,8,128]{2,1,0:T(8,128)} %get-tuple-element.65), calls=%async_computation.5 | async-start | bytes 1048576 | tf_op jit(solution)/shard_map/all_to_all | solution.py:391
  102.8 3.0 %collective-permute-start.5 = (f32[16,1024]{1,0:T(8,128)S(1)}, f32[16,1024]{1,0:T(8,128)S(1)}, u32[]{:S(2)}, u32[]{:S(2)}) collective-permute-start(f32[16,1024]{1,0:T(8,128)S(1)} %get-tuple-element.64), channel_id=1, source_target_pairs={{0,16},{16,0},{32,48},{48,32},{64,80},{80,64},{96,112},{112,96},{1... | collective-permute-start | bytes 196616 | tf_op jit(solution)/shard_map/ppermute | solution.py:395
  105.8 7.0 %collective-permute-done.5.far_ref = f32[16,1024]{1,0:T(8,128)S(1)} collective-permute-done((f32[16,1024]{1,0:T(8,128)S(1)}, f32[16,1024]{1,0:T(8,128)S(1)}, u32[]{:S(2)}, u32[]{:S(2)}) %collective-permute-start.5) | collective-permute-done | bytes 65568 | tf_op jit(solution)/shard_map/ppermute | solution.py:395
  112.9 1.0 orthonormal_image.1
  113.9 2.5 %all-to-all-done.5.received_ref = f32[128,8,128]{2,1,0:T(8,128)S(1)} async-done(((f32[128,8,128]{2,1,0:T(8,128)}), f32[128,8,128]{2,1,0:T(8,128)S(1)}, u32[]{:S(2)}, u32[]{:S(2)}) %all-to-all-start.5) | async-done | bytes 524320 | tf_op jit(solution)/shard_map/all_to_all | solution.py:391
  116.3 1.2 %projected.1 = f32[48,48]{1,0:T(8,128)} custom-call(f32[128,8,128]{2,1,0:T(8,128)S(1)} %all-to-all-done.5.received_ref, f32[48,48]{1,0:T(8,128)S(1)} %get-tuple-element.60.inverse_ref, f32[32,48]{1,0:T(8,128)S(1)} %get-tuple-element.66.early_ref), custom_call_target="tpu_custom_call" | custom-call | tf_op jit(solution)/shard_map/projected/pallas_call | solution.py:526
  (1 shorter events, 0.0 us)
Async XLA Ops:
  0.6 57.1 %copy-start.4 = (s32[1,1,384]{2,1,0:T(1,128)S(1)}, s32[1,1,384]{2,1,0:T(1,128)}, u32[]{:S(2)}) copy-start(s32[1,1,384]{2,1,0:T(1,128)} %cols_ref.3) | copy-start | bytes 4612
  2.3 22.3 %collective-permute-start = (f32[2,16,1024]{2,1,0:T(8,128)}, f32[2,16,1024]{2,1,0:T(8,128)S(1)}, u32[]{:S(2)}, u32[]{:S(2)}) collective-permute-start(f32[2,16,1024]{2,1,0:T(8,128)} %get-tuple-element.36.stack_hbm), channel_id=1, source_target_pairs={{0,16},{16,0},{32,48},{48,32},{64,80},{80,64},{96,112},{112,96},{1... | collective-permute-start | bytes 393224 | tf_op jit(solution)/shard_map/ppermute | solution.py:395
  5.9 18.6 %all-to-all-start = ((f32[128,1,128]{2,1,0:T(1,128)}), f32[128,1,128]{2,1,0:T(1,128)S(1)}, u32[]{:S(2)}, u32[]{:S(2)}) async-start(f32[128,1,128]{2,1,0:T(1,128)} %bitcast.10), calls=%async_computation | async-start | bytes 131072 | tf_op jit(solution)/shard_map/all_to_all | solution.py:391
  15.0 0.9 copy-start
  15.9 0.8 copy-start.1
  16.7 0.8 copy-start.2
  17.6 0.7 copy-start.5
  39.1 6.1 %collective-permute-start.1 = (f32[8,10,16,128]{3,2,1,0:T(8,128)S(1)}, f32[8,10,16,128]{3,2,1,0:T(8,128)S(1)}, u32[]{:S(2)}, u32[]{:S(2)}) collective-permute-start(f32[8,10,16,128]{3,2,1,0:T(8,128)S(1)} %all_to_all.37.own_ref), channel_id=1, source_target_pairs={{0,1},{1,0},{2,3},{3,2},{4,5},{5,4},{6,7},{7,6},{8,9},{9,8},{10,11... | collective-permute-start | bytes 1966088 | tf_op jit(solution)/shard_map/ppermute | solution.py:395
  41.1 13.1 %all-to-all-start.2 = ((f32[4,16,16,128]{3,2,1,0:T(8,128)}), f32[4,16,16,128]{3,2,1,0:T(8,128)S(1)}, u32[]{:S(2)}, u32[]{:S(2)}) async-start(f32[4,16,16,128]{3,2,1,0:T(8,128)} %get-tuple-element.49), calls=%async_computation.2 | async-start | bytes 1048576 | tf_op jit(solution)/shard_map/all_to_all | solution.py:391
  45.2 0.7 copy-start.3
  54.2 12.9 %all-to-all-start.3 = ((f32[4,18,16,128]{3,2,1,0:T(8,128)}), f32[4,18,16,128]{3,2,1,0:T(8,128)S(1)}, u32[]{:S(2)}, u32[]{:S(2)}) async-start(f32[4,18,16,128]{3,2,1,0:T(8,128)} %bitcast.4), calls=%async_computation.3 | async-start | bytes 1179648 | tf_op jit(solution)/shard_map/all_to_all | solution.py:391
  67.1 3.2 %collective-permute-start.2 = (f32[64,16,128]{2,1,0:T(8,128)S(1)}, f32[64,16,128]{2,1,0:T(8,128)S(1)}, u32[]{:S(2)}, u32[]{:S(2)}) collective-permute-start(f32[64,16,128]{2,1,0:T(8,128)S(1)} %get-tuple-element.55), channel_id=1, source_target_pairs={{0,1},{1,0},{2,3},{3,2},{4,5},{5,4},{6,7},{7,6},{8,9},{9,8},{10,11... | collective-permute-start | bytes 1572872 | tf_op jit(solution)/shard_map/ppermute | solution.py:395
  71.2 19.0 %all-to-all-start.4 = ((f32[8,8,16,128]{3,2,1,0:T(8,128)}), f32[8,8,16,128]{3,2,1,0:T(8,128)S(1)}, u32[]{:S(2)}, u32[]{:S(2)}) async-start(f32[8,8,16,128]{3,2,1,0:T(8,128)} %bitcast.5), calls=%async_computation.4 | async-start | bytes 1048576 | tf_op jit(solution)/shard_map/all_to_all | solution.py:391
  74.7 15.5 %collective-permute-start.4 = (f32[16,1024]{1,0:T(8,128)S(1)}, f32[16,1024]{1,0:T(8,128)S(1)}, u32[]{:S(2)}, u32[]{:S(2)}) collective-permute-start(f32[16,1024]{1,0:T(8,128)S(1)} %get-tuple-element.44.previous_ref), channel_id=1, source_target_pairs={{0,16},{16,0},{32,48},{48,32},{64,80},{80,64},{96,112},{112,96},{1... | collective-permute-start | bytes 196616 | tf_op jit(solution)/shard_map/ppermute | solution.py:395
  76.4 8.2 %collective-permute-start.3 = (f32[2,16,128]{2,1,0:T(8,128)S(1)}, f32[2,16,128]{2,1,0:T(8,128)S(1)}, u32[]{:S(2)}, u32[]{:S(2)}) collective-permute-start(f32[2,16,128]{2,1,0:T(8,128)S(1)} %slice_reduce_fusion.sums_ref), channel_id=1, source_target_pairs={{0,16},{16,0},{32,48},{48,32},{64,80},{80,64},{96,112},{112,96},{1... | collective-permute-start | bytes 49160 | tf_op jit(solution)/shard_map/ppermute | solution.py:395
  91.5 24.8 %all-to-all-start.5 = ((f32[128,8,128]{2,1,0:T(8,128)}), f32[128,8,128]{2,1,0:T(8,128)S(1)}, u32[]{:S(2)}, u32[]{:S(2)}) async-start(f32[128,8,128]{2,1,0:T(8,128)} %get-tuple-element.65), calls=%async_computation.5 | async-start | bytes 1048576 | tf_op jit(solution)/shard_map/all_to_all | solution.py:391
  102.8 10.0 %collective-permute-start.5 = (f32[16,1024]{1,0:T(8,128)S(1)}, f32[16,1024]{1,0:T(8,128)S(1)}, u32[]{:S(2)}, u32[]{:S(2)}) collective-permute-start(f32[16,1024]{1,0:T(8,128)S(1)} %get-tuple-element.64), channel_id=1, source_target_pairs={{0,16},{16,0},{32,48},{48,32},{64,80},{80,64},{96,112},{112,96},{1... | collective-permute-start | bytes 196616 | tf_op jit(solution)/shard_map/ppermute | solution.py:395

commit v4 on v3

v4 whole, which is shorter than its diff:
```python
import functools
import math

import jax
import jax.numpy as jnp
from jax import lax
from jax.experimental import pallas as pl
from jax.experimental.pallas import tpu as pltpu
from jax.sharding import PartitionSpec as P

EPSILON = 1e-06
HIGHEST_PRECISION = lax.Precision.HIGHEST
LANES = 128
VMEM_BYTES = 32 << 20
FULL_VMEM_BYTES = 60 << 20
NT = (((1,), (1,)), ((), ()))
NN = (((1,), (0,)), ((), ()))


def exact_dot(first, second, dims):
    return lax.dot_general(
        first, second, dims, precision=HIGHEST_PRECISION, preferred_element_type=jnp.float32
    )


def call(kernel, out_shapes, name):
    return pl.pallas_call(
        kernel,
        out_shape=[jax.ShapeDtypeStruct(shape, jnp.float32) for shape in out_shapes],
        compiler_params=pltpu.CompilerParams(vmem_limit_bytes=VMEM_BYTES),
        name=name,
    )


def block(array, index):
    return array[:, index * LANES : (index + 1) * LANES]


def stage_kernel(vectors_hbm, hvectors_hbm, slots_ref, stack_ref, arrived):
    copies = [
        pltpu.make_async_copy(source, stack_ref.at[index], arrived.at[index])
        for index, source in enumerate((vectors_hbm, hvectors_hbm))
    ]
    for copy in copies:
        copy.start()
    for copy in copies:
        copy.wait()
    vectors = stack_ref[0]
    hvectors = stack_ref[1]
    members = vectors.shape[0]
    top = jnp.sum(vectors * hvectors, axis=1, keepdims=True)
    bottom = jnp.sum(vectors * vectors, axis=1, keepdims=True)
    lane = lax.broadcasted_iota(jnp.int32, (members, LANES), 1)
    line = lax.broadcasted_iota(jnp.int32, (members, LANES), 0)
    spread = jnp.where(lane == line, top, 0.0) + jnp.where(lane == line + members, bottom, 0.0)
    sums = jnp.sum(spread, axis=0, keepdims=True)
    slots_ref[...] = jnp.broadcast_to(sums, slots_ref.shape)


def prepare_kernel(
    rows_ref,
    vectors_hbm,
    previous_hbm,
    hvectors_hbm,
    hprevious_hbm,
    rows_out_ref,
    basis_ref,
    images_ref,
    arrived,
):
    copies = [
        pltpu.make_async_copy(source, target.at[place], arrived.at[index])
        for index, (source, target, place) in enumerate(
            (
                (vectors_hbm, basis_ref, 0),
                (previous_hbm, basis_ref, 1),
                (hvectors_hbm, images_ref, 0),
                (hprevious_hbm, images_ref, 1),
            )
        )
    ]
    for copy in copies:
        copy.start()
    rows = rows_ref[...]
    core = lax.rem(lax.axis_index("col"), 2)
    chips = lax.axis_size("col") // 2
    blocks = basis_ref.shape[2] // LANES
    index, peer = rows % blocks, rows // blocks
    other = jnp.where(peer % 2 == core, 0, 1)
    rows_out_ref[...] = (other * chips + peer // 2) * blocks + index
    for copy in copies:
        copy.wait()


def residual_kernel(sums_ref, basis_ref, images_ref, residual_ref, slots_ref):
    members = basis_ref.shape[1]
    sums = jnp.sum(sums_ref[...], axis=0, keepdims=True)
    lane = lax.broadcasted_iota(jnp.int32, (members, LANES), 1)
    line = lax.broadcasted_iota(jnp.int32, (members, LANES), 0)
    top = jnp.sum(jnp.where(lane == line, sums, 0.0), axis=1, keepdims=True)
    bottom = jnp.sum(jnp.where(lane == line + members, sums, 0.0), axis=1, keepdims=True)
    residual = images_ref[0] - (top / (bottom + EPSILON)) * basis_ref[0]
    residual_ref[...] = residual
    blocks = residual.shape[1] // LANES
    for index in range(blocks):
        for slot in range(slots_ref.shape[0]):
            slots_ref[slot, index] = block(residual, index)
    basis = jnp.concatenate([basis_ref[0], residual, basis_ref[1]], axis=0)
    gram = exact_dot(basis, basis, NT)
    early = exact_dot(jnp.concatenate([images_ref[0], images_ref[1]], axis=0), basis, NT)
    extra = [
        gram[:members],
        gram[members : 2 * members],
        gram[2 * members :],
        early[:members],
        early[members:],
    ]
    for index, part in enumerate(pack_rows(extra)):
        for slot in range(slots_ref.shape[0]):
            slots_ref[slot, blocks + index] = part


def pair_kernel(residual_ref, far_ref, slots_ref):
    x_hi = lax.rem(lax.axis_index("row"), 2)
    blocks = residual_ref.shape[1] // LANES
    for place, rows in ((x_hi, residual_ref[...]), (1 - x_hi, far_ref[...])):
        for index in range(blocks):
            for slot in range(slots_ref.shape[0]):
                slots_ref[slot, place * blocks + index] = block(rows, index)


def pack_rows(parts):
    first, second, third, fourth, fifth = parts
    members = first.shape[0]
    pieces = [fifth[:, i * members : (i + 1) * members] for i in range(3)]
    zero = jnp.zeros((members, members), jnp.float32)
    return [
        jnp.concatenate([first, second, pieces[0], pieces[1]], axis=1),
        jnp.concatenate([third, fourth, pieces[2], zero], axis=1),
    ]


def unpack_rows(one, two):
    members = one.shape[0]
    wide = 3 * members
    fifth = jnp.concatenate([one[:, 2 * wide :], two[:, 2 * wide : 2 * wide + members]], axis=1)
    return [one[:, :wide], one[:, wide : 2 * wide], two[:, :wide], two[:, wide : 2 * wide], fifth]


def factor_kernel(sums_ref, far_ref, inverse_ref, early_ref):
    extras = [sums_ref[index] + far_ref[index] for index in range(2)]
    members = extras[0].shape[0]
    order = 3 * members
    first, second, third, fourth, fifth = unpack_rows(*extras)
    early_ref[...] = jnp.concatenate([fourth, fifth], axis=0)
    gram = jnp.concatenate([first, second, third], axis=0)
    line = lax.broadcasted_iota(jnp.int32, (order, order), 0)
    lane = lax.broadcasted_iota(jnp.int32, (order, order), 1)
    work = jnp.concatenate([gram, jnp.where(line == lane, 1.0, 0.0)], axis=1)
    rows = lax.broadcasted_iota(jnp.int32, (order, 1), 0)
    for step in range(order):
        pivot = work[step : step + 1, step : step + 1]
        scale = lax.rsqrt(pivot)
        scale = scale * (1.5 - 0.5 * pivot * scale * scale)
        lead = work[step : step + 1, :] * scale
        column = work[:, step : step + 1] * scale
        work = jnp.where(rows == step, lead, jnp.where(rows > step, work - column * lead, work))
    inverse_ref[...] = work[:, order:]


def orthonormal_kernel(inverse_ref, basis_ref, residual_ref, out_ref, *, row_scale):
    rows = jnp.concatenate([basis_ref[0], residual_ref[...], basis_ref[1]], axis=0)
    out_ref[...] = exact_dot(inverse_ref[...] * row_scale, rows, NN)


def orthonormal_image_kernel(
    inverse_ref, images_ref, image_ref, far_ref, out_ref, *, row_scale
):
    image = image_ref[...] + far_ref[...]
    rows = jnp.concatenate([images_ref[0], image, images_ref[1]], axis=0)
    out_ref[...] = exact_dot(inverse_ref[...] * row_scale, rows, NN)


def sum_peers(parts_ref, index):
    part = parts_ref[0, index]
    for peer in range(1, parts_ref.shape[0]):
        part = part + parts_ref[peer, index]
    return part


def image_kernel(
    col_parts_ref,
    row_parts_ref,
    basis_ref,
    residual_ref,
    far_basis_ref,
    far_residual_ref,
    image_ref,
    to_far_ref,
    slots_ref,
):
    x_hi = lax.rem(lax.axis_index("row"), 2)
    blocks = image_ref.shape[1] // LANES
    for index in range(blocks):
        lanes = slice(index * LANES, (index + 1) * LANES)
        image_ref[:, lanes] = sum_peers(col_parts_ref, index) + sum_peers(
            row_parts_ref, x_hi * blocks + index
        )
        to_far_ref[:, lanes] = sum_peers(row_parts_ref, (1 - x_hi) * blocks + index)
    basis = jnp.concatenate([basis_ref[0], residual_ref[...], basis_ref[1]], axis=0)
    late = exact_dot(image_ref[...], basis, NT)
    basis = jnp.concatenate([far_basis_ref[0], far_residual_ref[...], far_basis_ref[1]], axis=0)
    late = late + exact_dot(to_far_ref[...], basis, NT)
    half = late.shape[0] // 2
    pad = jnp.zeros((half, LANES // 2 - late.shape[1]), jnp.float32)
    packed = jnp.concatenate([late[:half], pad, late[half:], pad], axis=1)
    slots_ref[...] = jnp.broadcast_to(packed[None], slots_ref.shape)


def projected_kernel(received_ref, inverse_ref, early_ref, projected_ref):
    packed = jnp.sum(received_ref[...], axis=0)
    early = early_ref[...]
    members = early.shape[0] // 2
    wide = early.shape[1]
    half = LANES // 2
    late = jnp.concatenate([packed[:, :wide], packed[:, half : half + wide]], axis=0)
    mixed_t = jnp.concatenate([early[:members], late, early[members:]], axis=0)
    inverse = inverse_ref[...]
    half_done = exact_dot(inverse, mixed_t, NT)
    projected_ref[...] = exact_dot(half_done, inverse, NT)


def split_blocks(x_ref, split_ref, start, per_peer):
    def split(peer, carry):
        for index in range(per_peer):
            value = x_ref[peer, index]
            high = value.astype(jnp.bfloat16)
            low = (value - high.astype(jnp.float32)).astype(jnp.bfloat16)
            split_ref[start + peer * per_peer + index] = jnp.concatenate([high, low], axis=0)
        return carry

    lax.fori_loop(0, x_ref.shape[0], split, 0)


def group_size(slots):
    return math.gcd(slots, 24)


def group_count(count_ref, slots):
    return (jnp.minimum(count_ref[0, 0], slots) + group_size(slots) - 1) // group_size(slots)


def group_copy(tiles_hbm, tiles_ref, arrived, counter):
    size = group_size(tiles_ref.shape[0])
    part = pl.ds(counter * size, size)
    return pltpu.make_async_copy(tiles_hbm.at[part], tiles_ref.at[part], arrived.at[counter])


def start_tiles(count_ref, tiles_hbm, tiles_ref, arrived):
    def start(counter, carry):
        group_copy(tiles_hbm, tiles_ref, arrived, counter).start()
        return carry

    lax.fori_loop(0, group_count(count_ref, tiles_ref.shape[0]), start, 0)


def tile_groups(
    count_ref, tiles_hbm, tiles_ref, arrived, split_ref, out_ref, source_of, target_of, dims
):
    slots = tiles_ref.shape[0]
    unroll = group_size(slots)
    live = count_ref[0, 0]
    members = split_ref.shape[1] // 2

    def group(counter, carry):
        group_copy(tiles_hbm, tiles_ref, arrived, counter).wait()
        base = counter * unroll
        products = []
        for offset in range(unroll):
            slot = base + offset
            product = lax.dot_general(
                split_ref[source_of(slot)], tiles_ref[slot], dims, preferred_element_type=jnp.float32
            )
            product = product[:members] + product[members:]
            products.append(jnp.where(slot < live, product, 0.0))
        for offset in range(unroll):
            target = target_of(base + offset)
            out_ref[target] = out_ref[target] + products[offset]
        return carry

    lax.fori_loop(0, group_count(count_ref, slots), group, 0)


def backward_kernel(
    count_ref,
    rows_ref,
    cols_ref,
    tiles_hbm,
    own_ref,
    other_ref,
    out_ref,
    tiles_ref,
    arrived,
    split_ref,
):
    start_tiles(count_ref, tiles_hbm, tiles_ref, arrived)
    peers, width = own_ref.shape[:2]
    per_peer = split_ref.shape[0] // (2 * peers)
    extra = width - per_peer
    pair = 2 * per_peer
    out_ref[...] = jnp.zeros_like(out_ref)
    split_blocks(own_ref, split_ref, 0, per_peer)
    split_blocks(other_ref, split_ref, peers * per_peer, per_peer)
    for index in range(extra):
        part = sum_peers(own_ref, per_peer + index) + sum_peers(other_ref, per_peer + index)
        for start in range(pair, out_ref.shape[0], pair + extra):
            out_ref[start + index] = part
    tile_groups(
        count_ref,
        tiles_hbm,
        tiles_ref,
        arrived,
        split_ref,
        out_ref,
        lambda slot: rows_ref[0, 0, slot],
        lambda slot: cols_ref[0, 0, slot] + extra * (cols_ref[0, 0, slot] // pair),
        NN,
    )


def forward_kernel(
    count_ref,
    rows_ref,
    cols_ref,
    tiles_hbm,
    x_ref,
    own_ref,
    other_ref,
    tiles_ref,
    arrived,
    split_ref,
    totals_ref,
):
    start_tiles(count_ref, tiles_hbm, tiles_ref, arrived)
    totals_ref[...] = jnp.zeros_like(totals_ref)
    split_blocks(x_ref, split_ref, 0, x_ref.shape[1])
    tile_groups(
        count_ref,
        tiles_hbm,
        tiles_ref,
        arrived,
        split_ref,
        totals_ref,
        lambda slot: cols_ref[0, 0, slot],
        lambda slot: rows_ref[0, 0, slot],
        NT,
    )
    half = totals_ref.shape[0] // 2
    own_ref[...] = totals_ref[:half]
    other_ref[...] = totals_ref[half:]


def tile_call(kernel, count, rows, cols, tiles, arrays, out_shapes, scratch, name):
    smem = pl.BlockSpec(memory_space=pltpu.SMEM)
    vmem = pl.BlockSpec(memory_space=pltpu.VMEM)
    return pl.pallas_call(
        kernel,
        out_shape=[jax.ShapeDtypeStruct(shape, jnp.float32) for shape in out_shapes],
        in_specs=[smem] * 3 + [pl.BlockSpec(memory_space=pl.ANY)] + [vmem] * len(arrays),
        out_specs=[vmem] * len(out_shapes),
        scratch_shapes=[
            pltpu.VMEM(tiles.shape, tiles.dtype),
            pltpu.SemaphoreType.DMA((tiles.shape[0] // group_size(tiles.shape[0]),)),
        ]
        + scratch,
        compiler_params=pltpu.CompilerParams(vmem_limit_bytes=FULL_VMEM_BYTES),
        name=name,
    )(count, rows, cols, tiles, *arrays)


def exchange(slots, axes, groups=None):
    return lax.all_to_all(slots, axes, 0, 0, axis_index_groups=groups, tiled=True)


def swap(array, axis, distance):
    return lax.ppermute(array, axis, [(i, i ^ distance) for i in range(lax.axis_size(axis))])


def on_device(
    tile_blocks, tile_rows, tile_cols, tile_count, vectors, hvectors, previous, hprevious
):
    n_row = lax.axis_size("row")
    n_col = lax.axis_size("col")
    everyone = ("row", "col")
    chips = n_col // 2
    lines = n_row // 2
    core_groups = [[2 * chip + core for chip in range(chips)] for core in (0, 1)]
    z_groups = [[2 * line + x for line in range(lines)] for x in (0, 1)]
    members, piece = vectors.shape
    blocks = piece // LANES
    pair = 2 * blocks
    order = 3 * members
    tiles = tile_blocks[0, 0]
    row_scale = math.sqrt(piece * n_row * n_col)
    f32 = jnp.float32

    hbm_spec = pl.BlockSpec(memory_space=pl.ANY)
    vmem_spec = pl.BlockSpec(memory_space=pltpu.VMEM)
    params = pltpu.CompilerParams(vmem_limit_bytes=VMEM_BYTES)
    (sums,) = pl.pallas_call(
        stage_kernel,
        out_shape=[jax.ShapeDtypeStruct((n_row * n_col, LANES), f32)],
        in_specs=[hbm_spec, hbm_spec],
        out_specs=[vmem_spec],
        scratch_shapes=[
            pltpu.VMEM((2, members, piece), f32),
            pltpu.SemaphoreType.DMA((2,)),
        ],
        compiler_params=pltpu.CompilerParams(vmem_limit_bytes=FULL_VMEM_BYTES),
        name="stage",
    )(vectors, hvectors)
    rows, basis, images = pl.pallas_call(
        prepare_kernel,
        out_shape=[
            jax.ShapeDtypeStruct(tile_rows.shape, jnp.int32),
            jax.ShapeDtypeStruct((2, members, piece), f32),
            jax.ShapeDtypeStruct((2, members, piece), f32),
        ],
        in_specs=[vmem_spec] + [hbm_spec] * 4,
        out_specs=[vmem_spec] * 3,
        scratch_shapes=[pltpu.SemaphoreType.DMA((4,))],
        compiler_params=params,
        name="prepare",
    )(tile_rows, vectors, previous, hvectors, hprevious)
    sums = exchange(sums, everyone)
    sums, rows, basis, images = lax.optimization_barrier((sums, rows, basis, images))
    residual, col_slots = call(
        residual_kernel, [(members, piece), (chips, blocks + 2, members, LANES)], "residual"
    )(sums, basis, images)
    far_residual = swap(residual, "row", 1)
    (row_slots,) = call(pair_kernel, [(lines, pair, members, LANES)], "pair")(residual, far_residual)
    own_range = exchange(col_slots, "col", core_groups)
    own_range, row_slots, sent_basis = lax.optimization_barrier((own_range, row_slots, basis))
    far_basis = swap(sent_basis, "row", 1)
    other_range = swap(own_range, "col", 1)
    col_range = exchange(row_slots, "row", z_groups)
    (col_totals,) = tile_call(
        backward_kernel,
        tile_count,
        rows,
        tile_cols,
        tiles,
        (own_range, other_range),
        [(lines * (pair + 2), members, LANES)],
        [pltpu.VMEM((n_col * blocks, 2 * members, LANES), jnp.bfloat16)],
        "backward_tiles",
    )
    col_totals, col_range, far_basis = lax.optimization_barrier((col_totals, col_range, far_basis))
    row_parts = exchange(col_totals.reshape(lines, pair + 2, members, LANES), "row", z_groups)
    half = (chips * blocks, members, LANES)
    own_totals, other_totals = tile_call(
        forward_kernel,
        tile_count,
        rows,
        tile_cols,
        tiles,
        (col_range,),
        [half, half],
        [
            pltpu.VMEM((lines * pair, 2 * members, LANES), jnp.bfloat16),
            pltpu.VMEM((n_col * blocks, members, LANES), f32),
        ],
        "forward_tiles",
    )
    row_parts, own_totals, other_totals = lax.optimization_barrier(
        (row_parts, own_totals, other_totals)
    )
    totals = own_totals + swap(other_totals, "col", 1)
    col_parts = exchange(totals.reshape(chips, blocks, members, LANES), "col", core_groups)
    gram_sums = jnp.sum(row_parts[:, pair:], axis=0)
    gram_far = swap(gram_sums, "row", 1)
    col_parts, gram_far = lax.optimization_barrier((col_parts, gram_far))
    image, to_far, slots = call(
        image_kernel,
        [(members, piece)] * 2 + [(n_row * n_col, members // 2, LANES)],
        "image",
    )(col_parts, row_parts, basis, residual, far_basis, far_residual)
    late = exchange(slots, everyone)
    to_far, gram_sums, gram_far = lax.optimization_barrier((to_far, gram_sums, gram_far))
    from_far = swap(to_far, "row", 1)
    inverse, early = call(factor_kernel, [(order, order), (2 * members, order)], "factor")(
        gram_sums, gram_far
    )
    (orthonormal,) = call(
        functools.partial(orthonormal_kernel, row_scale=row_scale), [(order, piece)], "orthonormal"
    )(inverse, basis, residual)
    (orthonormal_image,) = call(
        functools.partial(orthonormal_image_kernel, row_scale=row_scale),
        [(order, piece)],
        "orthonormal_image",
    )(inverse, images, image, from_far)
    (projected,) = call(projected_kernel, [(order, order)], "projected")(late, inverse, early)
    return (orthonormal, orthonormal_image, projected)


def solution(mesh):
    in_specs = (
        P("row", "col", None, None, None),
        P("row", "col", None),
        P("row", "col", None),
        P("row", "col"),
        P(None, ("row", "col")),
        P(None, ("row", "col")),
        P(None, ("row", "col")),
        P(None, ("row", "col")),
    )
    out_specs = (P(None, ("row", "col")), P(None, ("row", "col")), P())
    return jax.shard_map(
        on_device, mesh=mesh, in_specs=in_specs, out_specs=out_specs, check_vma=False
    )
```

time: 117 us -> 113 us (0.966); the launches traced: 118 us -> 112 us
  blocking collectives: 12.9 us -> 0 us
  starting transfers between devices: 44.2 us -> 48.2 us
  waiting for transfers between devices: 29.8 us -> 32.5 us
  Pallas kernels: 24.5 us -> 22.7 us
    all_to_all x1 -> x0, blocking collectives: 12.9 us -> none  [exchange(): lax.all_to_all(slots, axes, 0, 0, axis_index_groups=groups, tiled=True)]
    all_to_all x5 -> x6, starting transfers between devices: 30.8 us -> 36.7 us  [exchange(): lax.all_to_all(slots, axes, 0, 0, axis_index_groups=groups, tiled=True)]
    ppermute x6, waiting for transfers between devices: 15.5 us -> 18.9 us  [swap(): lax.ppermute(array, axis, [(i, i ^ distance) for i in range(lax.axis_size...]
    ppermute x6, starting transfers between devices: 13.4 us -> 11.5 us  [swap(): lax.ppermute(array, axis, [(i, i ^ distance) for i in range(lax.axis_size...]
    pallas_call x3 -> x4, Pallas kernels: 13.4 us -> 11.7 us  [the longest x2 9.38 us: tile_call(): pl.pallas_call(kernel, out_shape=[jax.ShapeDtypeStruct(shape, jnp.float32...]
    unnamed x12 -> x18, local copies, waits for them, and re-layouts: 3.94 us -> 4.91 us
    all_to_all x5 -> x6, waiting for transfers between devices: 14.3 us -> 13.6 us  [exchange(): lax.all_to_all(slots, axes, 0, 0, axis_index_groups=groups, tiled=True)]
  transfers between devices with their start and end apart: 11 -> 12, of which waited for: 7 -> 8; matrix products, arithmetic and copies ran while one was open for 0% -> 0% of each run, Pallas kernels for 16% -> 15%
where the time goes in v4:
time: 113 us; the launch traced here: 112 us
  starting transfers between devices  48.2 us (43%)
  waiting for transfers between devices  32.5 us (29%)
  Pallas kernels  22.7 us (20%)
  local copies, waits for them, and re-layouts  4.91 us (4%)
  other arithmetic  1.93 us (2%)
  between operations  1.43 us (1%)
    all_to_all x6, starting transfers between devices, exchange(): lax.all_to_all(slots, axes, 0, 0, axis_index_groups=groups, tiled=True)  36.7 us
    ppermute x6, waiting for transfers between devices, swap(): lax.ppermute(array, axis, [(i, i ^ distance) for i in range(lax.axis_size...  18.9 us
    all_to_all x6, waiting for transfers between devices, exchange(): lax.all_to_all(slots, axes, 0, 0, axis_index_groups=groups, tiled=True)  13.6 us
    ppermute x6, starting transfers between devices, swap(): lax.ppermute(array, axis, [(i, i ^ distance) for i in range(lax.axis_size...  11.5 us
    pallas_call x2, Pallas kernels, tile_call(): pl.pallas_call(kernel, out_shape=[jax.ShapeDtypeStruct(shape, jnp.float32...  9.38 us
    unnamed x18, local copies, waits for them, and re-layouts  4.91 us
    pallas_call x1, Pallas kernels, on_device(): call(factor_kernel, [(order, order), (2 * members, order)], 'factor')  4.48 us
  transfers between devices with their start and end apart: 12, of which 8 were waited for; matrix products, arithmetic and copies ran while one was open for 0% of the time, Pallas kernels for 15%

profile of v4, /device:TPU:1, one launch (start us, length us, event | category | flops | bytes accessed | tf_op | source)
XLA Modules:
  0.0 111.7 jit_solution(14070199232117434267)
XLA Ops:
  0.6 1.6 %stage.1 = f32[128,128]{1,0:T(8,128)} custom-call(f32[16,1024]{1,0:T(8,128)} %vectors_hbm.3, f32[16,1024]{1,0:T(8,128)} %hvectors_hbm.3), custom_call_target="tpu_custom_call" | custom-call | tf_op jit(solution)/shard_map/stage/pallas_call | solution.py:410
  2.3 11.5 %all-to-all-start = ((f32[128,1,128]{2,1,0:T(1,128)}), f32[128,1,128]{2,1,0:T(1,128)S(1)}, u32[]{:S(2)}, u32[]{:S(2)}) async-start(f32[128,1,128]{2,1,0:T(1,128)} %bitcast.11), calls=%async_computation | async-start | bytes 131072 | tf_op jit(solution)/shard_map/all_to_all | solution.py:382
  13.8 0.0 copy-start
  13.8 0.8 copy-done
  14.6 0.0 copy-start.1
  14.6 0.8 copy-done.1
  15.4 0.0 copy-start.2
  15.5 0.8 copy-done.2
  16.3 0.0 copy-start.3
  16.3 0.8 copy-done.3
  17.1 0.0 copy-start.5
  17.1 0.7 copy-done.5
  17.8 0.4 prepare.1
  18.2 0.0 copy-start.4
  18.2 5.1 %all-to-all-done = f32[128,1,128]{2,1,0:T(1,128)S(1)} async-done(((f32[128,1,128]{2,1,0:T(1,128)}), f32[128,1,128]{2,1,0:T(1,128)S(1)}, u32[]{:S(2)}, u32[]{:S(2)}) %all-to-all-start) | async-done | bytes 65568 | tf_op jit(solution)/shard_map/all_to_all | solution.py:382
  23.3 0.0 copy-done.4
  23.3 1.5 %residual.1 = (f32[16,1024]{1,0:T(8,128)S(1)}, f32[8,10,16,128]{3,2,1,0:T(8,128)}) custom-call(f32[128,128]{1,0:T(8,128)S(1)} %bitcast.7, f32[2,16,1024]{2,1,0:T(8,128)S(1)} %get-tuple-element.44.basis_ref, f32[2,16,1024]{2,1,0:T(8,128)S(1)} %get-tuple-element.39.images_ref), custom_call_target="tpu_custom_call" | custom-call | tf_op jit(solution)/shard_map/residual/pallas_call | solution.py:437
  24.8 3.5 %all-to-all-start.1 = ((f32[8,10,16,128]{3,2,1,0:T(8,128)}), f32[8,10,16,128]{3,2,1,0:T(8,128)S(1)}, u32[]{:S(2)}, u32[]{:S(2)}) async-start(f32[8,10,16,128]{3,2,1,0:T(8,128)} %get-tuple-element.40), calls=%async_computation.1 | async-start | bytes 1310720 | tf_op jit(solution)/shard_map/all_to_all | solution.py:382
  28.4 1.2 %collective-permute-start = (f32[16,1024]{1,0:T(8,128)S(1)}, f32[16,1024]{1,0:T(8,128)S(1)}, u32[]{:S(2)}, u32[]{:S(2)}) collective-permute-start(f32[16,1024]{1,0:T(8,128)S(1)} %get-tuple-element.41.residual_ref), channel_id=1, source_target_pairs={{0,16},{16,0},{32,48},{48,32},{64,80},{80,64},{96,112},{112,96},{1... | collective-permute-start | bytes 196616 | tf_op jit(solution)/shard_map/ppermute | solution.py:386
  29.5 9.0 %collective-permute-done.far_ref.far_residual_ref = f32[16,1024]{1,0:T(8,128)S(1)} collective-permute-done((f32[16,1024]{1,0:T(8,128)S(1)}, f32[16,1024]{1,0:T(8,128)S(1)}, u32[]{:S(2)}, u32[]{:S(2)}) %collective-permute-start) | collective-permute-done | bytes 65568 | tf_op jit(solution)/shard_map/ppermute | solution.py:386
  38.5 0.9 pair.1
  39.4 0.0 all-to-all-done.1.own_ref
  39.4 0.0 copy-start.6
  39.4 1.2 %collective-permute-start.1 = (f32[8,10,16,128]{3,2,1,0:T(8,128)S(1)}, f32[8,10,16,128]{3,2,1,0:T(8,128)S(1)}, u32[]{:S(2)}, u32[]{:S(2)}) collective-permute-start(f32[8,10,16,128]{3,2,1,0:T(8,128)S(1)} %all-to-all-done.1.own_ref), channel_id=1, source_target_pairs={{0,1},{1,0},{2,3},{3,2},{4,5},{5,4},{6,7},{7,6},{8,9},{9,8},{10,11... | collective-permute-start | bytes 1966088 | tf_op jit(solution)/shard_map/ppermute | solution.py:386
  40.6 3.5 %all-to-all-start.2 = ((f32[4,16,16,128]{3,2,1,0:T(8,128)}), f32[4,16,16,128]{3,2,1,0:T(8,128)S(1)}, u32[]{:S(2)}, u32[]{:S(2)}) async-start(f32[4,16,16,128]{3,2,1,0:T(8,128)} %pair.1), calls=%async_computation.2 | async-start | bytes 1048576 | tf_op jit(solution)/shard_map/all_to_all | solution.py:382
  44.0 1.9 %collective-permute-start.2 = (f32[2,16,1024]{2,1,0:T(8,128)S(1)}, f32[2,16,1024]{2,1,0:T(8,128)S(1)}, u32[]{:S(2)}, u32[]{:S(2)}) collective-permute-start(f32[2,16,1024]{2,1,0:T(8,128)S(1)} %get-tuple-element.44.basis_ref), channel_id=1, source_target_pairs={{0,16},{16,0},{32,48},{48,32},{64,80},{80,64},{96,112},{112,96},{1... | collective-permute-start | bytes 393224 | tf_op jit(solution)/shard_map/ppermute | solution.py:386
  46.6 0.0 collective-permute-done.1.other_ref
  46.6 0.0 copy-start.8
  46.6 0.0 copy-done.6
  46.6 0.9 copy-done.8
  47.5 4.4 %backward_tiles.1 = f32[72,16,128]{2,1,0:T(8,128)} custom-call(s32[1,1]{1,0:T(1,128)S(6)} %copy.12.count_ref, s32[1,1,384]{2,1,0:T(1,128)} %copy-done.4, s32[1,1,384]{2,1,0:T(1,128)} %cols_ref.3, bf16[384,128,128]{2,1,0:T(8,128)(2,1)} %bitcast.8, f32[8,10,16,128]{3,2,1,0:T(8,128)} %copy-done.6, f32[8,10,16,128]{3,2,1,0:T(8,128)} %copy-done.8), custom_call_target="tpu_custom_call" | custom-call | tf_op jit(solution)/shard_map/backward_tiles/pallas_call | solution.py:366
  51.9 0.0 collective-permute-done.2.far_basis_ref
  51.9 1.7 %all-to-all-done.2.x_ref = f32[4,16,16,128]{3,2,1,0:T(8,128)S(1)} async-done(((f32[4,16,16,128]{3,2,1,0:T(8,128)}), f32[4,16,16,128]{3,2,1,0:T(8,128)S(1)}, u32[]{:S(2)}, u32[]{:S(2)}) %all-to-all-start.2) | async-done | bytes 524320 | tf_op jit(solution)/shard_map/all_to_all | solution.py:382
  53.6 0.0 copy-start.7
  53.6 3.5 %all-to-all-start.3 = ((f32[4,18,16,128]{3,2,1,0:T(8,128)}), f32[4,18,16,128]{3,2,1,0:T(8,128)S(1)}, u32[]{:S(2)}, u32[]{:S(2)}) async-start(f32[4,18,16,128]{3,2,1,0:T(8,128)} %bitcast.10), calls=%async_computation.3 | async-start | bytes 1179648 | tf_op jit(solution)/shard_map/all_to_all | solution.py:382
  57.1 0.0 copy-done.7
  57.1 5.0 %forward_tiles.1 = (f32[64,16,128]{2,1,0:T(8,128)}, f32[64,16,128]{2,1,0:T(8,128)}) custom-call(s32[1,1]{1,0:T(1,128)S(6)} %copy.12.count_ref, s32[1,1,384]{2,1,0:T(1,128)} %copy-done.4, s32[1,1,384]{2,1,0:T(1,128)} %cols_ref.3, bf16[384,128,128]{2,1,0:T(8,128)(2,1)} %bitcast.9, f32[4,16,16,128]{3,2,1,0:T(8,128)} %copy-done.7), custom_call_target="tpu_custom_call" | custom-call | tf_op jit(solution)/shard_map/forward_tiles/pallas_call | solution.py:366
  62.1 4.3 %all-to-all-done.3.row_parts_ref = f32[4,18,16,128]{3,2,1,0:T(8,128)S(1)} async-done(((f32[4,18,16,128]{3,2,1,0:T(8,128)}), f32[4,18,16,128]{3,2,1,0:T(8,128)S(1)}, u32[]{:S(2)}, u32[]{:S(2)}) %all-to-all-start.3) | async-done | bytes 589856 | tf_op jit(solution)/shard_map/all_to_all | solution.py:382
  66.4 1.8 %collective-permute-start.3 = (f32[64,16,128]{2,1,0:T(8,128)}, f32[64,16,128]{2,1,0:T(8,128)S(1)}, u32[]{:S(2)}, u32[]{:S(2)}) collective-permute-start(f32[64,16,128]{2,1,0:T(8,128)} %get-tuple-element.50), channel_id=1, source_target_pairs={{0,1},{1,0},{2,3},{3,2},{4,5},{5,4},{6,7},{7,6},{8,9},{9,8},{10,11... | collective-permute-start | bytes 1572872 | tf_op jit(solution)/shard_map/ppermute | solution.py:386
  68.2 1.7 %collective-permute-done.3 = f32[64,16,128]{2,1,0:T(8,128)S(1)} collective-permute-done((f32[64,16,128]{2,1,0:T(8,128)}, f32[64,16,128]{2,1,0:T(8,128)S(1)}, u32[]{:S(2)}, u32[]{:S(2)}) %collective-permute-start.3) | collective-permute-done | bytes 524320 | tf_op jit(solution)/shard_map/ppermute | solution.py:386
  70.0 1.9 %add.3 = f32[64,16,128]{2,1,0:T(8,128)} add(f32[64,16,128]{2,1,0:T(8,128)} %get-tuple-element.49, f32[64,16,128]{2,1,0:T(8,128)S(1)} %collective-permute-done.3) | non-fusion elementwise | flops 131072 | bytes 1572864 | tf_op jit(solution)/shard_map/add | solution.py:478
  71.9 5.5 %all-to-all-start.4 = ((f32[8,8,16,128]{3,2,1,0:T(8,128)}), f32[8,8,16,128]{3,2,1,0:T(8,128)S(1)}, u32[]{:S(2)}, u32[]{:S(2)}) async-start(f32[8,8,16,128]{3,2,1,0:T(8,128)} %bitcast.5), calls=%async_computation.4 | async-start | bytes 1048576 | tf_op jit(solution)/shard_map/all_to_all | solution.py:382
  77.4 2.6 %collective-permute-start.4 = (f32[2,16,128]{2,1,0:T(8,128)S(1)}, f32[2,16,128]{2,1,0:T(8,128)S(1)}, u32[]{:S(2)}, u32[]{:S(2)}) collective-permute-start(f32[2,16,128]{2,1,0:T(8,128)S(1)} %slice_reduce_fusion.sums_ref), channel_id=1, source_target_pairs={{0,16},{16,0},{32,48},{48,32},{64,80},{80,64},{96,112},{112,96},{1... | collective-permute-start | bytes 49160 | tf_op jit(solution)/shard_map/ppermute | solution.py:386
  80.0 6.5 %collective-permute-done.4.far_ref = f32[2,16,128]{2,1,0:T(8,128)S(1)} collective-permute-done((f32[2,16,128]{2,1,0:T(8,128)S(1)}, f32[2,16,128]{2,1,0:T(8,128)S(1)}, u32[]{:S(2)}, u32[]{:S(2)}) %collective-permute-start.4) | collective-permute-done | bytes 16416 | tf_op jit(solution)/shard_map/ppermute | solution.py:386
  86.5 0.0 all-to-all-done.4.col_parts_ref
  86.5 1.4 %image.1 = (f32[16,1024]{1,0:T(8,128)S(1)}, f32[16,1024]{1,0:T(8,128)S(1)}, f32[128,8,128]{2,1,0:T(8,128)}) custom-call(f32[8,8,16,128]{3,2,1,0:T(8,128)S(1)} %all-to-all-done.4.col_parts_ref, f32[4,18,16,128]{3,2,1,0:T(8,128)S(1)} %all-to-all-done.3.row_parts_ref, f32[2,16,1024]{2,1,0:T(8,128)S(1)} %get-tuple-element.44.basis_ref, ...), custom_call_target="tpu_custom_call" | custom-call | tf_op jit(solution)/shard_map/image/pallas_call | solution.py:483
  87.8 9.2 %all-to-all-start.5 = ((f32[128,8,128]{2,1,0:T(8,128)}), f32[128,8,128]{2,1,0:T(8,128)S(1)}, u32[]{:S(2)}, u32[]{:S(2)}) async-start(f32[128,8,128]{2,1,0:T(8,128)} %get-tuple-element.61), calls=%async_computation.5 | async-start | bytes 1048576 | tf_op jit(solution)/shard_map/all_to_all | solution.py:382
  97.0 3.0 %collective-permute-start.5 = (f32[16,1024]{1,0:T(8,128)S(1)}, f32[16,1024]{1,0:T(8,128)S(1)}, u32[]{:S(2)}, u32[]{:S(2)}) collective-permute-start(f32[16,1024]{1,0:T(8,128)S(1)} %get-tuple-element.60), channel_id=1, source_target_pairs={{0,16},{16,0},{32,48},{48,32},{64,80},{80,64},{96,112},{112,96},{1... | collective-permute-start | bytes 196616 | tf_op jit(solution)/shard_map/ppermute | solution.py:386
  100.0 4.5 %factor.1 = (f32[48,48]{1,0:T(8,128)S(1)}, f32[32,48]{1,0:T(8,128)S(1)}) custom-call(f32[2,16,128]{2,1,0:T(8,128)S(1)} %slice_reduce_fusion.sums_ref, f32[2,16,128]{2,1,0:T(8,128)S(1)} %collective-permute-done.4.far_ref), custom_call_target="tpu_custom_call" | custom-call | tf_op jit(solution)/shard_map/factor/pallas_call | solution.py:491
  104.5 1.0 orthonormal.1
  105.5 1.6 %collective-permute-done.5.far_ref = f32[16,1024]{1,0:T(8,128)S(1)} collective-permute-done((f32[16,1024]{1,0:T(8,128)S(1)}, f32[16,1024]{1,0:T(8,128)S(1)}, u32[]{:S(2)}, u32[]{:S(2)}) %collective-permute-start.5) | collective-permute-done | bytes 65568 | tf_op jit(solution)/shard_map/ppermute | solution.py:386
  107.1 1.0 orthonormal_image.1
  108.0 2.5 %all-to-all-done.5.received_ref = f32[128,8,128]{2,1,0:T(8,128)S(1)} async-done(((f32[128,8,128]{2,1,0:T(8,128)}), f32[128,8,128]{2,1,0:T(8,128)S(1)}, u32[]{:S(2)}, u32[]{:S(2)}) %all-to-all-start.5) | async-done | bytes 524320 | tf_op jit(solution)/shard_map/all_to_all | solution.py:382
  110.5 1.2 %projected.1 = f32[48,48]{1,0:T(8,128)} custom-call(f32[128,8,128]{2,1,0:T(8,128)S(1)} %all-to-all-done.5.received_ref, f32[48,48]{1,0:T(8,128)S(1)} %get-tuple-element.58.inverse_ref, f32[32,48]{1,0:T(8,128)S(1)} %get-tuple-element.62.early_ref), custom_call_target="tpu_custom_call" | custom-call | tf_op jit(solution)/shard_map/projected/pallas_call | solution.py:502
  (1 shorter events, 0.0 us)
Async XLA Ops:
  2.3 21.0 %all-to-all-start = ((f32[128,1,128]{2,1,0:T(1,128)}), f32[128,1,128]{2,1,0:T(1,128)S(1)}, u32[]{:S(2)}, u32[]{:S(2)}) async-start(f32[128,1,128]{2,1,0:T(1,128)} %bitcast.11), calls=%async_computation | async-start | bytes 131072 | tf_op jit(solution)/shard_map/all_to_all | solution.py:382
  13.8 0.8 copy-start
  14.6 0.8 copy-start.1
  15.4 0.8 copy-start.2
  16.3 0.8 copy-start.3
  17.1 0.7 copy-start.5
  18.2 5.1 %copy-start.4 = (s32[1,1,384]{2,1,0:T(1,128)}, s32[1,1,384]{2,1,0:T(1,128)S(1)}, u32[]{:S(2)}) copy-start(s32[1,1,384]{2,1,0:T(1,128)S(1)} %get-tuple-element.36.rows_ref) | copy-start | bytes 4612
  24.8 14.6 %all-to-all-start.1 = ((f32[8,10,16,128]{3,2,1,0:T(8,128)}), f32[8,10,16,128]{3,2,1,0:T(8,128)S(1)}, u32[]{:S(2)}, u32[]{:S(2)}) async-start(f32[8,10,16,128]{3,2,1,0:T(8,128)} %get-tuple-element.40), calls=%async_computation.1 | async-start | bytes 1310720 | tf_op jit(solution)/shard_map/all_to_all | solution.py:382
  28.4 10.2 %collective-permute-start = (f32[16,1024]{1,0:T(8,128)S(1)}, f32[16,1024]{1,0:T(8,128)S(1)}, u32[]{:S(2)}, u32[]{:S(2)}) collective-permute-start(f32[16,1024]{1,0:T(8,128)S(1)} %get-tuple-element.41.residual_ref), channel_id=1, source_target_pairs={{0,16},{16,0},{32,48},{48,32},{64,80},{80,64},{96,112},{112,96},{1... | collective-permute-start | bytes 196616 | tf_op jit(solution)/shard_map/ppermute | solution.py:386
  39.4 7.2 %copy-start.6 = (f32[8,10,16,128]{3,2,1,0:T(8,128)}, f32[8,10,16,128]{3,2,1,0:T(8,128)S(1)}, u32[]{:S(2)}) copy-start(f32[8,10,16,128]{3,2,1,0:T(8,128)S(1)} %all-to-all-done.1.own_ref) | copy-start | bytes 1966084
  39.4 7.2 %collective-permute-start.1 = (f32[8,10,16,128]{3,2,1,0:T(8,128)S(1)}, f32[8,10,16,128]{3,2,1,0:T(8,128)S(1)}, u32[]{:S(2)}, u32[]{:S(2)}) collective-permute-start(f32[8,10,16,128]{3,2,1,0:T(8,128)S(1)} %all-to-all-done.1.own_ref), channel_id=1, source_target_pairs={{0,1},{1,0},{2,3},{3,2},{4,5},{5,4},{6,7},{7,6},{8,9},{9,8},{10,11... | collective-permute-start | bytes 1966088 | tf_op jit(solution)/shard_map/ppermute | solution.py:386
  40.6 13.1 %all-to-all-start.2 = ((f32[4,16,16,128]{3,2,1,0:T(8,128)}), f32[4,16,16,128]{3,2,1,0:T(8,128)S(1)}, u32[]{:S(2)}, u32[]{:S(2)}) async-start(f32[4,16,16,128]{3,2,1,0:T(8,128)} %pair.1), calls=%async_computation.2 | async-start | bytes 1048576 | tf_op jit(solution)/shard_map/all_to_all | solution.py:382
  44.0 7.9 %collective-permute-start.2 = (f32[2,16,1024]{2,1,0:T(8,128)S(1)}, f32[2,16,1024]{2,1,0:T(8,128)S(1)}, u32[]{:S(2)}, u32[]{:S(2)}) collective-permute-start(f32[2,16,1024]{2,1,0:T(8,128)S(1)} %get-tuple-element.44.basis_ref), channel_id=1, source_target_pairs={{0,16},{16,0},{32,48},{48,32},{64,80},{80,64},{96,112},{112,96},{1... | collective-permute-start | bytes 393224 | tf_op jit(solution)/shard_map/ppermute | solution.py:386
  46.6 0.9 copy-start.8
  53.6 3.5 %copy-start.7 = (f32[4,16,16,128]{3,2,1,0:T(8,128)}, f32[4,16,16,128]{3,2,1,0:T(8,128)S(1)}, u32[]{:S(2)}) copy-start(f32[4,16,16,128]{3,2,1,0:T(8,128)S(1)} %all-to-all-done.2.x_ref) | copy-start | bytes 1572868
  53.6 12.8 %all-to-all-start.3 = ((f32[4,18,16,128]{3,2,1,0:T(8,128)}), f32[4,18,16,128]{3,2,1,0:T(8,128)S(1)}, u32[]{:S(2)}, u32[]{:S(2)}) async-start(f32[4,18,16,128]{3,2,1,0:T(8,128)} %bitcast.10), calls=%async_computation.3 | async-start | bytes 1179648 | tf_op jit(solution)/shard_map/all_to_all | solution.py:382
  66.4 3.5 %collective-permute-start.3 = (f32[64,16,128]{2,1,0:T(8,128)}, f32[64,16,128]{2,1,0:T(8,128)S(1)}, u32[]{:S(2)}, u32[]{:S(2)}) collective-permute-start(f32[64,16,128]{2,1,0:T(8,128)} %get-tuple-element.50), channel_id=1, source_target_pairs={{0,1},{1,0},{2,3},{3,2},{4,5},{5,4},{6,7},{7,6},{8,9},{9,8},{10,11... | collective-permute-start | bytes 1572872 | tf_op jit(solution)/shard_map/ppermute | solution.py:386
  71.9 14.6 %all-to-all-start.4 = ((f32[8,8,16,128]{3,2,1,0:T(8,128)}), f32[8,8,16,128]{3,2,1,0:T(8,128)S(1)}, u32[]{:S(2)}, u32[]{:S(2)}) async-start(f32[8,8,16,128]{3,2,1,0:T(8,128)} %bitcast.5), calls=%async_computation.4 | async-start | bytes 1048576 | tf_op jit(solution)/shard_map/all_to_all | solution.py:382
  77.4 9.1 %collective-permute-start.4 = (f32[2,16,128]{2,1,0:T(8,128)S(1)}, f32[2,16,128]{2,1,0:T(8,128)S(1)}, u32[]{:S(2)}, u32[]{:S(2)}) collective-permute-start(f32[2,16,128]{2,1,0:T(8,128)S(1)} %slice_reduce_fusion.sums_ref), channel_id=1, source_target_pairs={{0,16},{16,0},{32,48},{48,32},{64,80},{80,64},{96,112},{112,96},{1... | collective-permute-start | bytes 49160 | tf_op jit(solution)/shard_map/ppermute | solution.py:386
  87.8 22.7 %all-to-all-start.5 = ((f32[128,8,128]{2,1,0:T(8,128)}), f32[128,8,128]{2,1,0:T(8,128)S(1)}, u32[]{:S(2)}, u32[]{:S(2)}) async-start(f32[128,8,128]{2,1,0:T(8,128)} %get-tuple-element.61), calls=%async_computation.5 | async-start | bytes 1048576 | tf_op jit(solution)/shard_map/all_to_all | solution.py:382
  97.0 10.0 %collective-permute-start.5 = (f32[16,1024]{1,0:T(8,128)S(1)}, f32[16,1024]{1,0:T(8,128)S(1)}, u32[]{:S(2)}, u32[]{:S(2)}) collective-permute-start(f32[16,1024]{1,0:T(8,128)S(1)} %get-tuple-element.60), channel_id=1, source_target_pairs={{0,16},{16,0},{32,48},{48,32},{64,80},{80,64},{96,112},{112,96},{1... | collective-permute-start | bytes 196616 | tf_op jit(solution)/shard_map/ppermute | solution.py:386

commit v5 on v4

--- a/solution.py
+++ b/solution.py
@@ -13,6 +13,7 @@
 LANES = 128
 VMEM_BYTES = 32 << 20
 FULL_VMEM_BYTES = 60 << 20
+TILE_VMEM_BYTES = 54 << 20
 NT = (((1,), (1,)), ((), ()))
 NN = (((1,), (0,)), ((), ()))
 
@@ -92,7 +93,7 @@
         copy.wait()
 
 
-def residual_kernel(sums_ref, basis_ref, images_ref, residual_ref, slots_ref):
+def residual_kernel(sums_ref, basis_ref, images_ref, residual_ref, col_slots_ref, row_slots_ref):
     members = basis_ref.shape[1]
     sums = jnp.sum(sums_ref[...], axis=0, keepdims=True)
     lane = lax.broadcasted_iota(jnp.int32, (members, LANES), 1)
@@ -103,8 +104,9 @@
     residual_ref[...] = residual
     blocks = residual.shape[1] // LANES
     for index in range(blocks):
-        for slot in range(slots_ref.shape[0]):
-            slots_ref[slot, index] = block(residual, index)
+        for slots_ref in (col_slots_ref, row_slots_ref):
+            for slot in range(slots_ref.shape[0]):
+                slots_ref[slot, index] = block(residual, index)
     basis = jnp.concatenate([basis_ref[0], residual, basis_ref[1]], axis=0)
     gram = exact_dot(basis, basis, NT)
     early = exact_dot(jnp.concatenate([images_ref[0], images_ref[1]], axis=0), basis, NT)
@@ -116,17 +118,8 @@
         early[members:],
     ]
     for index, part in enumerate(pack_rows(extra)):
-        for slot in range(slots_ref.shape[0]):
-            slots_ref[slot, blocks + index] = part
-
-
-def pair_kernel(residual_ref, far_ref, slots_ref):
-    x_hi = lax.rem(lax.axis_index("row"), 2)
-    blocks = residual_ref.shape[1] // LANES
-    for place, rows in ((x_hi, residual_ref[...]), (1 - x_hi, far_ref[...])):
-        for index in range(blocks):
-            for slot in range(slots_ref.shape[0]):
-                slots_ref[slot, place * blocks + index] = block(rows, index)
+        for slot in range(col_slots_ref.shape[0]):
+            col_slots_ref[slot, blocks + index] = part
 
 
 def pack_rows(parts):
@@ -147,8 +140,16 @@
     return [one[:, :wide], one[:, wide : 2 * wide], two[:, :wide], two[:, wide : 2 * wide], fifth]
 
 
-def factor_kernel(sums_ref, far_ref, inverse_ref, early_ref):
-    extras = [sums_ref[index] + far_ref[index] for index in range(2)]
+def sum_peers(parts_ref, index):
+    part = parts_ref[0, index]
+    for peer in range(1, parts_ref.shape[0]):
+        part = part + parts_ref[peer, index]
+    return part
+
+
+def factor_kernel(parts_ref, inverse_ref, early_ref):
+    width = parts_ref.shape[1]
+    extras = [sum_peers(parts_ref, width - 2), sum_peers(parts_ref, width - 1)]
     members = extras[0].shape[0]
     order = 3 * members
     first, second, third, fourth, fifth = unpack_rows(*extras)
@@ -173,44 +174,19 @@
     out_ref[...] = exact_dot(inverse_ref[...] * row_scale, rows, NN)
 
 
-def orthonormal_image_kernel(
-    inverse_ref, images_ref, image_ref, far_ref, out_ref, *, row_scale
-):
-    image = image_ref[...] + far_ref[...]
-    rows = jnp.concatenate([images_ref[0], image, images_ref[1]], axis=0)
+def orthonormal_image_kernel(inverse_ref, images_ref, image_ref, out_ref, *, row_scale):
+    rows = jnp.concatenate([images_ref[0], image_ref[...], images_ref[1]], axis=0)
     out_ref[...] = exact_dot(inverse_ref[...] * row_scale, rows, NN)
 
 
-def sum_peers(parts_ref, index):
-    part = parts_ref[0, index]
-    for peer in range(1, parts_ref.shape[0]):
-        part = part + parts_ref[peer, index]
-    return part
-
-
-def image_kernel(
-    col_parts_ref,
-    row_parts_ref,
-    basis_ref,
-    residual_ref,
-    far_basis_ref,
-    far_residual_ref,
-    image_ref,
-    to_far_ref,
-    slots_ref,
-):
-    x_hi = lax.rem(lax.axis_index("row"), 2)
+def image_kernel(col_parts_ref, row_parts_ref, basis_ref, residual_ref, image_ref, slots_ref):
     blocks = image_ref.shape[1] // LANES
     for index in range(blocks):
-        lanes = slice(index * LANES, (index + 1) * LANES)
-        image_ref[:, lanes] = sum_peers(col_parts_ref, index) + sum_peers(
-            row_parts_ref, x_hi * blocks + index
-        )
-        to_far_ref[:, lanes] = sum_peers(row_parts_ref, (1 - x_hi) * blocks + index)
+        image_ref[:, index * LANES : (index + 1) * LANES] = sum_peers(
+            col_parts_ref, index
+        ) + sum_peers(row_parts_ref, index)
     basis = jnp.concatenate([basis_ref[0], residual_ref[...], basis_ref[1]], axis=0)
     late = exact_dot(image_ref[...], basis, NT)
-    basis = jnp.concatenate([far_basis_ref[0], far_residual_ref[...], far_basis_ref[1]], axis=0)
-    late = late + exact_dot(to_far_ref[...], basis, NT)
     half = late.shape[0] // 2
     pad = jnp.zeros((half, LANES // 2 - late.shape[1]), jnp.float32)
     packed = jnp.concatenate([late[:half], pad, late[half:], pad], axis=1)
@@ -307,13 +283,12 @@
     peers, width = own_ref.shape[:2]
     per_peer = split_ref.shape[0] // (2 * peers)
     extra = width - per_peer
-    pair = 2 * per_peer
     out_ref[...] = jnp.zeros_like(out_ref)
     split_blocks(own_ref, split_ref, 0, per_peer)
     split_blocks(other_ref, split_ref, peers * per_peer, per_peer)
     for index in range(extra):
         part = sum_peers(own_ref, per_peer + index) + sum_peers(other_ref, per_peer + index)
-        for start in range(pair, out_ref.shape[0], pair + extra):
+        for start in range(per_peer, out_ref.shape[0], width):
             out_ref[start + index] = part
     tile_groups(
         count_ref,
@@ -323,7 +298,7 @@
         split_ref,
         out_ref,
         lambda slot: rows_ref[0, 0, slot],
-        lambda slot: cols_ref[0, 0, slot] + extra * (cols_ref[0, 0, slot] // pair),
+        lambda slot: cols_ref[0, 0, slot] + extra * (cols_ref[0, 0, slot] // per_peer),
         NN,
     )
 
@@ -373,7 +348,7 @@
             pltpu.SemaphoreType.DMA((tiles.shape[0] // group_size(tiles.shape[0]),)),
         ]
         + scratch,
-        compiler_params=pltpu.CompilerParams(vmem_limit_bytes=FULL_VMEM_BYTES),
+        compiler_params=pltpu.CompilerParams(vmem_limit_bytes=TILE_VMEM_BYTES),
         name=name,
     )(count, rows, cols, tiles, *arrays)
 
@@ -393,12 +368,9 @@
     n_col = lax.axis_size("col")
     everyone = ("row", "col")
     chips = n_col // 2
-    lines = n_row // 2
     core_groups = [[2 * chip + core for chip in range(chips)] for core in (0, 1)]
-    z_groups = [[2 * line + x for line in range(lines)] for x in (0, 1)]
     members, piece = vectors.shape
     blocks = piece // LANES
-    pair = 2 * blocks
     order = 3 * members
     tiles = tile_blocks[0, 0]
     row_scale = math.sqrt(piece * n_row * n_col)
@@ -434,16 +406,19 @@
     )(tile_rows, vectors, previous, hvectors, hprevious)
     sums = exchange(sums, everyone)
     sums, rows, basis, images = lax.optimization_barrier((sums, rows, basis, images))
-    residual, col_slots = call(
-        residual_kernel, [(members, piece), (chips, blocks + 2, members, LANES)], "residual"
+    residual, col_slots, row_slots = call(
+        residual_kernel,
+        [
+            (members, piece),
+            (chips, blocks + 2, members, LANES),
+            (n_row, blocks, members, LANES),
+        ],
+        "residual",
     )(sums, basis, images)
-    far_residual = swap(residual, "row", 1)
-    (row_slots,) = call(pair_kernel, [(lines, pair, members, LANES)], "pair")(residual, far_residual)
     own_range = exchange(col_slots, "col", core_groups)
-    own_range, row_slots, sent_basis = lax.optimization_barrier((own_range, row_slots, basis))
-    far_basis = swap(sent_basis, "row", 1)
+    own_range, row_slots = lax.optimization_barrier((own_range, row_slots))
     other_range = swap(own_range, "col", 1)
-    col_range = exchange(row_slots, "row", z_groups)
+    col_range = exchange(row_slots, "row")
     (col_totals,) = tile_call(
         backward_kernel,
         tile_count,
@@ -451,12 +426,12 @@
         tile_cols,
         tiles,
         (own_range, other_range),
-        [(lines * (pair + 2), members, LANES)],
+        [(n_row * (blocks + 2), members, LANES)],
         [pltpu.VMEM((n_col * blocks, 2 * members, LANES), jnp.bfloat16)],
         "backward_tiles",
     )
-    col_totals, col_range, far_basis = lax.optimization_barrier((col_totals, col_range, far_basis))
-    row_parts = exchange(col_totals.reshape(lines, pair + 2, members, LANES), "row", z_groups)
+    col_totals, col_range = lax.optimization_barrier((col_totals, col_range))
+    row_parts = exchange(col_totals.reshape(n_row, blocks + 2, members, LANES), "row")
     half = (chips * blocks, members, LANES)
     own_totals, other_totals = tile_call(
         forward_kernel,
@@ -467,7 +442,7 @@
         (col_range,),
         [half, half],
         [
-            pltpu.VMEM((lines * pair, 2 * members, LANES), jnp.bfloat16),
+            pltpu.VMEM((n_row * blocks, 2 * members, LANES), jnp.bfloat16),
             pltpu.VMEM((n_col * blocks, members, LANES), f32),
         ],
         "forward_tiles",
@@ -477,28 +452,20 @@
     )
     totals = own_totals + swap(other_totals, "col", 1)
     col_parts = exchange(totals.reshape(chips, blocks, members, LANES), "col", core_groups)
-    gram_sums = jnp.sum(row_parts[:, pair:], axis=0)
-    gram_far = swap(gram_sums, "row", 1)
-    col_parts, gram_far = lax.optimization_barrier((col_parts, gram_far))
-    image, to_far, slots = call(
-        image_kernel,
-        [(members, piece)] * 2 + [(n_row * n_col, members // 2, LANES)],
-        "image",
-    )(col_parts, row_parts, basis, residual, far_basis, far_residual)
-    late = exchange(slots, everyone)
-    to_far, gram_sums, gram_far = lax.optimization_barrier((to_far, gram_sums, gram_far))
-    from_far = swap(to_far, "row", 1)
-    inverse, early = call(factor_kernel, [(order, order), (2 * members, order)], "factor")(
-        gram_sums, gram_far
-    )
+    inverse, early = call(factor_kernel, [(order, order), (2 * members, order)], "factor")(row_parts)
     (orthonormal,) = call(
         functools.partial(orthonormal_kernel, row_scale=row_scale), [(order, piece)], "orthonormal"
     )(inverse, basis, residual)
+    col_parts, inverse, orthonormal = lax.optimization_barrier((col_parts, inverse, orthonormal))
+    image, slots = call(
+        image_kernel, [(members, piece), (n_row * n_col, members // 2, LANES)], "image"
+    )(col_parts, row_parts, basis, residual)
+    late = exchange(slots, everyone)
     (orthonormal_image,) = call(
         functools.partial(orthonormal_image_kernel, row_scale=row_scale),
         [(order, piece)],
         "orthonormal_image",
-    )(inverse, images, image, from_far)
+    )(inverse, images, image)
     (projected,) = call(projected_kernel, [(order, order)], "projected")(late, inverse, early)
     return (orthonormal, orthonormal_image, projected)
 

time: 113 us -> 111 us (0.982); the launches traced: 112 us -> 112 us
  blocking collectives: 0 us -> 12.9 us
  starting transfers between devices: 48.2 us -> 35.8 us
    all_to_all x6 -> x5, waiting for transfers between devices: 13.6 us -> 31.2 us  [exchange(): lax.all_to_all(slots, axes, 0, 0, axis_index_groups=groups, tiled=True)]
    ppermute x6 -> x2, waiting for transfers between devices: 18.9 us -> 1.75 us  [swap(): lax.ppermute(array, axis, [(i, i ^ distance) for i in range(lax.axis_size...]
    all_to_all x0 -> x1, blocking collectives: none -> 12.9 us  [exchange(): lax.all_to_all(slots, axes, 0, 0, axis_index_groups=groups, tiled=True)]
    ppermute x6 -> x2, starting transfers between devices: 11.5 us -> 4.33 us  [swap(): lax.ppermute(array, axis, [(i, i ^ distance) for i in range(lax.axis_size...]
    all_to_all x6 -> x5, starting transfers between devices: 36.7 us -> 31.5 us  [exchange(): lax.all_to_all(slots, axes, 0, 0, axis_index_groups=groups, tiled=True)]
  transfers between devices with their start and end apart: 12 -> 7, of which waited for: 8 -> 6; matrix products, arithmetic and copies ran while one was open for 0% -> 0% of each run, Pallas kernels for 15% -> 15%
where the time goes in v5:
time: 111 us; the launch traced here: 112 us
  starting transfers between devices  35.8 us (32%)
  waiting for transfers between devices  33 us (30%)
  Pallas kernels  22.2 us (20%)
  blocking collectives  12.9 us (12%)
  local copies, waits for them, and re-layouts  4.88 us (4%)
  other arithmetic  1.91 us (2%)
  between operations  1.41 us (1%)
    all_to_all x5, starting transfers between devices, exchange(): lax.all_to_all(slots, axes, 0, 0, axis_index_groups=groups, tiled=True)  31.5 us
    all_to_all x5, waiting for transfers between devices, exchange(): lax.all_to_all(slots, axes, 0, 0, axis_index_groups=groups, tiled=True)  31.2 us
    all_to_all x1, blocking collectives, exchange(): lax.all_to_all(slots, axes, 0, 0, axis_index_groups=groups, tiled=True)  12.9 us
    pallas_call x2, Pallas kernels, tile_call(): pl.pallas_call(kernel, out_shape=[jax.ShapeDtypeStruct(shape, jnp.float32...  10.3 us
    unnamed x18, local copies, waits for them, and re-layouts  4.88 us
    pallas_call x1, Pallas kernels, on_device(): call(factor_kernel, [(order, order), (2 * members, order)], 'factor')  4.48 us
    ppermute x2, starting transfers between devices, swap(): lax.ppermute(array, axis, [(i, i ^ distance) for i in range(lax.axis_size...  4.33 us
  transfers between devices with their start and end apart: 7, of which 6 were waited for; matrix products, arithmetic and copies ran while one was open for 0% of the time, Pallas kernels for 15%

profile of v5, /device:TPU:1, one launch (start us, length us, event | category | flops | bytes accessed | tf_op | source)
XLA Modules:
  0.0 112.0 jit_solution(15673185516327937231)
XLA Ops:
  0.6 1.6 %stage.1 = f32[128,128]{1,0:T(8,128)} custom-call(f32[16,1024]{1,0:T(8,128)} %vectors_hbm.3, f32[16,1024]{1,0:T(8,128)} %hvectors_hbm.3), custom_call_target="tpu_custom_call" | custom-call | tf_op jit(solution)/shard_map/stage/pallas_call | solution.py:382
  2.3 11.5 %all-to-all-start = ((f32[128,1,128]{2,1,0:T(1,128)}), f32[128,1,128]{2,1,0:T(1,128)S(1)}, u32[]{:S(2)}, u32[]{:S(2)}) async-start(f32[128,1,128]{2,1,0:T(1,128)} %bitcast.11), calls=%async_computation | async-start | bytes 131072 | tf_op jit(solution)/shard_map/all_to_all | solution.py:357
  13.8 0.0 copy-start
  13.8 0.8 copy-done
  14.6 0.0 copy-start.1
  14.6 0.8 copy-done.1
  15.4 0.0 copy-start.2
  15.5 0.8 copy-done.2
  16.3 0.0 copy-start.3
  16.3 0.8 copy-done.3
  17.1 0.0 copy-start.5
  17.1 0.7 copy-done.5
  17.8 0.4 prepare.1
  18.2 0.0 copy-start.4
  18.2 5.1 %all-to-all-done = f32[128,1,128]{2,1,0:T(1,128)S(1)} async-done(((f32[128,1,128]{2,1,0:T(1,128)}), f32[128,1,128]{2,1,0:T(1,128)S(1)}, u32[]{:S(2)}, u32[]{:S(2)}) %all-to-all-start) | async-done | bytes 65568 | tf_op jit(solution)/shard_map/all_to_all | solution.py:357
  23.3 1.0 residual.1
  24.3 12.9 %all_to_all.37.own_ref = f32[8,10,16,128]{3,2,1,0:T(8,128)S(1)} all-to-all(f32[8,10,16,128]{3,2,1,0:T(8,128)S(1)} %get-tuple-element.36), channel_id=1, replica_groups={{0,2,4,6,8,10,12,14},{1,3,5,7,9,11,13,15},{16,18,20,22,24,26,28,30},{17..., dimensions={0} | all-to-all | bytes 1310720 | tf_op jit(solution)/shard_map/all_to_all | solution.py:357
  37.2 0.0 copy-start.6
  37.2 2.0 %collective-permute-start = (f32[8,10,16,128]{3,2,1,0:T(8,128)S(1)}, f32[8,10,16,128]{3,2,1,0:T(8,128)S(1)}, u32[]{:S(2)}, u32[]{:S(2)}) collective-permute-start(f32[8,10,16,128]{3,2,1,0:T(8,128)S(1)} %all_to_all.37.own_ref), channel_id=1, source_target_pairs={{0,1},{1,0},{2,3},{3,2},{4,5},{5,4},{6,7},{7,6},{8,9},{9,8},{10,11... | collective-permute-start | bytes 1966088 | tf_op jit(solution)/shard_map/ppermute | solution.py:361
  39.2 4.0 %all-to-all-start.2 = ((f32[8,8,16,128]{3,2,1,0:T(8,128)}), f32[8,8,16,128]{3,2,1,0:T(8,128)S(1)}, u32[]{:S(2)}, u32[]{:S(2)}) async-start(f32[8,8,16,128]{3,2,1,0:T(8,128)} %get-tuple-element.39), calls=%async_computation.2 | async-start | bytes 1048576 | tf_op jit(solution)/shard_map/all_to_all | solution.py:357
  43.8 0.0 collective-permute-done.other_ref
  43.8 0.0 copy-start.8
  43.8 0.0 copy-done.4
  43.8 0.0 copy-done.6
  43.8 0.8 copy-done.8
  44.7 4.8 %backward_tiles.1 = f32[80,16,128]{2,1,0:T(8,128)} custom-call(s32[1,1]{1,0:T(1,128)S(6)} %copy.12.count_ref, s32[1,1,384]{2,1,0:T(1,128)} %copy-done.4, s32[1,1,384]{2,1,0:T(1,128)} %cols_ref.3, bf16[384,128,128]{2,1,0:T(8,128)(2,1)} %bitcast.8, f32[8,10,16,128]{3,2,1,0:T(8,128)} %copy-done.6, f32[8,10,16,128]{3,2,1,0:T(8,128)} %copy-done.8), custom_call_target="tpu_custom_call" | custom-call | tf_op jit(solution)/shard_map/backward_tiles/pallas_call | solution.py:341
  49.4 4.8 %all-to-all-done.2.x_ref = f32[8,8,16,128]{3,2,1,0:T(8,128)S(1)} async-done(((f32[8,8,16,128]{3,2,1,0:T(8,128)}), f32[8,8,16,128]{3,2,1,0:T(8,128)S(1)}, u32[]{:S(2)}, u32[]{:S(2)}) %all-to-all-start.2) | async-done | bytes 524320 | tf_op jit(solution)/shard_map/all_to_all | solution.py:357
  54.3 0.0 copy-start.7
  54.3 3.5 %all-to-all-start.3 = ((f32[8,10,16,128]{3,2,1,0:T(8,128)}), f32[8,10,16,128]{3,2,1,0:T(8,128)S(1)}, u32[]{:S(2)}, u32[]{:S(2)}) async-start(f32[8,10,16,128]{3,2,1,0:T(8,128)} %bitcast.10), calls=%async_computation.3 | async-start | bytes 1310720 | tf_op jit(solution)/shard_map/all_to_all | solution.py:357
  57.8 0.0 copy-done.7
  57.9 5.5 %forward_tiles.1 = (f32[64,16,128]{2,1,0:T(8,128)}, f32[64,16,128]{2,1,0:T(8,128)}) custom-call(s32[1,1]{1,0:T(1,128)S(6)} %copy.12.count_ref, s32[1,1,384]{2,1,0:T(1,128)} %copy-done.4, s32[1,1,384]{2,1,0:T(1,128)} %cols_ref.3, bf16[384,128,128]{2,1,0:T(8,128)(2,1)} %bitcast.9, f32[8,8,16,128]{3,2,1,0:T(8,128)} %copy-done.7), custom_call_target="tpu_custom_call" | custom-call | tf_op jit(solution)/shard_map/forward_tiles/pallas_call | solution.py:341
  63.4 6.0 %all-to-all-done.3.parts_ref.row_parts_ref = f32[8,10,16,128]{3,2,1,0:T(8,128)S(1)} async-done(((f32[8,10,16,128]{3,2,1,0:T(8,128)}), f32[8,10,16,128]{3,2,1,0:T(8,128)S(1)}, u32[]{:S(2)}, u32[]{:S(2)}) %all-to-all-start.3) | async-done | bytes 655392 | tf_op jit(solution)/shard_map/all_to_all | solution.py:357
  69.4 2.3 %collective-permute-start.1 = (f32[64,16,128]{2,1,0:T(8,128)}, f32[64,16,128]{2,1,0:T(8,128)S(1)}, u32[]{:S(2)}, u32[]{:S(2)}) collective-permute-start(f32[64,16,128]{2,1,0:T(8,128)} %get-tuple-element.45), channel_id=1, source_target_pairs={{0,1},{1,0},{2,3},{3,2},{4,5},{5,4},{6,7},{7,6},{8,9},{9,8},{10,11... | collective-permute-start | bytes 1572872 | tf_op jit(solution)/shard_map/ppermute | solution.py:361
  71.7 1.7 %collective-permute-done.1 = f32[64,16,128]{2,1,0:T(8,128)S(1)} collective-permute-done((f32[64,16,128]{2,1,0:T(8,128)}, f32[64,16,128]{2,1,0:T(8,128)S(1)}, u32[]{:S(2)}, u32[]{:S(2)}) %collective-permute-start.1) | collective-permute-done | bytes 524320 | tf_op jit(solution)/shard_map/ppermute | solution.py:361
  73.5 1.9 %add.3 = f32[64,16,128]{2,1,0:T(8,128)} add(f32[64,16,128]{2,1,0:T(8,128)} %get-tuple-element.44, f32[64,16,128]{2,1,0:T(8,128)S(1)} %collective-permute-done.1) | non-fusion elementwise | flops 131072 | bytes 1572864 | tf_op jit(solution)/shard_map/add | solution.py:453
  75.4 3.6 %all-to-all-start.4 = ((f32[8,8,16,128]{3,2,1,0:T(8,128)}), f32[8,8,16,128]{3,2,1,0:T(8,128)S(1)}, u32[]{:S(2)}, u32[]{:S(2)}) async-start(f32[8,8,16,128]{3,2,1,0:T(8,128)} %bitcast.5), calls=%async_computation.4 | async-start | bytes 1048576 | tf_op jit(solution)/shard_map/all_to_all | solution.py:357
  79.0 4.5 %factor.1 = (f32[48,48]{1,0:T(8,128)S(1)}, f32[32,48]{1,0:T(8,128)S(1)}) custom-call(f32[8,10,16,128]{3,2,1,0:T(8,128)S(1)} %all-to-all-done.3.parts_ref.row_parts_ref), custom_call_target="tpu_custom_call" | custom-call | tf_op jit(solution)/shard_map/factor/pallas_call | solution.py:455
  83.5 1.0 orthonormal.1
  84.5 2.8 %all-to-all-done.4.col_parts_ref = f32[8,8,16,128]{3,2,1,0:T(8,128)S(1)} async-done(((f32[8,8,16,128]{3,2,1,0:T(8,128)}), f32[8,8,16,128]{3,2,1,0:T(8,128)S(1)}, u32[]{:S(2)}, u32[]{:S(2)}) %all-to-all-start.4) | async-done | bytes 524320 | tf_op jit(solution)/shard_map/all_to_all | solution.py:357
  87.3 1.2 %image.1 = (f32[16,1024]{1,0:T(8,128)S(1)}, f32[128,8,128]{2,1,0:T(8,128)}) custom-call(f32[8,8,16,128]{3,2,1,0:T(8,128)S(1)} %all-to-all-done.4.col_parts_ref, f32[8,10,16,128]{3,2,1,0:T(8,128)S(1)} %all-to-all-done.3.parts_ref.row_parts_ref, f32[2,16,1024]{2,1,0:T(8,128)S(1)} %get-tuple-element.34.basis_ref, f32[16,1024]{1,0:T(8,128)S(1)} %get-tuple-element.48.residual_ref), custom_call_target="tpu_custom_call" | custom-call | tf_op jit(solution)/shard_map/image/pallas_call | solution.py:460
  88.5 8.8 %all-to-all-start.5 = ((f32[128,8,128]{2,1,0:T(8,128)}), f32[128,8,128]{2,1,0:T(8,128)S(1)}, u32[]{:S(2)}, u32[]{:S(2)}) async-start(f32[128,8,128]{2,1,0:T(8,128)} %get-tuple-element.53), calls=%async_computation.5 | async-start | bytes 1048576 | tf_op jit(solution)/shard_map/all_to_all | solution.py:357
  97.3 1.0 orthonormal_image.1
  98.3 12.5 %all-to-all-done.5.received_ref = f32[128,8,128]{2,1,0:T(8,128)S(1)} async-done(((f32[128,8,128]{2,1,0:T(8,128)}), f32[128,8,128]{2,1,0:T(8,128)S(1)}, u32[]{:S(2)}, u32[]{:S(2)}) %all-to-all-start.5) | async-done | bytes 524320 | tf_op jit(solution)/shard_map/all_to_all | solution.py:357
  110.8 1.2 %projected.1 = f32[48,48]{1,0:T(8,128)} custom-call(f32[128,8,128]{2,1,0:T(8,128)S(1)} %all-to-all-done.5.received_ref, f32[48,48]{1,0:T(8,128)S(1)} %get-tuple-element.50.inverse_ref, f32[32,48]{1,0:T(8,128)S(1)} %get-tuple-element.54.early_ref), custom_call_target="tpu_custom_call" | custom-call | tf_op jit(solution)/shard_map/projected/pallas_call | solution.py:469
Async XLA Ops:
  2.3 21.0 %all-to-all-start = ((f32[128,1,128]{2,1,0:T(1,128)}), f32[128,1,128]{2,1,0:T(1,128)S(1)}, u32[]{:S(2)}, u32[]{:S(2)}) async-start(f32[128,1,128]{2,1,0:T(1,128)} %bitcast.11), calls=%async_computation | async-start | bytes 131072 | tf_op jit(solution)/shard_map/all_to_all | solution.py:357
  13.8 0.8 copy-start
  14.6 0.8 copy-start.1
  15.4 0.8 copy-start.2
  16.3 0.8 copy-start.3
  17.1 0.7 copy-start.5
  18.2 25.6 %copy-start.4 = (s32[1,1,384]{2,1,0:T(1,128)}, s32[1,1,384]{2,1,0:T(1,128)S(1)}, u32[]{:S(2)}) copy-start(s32[1,1,384]{2,1,0:T(1,128)S(1)} %get-tuple-element.32.rows_ref) | copy-start | bytes 4612
  37.2 6.7 %copy-start.6 = (f32[8,10,16,128]{3,2,1,0:T(8,128)}, f32[8,10,16,128]{3,2,1,0:T(8,128)S(1)}, u32[]{:S(2)}) copy-start(f32[8,10,16,128]{3,2,1,0:T(8,128)S(1)} %all_to_all.37.own_ref) | copy-start | bytes 1966084
  37.2 6.6 %collective-permute-start = (f32[8,10,16,128]{3,2,1,0:T(8,128)S(1)}, f32[8,10,16,128]{3,2,1,0:T(8,128)S(1)}, u32[]{:S(2)}, u32[]{:S(2)}) collective-permute-start(f32[8,10,16,128]{3,2,1,0:T(8,128)S(1)} %all_to_all.37.own_ref), channel_id=1, source_target_pairs={{0,1},{1,0},{2,3},{3,2},{4,5},{5,4},{6,7},{7,6},{8,9},{9,8},{10,11... | collective-permute-start | bytes 1966088 | tf_op jit(solution)/shard_map/ppermute | solution.py:361
  39.2 15.1 %all-to-all-start.2 = ((f32[8,8,16,128]{3,2,1,0:T(8,128)}), f32[8,8,16,128]{3,2,1,0:T(8,128)S(1)}, u32[]{:S(2)}, u32[]{:S(2)}) async-start(f32[8,8,16,128]{3,2,1,0:T(8,128)} %get-tuple-element.39), calls=%async_computation.2 | async-start | bytes 1048576 | tf_op jit(solution)/shard_map/all_to_all | solution.py:357
  43.8 0.9 copy-start.8
  54.3 3.6 %copy-start.7 = (f32[8,8,16,128]{3,2,1,0:T(8,128)}, f32[8,8,16,128]{3,2,1,0:T(8,128)S(1)}, u32[]{:S(2)}) copy-start(f32[8,8,16,128]{3,2,1,0:T(8,128)S(1)} %all-to-all-done.2.x_ref) | copy-start | bytes 1572868
  54.3 15.1 %all-to-all-start.3 = ((f32[8,10,16,128]{3,2,1,0:T(8,128)}), f32[8,10,16,128]{3,2,1,0:T(8,128)S(1)}, u32[]{:S(2)}, u32[]{:S(2)}) async-start(f32[8,10,16,128]{3,2,1,0:T(8,128)} %bitcast.10), calls=%async_computation.3 | async-start | bytes 1310720 | tf_op jit(solution)/shard_map/all_to_all | solution.py:357
  69.4 4.1 %collective-permute-start.1 = (f32[64,16,128]{2,1,0:T(8,128)}, f32[64,16,128]{2,1,0:T(8,128)S(1)}, u32[]{:S(2)}, u32[]{:S(2)}) collective-permute-start(f32[64,16,128]{2,1,0:T(8,128)} %get-tuple-element.45), channel_id=1, source_target_pairs={{0,1},{1,0},{2,3},{3,2},{4,5},{5,4},{6,7},{7,6},{8,9},{9,8},{10,11... | collective-permute-start | bytes 1572872 | tf_op jit(solution)/shard_map/ppermute | solution.py:361
  75.4 11.9 %all-to-all-start.4 = ((f32[8,8,16,128]{3,2,1,0:T(8,128)}), f32[8,8,16,128]{3,2,1,0:T(8,128)S(1)}, u32[]{:S(2)}, u32[]{:S(2)}) async-start(f32[8,8,16,128]{3,2,1,0:T(8,128)} %bitcast.5), calls=%async_computation.4 | async-start | bytes 1048576 | tf_op jit(solution)/shard_map/all_to_all | solution.py:357
  88.5 22.3 %all-to-all-start.5 = ((f32[128,8,128]{2,1,0:T(8,128)}), f32[128,8,128]{2,1,0:T(8,128)S(1)}, u32[]{:S(2)}, u32[]{:S(2)}) async-start(f32[128,8,128]{2,1,0:T(8,128)} %get-tuple-element.53), calls=%async_computation.5 | async-start | bytes 1048576 | tf_op jit(solution)/shard_map/all_to_all | solution.py:357

commit v6 on v5

--- a/solution.py
+++ b/solution.py
@@ -60,11 +60,13 @@
 
 def prepare_kernel(
     rows_ref,
+    cols_ref,
     vectors_hbm,
     previous_hbm,
     hvectors_hbm,
     hprevious_hbm,
     rows_out_ref,
+    cols_out_ref,
     basis_ref,
     images_ref,
     arrived,
@@ -89,11 +91,17 @@
     index, peer = rows % blocks, rows // blocks
     other = jnp.where(peer % 2 == core, 0, 1)
     rows_out_ref[...] = (other * chips + peer // 2) * blocks + index
+    cols = cols_ref[...]
+    half = lax.rem(lax.axis_index("row"), 2)
+    lines = lax.axis_size("row") // 2
+    index, peer = cols % blocks, cols // blocks
+    other = jnp.where(peer % 2 == half, 0, 1)
+    cols_out_ref[...] = (other * lines + peer // 2) * blocks + index
     for copy in copies:
         copy.wait()
 
 
-def residual_kernel(sums_ref, basis_ref, images_ref, residual_ref, col_slots_ref, row_slots_ref):
+def residual_kernel(sums_ref, basis_ref, images_ref, residual_ref, slots_ref):
     members = basis_ref.shape[1]
     sums = jnp.sum(sums_ref[...], axis=0, keepdims=True)
     lane = lax.broadcasted_iota(jnp.int32, (members, LANES), 1)
@@ -104,9 +112,8 @@
     residual_ref[...] = residual
     blocks = residual.shape[1] // LANES
     for index in range(blocks):
-        for slots_ref in (col_slots_ref, row_slots_ref):
-            for slot in range(slots_ref.shape[0]):
-                slots_ref[slot, index] = block(residual, index)
+        for slot in range(slots_ref.shape[0]):
+            slots_ref[slot, index] = block(residual, index)
     basis = jnp.concatenate([basis_ref[0], residual, basis_ref[1]], axis=0)
     gram = exact_dot(basis, basis, NT)
     early = exact_dot(jnp.concatenate([images_ref[0], images_ref[1]], axis=0), basis, NT)
@@ -118,8 +125,31 @@
         early[members:],
     ]
     for index, part in enumerate(pack_rows(extra)):
-        for slot in range(col_slots_ref.shape[0]):
-            col_slots_ref[slot, blocks + index] = part
+        for slot in range(slots_ref.shape[0]):
+            slots_ref[slot, blocks + index] = part
+
+
+def line_kernel(first_ref, second_ref, third_ref, fourth_ref, line_ref):
+    lines, blocks = line_ref.shape[:2]
+    here = lax.axis_index("row") // 2
+    for shift, piece_ref in enumerate((first_ref, second_ref, third_ref, fourth_ref)):
+        place = lax.rem(here + lines - shift, lines)
+        for index in range(blocks):
+            line_ref[place, index] = piece_ref[:, index * LANES : (index + 1) * LANES]
+
+
+def halves_kernel(own_ref, received_ref, first_ref, second_ref, third_ref, fourth_ref):
+    here = lax.axis_index("row") // 2
+    outputs = (first_ref, second_ref, third_ref, fourth_ref)
+    lines = len(outputs)
+    blocks = (own_ref.shape[0] - first_ref.shape[0]) // (lines - 1)
+    for shift, out_ref in enumerate(outputs):
+        start = lax.rem(here + shift, lines) * blocks
+        for index in range(blocks):
+            out_ref[index] = own_ref[start + index] + received_ref[start + index]
+        for index in range(out_ref.shape[0] - blocks):
+            tail = lines * blocks + index
+            out_ref[blocks + index] = own_ref[tail] + received_ref[tail]
 
 
 def pack_rows(parts):
@@ -147,9 +177,10 @@
     return part
 
 
-def factor_kernel(parts_ref, inverse_ref, early_ref):
-    width = parts_ref.shape[1]
-    extras = [sum_peers(parts_ref, width - 2), sum_peers(parts_ref, width - 1)]
+def factor_kernel(first_ref, second_ref, third_ref, fourth_ref, inverse_ref, early_ref):
+    parts = [part_ref[first_ref.shape[0] - 2 :] for part_ref in (first_ref, second_ref, third_ref, fourth_ref)]
+    sums = parts[0] + parts[1] + parts[2] + parts[3]
+    extras = [sums[0], sums[1]]
     members = extras[0].shape[0]
     order = 3 * members
     first, second, third, fourth, fifth = unpack_rows(*extras)
@@ -179,12 +210,21 @@
     out_ref[...] = exact_dot(inverse_ref[...] * row_scale, rows, NN)
 
 
-def image_kernel(col_parts_ref, row_parts_ref, basis_ref, residual_ref, image_ref, slots_ref):
+def image_kernel(
+    col_parts_ref,
+    first_ref,
+    second_ref,
+    third_ref,
+    fourth_ref,
+    basis_ref,
+    residual_ref,
+    image_ref,
+    slots_ref,
+):
     blocks = image_ref.shape[1] // LANES
     for index in range(blocks):
-        image_ref[:, index * LANES : (index + 1) * LANES] = sum_peers(
-            col_parts_ref, index
-        ) + sum_peers(row_parts_ref, index)
+        part = first_ref[index] + second_ref[index] + third_ref[index] + fourth_ref[index]
+        image_ref[:, index * LANES : (index + 1) * LANES] = sum_peers(col_parts_ref, index) + part
     basis = jnp.concatenate([basis_ref[0], residual_ref[...], basis_ref[1]], axis=0)
     late = exact_dot(image_ref[...], basis, NT)
     half = late.shape[0] // 2
@@ -274,33 +314,37 @@
     tiles_hbm,
     own_ref,
     other_ref,
-    out_ref,
+    own_out_ref,
+    other_out_ref,
     tiles_ref,
     arrived,
     split_ref,
+    totals_ref,
 ):
     start_tiles(count_ref, tiles_hbm, tiles_ref, arrived)
     peers, width = own_ref.shape[:2]
     per_peer = split_ref.shape[0] // (2 * peers)
-    extra = width - per_peer
-    out_ref[...] = jnp.zeros_like(out_ref)
+    half = totals_ref.shape[0] // 2
+    totals_ref[...] = jnp.zeros_like(totals_ref)
     split_blocks(own_ref, split_ref, 0, per_peer)
     split_blocks(other_ref, split_ref, peers * per_peer, per_peer)
-    for index in range(extra):
+    for index in range(width - per_peer):
         part = sum_peers(own_ref, per_peer + index) + sum_peers(other_ref, per_peer + index)
-        for start in range(per_peer, out_ref.shape[0], width):
-            out_ref[start + index] = part
+        own_out_ref[half + index] = part
+        other_out_ref[half + index] = part
     tile_groups(
         count_ref,
         tiles_hbm,
         tiles_ref,
         arrived,
         split_ref,
-        out_ref,
+        totals_ref,
         lambda slot: rows_ref[0, 0, slot],
-        lambda slot: cols_ref[0, 0, slot] + extra * (cols_ref[0, 0, slot] // per_peer),
+        lambda slot: cols_ref[0, 0, slot],
         NN,
     )
+    own_out_ref[:half] = totals_ref[:half]
+    other_out_ref[:half] = totals_ref[half:]
 
 
 def forward_kernel(
@@ -308,7 +352,8 @@
     rows_ref,
     cols_ref,
     tiles_hbm,
-    x_ref,
+    line_ref,
+    far_line_ref,
     own_ref,
     other_ref,
     tiles_ref,
@@ -318,7 +363,9 @@
 ):
     start_tiles(count_ref, tiles_hbm, tiles_ref, arrived)
     totals_ref[...] = jnp.zeros_like(totals_ref)
-    split_blocks(x_ref, split_ref, 0, x_ref.shape[1])
+    lines, blocks = line_ref.shape[:2]
+    split_blocks(line_ref, split_ref, 0, blocks)
+    split_blocks(far_line_ref, split_ref, lines * blocks, blocks)
     tile_groups(
         count_ref,
         tiles_hbm,
@@ -361,6 +408,11 @@
     return lax.ppermute(array, axis, [(i, i ^ distance) for i in range(lax.axis_size(axis))])
 
 
+def shift_lines(array, shift):
+    size = lax.axis_size("row")
+    return lax.ppermute(array, "row", [(i, (i + 2 * shift) % size) for i in range(size)])
+
+
 def on_device(
     tile_blocks, tile_rows, tile_cols, tile_count, vectors, hvectors, previous, hprevious
 ):
@@ -371,6 +423,7 @@
     core_groups = [[2 * chip + core for chip in range(chips)] for core in (0, 1)]
     members, piece = vectors.shape
     blocks = piece // LANES
+    lines = n_row // 2
     order = 3 * members
     tiles = tile_blocks[0, 0]
     row_scale = math.sqrt(piece * n_row * n_col)
@@ -391,55 +444,56 @@
         compiler_params=pltpu.CompilerParams(vmem_limit_bytes=FULL_VMEM_BYTES),
         name="stage",
     )(vectors, hvectors)
-    rows, basis, images = pl.pallas_call(
+    rows, cols, basis, images = pl.pallas_call(
         prepare_kernel,
         out_shape=[
             jax.ShapeDtypeStruct(tile_rows.shape, jnp.int32),
+            jax.ShapeDtypeStruct(tile_cols.shape, jnp.int32),
             jax.ShapeDtypeStruct((2, members, piece), f32),
             jax.ShapeDtypeStruct((2, members, piece), f32),
         ],
-        in_specs=[vmem_spec] + [hbm_spec] * 4,
-        out_specs=[vmem_spec] * 3,
+        in_specs=[vmem_spec] * 2 + [hbm_spec] * 4,
+        out_specs=[vmem_spec] * 4,
         scratch_shapes=[pltpu.SemaphoreType.DMA((4,))],
         compiler_params=params,
         name="prepare",
-    )(tile_rows, vectors, previous, hvectors, hprevious)
+    )(tile_rows, tile_cols, vectors, previous, hvectors, hprevious)
     sums = exchange(sums, everyone)
-    sums, rows, basis, images = lax.optimization_barrier((sums, rows, basis, images))
-    residual, col_slots, row_slots = call(
-        residual_kernel,
-        [
-            (members, piece),
-            (chips, blocks + 2, members, LANES),
-            (n_row, blocks, members, LANES),
-        ],
-        "residual",
+    sums, rows, cols, basis, images = lax.optimization_barrier((sums, rows, cols, basis, images))
+    residual, slots = call(
+        residual_kernel, [(members, piece), (chips, blocks + 2, members, LANES)], "residual"
     )(sums, basis, images)
-    own_range = exchange(col_slots, "col", core_groups)
-    own_range, row_slots = lax.optimization_barrier((own_range, row_slots))
+    pieces = [residual] + [shift_lines(residual, shift) for shift in range(1, lines)]
+    (line,) = call(line_kernel, [(lines, blocks, members, LANES)], "line")(*pieces)
+    own_range = exchange(slots, "col", core_groups)
+    own_range, line = lax.optimization_barrier((own_range, line))
+    far_line = swap(line, "row", 1)
     other_range = swap(own_range, "col", 1)
-    col_range = exchange(row_slots, "row")
-    (col_totals,) = tile_call(
+    half = (lines * blocks + 2, members, LANES)
+    col_own, col_other = tile_call(
         backward_kernel,
         tile_count,
         rows,
-        tile_cols,
+        cols,
         tiles,
         (own_range, other_range),
-        [(n_row * (blocks + 2), members, LANES)],
-        [pltpu.VMEM((n_col * blocks, 2 * members, LANES), jnp.bfloat16)],
+        [half, half],
+        [
+            pltpu.VMEM((n_col * blocks, 2 * members, LANES), jnp.bfloat16),
+            pltpu.VMEM((n_row * blocks, members, LANES), f32),
+        ],
         "backward_tiles",
     )
-    col_totals, col_range = lax.optimization_barrier((col_totals, col_range))
-    row_parts = exchange(col_totals.reshape(n_row, blocks + 2, members, LANES), "row")
+    col_own, col_other, far_line = lax.optimization_barrier((col_own, col_other, far_line))
+    col_received = swap(col_other, "row", 1)
     half = (chips * blocks, members, LANES)
     own_totals, other_totals = tile_call(
         forward_kernel,
         tile_count,
         rows,
-        tile_cols,
+        cols,
         tiles,
-        (col_range,),
+        (line, far_line),
         [half, half],
         [
             pltpu.VMEM((n_row * blocks, 2 * members, LANES), jnp.bfloat16),
@@ -447,20 +501,25 @@
         ],
         "forward_tiles",
     )
-    row_parts, own_totals, other_totals = lax.optimization_barrier(
-        (row_parts, own_totals, other_totals)
+    col_received, own_totals, other_totals = lax.optimization_barrier(
+        (col_received, own_totals, other_totals)
     )
     totals = own_totals + swap(other_totals, "col", 1)
     col_parts = exchange(totals.reshape(chips, blocks, members, LANES), "col", core_groups)
-    inverse, early = call(factor_kernel, [(order, order), (2 * members, order)], "factor")(row_parts)
+    outs = call(halves_kernel, [(blocks + 2, members, LANES)] * lines, "halves")(
+        col_own, col_received
+    )
+    row_parts = [outs[0]] + [shift_lines(outs[shift], shift) for shift in range(1, lines)]
+    col_parts, *row_parts = lax.optimization_barrier((col_parts, *row_parts))
+    image, slots = call(
+        image_kernel, [(members, piece), (n_row * n_col, members // 2, LANES)], "image"
+    )(col_parts, *row_parts, basis, residual)
+    late = exchange(slots, everyone)
+    image, *row_parts = lax.optimization_barrier((image, *row_parts))
+    inverse, early = call(factor_kernel, [(order, order), (2 * members, order)], "factor")(*row_parts)
     (orthonormal,) = call(
         functools.partial(orthonormal_kernel, row_scale=row_scale), [(order, piece)], "orthonormal"
     )(inverse, basis, residual)
-    col_parts, inverse, orthonormal = lax.optimization_barrier((col_parts, inverse, orthonormal))
-    image, slots = call(
-        image_kernel, [(members, piece), (n_row * n_col, members // 2, LANES)], "image"
-    )(col_parts, row_parts, basis, residual)
-    late = exchange(slots, everyone)
     (orthonormal_image,) = call(
         functools.partial(orthonormal_image_kernel, row_scale=row_scale),
         [(order, piece)],

time: 111 us -> 103 us (0.928); the launches traced: 112 us -> 102 us
  blocking collectives: 12.9 us -> 0 us
  starting transfers between devices: 35.8 us -> 45.2 us
  waiting for transfers between devices: 33 us -> 24.2 us
  Pallas kernels: 22.2 us -> 23.5 us
  local copies, waits for them, and re-layouts: 4.88 us -> 6.14 us
    all_to_all x5 -> x4, waiting for transfers between devices: 31.2 us -> 14.3 us  [exchange(): lax.all_to_all(slots, axes, 0, 0, axis_index_groups=groups, tiled=True)]
    all_to_all x1 -> x0, blocking collectives: 12.9 us -> none  [exchange(): lax.all_to_all(slots, axes, 0, 0, axis_index_groups=groups, tiled=True)]
    ppermute x0 -> x6, starting transfers between devices: none -> 10.8 us  [shift_lines(): lax.ppermute(array, 'row', [(i, (i + 2 * shift) % size) for i in range(si...]
    ppermute x0 -> x6, waiting for transfers between devices: none -> 4.38 us  [shift_lines(): lax.ppermute(array, 'row', [(i, (i + 2 * shift) % size) for i in range(si...]
    ppermute x2 -> x4, waiting for transfers between devices: 1.75 us -> 5.51 us  [swap(): lax.ppermute(array, axis, [(i, i ^ distance) for i in range(lax.axis_size...]
    all_to_all x5 -> x4, starting transfers between devices: 31.5 us -> 28.5 us  [exchange(): lax.all_to_all(slots, axes, 0, 0, axis_index_groups=groups, tiled=True)]
    ppermute x2 -> x4, starting transfers between devices: 4.33 us -> 5.88 us  [swap(): lax.ppermute(array, axis, [(i, i ^ distance) for i in range(lax.axis_size...]
    unnamed x18 -> x26, local copies, waits for them, and re-layouts: 4.88 us -> 6.14 us
  transfers between devices with their start and end apart: 7 -> 14, of which waited for: 6 -> 10; matrix products, arithmetic and copies ran while one was open for 0% -> 0% of each run, Pallas kernels for 15% -> 18%
where the time goes in v6:
time: 103 us; the launch traced here: 102 us
  starting transfers between devices  45.2 us (44%)
  waiting for transfers between devices  24.2 us (23%)
  Pallas kernels  23.5 us (23%)
  local copies, waits for them, and re-layouts  6.14 us (6%)
  other arithmetic  1.91 us (2%)
  between operations  1.45 us (1%)
    all_to_all x4, starting transfers between devices, exchange(): lax.all_to_all(slots, axes, 0, 0, axis_index_groups=groups, tiled=True)  28.5 us
    all_to_all x4, waiting for transfers between devices, exchange(): lax.all_to_all(slots, axes, 0, 0, axis_index_groups=groups, tiled=True)  14.3 us
    pallas_call x2, Pallas kernels, tile_call(): pl.pallas_call(kernel, out_shape=[jax.ShapeDtypeStruct(shape, jnp.float32...  11.1 us
    ppermute x6, starting transfers between devices, shift_lines(): lax.ppermute(array, 'row', [(i, (i + 2 * shift) % size) for i in range(si...  10.8 us
    unnamed x26, local copies, waits for them, and re-layouts  6.14 us
    ppermute x4, starting transfers between devices, swap(): lax.ppermute(array, axis, [(i, i ^ distance) for i in range(lax.axis_size...  5.88 us
    ppermute x4, waiting for transfers between devices, swap(): lax.ppermute(array, axis, [(i, i ^ distance) for i in range(lax.axis_size...  5.51 us
    pallas_call x1, Pallas kernels, on_device(): call(factor_kernel, [(order, order), (2 * members, order)], 'factor')  4.48 us
  transfers between devices with their start and end apart: 14, of which 10 were waited for; matrix products, arithmetic and copies ran while one was open for 0% of the time, Pallas kernels for 18%

profile of v6, /device:TPU:1, one launch (start us, length us, event | category | flops | bytes accessed | tf_op | source)
XLA Modules:
  0.0 102.4 jit_solution(5862305080241491216)
XLA Ops:
  0.6 1.6 %stage.1 = f32[128,128]{1,0:T(8,128)} custom-call(f32[16,1024]{1,0:T(8,128)} %vectors_hbm.3, f32[16,1024]{1,0:T(8,128)} %hvectors_hbm.3), custom_call_target="tpu_custom_call" | custom-call | tf_op jit(solution)/shard_map/stage/pallas_call | solution.py:435
  2.3 11.5 %all-to-all-start = ((f32[128,1,128]{2,1,0:T(1,128)}), f32[128,1,128]{2,1,0:T(1,128)S(1)}, u32[]{:S(2)}, u32[]{:S(2)}) async-start(f32[128,1,128]{2,1,0:T(1,128)} %bitcast.9), calls=%async_computation | async-start | bytes 131072 | tf_op jit(solution)/shard_map/all_to_all | solution.py:404
  13.8 0.0 copy-start.2
  13.8 0.8 copy-done.2
  14.6 0.0 copy-start.3
  14.6 0.8 copy-done.3
  15.4 0.0 copy-start.4
  15.5 0.8 copy-done.4
  16.3 0.0 copy-start.5
  16.3 0.8 copy-done.5
  17.1 0.0 copy-start.8
  17.1 0.7 copy-done.8
  17.8 0.0 copy-start.9
  17.8 0.7 copy-done.9
  18.5 0.4 prepare.1
  18.9 0.0 copy-start.6
  18.9 0.6 copy-done.6
  19.4 0.0 copy-start.7
  19.4 3.9 %all-to-all-done = f32[128,1,128]{2,1,0:T(1,128)S(1)} async-done(((f32[128,1,128]{2,1,0:T(1,128)}), f32[128,1,128]{2,1,0:T(1,128)S(1)}, u32[]{:S(2)}, u32[]{:S(2)}) %all-to-all-start) | async-done | bytes 65568 | tf_op jit(solution)/shard_map/all_to_all | solution.py:404
  23.3 0.0 copy-done.7
  23.3 1.5 %residual.1 = (f32[16,1024]{1,0:T(8,128)S(1)}, f32[8,10,16,128]{3,2,1,0:T(8,128)}) custom-call(f32[128,128]{1,0:T(8,128)S(1)} %bitcast.6, f32[2,16,1024]{2,1,0:T(8,128)S(1)} %get-tuple-element.51.basis_ref, f32[2,16,1024]{2,1,0:T(8,128)S(1)} %get-tuple-element.52.images_ref), custom_call_target="tpu_custom_call" | custom-call | tf_op jit(solution)/shard_map/residual/pallas_call | solution.py:463
  24.8 3.5 %all-to-all-start.1 = ((f32[8,10,16,128]{3,2,1,0:T(8,128)}), f32[8,10,16,128]{3,2,1,0:T(8,128)S(1)}, u32[]{:S(2)}, u32[]{:S(2)}) async-start(f32[8,10,16,128]{3,2,1,0:T(8,128)} %get-tuple-element.53), calls=%async_computation.1 | async-start | bytes 1310720 | tf_op jit(solution)/shard_map/all_to_all | solution.py:404
  28.4 0.3 collective-permute-start
  28.6 2.3 %collective-permute-start.1 = (f32[16,1024]{1,0:T(8,128)S(1)}, f32[16,1024]{1,0:T(8,128)S(1)}, u32[]{:S(2)}, u32[]{:S(2)}) collective-permute-start(f32[16,1024]{1,0:T(8,128)S(1)} %get-tuple-element.54.first_ref.residual_ref), channel_id=1, source_target_pairs={{0,64},{16,80},{32,96},{48,112},{64,0},{80,16},{96,32},{112,48},{1... | collective-permute-start | bytes 196616 | tf_op jit(solution)/shard_map/ppermute | solution.py:413
  31.0 0.9 collective-permute-start.2
  31.9 1.6 %collective-permute-done.second_ref = f32[16,1024]{1,0:T(8,128)S(1)} collective-permute-done((f32[16,1024]{1,0:T(8,128)S(1)}, f32[16,1024]{1,0:T(8,128)S(1)}, u32[]{:S(2)}, u32[]{:S(2)}) %collective-permute-start) | collective-permute-done | bytes 65568 | tf_op jit(solution)/shard_map/ppermute | solution.py:413
  33.5 0.2 collective-permute-done.1.third_ref
  33.6 0.8 collective-permute-done.2.fourth_ref
  34.4 0.0 copy-start
  34.4 3.4 %all-to-all-done.1.own_ref = f32[8,10,16,128]{3,2,1,0:T(8,128)S(1)} async-done(((f32[8,10,16,128]{3,2,1,0:T(8,128)}), f32[8,10,16,128]{3,2,1,0:T(8,128)S(1)}, u32[]{:S(2)}, u32[]{:S(2)}) %all-to-all-start.1) | async-done | bytes 655392 | tf_op jit(solution)/shard_map/all_to_all | solution.py:404
  37.9 0.0 copy-start.10
  37.9 2.0 %collective-permute-start.3 = (f32[8,10,16,128]{3,2,1,0:T(8,128)S(1)}, f32[8,10,16,128]{3,2,1,0:T(8,128)S(1)}, u32[]{:S(2)}, u32[]{:S(2)}) collective-permute-start(f32[8,10,16,128]{3,2,1,0:T(8,128)S(1)} %all-to-all-done.1.own_ref), channel_id=1, source_target_pairs={{0,1},{1,0},{2,3},{3,2},{4,5},{5,4},{6,7},{7,6},{8,9},{9,8},{10,11... | collective-permute-start | bytes 1966088 | tf_op jit(solution)/shard_map/ppermute | solution.py:408
  39.9 1.1 %collective-permute-start.4 = (f32[4,8,16,128]{3,2,1,0:T(8,128)S(1)}, f32[4,8,16,128]{3,2,1,0:T(8,128)S(1)}, u32[]{:S(2)}, u32[]{:S(2)}) collective-permute-start(f32[4,8,16,128]{3,2,1,0:T(8,128)S(1)} %line.1.line_ref), channel_id=1, source_target_pairs={{0,16},{16,0},{32,48},{48,32},{64,80},{80,64},{96,112},{112,96},{1... | collective-permute-start | bytes 786440 | tf_op jit(solution)/shard_map/ppermute | solution.py:408
  41.6 0.0 collective-permute-done.3.other_ref
  41.7 0.0 copy-start.11
  41.7 0.0 copy-done.10
  41.7 0.8 copy-done.11
  42.5 5.1 %backward_tiles.1 = (f32[34,16,128]{2,1,0:T(8,128)}, f32[34,16,128]{2,1,0:T(8,128)}) custom-call(s32[1,1]{1,0:T(1,128)S(6)} %copy.12.count_ref, s32[1,1,384]{2,1,0:T(1,128)} %copy-done.6, s32[1,1,384]{2,1,0:T(1,128)} %copy-done.7, bf16[384,128,128]{2,1,0:T(8,128)(2,1)} %bitcast.7, f32[8,10,16,128]{3,2,1,0:T(8,128)} %copy-done.10, f32[8,10,16,128]{3,2,1,0:T(8,128)} %copy-done.11), custom_call_target="tpu_custom_call" | custom-call | tf_op jit(solution)/shard_map/backward_tiles/pallas_call | solution.py:388
  47.6 0.0 copy-start.1
  47.6 1.7 %collective-permute-done.4.far_line_ref = f32[4,8,16,128]{3,2,1,0:T(8,128)S(1)} collective-permute-done((f32[4,8,16,128]{3,2,1,0:T(8,128)S(1)}, f32[4,8,16,128]{3,2,1,0:T(8,128)S(1)}, u32[]{:S(2)}, u32[]{:S(2)}) %collective-permute-start.4) | collective-permute-done | bytes 262176 | tf_op jit(solution)/shard_map/ppermute | solution.py:408
  49.4 1.1 %collective-permute-start.5 = (f32[34,16,128]{2,1,0:T(8,128)}, f32[34,16,128]{2,1,0:T(8,128)S(1)}, u32[]{:S(2)}, u32[]{:S(2)}) collective-permute-start(f32[34,16,128]{2,1,0:T(8,128)} %get-tuple-element.59), channel_id=1, source_target_pairs={{0,16},{16,0},{32,48},{48,32},{64,80},{80,64},{96,112},{112,96},{1... | collective-permute-start | bytes 835592 | tf_op jit(solution)/shard_map/ppermute | solution.py:408
  50.4 0.0 copy-done
  50.4 0.0 copy-done.12
  50.4 6.0 %forward_tiles.1 = (f32[64,16,128]{2,1,0:T(8,128)}, f32[64,16,128]{2,1,0:T(8,128)}) custom-call(s32[1,1]{1,0:T(1,128)S(6)} %copy.12.count_ref, s32[1,1,384]{2,1,0:T(1,128)} %copy-done.6, s32[1,1,384]{2,1,0:T(1,128)} %copy-done.7, bf16[384,128,128]{2,1,0:T(8,128)(2,1)} %bitcast.8, f32[4,8,16,128]{3,2,1,0:T(8,128)} %copy-done, f32[4,8,16,128]{3,2,1,0:T(8,128)} %copy-done.12), custom_call_target="tpu_custom_call" | custom-call | tf_op jit(solution)/shard_map/forward_tiles/pallas_call | solution.py:388
  56.4 2.0 %collective-permute-done.5.received_ref = f32[34,16,128]{2,1,0:T(8,128)S(1)} collective-permute-done((f32[34,16,128]{2,1,0:T(8,128)}, f32[34,16,128]{2,1,0:T(8,128)S(1)}, u32[]{:S(2)}, u32[]{:S(2)}) %collective-permute-start.5) | collective-permute-done | bytes 278560 | tf_op jit(solution)/shard_map/ppermute | solution.py:408
  58.5 1.7 %collective-permute-start.6 = (f32[64,16,128]{2,1,0:T(8,128)}, f32[64,16,128]{2,1,0:T(8,128)S(1)}, u32[]{:S(2)}, u32[]{:S(2)}) collective-permute-start(f32[64,16,128]{2,1,0:T(8,128)} %get-tuple-element.64), channel_id=1, source_target_pairs={{0,1},{1,0},{2,3},{3,2},{4,5},{5,4},{6,7},{7,6},{8,9},{9,8},{10,11... | collective-permute-start | bytes 1572872 | tf_op jit(solution)/shard_map/ppermute | solution.py:408
  60.1 1.7 %collective-permute-done.6 = f32[64,16,128]{2,1,0:T(8,128)S(1)} collective-permute-done((f32[64,16,128]{2,1,0:T(8,128)}, f32[64,16,128]{2,1,0:T(8,128)S(1)}, u32[]{:S(2)}, u32[]{:S(2)}) %collective-permute-start.6) | collective-permute-done | bytes 524320 | tf_op jit(solution)/shard_map/ppermute | solution.py:408
  61.9 1.9 %add.3 = f32[64,16,128]{2,1,0:T(8,128)} add(f32[64,16,128]{2,1,0:T(8,128)} %get-tuple-element.63, f32[64,16,128]{2,1,0:T(8,128)S(1)} %collective-permute-done.6) | non-fusion elementwise | flops 131072 | bytes 1572864 | tf_op jit(solution)/shard_map/add | solution.py:507
  63.8 3.5 %all-to-all-start.2 = ((f32[8,8,16,128]{3,2,1,0:T(8,128)}), f32[8,8,16,128]{3,2,1,0:T(8,128)S(1)}, u32[]{:S(2)}, u32[]{:S(2)}) async-start(f32[8,8,16,128]{3,2,1,0:T(8,128)} %bitcast.4), calls=%async_computation.2 | async-start | bytes 1048576 | tf_op jit(solution)/shard_map/all_to_all | solution.py:404
  67.3 0.0 copy-done.1
  67.4 0.3 collective-permute-start.7
  67.6 5.1 %collective-permute-start.8 = (f32[10,16,128]{2,1,0:T(8,128)S(1)}, f32[10,16,128]{2,1,0:T(8,128)S(1)}, u32[]{:S(2)}, u32[]{:S(2)}) collective-permute-start(f32[10,16,128]{2,1,0:T(8,128)S(1)} %get-tuple-element.69), channel_id=1, source_target_pairs={{0,64},{16,80},{32,96},{48,112},{64,0},{80,16},{96,32},{112,48},{1... | collective-permute-start | bytes 245768 | tf_op jit(solution)/shard_map/ppermute | solution.py:413
  72.7 2.0 %collective-permute-start.9 = (f32[10,16,128]{2,1,0:T(8,128)S(1)}, f32[10,16,128]{2,1,0:T(8,128)S(1)}, u32[]{:S(2)}, u32[]{:S(2)}) collective-permute-start(f32[10,16,128]{2,1,0:T(8,128)S(1)} %get-tuple-element.70), channel_id=1, source_target_pairs={{0,96},{16,112},{32,0},{48,16},{64,32},{80,48},{96,64},{112,80},{1... | collective-permute-start | bytes 245768 | tf_op jit(solution)/shard_map/ppermute | solution.py:413
  74.7 0.0 collective-permute-done.7.second_ref
  74.7 1.9 %collective-permute-done.8.third_ref = f32[10,16,128]{2,1,0:T(8,128)S(1)} collective-permute-done((f32[10,16,128]{2,1,0:T(8,128)S(1)}, f32[10,16,128]{2,1,0:T(8,128)S(1)}, u32[]{:S(2)}, u32[]{:S(2)}) %collective-permute-start.8) | collective-permute-done | bytes 81952 | tf_op jit(solution)/shard_map/ppermute | solution.py:413
  76.6 0.0 collective-permute-done.9.fourth_ref
  76.6 0.0 all-to-all-done.2.col_parts_ref
  76.6 1.2 %image.1 = (f32[16,1024]{1,0:T(8,128)S(1)}, f32[128,8,128]{2,1,0:T(8,128)}) custom-call(f32[8,8,16,128]{3,2,1,0:T(8,128)S(1)} %all-to-all-done.2.col_parts_ref, f32[10,16,128]{2,1,0:T(8,128)S(1)} %get-tuple-element.77.first_ref, f32[10,16,128]{2,1,0:T(8,128)S(1)} %collective-permute-done.7.second_ref, f32[10,16,128]{2,1,0:T(8,128)S(1)} %collective-permute-done.8.third_ref, ...), custom_call_target="tpu_custom_call" | custom-call | tf_op jit(solution)/shard_map/image/pallas_call | solution.py:514
  77.8 10.0 %all-to-all-start.3 = ((f32[128,8,128]{2,1,0:T(8,128)}), f32[128,8,128]{2,1,0:T(8,128)S(1)}, u32[]{:S(2)}, u32[]{:S(2)}) async-start(f32[128,8,128]{2,1,0:T(8,128)} %get-tuple-element.83), calls=%async_computation.3 | async-start | bytes 1048576 | tf_op jit(solution)/shard_map/all_to_all | solution.py:404
  87.7 4.5 %factor.1 = (f32[48,48]{1,0:T(8,128)S(1)}, f32[32,48]{1,0:T(8,128)S(1)}) custom-call(f32[10,16,128]{2,1,0:T(8,128)S(1)} %get-tuple-element.77.first_ref, f32[10,16,128]{2,1,0:T(8,128)S(1)} %collective-permute-done.7.second_ref, f32[10,16,128]{2,1,0:T(8,128)S(1)} %collective-permute-done.8.third_ref, f32[10,16,128]{2,1,0:T(8,128)S(1)} %collective-permute-done.9.fourth_ref), custom_call_target="tpu_custom_call" | custom-call | tf_op jit(solution)/shard_map/factor/pallas_call | solution.py:519
  92.2 1.0 orthonormal.1
  93.2 1.0 orthonormal_image.1
  94.2 7.0 %all-to-all-done.3.received_ref = f32[128,8,128]{2,1,0:T(8,128)S(1)} async-done(((f32[128,8,128]{2,1,0:T(8,128)}), f32[128,8,128]{2,1,0:T(8,128)S(1)}, u32[]{:S(2)}, u32[]{:S(2)}) %all-to-all-start.3) | async-done | bytes 524320 | tf_op jit(solution)/shard_map/all_to_all | solution.py:404
  101.2 1.2 %projected.1 = f32[48,48]{1,0:T(8,128)} custom-call(f32[128,8,128]{2,1,0:T(8,128)S(1)} %all-to-all-done.3.received_ref, f32[48,48]{1,0:T(8,128)S(1)} %get-tuple-element.81.inverse_ref, f32[32,48]{1,0:T(8,128)S(1)} %get-tuple-element.84.early_ref), custom_call_target="tpu_custom_call" | custom-call | tf_op jit(solution)/shard_map/projected/pallas_call | solution.py:528
  (3 shorter events, 0.1 us)
Async XLA Ops:
  2.3 21.0 %all-to-all-start = ((f32[128,1,128]{2,1,0:T(1,128)}), f32[128,1,128]{2,1,0:T(1,128)S(1)}, u32[]{:S(2)}, u32[]{:S(2)}) async-start(f32[128,1,128]{2,1,0:T(1,128)} %bitcast.9), calls=%async_computation | async-start | bytes 131072 | tf_op jit(solution)/shard_map/all_to_all | solution.py:404
  13.8 0.8 copy-start.2
  14.6 0.8 copy-start.3
  15.4 0.8 copy-start.4
  16.3 0.8 copy-start.5
  17.1 0.7 copy-start.8
  17.8 0.7 copy-start.9
  18.9 0.6 copy-start.6
  19.4 3.9 %copy-start.7 = (s32[1,1,384]{2,1,0:T(1,128)}, s32[1,1,384]{2,1,0:T(1,128)S(1)}, u32[]{:S(2)}) copy-start(s32[1,1,384]{2,1,0:T(1,128)S(1)} %get-tuple-element.49.cols_ref) | copy-start | bytes 4612
  24.8 13.0 %all-to-all-start.1 = ((f32[8,10,16,128]{3,2,1,0:T(8,128)}), f32[8,10,16,128]{3,2,1,0:T(8,128)S(1)}, u32[]{:S(2)}, u32[]{:S(2)}) async-start(f32[8,10,16,128]{3,2,1,0:T(8,128)} %get-tuple-element.53), calls=%async_computation.1 | async-start | bytes 1310720 | tf_op jit(solution)/shard_map/all_to_all | solution.py:404
  28.4 5.1 %collective-permute-start = (f32[16,1024]{1,0:T(8,128)S(1)}, f32[16,1024]{1,0:T(8,128)S(1)}, u32[]{:S(2)}, u32[]{:S(2)}) collective-permute-start(f32[16,1024]{1,0:T(8,128)S(1)} %get-tuple-element.54.first_ref.residual_ref), channel_id=1, source_target_pairs={{0,32},{16,48},{32,64},{48,80},{64,96},{80,112},{96,0},{112,16},{1... | collective-permute-start | bytes 196616 | tf_op jit(solution)/shard_map/ppermute | solution.py:413
  28.6 5.0 %collective-permute-start.1 = (f32[16,1024]{1,0:T(8,128)S(1)}, f32[16,1024]{1,0:T(8,128)S(1)}, u32[]{:S(2)}, u32[]{:S(2)}) collective-permute-start(f32[16,1024]{1,0:T(8,128)S(1)} %get-tuple-element.54.first_ref.residual_ref), channel_id=1, source_target_pairs={{0,64},{16,80},{32,96},{48,112},{64,0},{80,16},{96,32},{112,48},{1... | collective-permute-start | bytes 196616 | tf_op jit(solution)/shard_map/ppermute | solution.py:413
  31.0 3.4 %collective-permute-start.2 = (f32[16,1024]{1,0:T(8,128)S(1)}, f32[16,1024]{1,0:T(8,128)S(1)}, u32[]{:S(2)}, u32[]{:S(2)}) collective-permute-start(f32[16,1024]{1,0:T(8,128)S(1)} %get-tuple-element.54.first_ref.residual_ref), channel_id=1, source_target_pairs={{0,96},{16,112},{32,0},{48,16},{64,32},{80,48},{96,64},{112,80},{1... | collective-permute-start | bytes 196616 | tf_op jit(solution)/shard_map/ppermute | solution.py:413
  34.4 16.0 %copy-start = (f32[4,8,16,128]{3,2,1,0:T(8,128)}, f32[4,8,16,128]{3,2,1,0:T(8,128)S(1)}, u32[]{:S(2)}) copy-start(f32[4,8,16,128]{3,2,1,0:T(8,128)S(1)} %line.1.line_ref) | copy-start | bytes 786436
  37.9 3.8 %copy-start.10 = (f32[8,10,16,128]{3,2,1,0:T(8,128)}, f32[8,10,16,128]{3,2,1,0:T(8,128)S(1)}, u32[]{:S(2)}) copy-start(f32[8,10,16,128]{3,2,1,0:T(8,128)S(1)} %all-to-all-done.1.own_ref) | copy-start | bytes 1966084
  37.9 3.8 %collective-permute-start.3 = (f32[8,10,16,128]{3,2,1,0:T(8,128)S(1)}, f32[8,10,16,128]{3,2,1,0:T(8,128)S(1)}, u32[]{:S(2)}, u32[]{:S(2)}) collective-permute-start(f32[8,10,16,128]{3,2,1,0:T(8,128)S(1)} %all-to-all-done.1.own_ref), channel_id=1, source_target_pairs={{0,1},{1,0},{2,3},{3,2},{4,5},{5,4},{6,7},{7,6},{8,9},{9,8},{10,11... | collective-permute-start | bytes 1966088 | tf_op jit(solution)/shard_map/ppermute | solution.py:408
  39.9 9.4 %collective-permute-start.4 = (f32[4,8,16,128]{3,2,1,0:T(8,128)S(1)}, f32[4,8,16,128]{3,2,1,0:T(8,128)S(1)}, u32[]{:S(2)}, u32[]{:S(2)}) collective-permute-start(f32[4,8,16,128]{3,2,1,0:T(8,128)S(1)} %line.1.line_ref), channel_id=1, source_target_pairs={{0,16},{16,0},{32,48},{48,32},{64,80},{80,64},{96,112},{112,96},{1... | collective-permute-start | bytes 786440 | tf_op jit(solution)/shard_map/ppermute | solution.py:408
  41.7 0.9 copy-start.11
  47.6 19.7 %copy-start.1 = (f32[34,16,128]{2,1,0:T(8,128)S(1)}, f32[34,16,128]{2,1,0:T(8,128)}, u32[]{:S(2)}) copy-start(f32[34,16,128]{2,1,0:T(8,128)} %get-tuple-element.65.own_ref) | copy-start | bytes 835588
  49.4 1.1 %copy-start.12 = (f32[4,8,16,128]{3,2,1,0:T(8,128)}, f32[4,8,16,128]{3,2,1,0:T(8,128)S(1)}, u32[]{:S(2)}) copy-start(f32[4,8,16,128]{3,2,1,0:T(8,128)S(1)} %collective-permute-done.4.far_line_ref) | copy-start | bytes 786436
  49.4 9.1 %collective-permute-start.5 = (f32[34,16,128]{2,1,0:T(8,128)}, f32[34,16,128]{2,1,0:T(8,128)S(1)}, u32[]{:S(2)}, u32[]{:S(2)}) collective-permute-start(f32[34,16,128]{2,1,0:T(8,128)} %get-tuple-element.59), channel_id=1, source_target_pairs={{0,16},{16,0},{32,48},{48,32},{64,80},{80,64},{96,112},{112,96},{1... | collective-permute-start | bytes 835592 | tf_op jit(solution)/shard_map/ppermute | solution.py:408
  58.5 3.4 %collective-permute-start.6 = (f32[64,16,128]{2,1,0:T(8,128)}, f32[64,16,128]{2,1,0:T(8,128)S(1)}, u32[]{:S(2)}, u32[]{:S(2)}) collective-permute-start(f32[64,16,128]{2,1,0:T(8,128)} %get-tuple-element.64), channel_id=1, source_target_pairs={{0,1},{1,0},{2,3},{3,2},{4,5},{5,4},{6,7},{7,6},{8,9},{9,8},{10,11... | collective-permute-start | bytes 1572872 | tf_op jit(solution)/shard_map/ppermute | solution.py:408
  63.8 12.8 %all-to-all-start.2 = ((f32[8,8,16,128]{3,2,1,0:T(8,128)}), f32[8,8,16,128]{3,2,1,0:T(8,128)S(1)}, u32[]{:S(2)}, u32[]{:S(2)}) async-start(f32[8,8,16,128]{3,2,1,0:T(8,128)} %bitcast.4), calls=%async_computation.2 | async-start | bytes 1048576 | tf_op jit(solution)/shard_map/all_to_all | solution.py:404
  67.4 7.3 %collective-permute-start.7 = (f32[10,16,128]{2,1,0:T(8,128)S(1)}, f32[10,16,128]{2,1,0:T(8,128)S(1)}, u32[]{:S(2)}, u32[]{:S(2)}) collective-permute-start(f32[10,16,128]{2,1,0:T(8,128)S(1)} %get-tuple-element.68), channel_id=1, source_target_pairs={{0,32},{16,48},{32,64},{48,80},{64,96},{80,112},{96,0},{112,16},{1... | collective-permute-start | bytes 245768 | tf_op jit(solution)/shard_map/ppermute | solution.py:413
  67.6 8.9 %collective-permute-start.8 = (f32[10,16,128]{2,1,0:T(8,128)S(1)}, f32[10,16,128]{2,1,0:T(8,128)S(1)}, u32[]{:S(2)}, u32[]{:S(2)}) collective-permute-start(f32[10,16,128]{2,1,0:T(8,128)S(1)} %get-tuple-element.69), channel_id=1, source_target_pairs={{0,64},{16,80},{32,96},{48,112},{64,0},{80,16},{96,32},{112,48},{1... | collective-permute-start | bytes 245768 | tf_op jit(solution)/shard_map/ppermute | solution.py:413
  72.7 3.9 %collective-permute-start.9 = (f32[10,16,128]{2,1,0:T(8,128)S(1)}, f32[10,16,128]{2,1,0:T(8,128)S(1)}, u32[]{:S(2)}, u32[]{:S(2)}) collective-permute-start(f32[10,16,128]{2,1,0:T(8,128)S(1)} %get-tuple-element.70), channel_id=1, source_target_pairs={{0,96},{16,112},{32,0},{48,16},{64,32},{80,48},{96,64},{112,80},{1... | collective-permute-start | bytes 245768 | tf_op jit(solution)/shard_map/ppermute | solution.py:413
  77.8 23.5 %all-to-all-start.3 = ((f32[128,8,128]{2,1,0:T(8,128)}), f32[128,8,128]{2,1,0:T(8,128)S(1)}, u32[]{:S(2)}, u32[]{:S(2)}) async-start(f32[128,8,128]{2,1,0:T(8,128)} %get-tuple-element.83), calls=%async_computation.3 | async-start | bytes 1048576 | tf_op jit(solution)/shard_map/all_to_all | solution.py:404

commit v7 on v6

--- a/solution.py
+++ b/solution.py
@@ -13,7 +13,8 @@
 LANES = 128
 VMEM_BYTES = 32 << 20
 FULL_VMEM_BYTES = 60 << 20
-TILE_VMEM_BYTES = 54 << 20
+TILE_VMEM_BYTES = 48<<20
+GROUP = 64
 NT = (((1,), (1,)), ((), ()))
 NN = (((1,), (0,)), ((), ()))
 
@@ -59,17 +60,7 @@
 
 
 def prepare_kernel(
-    rows_ref,
-    cols_ref,
-    vectors_hbm,
-    previous_hbm,
-    hvectors_hbm,
-    hprevious_hbm,
-    rows_out_ref,
-    cols_out_ref,
-    basis_ref,
-    images_ref,
-    arrived,
+    vectors_hbm, previous_hbm, hvectors_hbm, hprevious_hbm, basis_ref, images_ref, arrived
 ):
     copies = [
         pltpu.make_async_copy(source, target.at[place], arrived.at[index])
@@ -84,21 +75,23 @@
     ]
     for copy in copies:
         copy.start()
+    for copy in copies:
+        copy.wait()
+
+
+def places_kernel(rows_ref, cols_ref, rows_out_ref, cols_out_ref, *, blocks, gap):
+    chips = lax.axis_size("col") // 2
+    lines = lax.axis_size("row") // 2
+    core = lax.rem(lax.axis_index("col"), 2)
     rows = rows_ref[...]
-    core = lax.rem(lax.axis_index("col"), 2)
-    chips = lax.axis_size("col") // 2
-    blocks = basis_ref.shape[2] // LANES
     index, peer = rows % blocks, rows // blocks
     other = jnp.where(peer % 2 == core, 0, 1)
     rows_out_ref[...] = (other * chips + peer // 2) * blocks + index
+    half = lax.rem(lax.axis_index("row"), 2)
     cols = cols_ref[...]
-    half = lax.rem(lax.axis_index("row"), 2)
-    lines = lax.axis_size("row") // 2
     index, peer = cols % blocks, cols // blocks
     other = jnp.where(peer % 2 == half, 0, 1)
-    cols_out_ref[...] = (other * lines + peer // 2) * blocks + index
-    for copy in copies:
-        copy.wait()
+    cols_out_ref[...] = (other * lines + peer // 2) * blocks + index + other * gap
 
 
 def residual_kernel(sums_ref, basis_ref, images_ref, residual_ref, slots_ref):
@@ -259,11 +252,11 @@
 
 
 def group_size(slots):
-    return math.gcd(slots, 24)
-
-
-def group_count(count_ref, slots):
-    return (jnp.minimum(count_ref[0, 0], slots) + group_size(slots) - 1) // group_size(slots)
+    return math.gcd(slots, GROUP)
+
+
+def group_count(live, slots):
+    return (jnp.minimum(live, slots) + group_size(slots) - 1) // group_size(slots)
 
 
 def group_copy(tiles_hbm, tiles_ref, arrived, counter):
@@ -272,21 +265,55 @@
     return pltpu.make_async_copy(tiles_hbm.at[part], tiles_ref.at[part], arrived.at[counter])
 
 
-def start_tiles(count_ref, tiles_hbm, tiles_ref, arrived):
+def tile_kernel(
+    count_ref,
+    rows_hbm,
+    cols_hbm,
+    tiles_hbm,
+    own_ref,
+    other_ref,
+    own_out_hbm,
+    other_out_hbm,
+    rows_ref,
+    cols_ref,
+    tiles_ref,
+    split_ref,
+    totals_ref,
+    arrived,
+    moved,
+    *,
+    forward,
+):
+    slots = tiles_ref.shape[0]
+    live = count_ref[0, 0]
+    rows_copy = pltpu.make_async_copy(rows_hbm, rows_ref, moved.at[2])
+    cols_copy = pltpu.make_async_copy(cols_hbm, cols_ref, moved.at[3])
+    for copy in (rows_copy, cols_copy):
+        copy.start()
+
     def start(counter, carry):
         group_copy(tiles_hbm, tiles_ref, arrived, counter).start()
         return carry
 
-    lax.fori_loop(0, group_count(count_ref, tiles_ref.shape[0]), start, 0)
-
-
-def tile_groups(
-    count_ref, tiles_hbm, tiles_ref, arrived, split_ref, out_ref, source_of, target_of, dims
-):
-    slots = tiles_ref.shape[0]
+    lax.fori_loop(0, group_count(live, slots), start, 0)
+    totals_ref[...] = jnp.zeros_like(totals_ref)
+    peers = own_ref.shape[0]
+    split_half = split_ref.shape[0] // 2
+    blocks = split_half // peers if forward else own_ref.shape[1] - 2
+    half = totals_ref.shape[0] // 2
+    split_blocks(own_ref, split_ref, 0, blocks)
+    split_blocks(other_ref, split_ref, split_half, blocks)
+    if not forward:
+        extra = own_ref.shape[1] - blocks
+        for index in range(extra):
+            part = sum_peers(own_ref, blocks + index) + sum_peers(other_ref, blocks + index)
+            totals_ref[half - extra + index] = part
+            totals_ref[2 * half - extra + index] = part
+    rows_copy.wait()
+    cols_copy.wait()
     unroll = group_size(slots)
-    live = count_ref[0, 0]
     members = split_ref.shape[1] // 2
+    source_ref, target_ref = (cols_ref, rows_ref) if forward else (rows_ref, cols_ref)
 
     def group(counter, carry):
         group_copy(tiles_hbm, tiles_ref, arrived, counter).wait()
@@ -295,109 +322,56 @@
         for offset in range(unroll):
             slot = base + offset
             product = lax.dot_general(
-                split_ref[source_of(slot)], tiles_ref[slot], dims, preferred_element_type=jnp.float32
+                split_ref[source_ref[0, 0, slot]],
+                tiles_ref[slot],
+                NT if forward else NN,
+                preferred_element_type=jnp.float32,
             )
             product = product[:members] + product[members:]
             products.append(jnp.where(slot < live, product, 0.0))
         for offset in range(unroll):
-            target = target_of(base + offset)
-            out_ref[target] = out_ref[target] + products[offset]
+            target = target_ref[0, 0, base + offset]
+            totals_ref[target] = totals_ref[target] + products[offset]
         return carry
 
-    lax.fori_loop(0, group_count(count_ref, slots), group, 0)
-
-
-def backward_kernel(
-    count_ref,
-    rows_ref,
-    cols_ref,
-    tiles_hbm,
-    own_ref,
-    other_ref,
-    own_out_ref,
-    other_out_ref,
-    tiles_ref,
-    arrived,
-    split_ref,
-    totals_ref,
-):
-    start_tiles(count_ref, tiles_hbm, tiles_ref, arrived)
-    peers, width = own_ref.shape[:2]
-    per_peer = split_ref.shape[0] // (2 * peers)
-    half = totals_ref.shape[0] // 2
-    totals_ref[...] = jnp.zeros_like(totals_ref)
-    split_blocks(own_ref, split_ref, 0, per_peer)
-    split_blocks(other_ref, split_ref, peers * per_peer, per_peer)
-    for index in range(width - per_peer):
-        part = sum_peers(own_ref, per_peer + index) + sum_peers(other_ref, per_peer + index)
-        own_out_ref[half + index] = part
-        other_out_ref[half + index] = part
-    tile_groups(
-        count_ref,
-        tiles_hbm,
-        tiles_ref,
-        arrived,
-        split_ref,
-        totals_ref,
-        lambda slot: rows_ref[0, 0, slot],
-        lambda slot: cols_ref[0, 0, slot],
-        NN,
-    )
-    own_out_ref[:half] = totals_ref[:half]
-    other_out_ref[:half] = totals_ref[half:]
-
-
-def forward_kernel(
-    count_ref,
-    rows_ref,
-    cols_ref,
-    tiles_hbm,
-    line_ref,
-    far_line_ref,
-    own_ref,
-    other_ref,
-    tiles_ref,
-    arrived,
-    split_ref,
-    totals_ref,
-):
-    start_tiles(count_ref, tiles_hbm, tiles_ref, arrived)
-    totals_ref[...] = jnp.zeros_like(totals_ref)
-    lines, blocks = line_ref.shape[:2]
-    split_blocks(line_ref, split_ref, 0, blocks)
-    split_blocks(far_line_ref, split_ref, lines * blocks, blocks)
-    tile_groups(
-        count_ref,
-        tiles_hbm,
-        tiles_ref,
-        arrived,
-        split_ref,
-        totals_ref,
-        lambda slot: cols_ref[0, 0, slot],
-        lambda slot: rows_ref[0, 0, slot],
-        NT,
-    )
-    half = totals_ref.shape[0] // 2
-    own_ref[...] = totals_ref[:half]
-    other_ref[...] = totals_ref[half:]
-
-
-def tile_call(kernel, count, rows, cols, tiles, arrays, out_shapes, scratch, name):
+    lax.fori_loop(0, group_count(live, slots), group, 0)
+    outs = [
+        pltpu.make_async_copy(totals_ref.at[pl.ds(start, half)], out, moved.at[index])
+        for index, (start, out) in enumerate(((0, own_out_hbm), (half, other_out_hbm)))
+    ]
+    for copy in outs:
+        copy.start()
+    for copy in outs:
+        copy.wait()
+
+
+def tile_call(count, rows, cols, tiles, own, other, split_places, out_places, forward):
     smem = pl.BlockSpec(memory_space=pltpu.SMEM)
-    vmem = pl.BlockSpec(memory_space=pltpu.VMEM)
+    anywhere = pl.BlockSpec(memory_space=pl.ANY)
+    members = own.shape[2]
+    slots = tiles.shape[0]
+    out = jax.ShapeDtypeStruct((out_places, members, LANES), jnp.float32)
     return pl.pallas_call(
-        kernel,
-        out_shape=[jax.ShapeDtypeStruct(shape, jnp.float32) for shape in out_shapes],
-        in_specs=[smem] * 3 + [pl.BlockSpec(memory_space=pl.ANY)] + [vmem] * len(arrays),
-        out_specs=[vmem] * len(out_shapes),
+        functools.partial(tile_kernel, forward=forward),
+        out_shape=[out, out],
+        in_specs=[smem] + [anywhere] * 3 + [pl.BlockSpec(memory_space=pltpu.VMEM)] * 2,
+        out_specs=[anywhere] * 2,
         scratch_shapes=[
+            pltpu.SMEM(rows.shape, jnp.int32),
+            pltpu.SMEM(cols.shape, jnp.int32),
             pltpu.VMEM(tiles.shape, tiles.dtype),
-            pltpu.SemaphoreType.DMA((tiles.shape[0] // group_size(tiles.shape[0]),)),
-        ]
-        + scratch,
+            pltpu.VMEM((2 * split_places, 2 * members, LANES), jnp.bfloat16),
+            pltpu.VMEM((2 * out_places, members, LANES), jnp.float32),
+            pltpu.SemaphoreType.DMA((slots // group_size(slots),)),
+            pltpu.SemaphoreType.DMA((4,)),
+        ],
         compiler_params=pltpu.CompilerParams(vmem_limit_bytes=TILE_VMEM_BYTES),
-        name=name,
-    )(count, rows, cols, tiles, *arrays)
+        name="forward_tiles" if forward else "backward_tiles",
+    )(count, rows, cols, tiles, own, other)
+
+
+def join_kernel(own_ref, other_ref, out_ref):
+    out_ref[...] = own_ref[...] + other_ref[...]
 
 
 def exchange(slots, axes, groups=None):
@@ -444,67 +418,66 @@
         compiler_params=pltpu.CompilerParams(vmem_limit_bytes=FULL_VMEM_BYTES),
         name="stage",
     )(vectors, hvectors)
-    rows, cols, basis, images = pl.pallas_call(
+    basis, images = pl.pallas_call(
         prepare_kernel,
-        out_shape=[
-            jax.ShapeDtypeStruct(tile_rows.shape, jnp.int32),
-            jax.ShapeDtypeStruct(tile_cols.shape, jnp.int32),
-            jax.ShapeDtypeStruct((2, members, piece), f32),
-            jax.ShapeDtypeStruct((2, members, piece), f32),
-        ],
-        in_specs=[vmem_spec] * 2 + [hbm_spec] * 4,
-        out_specs=[vmem_spec] * 4,
+        out_shape=[jax.ShapeDtypeStruct((2, members, piece), f32)] * 2,
+        in_specs=[hbm_spec] * 4,
+        out_specs=[vmem_spec] * 2,
         scratch_shapes=[pltpu.SemaphoreType.DMA((4,))],
         compiler_params=params,
         name="prepare",
-    )(tile_rows, tile_cols, vectors, previous, hvectors, hprevious)
+    )(vectors, previous, hvectors, hprevious)
     sums = exchange(sums, everyone)
-    sums, rows, cols, basis, images = lax.optimization_barrier((sums, rows, cols, basis, images))
+    sums, basis, images = lax.optimization_barrier((sums, basis, images))
     residual, slots = call(
         residual_kernel, [(members, piece), (chips, blocks + 2, members, LANES)], "residual"
     )(sums, basis, images)
     pieces = [residual] + [shift_lines(residual, shift) for shift in range(1, lines)]
     (line,) = call(line_kernel, [(lines, blocks, members, LANES)], "line")(*pieces)
     own_range = exchange(slots, "col", core_groups)
-    own_range, line = lax.optimization_barrier((own_range, line))
+    residual, tile_rows, tile_cols = lax.optimization_barrier((residual, tile_rows, tile_cols))
+    rows, cols = pl.pallas_call(
+        functools.partial(places_kernel, blocks=blocks, gap=2),
+        out_shape=[jax.ShapeDtypeStruct(tile_rows.shape, jnp.int32)] * 2,
+        compiler_params=params,
+        name="places",
+    )(tile_rows, tile_cols)
+    own_range, line, rows, cols = lax.optimization_barrier((own_range, line, rows, cols))
     far_line = swap(line, "row", 1)
     other_range = swap(own_range, "col", 1)
-    half = (lines * blocks + 2, members, LANES)
     col_own, col_other = tile_call(
-        backward_kernel,
         tile_count,
         rows,
         cols,
         tiles,
-        (own_range, other_range),
-        [half, half],
-        [
-            pltpu.VMEM((n_col * blocks, 2 * members, LANES), jnp.bfloat16),
-            pltpu.VMEM((n_row * blocks, members, LANES), f32),
-        ],
-        "backward_tiles",
+        own_range,
+        other_range,
+        chips * blocks,
+        lines * blocks + 2,
+        False,
     )
     col_own, col_other, far_line = lax.optimization_barrier((col_own, col_other, far_line))
     col_received = swap(col_other, "row", 1)
-    half = (chips * blocks, members, LANES)
     own_totals, other_totals = tile_call(
-        forward_kernel,
         tile_count,
         rows,
         cols,
         tiles,
-        (line, far_line),
-        [half, half],
-        [
-            pltpu.VMEM((n_row * blocks, 2 * members, LANES), jnp.bfloat16),
-            pltpu.VMEM((n_col * blocks, members, LANES), f32),
-        ],
-        "forward_tiles",
+        line,
+        far_line,
+        lines * blocks + 2,
+        chips * blocks,
+        True,
     )
     col_received, own_totals, other_totals = lax.optimization_barrier(
         (col_received, own_totals, other_totals)
     )
-    totals = own_totals + swap(other_totals, "col", 1)
+    (totals,) = pl.pallas_call(
+        join_kernel,
+        out_shape=[jax.ShapeDtypeStruct(own_totals.shape, f32)],
+        compiler_params=pltpu.CompilerParams(vmem_limit_bytes=TILE_VMEM_BYTES),
+        name="join",
+    )(own_totals, swap(other_totals, "col", 1))
     col_parts = exchange(totals.reshape(chips, blocks, members, LANES), "col", core_groups)
     outs = call(halves_kernel, [(blocks + 2, members, LANES)] * lines, "halves")(
         col_own, col_received

time: 103 us -> 98 us (0.951)
  starting transfers between devices: 45.2 us -> 38.4 us
  waiting for transfers between devices: 24.2 us -> 30.2 us
  other arithmetic: 1.91 us -> 0 us
  local copies, waits for them, and re-layouts: 6.14 us -> 4.71 us
    ppermute x6, starting transfers between devices: 10.8 us -> 6.73 us  [shift_lines(): lax.ppermute(array, 'row', [(i, (i + 2 * shift) % size) for i in range(si...]
    all_to_all x4, waiting for transfers between devices: 14.3 us -> 17.6 us  [exchange(): lax.all_to_all(slots, axes, 0, 0, axis_index_groups=groups, tiled=True)]
    all_to_all x4, starting transfers between devices: 28.5 us -> 25.8 us  [exchange(): lax.all_to_all(slots, axes, 0, 0, axis_index_groups=groups, tiled=True)]
    ppermute x4, waiting for transfers between devices: 5.51 us -> 7.83 us  [swap(): lax.ppermute(array, axis, [(i, i ^ distance) for i in range(lax.axis_size...]
    add x1 -> x0, other arithmetic: 1.91 us -> none  [on_device(): totals = own_totals + swap(other_totals, 'col', 1)]
    unnamed x26 -> x12, local copies, waits for them, and re-layouts: 6.14 us -> 4.71 us
    pallas_call x3 -> x5, Pallas kernels: 11.4 us -> 10.4 us  [the longest x2 9.21 us: tile_call(): pl.pallas_call(functools.partial(tile_kernel, forward=forward), out_shape...]
  transfers between devices with their start and end apart: 14 -> 14, of which waited for: 10 -> 12; matrix products, arithmetic and copies ran while one was open for 0% -> 0% of each run, Pallas kernels for 18% -> 17%
where the time goes in v7:
time: 98 us; the launch traced here: 97.3 us
  starting transfers between devices  38.4 us (39%)
  waiting for transfers between devices  30.2 us (31%)
  Pallas kernels  22.5 us (23%)
  local copies, waits for them, and re-layouts  4.71 us (5%)
  between operations  1.4 us (1%)
    all_to_all x4, starting transfers between devices, exchange(): lax.all_to_all(slots, axes, 0, 0, axis_index_groups=groups, tiled=True)  25.8 us
    all_to_all x4, waiting for transfers between devices, exchange(): lax.all_to_all(slots, axes, 0, 0, axis_index_groups=groups, tiled=True)  17.6 us
    pallas_call x2, Pallas kernels, tile_call(): pl.pallas_call(functools.partial(tile_kernel, forward=forward), out_shape...  9.21 us
    ppermute x4, waiting for transfers between devices, swap(): lax.ppermute(array, axis, [(i, i ^ distance) for i in range(lax.axis_size...  7.83 us
    ppermute x6, starting transfers between devices, shift_lines(): lax.ppermute(array, 'row', [(i, (i + 2 * shift) % size) for i in range(si...  6.73 us
    ppermute x4, starting transfers between devices, swap(): lax.ppermute(array, axis, [(i, i ^ distance) for i in range(lax.axis_size...  5.89 us
    ppermute x6, waiting for transfers between devices, shift_lines(): lax.ppermute(array, 'row', [(i, (i + 2 * shift) % size) for i in range(si...  4.78 us
    unnamed x12, local copies, waits for them, and re-layouts  4.71 us
  transfers between devices with their start and end apart: 14, of which 12 were waited for; matrix products, arithmetic and copies ran while one was open for 0% of the time, Pallas kernels for 17%

profile of v7, /device:TPU:1, one launch (start us, length us, event | category | flops | bytes accessed | tf_op | source)
XLA Modules:
  0.0 97.3 jit_solution(695634554012885709)
XLA Ops:
  0.6 1.6 %stage.1 = f32[128,128]{1,0:T(8,128)} custom-call(f32[16,1024]{1,0:T(8,128)} %vectors_hbm.3, f32[16,1024]{1,0:T(8,128)} %hvectors_hbm.3), custom_call_target="tpu_custom_call" | custom-call | tf_op jit(solution)/shard_map/stage/pallas_call | solution.py:409
  2.3 11.5 %all-to-all-start = ((f32[128,1,128]{2,1,0:T(1,128)}), f32[128,1,128]{2,1,0:T(1,128)S(1)}, u32[]{:S(2)}, u32[]{:S(2)}) async-start(f32[128,1,128]{2,1,0:T(1,128)} %bitcast.9), calls=%async_computation | async-start | bytes 131072 | tf_op jit(solution)/shard_map/all_to_all | solution.py:378
  13.8 0.0 copy-start
  13.8 0.8 copy-done
  14.6 0.0 copy-start.1
  14.6 0.8 copy-done.1
  15.4 0.0 copy-start.2
  15.5 0.8 copy-done.2
  16.3 0.0 copy-start.3
  16.3 0.8 copy-done.3
  17.1 0.3 prepare.1
  17.5 5.8 %all-to-all-done = f32[128,1,128]{2,1,0:T(1,128)S(1)} async-done(((f32[128,1,128]{2,1,0:T(1,128)}), f32[128,1,128]{2,1,0:T(1,128)S(1)}, u32[]{:S(2)}, u32[]{:S(2)}) %all-to-all-start) | async-done | bytes 65568 | tf_op jit(solution)/shard_map/all_to_all | solution.py:378
  23.3 1.5 %residual.1 = (f32[16,1024]{1,0:T(8,128)S(1)}, f32[8,10,16,128]{3,2,1,0:T(8,128)}) custom-call(f32[128,128]{1,0:T(8,128)S(1)} %bitcast.6, f32[2,16,1024]{2,1,0:T(8,128)S(1)} %get-tuple-element.50.basis_ref, f32[2,16,1024]{2,1,0:T(8,128)S(1)} %get-tuple-element.51.images_ref), custom_call_target="tpu_custom_call" | custom-call | tf_op jit(solution)/shard_map/residual/pallas_call | solution.py:432
  24.8 3.5 %all-to-all-start.1 = ((f32[8,10,16,128]{3,2,1,0:T(8,128)}), f32[8,10,16,128]{3,2,1,0:T(8,128)S(1)}, u32[]{:S(2)}, u32[]{:S(2)}) async-start(f32[8,10,16,128]{3,2,1,0:T(8,128)} %get-tuple-element.52), calls=%async_computation.1 | async-start | bytes 1310720 | tf_op jit(solution)/shard_map/all_to_all | solution.py:378
  28.3 0.3 collective-permute-start
  28.6 1.3 %collective-permute-start.1 = (f32[16,1024]{1,0:T(8,128)S(1)}, f32[16,1024]{1,0:T(8,128)S(1)}, u32[]{:S(2)}, u32[]{:S(2)}) collective-permute-start(f32[16,1024]{1,0:T(8,128)S(1)} %get-tuple-element.81.first_ref.residual_ref), channel_id=1, source_target_pairs={{0,64},{16,80},{32,96},{48,112},{64,0},{80,16},{96,32},{112,48},{1... | collective-permute-start | bytes 196616 | tf_op jit(solution)/shard_map/ppermute | solution.py:387
  29.9 1.8 %collective-permute-start.2 = (f32[16,1024]{1,0:T(8,128)S(1)}, f32[16,1024]{1,0:T(8,128)S(1)}, u32[]{:S(2)}, u32[]{:S(2)}) collective-permute-start(f32[16,1024]{1,0:T(8,128)S(1)} %get-tuple-element.81.first_ref.residual_ref), channel_id=1, source_target_pairs={{0,96},{16,112},{32,0},{48,16},{64,32},{80,48},{96,64},{112,80},{1... | collective-permute-start | bytes 196616 | tf_op jit(solution)/shard_map/ppermute | solution.py:387
  31.7 0.0 copy-start.4
  31.7 0.7 copy-done.4
  32.4 0.0 copy-start.5
  32.4 0.7 copy-done.5
  33.1 0.0 collective-permute-done.second_ref
  33.1 1.0 %collective-permute-done.1.third_ref = f32[16,1024]{1,0:T(8,128)S(1)} collective-permute-done((f32[16,1024]{1,0:T(8,128)S(1)}, f32[16,1024]{1,0:T(8,128)S(1)}, u32[]{:S(2)}, u32[]{:S(2)}) %collective-permute-start.1) | collective-permute-done | bytes 65568 | tf_op jit(solution)/shard_map/ppermute | solution.py:387
  34.1 0.2 collective-permute-done.2.fourth_ref
  34.4 3.5 %all-to-all-done.1.own_ref = f32[8,10,16,128]{3,2,1,0:T(8,128)S(1)} async-done(((f32[8,10,16,128]{3,2,1,0:T(8,128)}), f32[8,10,16,128]{3,2,1,0:T(8,128)S(1)}, u32[]{:S(2)}, u32[]{:S(2)}) %all-to-all-start.1) | async-done | bytes 655392 | tf_op jit(solution)/shard_map/all_to_all | solution.py:378
  37.8 2.1 %collective-permute-start.3 = (f32[8,10,16,128]{3,2,1,0:T(8,128)S(1)}, f32[8,10,16,128]{3,2,1,0:T(8,128)S(1)}, u32[]{:S(2)}, u32[]{:S(2)}) collective-permute-start(f32[8,10,16,128]{3,2,1,0:T(8,128)S(1)} %all-to-all-done.1.own_ref), channel_id=1, source_target_pairs={{0,1},{1,0},{2,3},{3,2},{4,5},{5,4},{6,7},{7,6},{8,9},{9,8},{10,11... | collective-permute-start | bytes 1966088 | tf_op jit(solution)/shard_map/ppermute | solution.py:382
  39.9 1.1 %collective-permute-start.4 = (f32[4,8,16,128]{3,2,1,0:T(8,128)S(1)}, f32[4,8,16,128]{3,2,1,0:T(8,128)S(1)}, u32[]{:S(2)}, u32[]{:S(2)}) collective-permute-start(f32[4,8,16,128]{3,2,1,0:T(8,128)S(1)} %line.1.own_ref), channel_id=1, source_target_pairs={{0,16},{16,0},{32,48},{48,32},{64,80},{80,64},{96,112},{112,96},{1... | collective-permute-start | bytes 786440 | tf_op jit(solution)/shard_map/ppermute | solution.py:382
  41.6 0.0 collective-permute-done.3.other_ref
  41.6 3.8 %backward_tiles.1 = (f32[34,16,128]{2,1,0:T(8,128)S(1)}, f32[34,16,128]{2,1,0:T(8,128)S(1)}) custom-call(s32[1,1]{1,0:T(1,128)S(6)} %copy.12.count_ref, s32[1,1,384]{2,1,0:T(1,128)S(1)} %get-tuple-element.58.rows_hbm, s32[1,1,384]{2,1,0:T(1,128)S(1)} %get-tuple-element.59.cols_hbm, bf16[384,128,128]{2,1,0:T(8,128)(2,1)} %bitcast.7, ...), custom_call_target="tpu_custom_call" | custom-call | tf_op jit(solution)/shard_map/backward_tiles/pallas_call | solution.py:354
  45.5 3.9 %collective-permute-done.4.other_ref = f32[4,8,16,128]{3,2,1,0:T(8,128)S(1)} collective-permute-done((f32[4,8,16,128]{3,2,1,0:T(8,128)S(1)}, f32[4,8,16,128]{3,2,1,0:T(8,128)S(1)}, u32[]{:S(2)}, u32[]{:S(2)}) %collective-permute-start.4) | collective-permute-done | bytes 262176 | tf_op jit(solution)/shard_map/ppermute | solution.py:382
  49.3 1.1 %collective-permute-start.5 = (f32[34,16,128]{2,1,0:T(8,128)S(1)}, f32[34,16,128]{2,1,0:T(8,128)S(1)}, u32[]{:S(2)}, u32[]{:S(2)}) collective-permute-start(f32[34,16,128]{2,1,0:T(8,128)S(1)} %get-tuple-element.64), channel_id=1, source_target_pairs={{0,16},{16,0},{32,48},{48,32},{64,80},{80,64},{96,112},{112,96},{1... | collective-permute-start | bytes 835592 | tf_op jit(solution)/shard_map/ppermute | solution.py:382
  50.4 5.4 %forward_tiles.1 = (f32[64,16,128]{2,1,0:T(8,128)S(1)}, f32[64,16,128]{2,1,0:T(8,128)S(1)}) custom-call(s32[1,1]{1,0:T(1,128)S(6)} %copy.12.count_ref, s32[1,1,384]{2,1,0:T(1,128)S(1)} %get-tuple-element.58.rows_hbm, s32[1,1,384]{2,1,0:T(1,128)S(1)} %get-tuple-element.59.cols_hbm, bf16[384,128,128]{2,1,0:T(8,128)(2,1)} %bitcast.8, ...), custom_call_target="tpu_custom_call" | custom-call | tf_op jit(solution)/shard_map/forward_tiles/pallas_call | solution.py:354
  55.8 2.4 %collective-permute-done.5.received_ref = f32[34,16,128]{2,1,0:T(8,128)S(1)} collective-permute-done((f32[34,16,128]{2,1,0:T(8,128)S(1)}, f32[34,16,128]{2,1,0:T(8,128)S(1)}, u32[]{:S(2)}, u32[]{:S(2)}) %collective-permute-start.5) | collective-permute-done | bytes 278560 | tf_op jit(solution)/shard_map/ppermute | solution.py:382
  58.2 1.7 %collective-permute-start.6 = (f32[64,16,128]{2,1,0:T(8,128)S(1)}, f32[64,16,128]{2,1,0:T(8,128)S(1)}, u32[]{:S(2)}, u32[]{:S(2)}) collective-permute-start(f32[64,16,128]{2,1,0:T(8,128)S(1)} %get-tuple-element.69), channel_id=1, source_target_pairs={{0,1},{1,0},{2,3},{3,2},{4,5},{5,4},{6,7},{7,6},{8,9},{9,8},{10,11... | collective-permute-start | bytes 1572872 | tf_op jit(solution)/shard_map/ppermute | solution.py:382
  59.9 1.5 %collective-permute-done.6.other_ref = f32[64,16,128]{2,1,0:T(8,128)S(1)} collective-permute-done((f32[64,16,128]{2,1,0:T(8,128)S(1)}, f32[64,16,128]{2,1,0:T(8,128)S(1)}, u32[]{:S(2)}, u32[]{:S(2)}) %collective-permute-start.6) | collective-permute-done | bytes 524320 | tf_op jit(solution)/shard_map/ppermute | solution.py:382
  61.4 0.9 join.1
  62.3 3.5 %all-to-all-start.2 = ((f32[8,8,16,128]{3,2,1,0:T(8,128)}), f32[8,8,16,128]{3,2,1,0:T(8,128)S(1)}, u32[]{:S(2)}, u32[]{:S(2)}) async-start(f32[8,8,16,128]{3,2,1,0:T(8,128)} %bitcast.4), calls=%async_computation.2 | async-start | bytes 1048576 | tf_op jit(solution)/shard_map/all_to_all | solution.py:378
  65.8 0.1 halves.1
  65.9 0.3 collective-permute-start.7
  66.1 1.5 %collective-permute-start.8 = (f32[10,16,128]{2,1,0:T(8,128)S(1)}, f32[10,16,128]{2,1,0:T(8,128)S(1)}, u32[]{:S(2)}, u32[]{:S(2)}) collective-permute-start(f32[10,16,128]{2,1,0:T(8,128)S(1)} %get-tuple-element.74), channel_id=1, source_target_pairs={{0,64},{16,80},{32,96},{48,112},{64,0},{80,16},{96,32},{112,48},{1... | collective-permute-start | bytes 245768 | tf_op jit(solution)/shard_map/ppermute | solution.py:387
  67.7 1.5 %collective-permute-start.9 = (f32[10,16,128]{2,1,0:T(8,128)S(1)}, f32[10,16,128]{2,1,0:T(8,128)S(1)}, u32[]{:S(2)}, u32[]{:S(2)}) collective-permute-start(f32[10,16,128]{2,1,0:T(8,128)S(1)} %get-tuple-element.75), channel_id=1, source_target_pairs={{0,96},{16,112},{32,0},{48,16},{64,32},{80,48},{96,64},{112,80},{1... | collective-permute-start | bytes 245768 | tf_op jit(solution)/shard_map/ppermute | solution.py:387
  69.2 2.3 %collective-permute-done.7.second_ref = f32[10,16,128]{2,1,0:T(8,128)S(1)} collective-permute-done((f32[10,16,128]{2,1,0:T(8,128)S(1)}, f32[10,16,128]{2,1,0:T(8,128)S(1)}, u32[]{:S(2)}, u32[]{:S(2)}) %collective-permute-start.7) | collective-permute-done | bytes 81952 | tf_op jit(solution)/shard_map/ppermute | solution.py:387
  71.5 0.6 collective-permute-done.8.third_ref
  72.1 0.7 collective-permute-done.9.fourth_ref
  72.8 1.3 %all-to-all-done.2.col_parts_ref = f32[8,8,16,128]{3,2,1,0:T(8,128)S(1)} async-done(((f32[8,8,16,128]{3,2,1,0:T(8,128)}), f32[8,8,16,128]{3,2,1,0:T(8,128)S(1)}, u32[]{:S(2)}, u32[]{:S(2)}) %all-to-all-start.2) | async-done | bytes 524320 | tf_op jit(solution)/shard_map/all_to_all | solution.py:378
  74.1 1.2 %image.1 = (f32[16,1024]{1,0:T(8,128)S(1)}, f32[128,8,128]{2,1,0:T(8,128)}) custom-call(f32[8,8,16,128]{3,2,1,0:T(8,128)S(1)} %all-to-all-done.2.col_parts_ref, f32[10,16,128]{2,1,0:T(8,128)S(1)} %get-tuple-element.83.first_ref, f32[10,16,128]{2,1,0:T(8,128)S(1)} %collective-permute-done.7.second_ref, f32[10,16,128]{2,1,0:T(8,128)S(1)} %collective-permute-done.8.third_ref, ...), custom_call_target="tpu_custom_call" | custom-call | tf_op jit(solution)/shard_map/image/pallas_call | solution.py:487
  75.3 7.3 %all-to-all-start.3 = ((f32[128,8,128]{2,1,0:T(8,128)}), f32[128,8,128]{2,1,0:T(8,128)S(1)}, u32[]{:S(2)}, u32[]{:S(2)}) async-start(f32[128,8,128]{2,1,0:T(8,128)} %get-tuple-element.89), calls=%async_computation.3 | async-start | bytes 1048576 | tf_op jit(solution)/shard_map/all_to_all | solution.py:378
  82.6 4.5 %factor.1 = (f32[48,48]{1,0:T(8,128)S(1)}, f32[32,48]{1,0:T(8,128)S(1)}) custom-call(f32[10,16,128]{2,1,0:T(8,128)S(1)} %get-tuple-element.83.first_ref, f32[10,16,128]{2,1,0:T(8,128)S(1)} %collective-permute-done.7.second_ref, f32[10,16,128]{2,1,0:T(8,128)S(1)} %collective-permute-done.8.third_ref, f32[10,16,128]{2,1,0:T(8,128)S(1)} %collective-permute-done.9.fourth_ref), custom_call_target="tpu_custom_call" | custom-call | tf_op jit(solution)/shard_map/factor/pallas_call | solution.py:492
  87.1 1.0 %orthonormal.1 = f32[48,1024]{1,0:T(8,128)} custom-call(f32[48,48]{1,0:T(8,128)S(1)} %get-tuple-element.87.inverse_ref, f32[2,16,1024]{2,1,0:T(8,128)S(1)} %get-tuple-element.50.basis_ref, f32[16,1024]{1,0:T(8,128)S(1)} %get-tuple-element.81.first_ref.residual_ref), custom_call_target="tpu_custom_call" | custom-call | tf_op jit(solution)/shard_map/orthonormal/pallas_call | solution.py:493
  88.1 1.0 %orthonormal_image.1 = f32[48,1024]{1,0:T(8,128)} custom-call(f32[48,48]{1,0:T(8,128)S(1)} %get-tuple-element.87.inverse_ref, f32[2,16,1024]{2,1,0:T(8,128)S(1)} %get-tuple-element.51.images_ref, f32[16,1024]{1,0:T(8,128)S(1)} %get-tuple-element.88.image_ref), custom_call_target="tpu_custom_call" | custom-call | tf_op jit(solution)/shard_map/orthonormal_image/pallas_call | solution.py:496
  89.1 7.0 %all-to-all-done.3.received_ref = f32[128,8,128]{2,1,0:T(8,128)S(1)} async-done(((f32[128,8,128]{2,1,0:T(8,128)}), f32[128,8,128]{2,1,0:T(8,128)S(1)}, u32[]{:S(2)}, u32[]{:S(2)}) %all-to-all-start.3) | async-done | bytes 524320 | tf_op jit(solution)/shard_map/all_to_all | solution.py:378
  96.1 1.2 %projected.1 = f32[48,48]{1,0:T(8,128)} custom-call(f32[128,8,128]{2,1,0:T(8,128)S(1)} %all-to-all-done.3.received_ref, f32[48,48]{1,0:T(8,128)S(1)} %get-tuple-element.87.inverse_ref, f32[32,48]{1,0:T(8,128)S(1)} %get-tuple-element.90.early_ref), custom_call_target="tpu_custom_call" | custom-call | tf_op jit(solution)/shard_map/projected/pallas_call | solution.py:501
  (2 shorter events, 0.1 us)
Async XLA Ops:
  2.3 21.0 %all-to-all-start = ((f32[128,1,128]{2,1,0:T(1,128)}), f32[128,1,128]{2,1,0:T(1,128)S(1)}, u32[]{:S(2)}, u32[]{:S(2)}) async-start(f32[128,1,128]{2,1,0:T(1,128)} %bitcast.9), calls=%async_computation | async-start | bytes 131072 | tf_op jit(solution)/shard_map/all_to_all | solution.py:378
  13.8 0.8 copy-start
  14.6 0.8 copy-start.1
  15.4 0.8 copy-start.2
  16.3 0.8 copy-start.3
  24.8 13.0 %all-to-all-start.1 = ((f32[8,10,16,128]{3,2,1,0:T(8,128)}), f32[8,10,16,128]{3,2,1,0:T(8,128)S(1)}, u32[]{:S(2)}, u32[]{:S(2)}) async-start(f32[8,10,16,128]{3,2,1,0:T(8,128)} %get-tuple-element.52), calls=%async_computation.1 | async-start | bytes 1310720 | tf_op jit(solution)/shard_map/all_to_all | solution.py:378
  28.3 4.8 %collective-permute-start = (f32[16,1024]{1,0:T(8,128)S(1)}, f32[16,1024]{1,0:T(8,128)S(1)}, u32[]{:S(2)}, u32[]{:S(2)}) collective-permute-start(f32[16,1024]{1,0:T(8,128)S(1)} %get-tuple-element.81.first_ref.residual_ref), channel_id=1, source_target_pairs={{0,32},{16,48},{32,64},{48,80},{64,96},{80,112},{96,0},{112,16},{1... | collective-permute-start | bytes 196616 | tf_op jit(solution)/shard_map/ppermute | solution.py:387
  28.6 5.5 %collective-permute-start.1 = (f32[16,1024]{1,0:T(8,128)S(1)}, f32[16,1024]{1,0:T(8,128)S(1)}, u32[]{:S(2)}, u32[]{:S(2)}) collective-permute-start(f32[16,1024]{1,0:T(8,128)S(1)} %get-tuple-element.81.first_ref.residual_ref), channel_id=1, source_target_pairs={{0,64},{16,80},{32,96},{48,112},{64,0},{80,16},{96,32},{112,48},{1... | collective-permute-start | bytes 196616 | tf_op jit(solution)/shard_map/ppermute | solution.py:387
  29.9 4.4 %collective-permute-start.2 = (f32[16,1024]{1,0:T(8,128)S(1)}, f32[16,1024]{1,0:T(8,128)S(1)}, u32[]{:S(2)}, u32[]{:S(2)}) collective-permute-start(f32[16,1024]{1,0:T(8,128)S(1)} %get-tuple-element.81.first_ref.residual_ref), channel_id=1, source_target_pairs={{0,96},{16,112},{32,0},{48,16},{64,32},{80,48},{96,64},{112,80},{1... | collective-permute-start | bytes 196616 | tf_op jit(solution)/shard_map/ppermute | solution.py:387
  31.7 0.7 copy-start.4
  32.4 0.7 copy-start.5
  37.8 3.8 %collective-permute-start.3 = (f32[8,10,16,128]{3,2,1,0:T(8,128)S(1)}, f32[8,10,16,128]{3,2,1,0:T(8,128)S(1)}, u32[]{:S(2)}, u32[]{:S(2)}) collective-permute-start(f32[8,10,16,128]{3,2,1,0:T(8,128)S(1)} %all-to-all-done.1.own_ref), channel_id=1, source_target_pairs={{0,1},{1,0},{2,3},{3,2},{4,5},{5,4},{6,7},{7,6},{8,9},{9,8},{10,11... | collective-permute-start | bytes 1966088 | tf_op jit(solution)/shard_map/ppermute | solution.py:382
  39.9 9.4 %collective-permute-start.4 = (f32[4,8,16,128]{3,2,1,0:T(8,128)S(1)}, f32[4,8,16,128]{3,2,1,0:T(8,128)S(1)}, u32[]{:S(2)}, u32[]{:S(2)}) collective-permute-start(f32[4,8,16,128]{3,2,1,0:T(8,128)S(1)} %line.1.own_ref), channel_id=1, source_target_pairs={{0,16},{16,0},{32,48},{48,32},{64,80},{80,64},{96,112},{112,96},{1... | collective-permute-start | bytes 786440 | tf_op jit(solution)/shard_map/ppermute | solution.py:382
  49.3 8.9 %collective-permute-start.5 = (f32[34,16,128]{2,1,0:T(8,128)S(1)}, f32[34,16,128]{2,1,0:T(8,128)S(1)}, u32[]{:S(2)}, u32[]{:S(2)}) collective-permute-start(f32[34,16,128]{2,1,0:T(8,128)S(1)} %get-tuple-element.64), channel_id=1, source_target_pairs={{0,16},{16,0},{32,48},{48,32},{64,80},{80,64},{96,112},{112,96},{1... | collective-permute-start | bytes 835592 | tf_op jit(solution)/shard_map/ppermute | solution.py:382
  58.2 3.2 %collective-permute-start.6 = (f32[64,16,128]{2,1,0:T(8,128)S(1)}, f32[64,16,128]{2,1,0:T(8,128)S(1)}, u32[]{:S(2)}, u32[]{:S(2)}) collective-permute-start(f32[64,16,128]{2,1,0:T(8,128)S(1)} %get-tuple-element.69), channel_id=1, source_target_pairs={{0,1},{1,0},{2,3},{3,2},{4,5},{5,4},{6,7},{7,6},{8,9},{9,8},{10,11... | collective-permute-start | bytes 1572872 | tf_op jit(solution)/shard_map/ppermute | solution.py:382
  62.3 11.8 %all-to-all-start.2 = ((f32[8,8,16,128]{3,2,1,0:T(8,128)}), f32[8,8,16,128]{3,2,1,0:T(8,128)S(1)}, u32[]{:S(2)}, u32[]{:S(2)}) async-start(f32[8,8,16,128]{3,2,1,0:T(8,128)} %bitcast.4), calls=%async_computation.2 | async-start | bytes 1048576 | tf_op jit(solution)/shard_map/all_to_all | solution.py:378
  65.9 5.7 %collective-permute-start.7 = (f32[10,16,128]{2,1,0:T(8,128)S(1)}, f32[10,16,128]{2,1,0:T(8,128)S(1)}, u32[]{:S(2)}, u32[]{:S(2)}) collective-permute-start(f32[10,16,128]{2,1,0:T(8,128)S(1)} %get-tuple-element.73), channel_id=1, source_target_pairs={{0,32},{16,48},{32,64},{48,80},{64,96},{80,112},{96,0},{112,16},{1... | collective-permute-start | bytes 245768 | tf_op jit(solution)/shard_map/ppermute | solution.py:387
  66.1 6.0 %collective-permute-start.8 = (f32[10,16,128]{2,1,0:T(8,128)S(1)}, f32[10,16,128]{2,1,0:T(8,128)S(1)}, u32[]{:S(2)}, u32[]{:S(2)}) collective-permute-start(f32[10,16,128]{2,1,0:T(8,128)S(1)} %get-tuple-element.74), channel_id=1, source_target_pairs={{0,64},{16,80},{32,96},{48,112},{64,0},{80,16},{96,32},{112,48},{1... | collective-permute-start | bytes 245768 | tf_op jit(solution)/shard_map/ppermute | solution.py:387
  67.7 5.1 %collective-permute-start.9 = (f32[10,16,128]{2,1,0:T(8,128)S(1)}, f32[10,16,128]{2,1,0:T(8,128)S(1)}, u32[]{:S(2)}, u32[]{:S(2)}) collective-permute-start(f32[10,16,128]{2,1,0:T(8,128)S(1)} %get-tuple-element.75), channel_id=1, source_target_pairs={{0,96},{16,112},{32,0},{48,16},{64,32},{80,48},{96,64},{112,80},{1... | collective-permute-start | bytes 245768 | tf_op jit(solution)/shard_map/ppermute | solution.py:387
  75.3 20.8 %all-to-all-start.3 = ((f32[128,8,128]{2,1,0:T(8,128)}), f32[128,8,128]{2,1,0:T(8,128)S(1)}, u32[]{:S(2)}, u32[]{:S(2)}) async-start(f32[128,8,128]{2,1,0:T(8,128)} %get-tuple-element.89), calls=%async_computation.3 | async-start | bytes 1048576 | tf_op jit(solution)/shard_map/all_to_all | solution.py:378

commit v8 on v7

--- a/solution.py
+++ b/solution.py
@@ -220,9 +220,7 @@
         image_ref[:, index * LANES : (index + 1) * LANES] = sum_peers(col_parts_ref, index) + part
     basis = jnp.concatenate([basis_ref[0], residual_ref[...], basis_ref[1]], axis=0)
     late = exact_dot(image_ref[...], basis, NT)
-    half = late.shape[0] // 2
-    pad = jnp.zeros((half, LANES // 2 - late.shape[1]), jnp.float32)
-    packed = jnp.concatenate([late[:half], pad, late[half:], pad], axis=1)
+    packed = jnp.concatenate([late[row : row + 1] for row in range(late.shape[0])], axis=1)
     slots_ref[...] = jnp.broadcast_to(packed[None], slots_ref.shape)
 
 
@@ -231,8 +229,9 @@
     early = early_ref[...]
     members = early.shape[0] // 2
     wide = early.shape[1]
-    half = LANES // 2
-    late = jnp.concatenate([packed[:, :wide], packed[:, half : half + wide]], axis=0)
+    late = jnp.concatenate(
+        [packed[:, row * wide : (row + 1) * wide] for row in range(members)], axis=0
+    )
     mixed_t = jnp.concatenate([early[:members], late, early[members:]], axis=0)
     inverse = inverse_ref[...]
     half_done = exact_dot(inverse, mixed_t, NT)
@@ -485,7 +484,7 @@
     row_parts = [outs[0]] + [shift_lines(outs[shift], shift) for shift in range(1, lines)]
     col_parts, *row_parts = lax.optimization_barrier((col_parts, *row_parts))
     image, slots = call(
-        image_kernel, [(members, piece), (n_row * n_col, members // 2, LANES)], "image"
+        image_kernel, [(members, piece), (n_row * n_col, 1, members * order)], "image"
     )(col_parts, *row_parts, basis, residual)
     late = exchange(slots, everyone)
     image, *row_parts = lax.optimization_barrier((image, *row_parts))

time: 98 us -> 96.7 us (0.987)
  Pallas kernels: 22.5 us -> 20.8 us
    ppermute x4, waiting for transfers between devices: 7.83 us -> 9.73 us  [swap(): lax.ppermute(array, axis, [(i, i ^ distance) for i in range(lax.axis_size...]
    pallas_call x2, Pallas kernels: 9.21 us -> 7.31 us  [tile_call(): pl.pallas_call(functools.partial(tile_kernel, forward=forward), out_shape...]
    all_to_all x4, waiting for transfers between devices: 17.6 us -> 16.2 us  [exchange(): lax.all_to_all(slots, axes, 0, 0, axis_index_groups=groups, tiled=True)]
  transfers between devices with their start and end apart: 14 -> 14, of which waited for: 12 -> 12; matrix products, arithmetic and copies ran while one was open for 0% -> 0% of each run, Pallas kernels for 17% -> 15%
where the time goes in v8:
time: 96.7 us; the launch traced here: 96.1 us
  starting transfers between devices  38.4 us (40%)
  waiting for transfers between devices  30.8 us (32%)
  Pallas kernels  20.8 us (22%)
  local copies, waits for them, and re-layouts  4.71 us (5%)
  between operations  1.4 us (1%)
    all_to_all x4, starting transfers between devices, exchange(): lax.all_to_all(slots, axes, 0, 0, axis_index_groups=groups, tiled=True)  25.8 us
    all_to_all x4, waiting for transfers between devices, exchange(): lax.all_to_all(slots, axes, 0, 0, axis_index_groups=groups, tiled=True)  16.2 us
    ppermute x4, waiting for transfers between devices, swap(): lax.ppermute(array, axis, [(i, i ^ distance) for i in range(lax.axis_size...  9.73 us
    pallas_call x2, Pallas kernels, tile_call(): pl.pallas_call(functools.partial(tile_kernel, forward=forward), out_shape...  7.31 us
    ppermute x6, starting transfers between devices, shift_lines(): lax.ppermute(array, 'row', [(i, (i + 2 * shift) % size) for i in range(si...  6.73 us
    ppermute x4, starting transfers between devices, swap(): lax.ppermute(array, axis, [(i, i ^ distance) for i in range(lax.axis_size...  5.89 us
    ppermute x6, waiting for transfers between devices, shift_lines(): lax.ppermute(array, 'row', [(i, (i + 2 * shift) % size) for i in range(si...  4.78 us
    unnamed x12, local copies, waits for them, and re-layouts  4.71 us
  transfers between devices with their start and end apart: 14, of which 12 were waited for; matrix products, arithmetic and copies ran while one was open for 0% of the time, Pallas kernels for 15%

profile of v8, /device:TPU:1, one launch (start us, length us, event | category | flops | bytes accessed | tf_op | source)
XLA Modules:
  0.0 96.1 jit_solution(10167052855456766552)
XLA Ops:
  0.6 1.6 %stage.1 = f32[128,128]{1,0:T(8,128)} custom-call(f32[16,1024]{1,0:T(8,128)} %vectors_hbm.3, f32[16,1024]{1,0:T(8,128)} %hvectors_hbm.3), custom_call_target="tpu_custom_call" | custom-call | tf_op jit(solution)/shard_map/stage/pallas_call | solution.py:408
  2.3 11.5 %all-to-all-start = ((f32[128,1,128]{2,1,0:T(1,128)}), f32[128,1,128]{2,1,0:T(1,128)S(1)}, u32[]{:S(2)}, u32[]{:S(2)}) async-start(f32[128,1,128]{2,1,0:T(1,128)} %bitcast.9), calls=%async_computation | async-start | bytes 131072 | tf_op jit(solution)/shard_map/all_to_all | solution.py:377
  13.8 0.0 copy-start
  13.8 0.8 copy-done
  14.6 0.0 copy-start.1
  14.6 0.8 copy-done.1
  15.4 0.0 copy-start.2
  15.5 0.8 copy-done.2
  16.3 0.0 copy-start.3
  16.3 0.8 copy-done.3
  17.1 0.3 prepare.1
  17.5 5.8 %all-to-all-done = f32[128,1,128]{2,1,0:T(1,128)S(1)} async-done(((f32[128,1,128]{2,1,0:T(1,128)}), f32[128,1,128]{2,1,0:T(1,128)S(1)}, u32[]{:S(2)}, u32[]{:S(2)}) %all-to-all-start) | async-done | bytes 65568 | tf_op jit(solution)/shard_map/all_to_all | solution.py:377
  23.3 1.5 %residual.1 = (f32[16,1024]{1,0:T(8,128)S(1)}, f32[8,10,16,128]{3,2,1,0:T(8,128)}) custom-call(f32[128,128]{1,0:T(8,128)S(1)} %bitcast.6, f32[2,16,1024]{2,1,0:T(8,128)S(1)} %get-tuple-element.50.basis_ref, f32[2,16,1024]{2,1,0:T(8,128)S(1)} %get-tuple-element.51.images_ref), custom_call_target="tpu_custom_call" | custom-call | tf_op jit(solution)/shard_map/residual/pallas_call | solution.py:431
  24.8 3.5 %all-to-all-start.1 = ((f32[8,10,16,128]{3,2,1,0:T(8,128)}), f32[8,10,16,128]{3,2,1,0:T(8,128)S(1)}, u32[]{:S(2)}, u32[]{:S(2)}) async-start(f32[8,10,16,128]{3,2,1,0:T(8,128)} %get-tuple-element.52), calls=%async_computation.1 | async-start | bytes 1310720 | tf_op jit(solution)/shard_map/all_to_all | solution.py:377
  28.3 0.3 collective-permute-start
  28.6 1.3 %collective-permute-start.1 = (f32[16,1024]{1,0:T(8,128)S(1)}, f32[16,1024]{1,0:T(8,128)S(1)}, u32[]{:S(2)}, u32[]{:S(2)}) collective-permute-start(f32[16,1024]{1,0:T(8,128)S(1)} %get-tuple-element.81.first_ref.residual_ref), channel_id=1, source_target_pairs={{0,64},{16,80},{32,96},{48,112},{64,0},{80,16},{96,32},{112,48},{1... | collective-permute-start | bytes 196616 | tf_op jit(solution)/shard_map/ppermute | solution.py:386
  29.9 1.8 %collective-permute-start.2 = (f32[16,1024]{1,0:T(8,128)S(1)}, f32[16,1024]{1,0:T(8,128)S(1)}, u32[]{:S(2)}, u32[]{:S(2)}) collective-permute-start(f32[16,1024]{1,0:T(8,128)S(1)} %get-tuple-element.81.first_ref.residual_ref), channel_id=1, source_target_pairs={{0,96},{16,112},{32,0},{48,16},{64,32},{80,48},{96,64},{112,80},{1... | collective-permute-start | bytes 196616 | tf_op jit(solution)/shard_map/ppermute | solution.py:386
  31.7 0.0 copy-start.4
  31.7 0.7 copy-done.4
  32.4 0.0 copy-start.5
  32.4 0.7 copy-done.5
  33.1 0.0 collective-permute-done.second_ref
  33.1 1.0 %collective-permute-done.1.third_ref = f32[16,1024]{1,0:T(8,128)S(1)} collective-permute-done((f32[16,1024]{1,0:T(8,128)S(1)}, f32[16,1024]{1,0:T(8,128)S(1)}, u32[]{:S(2)}, u32[]{:S(2)}) %collective-permute-start.1) | collective-permute-done | bytes 65568 | tf_op jit(solution)/shard_map/ppermute | solution.py:386
  34.1 0.2 collective-permute-done.2.fourth_ref
  34.4 3.5 %all-to-all-done.1.own_ref = f32[8,10,16,128]{3,2,1,0:T(8,128)S(1)} async-done(((f32[8,10,16,128]{3,2,1,0:T(8,128)}), f32[8,10,16,128]{3,2,1,0:T(8,128)S(1)}, u32[]{:S(2)}, u32[]{:S(2)}) %all-to-all-start.1) | async-done | bytes 655392 | tf_op jit(solution)/shard_map/all_to_all | solution.py:377
  37.8 2.1 %collective-permute-start.3 = (f32[8,10,16,128]{3,2,1,0:T(8,128)S(1)}, f32[8,10,16,128]{3,2,1,0:T(8,128)S(1)}, u32[]{:S(2)}, u32[]{:S(2)}) collective-permute-start(f32[8,10,16,128]{3,2,1,0:T(8,128)S(1)} %all-to-all-done.1.own_ref), channel_id=1, source_target_pairs={{0,1},{1,0},{2,3},{3,2},{4,5},{5,4},{6,7},{7,6},{8,9},{9,8},{10,11... | collective-permute-start | bytes 1966088 | tf_op jit(solution)/shard_map/ppermute | solution.py:381
  39.9 1.1 %collective-permute-start.4 = (f32[4,8,16,128]{3,2,1,0:T(8,128)S(1)}, f32[4,8,16,128]{3,2,1,0:T(8,128)S(1)}, u32[]{:S(2)}, u32[]{:S(2)}) collective-permute-start(f32[4,8,16,128]{3,2,1,0:T(8,128)S(1)} %line.1.own_ref), channel_id=1, source_target_pairs={{0,16},{16,0},{32,48},{48,32},{64,80},{80,64},{96,112},{112,96},{1... | collective-permute-start | bytes 786440 | tf_op jit(solution)/shard_map/ppermute | solution.py:381
  41.6 0.0 collective-permute-done.3.other_ref
  41.6 3.1 %backward_tiles.1 = (f32[34,16,128]{2,1,0:T(8,128)S(1)}, f32[34,16,128]{2,1,0:T(8,128)S(1)}) custom-call(s32[1,1]{1,0:T(1,128)S(6)} %copy.12.count_ref, s32[1,1,384]{2,1,0:T(1,128)S(1)} %get-tuple-element.58.rows_hbm, s32[1,1,384]{2,1,0:T(1,128)S(1)} %get-tuple-element.59.cols_hbm, bf16[384,128,128]{2,1,0:T(8,128)(2,1)} %bitcast.7, ...), custom_call_target="tpu_custom_call" | custom-call | tf_op jit(solution)/shard_map/backward_tiles/pallas_call | solution.py:353
  44.8 4.6 %collective-permute-done.4.other_ref = f32[4,8,16,128]{3,2,1,0:T(8,128)S(1)} collective-permute-done((f32[4,8,16,128]{3,2,1,0:T(8,128)S(1)}, f32[4,8,16,128]{3,2,1,0:T(8,128)S(1)}, u32[]{:S(2)}, u32[]{:S(2)}) %collective-permute-start.4) | collective-permute-done | bytes 262176 | tf_op jit(solution)/shard_map/ppermute | solution.py:381
  49.3 1.1 %collective-permute-start.5 = (f32[34,16,128]{2,1,0:T(8,128)S(1)}, f32[34,16,128]{2,1,0:T(8,128)S(1)}, u32[]{:S(2)}, u32[]{:S(2)}) collective-permute-start(f32[34,16,128]{2,1,0:T(8,128)S(1)} %get-tuple-element.64), channel_id=1, source_target_pairs={{0,16},{16,0},{32,48},{48,32},{64,80},{80,64},{96,112},{112,96},{1... | collective-permute-start | bytes 835592 | tf_op jit(solution)/shard_map/ppermute | solution.py:381
  50.4 4.2 %forward_tiles.1 = (f32[64,16,128]{2,1,0:T(8,128)S(1)}, f32[64,16,128]{2,1,0:T(8,128)S(1)}) custom-call(s32[1,1]{1,0:T(1,128)S(6)} %copy.12.count_ref, s32[1,1,384]{2,1,0:T(1,128)S(1)} %get-tuple-element.58.rows_hbm, s32[1,1,384]{2,1,0:T(1,128)S(1)} %get-tuple-element.59.cols_hbm, bf16[384,128,128]{2,1,0:T(8,128)(2,1)} %bitcast.8, ...), custom_call_target="tpu_custom_call" | custom-call | tf_op jit(solution)/shard_map/forward_tiles/pallas_call | solution.py:353
  54.6 3.6 %collective-permute-done.5.received_ref = f32[34,16,128]{2,1,0:T(8,128)S(1)} collective-permute-done((f32[34,16,128]{2,1,0:T(8,128)S(1)}, f32[34,16,128]{2,1,0:T(8,128)S(1)}, u32[]{:S(2)}, u32[]{:S(2)}) %collective-permute-start.5) | collective-permute-done | bytes 278560 | tf_op jit(solution)/shard_map/ppermute | solution.py:381
  58.2 1.7 %collective-permute-start.6 = (f32[64,16,128]{2,1,0:T(8,128)S(1)}, f32[64,16,128]{2,1,0:T(8,128)S(1)}, u32[]{:S(2)}, u32[]{:S(2)}) collective-permute-start(f32[64,16,128]{2,1,0:T(8,128)S(1)} %get-tuple-element.69), channel_id=1, source_target_pairs={{0,1},{1,0},{2,3},{3,2},{4,5},{5,4},{6,7},{7,6},{8,9},{9,8},{10,11... | collective-permute-start | bytes 1572872 | tf_op jit(solution)/shard_map/ppermute | solution.py:381
  59.9 1.5 %collective-permute-done.6.other_ref = f32[64,16,128]{2,1,0:T(8,128)S(1)} collective-permute-done((f32[64,16,128]{2,1,0:T(8,128)S(1)}, f32[64,16,128]{2,1,0:T(8,128)S(1)}, u32[]{:S(2)}, u32[]{:S(2)}) %collective-permute-start.6) | collective-permute-done | bytes 524320 | tf_op jit(solution)/shard_map/ppermute | solution.py:381
  61.4 0.9 join.1
  62.3 3.5 %all-to-all-start.2 = ((f32[8,8,16,128]{3,2,1,0:T(8,128)}), f32[8,8,16,128]{3,2,1,0:T(8,128)S(1)}, u32[]{:S(2)}, u32[]{:S(2)}) async-start(f32[8,8,16,128]{3,2,1,0:T(8,128)} %bitcast.4), calls=%async_computation.2 | async-start | bytes 1048576 | tf_op jit(solution)/shard_map/all_to_all | solution.py:377
  65.8 0.1 halves.1
  65.9 0.3 collective-permute-start.7
  66.1 1.5 %collective-permute-start.8 = (f32[10,16,128]{2,1,0:T(8,128)S(1)}, f32[10,16,128]{2,1,0:T(8,128)S(1)}, u32[]{:S(2)}, u32[]{:S(2)}) collective-permute-start(f32[10,16,128]{2,1,0:T(8,128)S(1)} %get-tuple-element.74), channel_id=1, source_target_pairs={{0,64},{16,80},{32,96},{48,112},{64,0},{80,16},{96,32},{112,48},{1... | collective-permute-start | bytes 245768 | tf_op jit(solution)/shard_map/ppermute | solution.py:386
  67.7 1.5 %collective-permute-start.9 = (f32[10,16,128]{2,1,0:T(8,128)S(1)}, f32[10,16,128]{2,1,0:T(8,128)S(1)}, u32[]{:S(2)}, u32[]{:S(2)}) collective-permute-start(f32[10,16,128]{2,1,0:T(8,128)S(1)} %get-tuple-element.75), channel_id=1, source_target_pairs={{0,96},{16,112},{32,0},{48,16},{64,32},{80,48},{96,64},{112,80},{1... | collective-permute-start | bytes 245768 | tf_op jit(solution)/shard_map/ppermute | solution.py:386
  69.2 2.3 %collective-permute-done.7.second_ref = f32[10,16,128]{2,1,0:T(8,128)S(1)} collective-permute-done((f32[10,16,128]{2,1,0:T(8,128)S(1)}, f32[10,16,128]{2,1,0:T(8,128)S(1)}, u32[]{:S(2)}, u32[]{:S(2)}) %collective-permute-start.7) | collective-permute-done | bytes 81952 | tf_op jit(solution)/shard_map/ppermute | solution.py:386
  71.5 0.6 collective-permute-done.8.third_ref
  72.1 0.7 collective-permute-done.9.fourth_ref
  72.8 1.3 %all-to-all-done.2.col_parts_ref = f32[8,8,16,128]{3,2,1,0:T(8,128)S(1)} async-done(((f32[8,8,16,128]{3,2,1,0:T(8,128)}), f32[8,8,16,128]{3,2,1,0:T(8,128)S(1)}, u32[]{:S(2)}, u32[]{:S(2)}) %all-to-all-start.2) | async-done | bytes 524320 | tf_op jit(solution)/shard_map/all_to_all | solution.py:377
  74.1 1.2 %image.1 = (f32[16,1024]{1,0:T(8,128)S(1)}, f32[128,1,768]{2,1,0:T(1,128)}) custom-call(f32[8,8,16,128]{3,2,1,0:T(8,128)S(1)} %all-to-all-done.2.col_parts_ref, f32[10,16,128]{2,1,0:T(8,128)S(1)} %get-tuple-element.83.first_ref, f32[10,16,128]{2,1,0:T(8,128)S(1)} %collective-permute-done.7.second_ref, f32[10,16,128]{2,1,0:T(8,128)S(1)} %collective-permute-done.8.third_ref, ...), custom_call_target="tpu_custom_call" | custom-call | tf_op jit(solution)/shard_map/image/pallas_call | solution.py:486
  75.3 7.3 %all-to-all-start.3 = ((f32[128,1,768]{2,1,0:T(1,128)}), f32[128,1,768]{2,1,0:T(1,128)S(1)}, u32[]{:S(2)}, u32[]{:S(2)}) async-start(f32[128,1,768]{2,1,0:T(1,128)} %get-tuple-element.89), calls=%async_computation.3 | async-start | bytes 786432 | tf_op jit(solution)/shard_map/all_to_all | solution.py:377
  82.6 4.5 %factor.1 = (f32[48,48]{1,0:T(8,128)S(1)}, f32[32,48]{1,0:T(8,128)S(1)}) custom-call(f32[10,16,128]{2,1,0:T(8,128)S(1)} %get-tuple-element.83.first_ref, f32[10,16,128]{2,1,0:T(8,128)S(1)} %collective-permute-done.7.second_ref, f32[10,16,128]{2,1,0:T(8,128)S(1)} %collective-permute-done.8.third_ref, f32[10,16,128]{2,1,0:T(8,128)S(1)} %collective-permute-done.9.fourth_ref), custom_call_target="tpu_custom_call" | custom-call | tf_op jit(solution)/shard_map/factor/pallas_call | solution.py:491
  87.1 1.0 %orthonormal.1 = f32[48,1024]{1,0:T(8,128)} custom-call(f32[48,48]{1,0:T(8,128)S(1)} %get-tuple-element.87.inverse_ref, f32[2,16,1024]{2,1,0:T(8,128)S(1)} %get-tuple-element.50.basis_ref, f32[16,1024]{1,0:T(8,128)S(1)} %get-tuple-element.81.first_ref.residual_ref), custom_call_target="tpu_custom_call" | custom-call | tf_op jit(solution)/shard_map/orthonormal/pallas_call | solution.py:492
  88.1 1.0 %orthonormal_image.1 = f32[48,1024]{1,0:T(8,128)} custom-call(f32[48,48]{1,0:T(8,128)S(1)} %get-tuple-element.87.inverse_ref, f32[2,16,1024]{2,1,0:T(8,128)S(1)} %get-tuple-element.51.images_ref, f32[16,1024]{1,0:T(8,128)S(1)} %get-tuple-element.88.image_ref), custom_call_target="tpu_custom_call" | custom-call | tf_op jit(solution)/shard_map/orthonormal_image/pallas_call | solution.py:495
  89.1 5.6 %all-to-all-done.3.received_ref = f32[128,1,768]{2,1,0:T(1,128)S(1)} async-done(((f32[128,1,768]{2,1,0:T(1,128)}), f32[128,1,768]{2,1,0:T(1,128)S(1)}, u32[]{:S(2)}, u32[]{:S(2)}) %all-to-all-start.3) | async-done | bytes 393248 | tf_op jit(solution)/shard_map/all_to_all | solution.py:377
  94.7 1.4 %projected.1 = f32[48,48]{1,0:T(8,128)} custom-call(f32[128,1,768]{2,1,0:T(1,128)S(1)} %all-to-all-done.3.received_ref, f32[48,48]{1,0:T(8,128)S(1)} %get-tuple-element.87.inverse_ref, f32[32,48]{1,0:T(8,128)S(1)} %get-tuple-element.90.early_ref), custom_call_target="tpu_custom_call" | custom-call | tf_op jit(solution)/shard_map/projected/pallas_call | solution.py:500
  (2 shorter events, 0.1 us)
Async XLA Ops:
  2.3 21.0 %all-to-all-start = ((f32[128,1,128]{2,1,0:T(1,128)}), f32[128,1,128]{2,1,0:T(1,128)S(1)}, u32[]{:S(2)}, u32[]{:S(2)}) async-start(f32[128,1,128]{2,1,0:T(1,128)} %bitcast.9), calls=%async_computation | async-start | bytes 131072 | tf_op jit(solution)/shard_map/all_to_all | solution.py:377
  13.8 0.8 copy-start
  14.6 0.8 copy-start.1
  15.4 0.8 copy-start.2
  16.3 0.8 copy-start.3
  24.8 13.0 %all-to-all-start.1 = ((f32[8,10,16,128]{3,2,1,0:T(8,128)}), f32[8,10,16,128]{3,2,1,0:T(8,128)S(1)}, u32[]{:S(2)}, u32[]{:S(2)}) async-start(f32[8,10,16,128]{3,2,1,0:T(8,128)} %get-tuple-element.52), calls=%async_computation.1 | async-start | bytes 1310720 | tf_op jit(solution)/shard_map/all_to_all | solution.py:377
  28.3 4.8 %collective-permute-start = (f32[16,1024]{1,0:T(8,128)S(1)}, f32[16,1024]{1,0:T(8,128)S(1)}, u32[]{:S(2)}, u32[]{:S(2)}) collective-permute-start(f32[16,1024]{1,0:T(8,128)S(1)} %get-tuple-element.81.first_ref.residual_ref), channel_id=1, source_target_pairs={{0,32},{16,48},{32,64},{48,80},{64,96},{80,112},{96,0},{112,16},{1... | collective-permute-start | bytes 196616 | tf_op jit(solution)/shard_map/ppermute | solution.py:386
  28.6 5.5 %collective-permute-start.1 = (f32[16,1024]{1,0:T(8,128)S(1)}, f32[16,1024]{1,0:T(8,128)S(1)}, u32[]{:S(2)}, u32[]{:S(2)}) collective-permute-start(f32[16,1024]{1,0:T(8,128)S(1)} %get-tuple-element.81.first_ref.residual_ref), channel_id=1, source_target_pairs={{0,64},{16,80},{32,96},{48,112},{64,0},{80,16},{96,32},{112,48},{1... | collective-permute-start | bytes 196616 | tf_op jit(solution)/shard_map/ppermute | solution.py:386
  29.9 4.4 %collective-permute-start.2 = (f32[16,1024]{1,0:T(8,128)S(1)}, f32[16,1024]{1,0:T(8,128)S(1)}, u32[]{:S(2)}, u32[]{:S(2)}) collective-permute-start(f32[16,1024]{1,0:T(8,128)S(1)} %get-tuple-element.81.first_ref.residual_ref), channel_id=1, source_target_pairs={{0,96},{16,112},{32,0},{48,16},{64,32},{80,48},{96,64},{112,80},{1... | collective-permute-start | bytes 196616 | tf_op jit(solution)/shard_map/ppermute | solution.py:386
  31.7 0.7 copy-start.4
  32.4 0.7 copy-start.5
  37.8 3.8 %collective-permute-start.3 = (f32[8,10,16,128]{3,2,1,0:T(8,128)S(1)}, f32[8,10,16,128]{3,2,1,0:T(8,128)S(1)}, u32[]{:S(2)}, u32[]{:S(2)}) collective-permute-start(f32[8,10,16,128]{3,2,1,0:T(8,128)S(1)} %all-to-all-done.1.own_ref), channel_id=1, source_target_pairs={{0,1},{1,0},{2,3},{3,2},{4,5},{5,4},{6,7},{7,6},{8,9},{9,8},{10,11... | collective-permute-start | bytes 1966088 | tf_op jit(solution)/shard_map/ppermute | solution.py:381
  39.9 9.4 %collective-permute-start.4 = (f32[4,8,16,128]{3,2,1,0:T(8,128)S(1)}, f32[4,8,16,128]{3,2,1,0:T(8,128)S(1)}, u32[]{:S(2)}, u32[]{:S(2)}) collective-permute-start(f32[4,8,16,128]{3,2,1,0:T(8,128)S(1)} %line.1.own_ref), channel_id=1, source_target_pairs={{0,16},{16,0},{32,48},{48,32},{64,80},{80,64},{96,112},{112,96},{1... | collective-permute-start | bytes 786440 | tf_op jit(solution)/shard_map/ppermute | solution.py:381
  49.3 8.9 %collective-permute-start.5 = (f32[34,16,128]{2,1,0:T(8,128)S(1)}, f32[34,16,128]{2,1,0:T(8,128)S(1)}, u32[]{:S(2)}, u32[]{:S(2)}) collective-permute-start(f32[34,16,128]{2,1,0:T(8,128)S(1)} %get-tuple-element.64), channel_id=1, source_target_pairs={{0,16},{16,0},{32,48},{48,32},{64,80},{80,64},{96,112},{112,96},{1... | collective-permute-start | bytes 835592 | tf_op jit(solution)/shard_map/ppermute | solution.py:381
  58.2 3.2 %collective-permute-start.6 = (f32[64,16,128]{2,1,0:T(8,128)S(1)}, f32[64,16,128]{2,1,0:T(8,128)S(1)}, u32[]{:S(2)}, u32[]{:S(2)}) collective-permute-start(f32[64,16,128]{2,1,0:T(8,128)S(1)} %get-tuple-element.69), channel_id=1, source_target_pairs={{0,1},{1,0},{2,3},{3,2},{4,5},{5,4},{6,7},{7,6},{8,9},{9,8},{10,11... | collective-permute-start | bytes 1572872 | tf_op jit(solution)/shard_map/ppermute | solution.py:381
  62.3 11.8 %all-to-all-start.2 = ((f32[8,8,16,128]{3,2,1,0:T(8,128)}), f32[8,8,16,128]{3,2,1,0:T(8,128)S(1)}, u32[]{:S(2)}, u32[]{:S(2)}) async-start(f32[8,8,16,128]{3,2,1,0:T(8,128)} %bitcast.4), calls=%async_computation.2 | async-start | bytes 1048576 | tf_op jit(solution)/shard_map/all_to_all | solution.py:377
  65.9 5.7 %collective-permute-start.7 = (f32[10,16,128]{2,1,0:T(8,128)S(1)}, f32[10,16,128]{2,1,0:T(8,128)S(1)}, u32[]{:S(2)}, u32[]{:S(2)}) collective-permute-start(f32[10,16,128]{2,1,0:T(8,128)S(1)} %get-tuple-element.73), channel_id=1, source_target_pairs={{0,32},{16,48},{32,64},{48,80},{64,96},{80,112},{96,0},{112,16},{1... | collective-permute-start | bytes 245768 | tf_op jit(solution)/shard_map/ppermute | solution.py:386
  66.1 6.0 %collective-permute-start.8 = (f32[10,16,128]{2,1,0:T(8,128)S(1)}, f32[10,16,128]{2,1,0:T(8,128)S(1)}, u32[]{:S(2)}, u32[]{:S(2)}) collective-permute-start(f32[10,16,128]{2,1,0:T(8,128)S(1)} %get-tuple-element.74), channel_id=1, source_target_pairs={{0,64},{16,80},{32,96},{48,112},{64,0},{80,16},{96,32},{112,48},{1... | collective-permute-start | bytes 245768 | tf_op jit(solution)/shard_map/ppermute | solution.py:386
  67.7 5.1 %collective-permute-start.9 = (f32[10,16,128]{2,1,0:T(8,128)S(1)}, f32[10,16,128]{2,1,0:T(8,128)S(1)}, u32[]{:S(2)}, u32[]{:S(2)}) collective-permute-start(f32[10,16,128]{2,1,0:T(8,128)S(1)} %get-tuple-element.75), channel_id=1, source_target_pairs={{0,96},{16,112},{32,0},{48,16},{64,32},{80,48},{96,64},{112,80},{1... | collective-permute-start | bytes 245768 | tf_op jit(solution)/shard_map/ppermute | solution.py:386
  75.3 19.4 %all-to-all-start.3 = ((f32[128,1,768]{2,1,0:T(1,128)}), f32[128,1,768]{2,1,0:T(1,128)S(1)}, u32[]{:S(2)}, u32[]{:S(2)}) async-start(f32[128,1,768]{2,1,0:T(1,128)} %get-tuple-element.89), calls=%async_computation.3 | async-start | bytes 786432 | tf_op jit(solution)/shard_map/all_to_all | solution.py:377

commit v9 on v8

--- a/solution.py
+++ b/solution.py
@@ -79,14 +79,17 @@
         copy.wait()
 
 
-def places_kernel(rows_ref, cols_ref, rows_out_ref, cols_out_ref, *, blocks, gap):
+def places_kernel(rows_ref, cols_ref, rows_out_ref, targets_out_ref, cols_out_ref, *, blocks, gap):
     chips = lax.axis_size("col") // 2
     lines = lax.axis_size("row") // 2
     core = lax.rem(lax.axis_index("col"), 2)
     rows = rows_ref[...]
     index, peer = rows % blocks, rows // blocks
     other = jnp.where(peer % 2 == core, 0, 1)
-    rows_out_ref[...] = (other * chips + peer // 2) * blocks + index
+    chip = peer // 2
+    rows_out_ref[...] = (other * chips + chip) * blocks + index
+    places = (chip % (chips // 2)) * 2 + chip // (chips // 2)
+    targets_out_ref[...] = (other * chips + places) * blocks + index
     half = lax.rem(lax.axis_index("row"), 2)
     cols = cols_ref[...]
     index, peer = cols % blocks, cols // blocks
@@ -198,8 +201,11 @@
     out_ref[...] = exact_dot(inverse_ref[...] * row_scale, rows, NN)
 
 
-def orthonormal_image_kernel(inverse_ref, images_ref, image_ref, out_ref, *, row_scale):
-    rows = jnp.concatenate([images_ref[0], image_ref[...], images_ref[1]], axis=0)
+def orthonormal_image_kernel(
+    inverse_ref, images_ref, image_ref, from_lo_ref, out_ref, *, row_scale
+):
+    image = image_ref[...] + from_lo_ref[...]
+    rows = jnp.concatenate([images_ref[0], image, images_ref[1]], axis=0)
     out_ref[...] = exact_dot(inverse_ref[...] * row_scale, rows, NN)
 
 
@@ -211,15 +217,30 @@
     fourth_ref,
     basis_ref,
     residual_ref,
+    lo_basis_ref,
+    range_ref,
     image_ref,
+    to_lo_ref,
     slots_ref,
 ):
+    chips = range_ref.shape[0]
+    chip = lax.axis_index("col") // 2
+    x_lo = chip // (chips // 2)
+    partner = lax.rem(chip + chips // 2, chips)
     blocks = image_ref.shape[1] // LANES
     for index in range(blocks):
         part = first_ref[index] + second_ref[index] + third_ref[index] + fourth_ref[index]
-        image_ref[:, index * LANES : (index + 1) * LANES] = sum_peers(col_parts_ref, index) + part
+        image_ref[:, index * LANES : (index + 1) * LANES] = (
+            sum_peers(col_parts_ref, x_lo * blocks + index) + part
+        )
+        to_lo_ref[:, index * LANES : (index + 1) * LANES] = sum_peers(
+            col_parts_ref, (1 - x_lo) * blocks + index
+        )
     basis = jnp.concatenate([basis_ref[0], residual_ref[...], basis_ref[1]], axis=0)
     late = exact_dot(image_ref[...], basis, NT)
+    lo_residual = jnp.concatenate([range_ref[partner, index] for index in range(blocks)], axis=1)
+    basis = jnp.concatenate([lo_basis_ref[0], lo_residual, lo_basis_ref[1]], axis=0)
+    late = late + exact_dot(to_lo_ref[...], basis, NT)
     packed = jnp.concatenate([late[row : row + 1] for row in range(late.shape[0])], axis=1)
     slots_ref[...] = jnp.broadcast_to(packed[None], slots_ref.shape)
 
@@ -393,6 +414,11 @@
     n_col = lax.axis_size("col")
     everyone = ("row", "col")
     chips = n_col // 2
+    y_groups = [
+        [(half * chips // 2 + line) * 2 + core for line in range(chips // 2)]
+        for half in (0, 1)
+        for core in (0, 1)
+    ]
     core_groups = [[2 * chip + core for chip in range(chips)] for core in (0, 1)]
     members, piece = vectors.shape
     blocks = piece // LANES
@@ -435,13 +461,15 @@
     (line,) = call(line_kernel, [(lines, blocks, members, LANES)], "line")(*pieces)
     own_range = exchange(slots, "col", core_groups)
     residual, tile_rows, tile_cols = lax.optimization_barrier((residual, tile_rows, tile_cols))
-    rows, cols = pl.pallas_call(
+    rows, targets, cols = pl.pallas_call(
         functools.partial(places_kernel, blocks=blocks, gap=2),
-        out_shape=[jax.ShapeDtypeStruct(tile_rows.shape, jnp.int32)] * 2,
+        out_shape=[jax.ShapeDtypeStruct(tile_rows.shape, jnp.int32)] * 3,
         compiler_params=params,
         name="places",
     )(tile_rows, tile_cols)
-    own_range, line, rows, cols = lax.optimization_barrier((own_range, line, rows, cols))
+    own_range, line, rows, targets, cols = lax.optimization_barrier(
+        (own_range, line, rows, targets, cols)
+    )
     far_line = swap(line, "row", 1)
     other_range = swap(own_range, "col", 1)
     col_own, col_other = tile_call(
@@ -459,7 +487,7 @@
     col_received = swap(col_other, "row", 1)
     own_totals, other_totals = tile_call(
         tile_count,
-        rows,
+        targets,
         cols,
         tiles,
         line,
@@ -471,21 +499,24 @@
     col_received, own_totals, other_totals = lax.optimization_barrier(
         (col_received, own_totals, other_totals)
     )
+    outs = call(halves_kernel, [(blocks + 2, members, LANES)] * lines, "halves")(
+        col_own, col_received
+    )
+    other_totals, *outs = lax.optimization_barrier((swap(other_totals, "col", 1), *outs))
     (totals,) = pl.pallas_call(
         join_kernel,
         out_shape=[jax.ShapeDtypeStruct(own_totals.shape, f32)],
         compiler_params=pltpu.CompilerParams(vmem_limit_bytes=TILE_VMEM_BYTES),
         name="join",
-    )(own_totals, swap(other_totals, "col", 1))
-    col_parts = exchange(totals.reshape(chips, blocks, members, LANES), "col", core_groups)
-    outs = call(halves_kernel, [(blocks + 2, members, LANES)] * lines, "halves")(
-        col_own, col_received
-    )
+    )(own_totals, other_totals)
+    col_parts = exchange(totals.reshape(chips // 2, 2 * blocks, members, LANES), "col", y_groups)
+    lo_basis = swap(basis, "col", chips)
     row_parts = [outs[0]] + [shift_lines(outs[shift], shift) for shift in range(1, lines)]
-    col_parts, *row_parts = lax.optimization_barrier((col_parts, *row_parts))
-    image, slots = call(
-        image_kernel, [(members, piece), (n_row * n_col, 1, members * order)], "image"
-    )(col_parts, *row_parts, basis, residual)
+    col_parts, lo_basis, *row_parts = lax.optimization_barrier((col_parts, lo_basis, *row_parts))
+    image, to_lo, slots = call(
+        image_kernel, [(members, piece)] * 2 + [(n_row * n_col, 1, members * order)], "image"
+    )(col_parts, *row_parts, basis, residual, lo_basis, own_range)
+    from_lo = swap(to_lo, "col", chips)
     late = exchange(slots, everyone)
     image, *row_parts = lax.optimization_barrier((image, *row_parts))
     inverse, early = call(factor_kernel, [(order, order), (2 * members, order)], "factor")(*row_parts)
@@ -496,7 +527,7 @@
         functools.partial(orthonormal_image_kernel, row_scale=row_scale),
         [(order, piece)],
         "orthonormal_image",
-    )(inverse, images, image)
+    )(inverse, images, image, from_lo)
     (projected,) = call(projected_kernel, [(order, order)], "projected")(late, inverse, early)
     return (orthonormal, orthonormal_image, projected)
 

time: 96.7 us -> 97.7 us (1.010)
  starting transfers between devices: 38.4 us -> 40.4 us
  Pallas kernels: 20.8 us -> 19 us
    ppermute x4 -> x6, waiting for transfers between devices: 9.73 us -> 12.6 us  [swap(): lax.ppermute(array, axis, [(i, i ^ distance) for i in range(lax.axis_size...]
    ppermute x4 -> x6, starting transfers between devices: 5.89 us -> 8.56 us  [swap(): lax.ppermute(array, axis, [(i, i ^ distance) for i in range(lax.axis_size...]
    all_to_all x4, waiting for transfers between devices: 16.2 us -> 14.2 us  [exchange(): lax.all_to_all(slots, axes, 0, 0, axis_index_groups=groups, tiled=True)]
    pallas_call x2, Pallas kernels: 7.31 us -> 5.43 us  [tile_call(): pl.pallas_call(functools.partial(tile_kernel, forward=forward), out_shape...]
  transfers between devices with their start and end apart: 14 -> 16, of which waited for: 12 -> 13; matrix products, arithmetic and copies ran while one was open for 0% -> 0% of each run, Pallas kernels for 15% -> 13%
where the time goes in v9:
time: 97.7 us; the launch traced here: 97 us
  starting transfers between devices  40.4 us (41%)
  waiting for transfers between devices  31.6 us (32%)
  Pallas kernels  19 us (19%)
  local copies, waits for them, and re-layouts  4.71 us (5%)
  between operations  1.4 us (1%)
    all_to_all x4, starting transfers between devices, exchange(): lax.all_to_all(slots, axes, 0, 0, axis_index_groups=groups, tiled=True)  25.8 us
    all_to_all x4, waiting for transfers between devices, exchange(): lax.all_to_all(slots, axes, 0, 0, axis_index_groups=groups, tiled=True)  14.2 us
    ppermute x6, waiting for transfers between devices, swap(): lax.ppermute(array, axis, [(i, i ^ distance) for i in range(lax.axis_size...  12.6 us
    ppermute x6, starting transfers between devices, swap(): lax.ppermute(array, axis, [(i, i ^ distance) for i in range(lax.axis_size...  8.56 us
    ppermute x6, starting transfers between devices, shift_lines(): lax.ppermute(array, 'row', [(i, (i + 2 * shift) % size) for i in range(si...  6.05 us
    pallas_call x2, Pallas kernels, tile_call(): pl.pallas_call(functools.partial(tile_kernel, forward=forward), out_shape...  5.43 us
    unnamed x12, local copies, waits for them, and re-layouts  4.71 us
    ppermute x6, waiting for transfers between devices, shift_lines(): lax.ppermute(array, 'row', [(i, (i + 2 * shift) % size) for i in range(si...  4.7 us
  transfers between devices with their start and end apart: 16, of which 13 were waited for; matrix products, arithmetic and copies ran while one was open for 0% of the time, Pallas kernels for 13%

profile of v9, /device:TPU:1, one launch (start us, length us, event | category | flops | bytes accessed | tf_op | source)
XLA Modules:
  0.0 97.0 jit_solution(14713996244804583390)
XLA Ops:
  0.6 1.6 %stage.1 = f32[128,128]{1,0:T(8,128)} custom-call(f32[16,1024]{1,0:T(8,128)} %vectors_hbm.3, f32[16,1024]{1,0:T(8,128)} %hvectors_hbm.3), custom_call_target="tpu_custom_call" | custom-call | tf_op jit(solution)/shard_map/stage/pallas_call | solution.py:434
  2.3 11.5 %all-to-all-start = ((f32[128,1,128]{2,1,0:T(1,128)}), f32[128,1,128]{2,1,0:T(1,128)S(1)}, u32[]{:S(2)}, u32[]{:S(2)}) async-start(f32[128,1,128]{2,1,0:T(1,128)} %bitcast.9), calls=%async_computation | async-start | bytes 131072 | tf_op jit(solution)/shard_map/all_to_all | solution.py:398
  13.8 0.0 copy-start
  13.8 0.8 copy-done
  14.6 0.0 copy-start.1
  14.6 0.8 copy-done.1
  15.4 0.0 copy-start.2
  15.5 0.8 copy-done.2
  16.3 0.0 copy-start.3
  16.3 0.8 copy-done.3
  17.1 0.3 prepare.1
  17.5 5.8 %all-to-all-done = f32[128,1,128]{2,1,0:T(1,128)S(1)} async-done(((f32[128,1,128]{2,1,0:T(1,128)}), f32[128,1,128]{2,1,0:T(1,128)S(1)}, u32[]{:S(2)}, u32[]{:S(2)}) %all-to-all-start) | async-done | bytes 65568 | tf_op jit(solution)/shard_map/all_to_all | solution.py:398
  23.3 1.5 %residual.1 = (f32[16,1024]{1,0:T(8,128)S(1)}, f32[8,10,16,128]{3,2,1,0:T(8,128)}) custom-call(f32[128,128]{1,0:T(8,128)S(1)} %bitcast.6, f32[2,16,1024]{2,1,0:T(8,128)S(1)} %get-tuple-element.59.basis_ref, f32[2,16,1024]{2,1,0:T(8,128)S(1)} %get-tuple-element.60.images_ref), custom_call_target="tpu_custom_call" | custom-call | tf_op jit(solution)/shard_map/residual/pallas_call | solution.py:457
  24.8 3.5 %all-to-all-start.1 = ((f32[8,10,16,128]{3,2,1,0:T(8,128)}), f32[8,10,16,128]{3,2,1,0:T(8,128)S(1)}, u32[]{:S(2)}, u32[]{:S(2)}) async-start(f32[8,10,16,128]{3,2,1,0:T(8,128)} %get-tuple-element.61), calls=%async_computation.1 | async-start | bytes 1310720 | tf_op jit(solution)/shard_map/all_to_all | solution.py:398
  28.3 0.3 collective-permute-start
  28.6 1.3 %collective-permute-start.1 = (f32[16,1024]{1,0:T(8,128)S(1)}, f32[16,1024]{1,0:T(8,128)S(1)}, u32[]{:S(2)}, u32[]{:S(2)}) collective-permute-start(f32[16,1024]{1,0:T(8,128)S(1)} %get-tuple-element.97.first_ref.residual_ref), channel_id=1, source_target_pairs={{0,64},{16,80},{32,96},{48,112},{64,0},{80,16},{96,32},{112,48},{1... | collective-permute-start | bytes 196616 | tf_op jit(solution)/shard_map/ppermute | solution.py:407
  29.9 1.8 %collective-permute-start.2 = (f32[16,1024]{1,0:T(8,128)S(1)}, f32[16,1024]{1,0:T(8,128)S(1)}, u32[]{:S(2)}, u32[]{:S(2)}) collective-permute-start(f32[16,1024]{1,0:T(8,128)S(1)} %get-tuple-element.97.first_ref.residual_ref), channel_id=1, source_target_pairs={{0,96},{16,112},{32,0},{48,16},{64,32},{80,48},{96,64},{112,80},{1... | collective-permute-start | bytes 196616 | tf_op jit(solution)/shard_map/ppermute | solution.py:407
  31.7 0.0 copy-start.4
  31.7 0.7 copy-done.4
  32.4 0.0 copy-start.5
  32.4 0.7 copy-done.5
  33.1 0.0 collective-permute-done.second_ref
  33.1 1.0 %collective-permute-done.1.third_ref = f32[16,1024]{1,0:T(8,128)S(1)} collective-permute-done((f32[16,1024]{1,0:T(8,128)S(1)}, f32[16,1024]{1,0:T(8,128)S(1)}, u32[]{:S(2)}, u32[]{:S(2)}) %collective-permute-start.1) | collective-permute-done | bytes 65568 | tf_op jit(solution)/shard_map/ppermute | solution.py:407
  34.1 0.2 collective-permute-done.2.fourth_ref
  34.4 3.5 %all-to-all-done.1.own_ref.range_ref = f32[8,10,16,128]{3,2,1,0:T(8,128)S(1)} async-done(((f32[8,10,16,128]{3,2,1,0:T(8,128)}), f32[8,10,16,128]{3,2,1,0:T(8,128)S(1)}, u32[]{:S(2)}, u32[]{:S(2)}) %all-to-all-start.1) | async-done | bytes 655392 | tf_op jit(solution)/shard_map/all_to_all | solution.py:398
  37.8 2.1 %collective-permute-start.3 = (f32[8,10,16,128]{3,2,1,0:T(8,128)S(1)}, f32[8,10,16,128]{3,2,1,0:T(8,128)S(1)}, u32[]{:S(2)}, u32[]{:S(2)}) collective-permute-start(f32[8,10,16,128]{3,2,1,0:T(8,128)S(1)} %all-to-all-done.1.own_ref.range_ref), channel_id=1, source_target_pairs={{0,1},{1,0},{2,3},{3,2},{4,5},{5,4},{6,7},{7,6},{8,9},{9,8},{10,11... | collective-permute-start | bytes 1966088 | tf_op jit(solution)/shard_map/ppermute | solution.py:402
  39.9 1.1 %collective-permute-start.4 = (f32[4,8,16,128]{3,2,1,0:T(8,128)S(1)}, f32[4,8,16,128]{3,2,1,0:T(8,128)S(1)}, u32[]{:S(2)}, u32[]{:S(2)}) collective-permute-start(f32[4,8,16,128]{3,2,1,0:T(8,128)S(1)} %line.1.own_ref), channel_id=1, source_target_pairs={{0,16},{16,0},{32,48},{48,32},{64,80},{80,64},{96,112},{112,96},{1... | collective-permute-start | bytes 786440 | tf_op jit(solution)/shard_map/ppermute | solution.py:402
  41.6 0.0 collective-permute-done.3.other_ref
  41.6 2.5 %backward_tiles.1 = (f32[34,16,128]{2,1,0:T(8,128)S(1)}, f32[34,16,128]{2,1,0:T(8,128)S(1)}) custom-call(s32[1,1]{1,0:T(1,128)S(6)} %copy.12.count_ref, s32[1,1,384]{2,1,0:T(1,128)S(1)} %get-tuple-element.68.rows_hbm, s32[1,1,384]{2,1,0:T(1,128)S(1)} %get-tuple-element.69.cols_hbm, bf16[384,128,128]{2,1,0:T(8,128)(2,1)} %bitcast.7, ...), custom_call_target="tpu_custom_call" | custom-call | tf_op jit(solution)/shard_map/backward_tiles/pallas_call | solution.py:374
  44.1 5.2 %collective-permute-done.4.other_ref = f32[4,8,16,128]{3,2,1,0:T(8,128)S(1)} collective-permute-done((f32[4,8,16,128]{3,2,1,0:T(8,128)S(1)}, f32[4,8,16,128]{3,2,1,0:T(8,128)S(1)}, u32[]{:S(2)}, u32[]{:S(2)}) %collective-permute-start.4) | collective-permute-done | bytes 262176 | tf_op jit(solution)/shard_map/ppermute | solution.py:402
  49.3 1.1 %collective-permute-start.5 = (f32[34,16,128]{2,1,0:T(8,128)S(1)}, f32[34,16,128]{2,1,0:T(8,128)S(1)}, u32[]{:S(2)}, u32[]{:S(2)}) collective-permute-start(f32[34,16,128]{2,1,0:T(8,128)S(1)} %get-tuple-element.74), channel_id=1, source_target_pairs={{0,16},{16,0},{32,48},{48,32},{64,80},{80,64},{96,112},{112,96},{1... | collective-permute-start | bytes 835592 | tf_op jit(solution)/shard_map/ppermute | solution.py:402
  50.4 3.0 %forward_tiles.1 = (f32[64,16,128]{2,1,0:T(8,128)S(1)}, f32[64,16,128]{2,1,0:T(8,128)S(1)}) custom-call(s32[1,1]{1,0:T(1,128)S(6)} %copy.12.count_ref, s32[1,1,384]{2,1,0:T(1,128)S(1)} %get-tuple-element.75.rows_hbm, s32[1,1,384]{2,1,0:T(1,128)S(1)} %get-tuple-element.69.cols_hbm, bf16[384,128,128]{2,1,0:T(8,128)(2,1)} %bitcast.8, ...), custom_call_target="tpu_custom_call" | custom-call | tf_op jit(solution)/shard_map/forward_tiles/pallas_call | solution.py:374
  53.4 4.8 %collective-permute-done.5.received_ref = f32[34,16,128]{2,1,0:T(8,128)S(1)} collective-permute-done((f32[34,16,128]{2,1,0:T(8,128)S(1)}, f32[34,16,128]{2,1,0:T(8,128)S(1)}, u32[]{:S(2)}, u32[]{:S(2)}) %collective-permute-start.5) | collective-permute-done | bytes 278560 | tf_op jit(solution)/shard_map/ppermute | solution.py:402
  58.2 1.7 %collective-permute-start.6 = (f32[64,16,128]{2,1,0:T(8,128)S(1)}, f32[64,16,128]{2,1,0:T(8,128)S(1)}, u32[]{:S(2)}, u32[]{:S(2)}) collective-permute-start(f32[64,16,128]{2,1,0:T(8,128)S(1)} %get-tuple-element.80), channel_id=1, source_target_pairs={{0,1},{1,0},{2,3},{3,2},{4,5},{5,4},{6,7},{7,6},{8,9},{9,8},{10,11... | collective-permute-start | bytes 1572872 | tf_op jit(solution)/shard_map/ppermute | solution.py:402
  59.9 1.5 %collective-permute-done.6.other_ref = f32[64,16,128]{2,1,0:T(8,128)S(1)} collective-permute-done((f32[64,16,128]{2,1,0:T(8,128)S(1)}, f32[64,16,128]{2,1,0:T(8,128)S(1)}, u32[]{:S(2)}, u32[]{:S(2)}) %collective-permute-start.6) | collective-permute-done | bytes 524320 | tf_op jit(solution)/shard_map/ppermute | solution.py:402
  61.4 0.8 join.1
  62.3 3.5 %all-to-all-start.2 = ((f32[4,16,16,128]{3,2,1,0:T(8,128)}), f32[4,16,16,128]{3,2,1,0:T(8,128)S(1)}, u32[]{:S(2)}, u32[]{:S(2)}) async-start(f32[4,16,16,128]{3,2,1,0:T(8,128)} %bitcast.4), calls=%async_computation.2 | async-start | bytes 1048576 | tf_op jit(solution)/shard_map/all_to_all | solution.py:398
  65.8 1.2 %collective-permute-start.7 = (f32[2,16,1024]{2,1,0:T(8,128)S(1)}, f32[2,16,1024]{2,1,0:T(8,128)S(1)}, u32[]{:S(2)}, u32[]{:S(2)}) collective-permute-start(f32[2,16,1024]{2,1,0:T(8,128)S(1)} %get-tuple-element.59.basis_ref), channel_id=1, source_target_pairs={{0,8},{1,9},{2,10},{3,11},{4,12},{5,13},{6,14},{7,15},{8,0},{9,1},... | collective-permute-start | bytes 393224 | tf_op jit(solution)/shard_map/ppermute | solution.py:402
  67.0 0.3 collective-permute-start.10
  67.3 1.2 %collective-permute-start.8 = (f32[10,16,128]{2,1,0:T(8,128)S(1)}, f32[10,16,128]{2,1,0:T(8,128)S(1)}, u32[]{:S(2)}, u32[]{:S(2)}) collective-permute-start(f32[10,16,128]{2,1,0:T(8,128)S(1)} %get-tuple-element.89), channel_id=1, source_target_pairs={{0,32},{16,48},{32,64},{48,80},{64,96},{80,112},{96,0},{112,16},{1... | collective-permute-start | bytes 245768 | tf_op jit(solution)/shard_map/ppermute | solution.py:407
  68.4 1.2 %collective-permute-start.9 = (f32[10,16,128]{2,1,0:T(8,128)S(1)}, f32[10,16,128]{2,1,0:T(8,128)S(1)}, u32[]{:S(2)}, u32[]{:S(2)}) collective-permute-start(f32[10,16,128]{2,1,0:T(8,128)S(1)} %get-tuple-element.90), channel_id=1, source_target_pairs={{0,64},{16,80},{32,96},{48,112},{64,0},{80,16},{96,32},{112,48},{1... | collective-permute-start | bytes 245768 | tf_op jit(solution)/shard_map/ppermute | solution.py:407
  69.7 0.9 collective-permute-done.7.lo_basis_ref
  70.6 0.0 collective-permute-done.10.fourth_ref
  70.6 1.5 %collective-permute-done.8.second_ref = f32[10,16,128]{2,1,0:T(8,128)S(1)} collective-permute-done((f32[10,16,128]{2,1,0:T(8,128)S(1)}, f32[10,16,128]{2,1,0:T(8,128)S(1)}, u32[]{:S(2)}, u32[]{:S(2)}) %collective-permute-start.8) | collective-permute-done | bytes 81952 | tf_op jit(solution)/shard_map/ppermute | solution.py:407
  72.1 2.0 %collective-permute-done.9.third_ref = f32[10,16,128]{2,1,0:T(8,128)S(1)} collective-permute-done((f32[10,16,128]{2,1,0:T(8,128)S(1)}, f32[10,16,128]{2,1,0:T(8,128)S(1)}, u32[]{:S(2)}, u32[]{:S(2)}) %collective-permute-start.9) | collective-permute-done | bytes 81952 | tf_op jit(solution)/shard_map/ppermute | solution.py:407
  74.0 0.9 all-to-all-done.2.col_parts_ref
  75.0 1.3 %image.1 = (f32[16,1024]{1,0:T(8,128)S(1)}, f32[16,1024]{1,0:T(8,128)S(1)}, f32[128,1,768]{2,1,0:T(1,128)}) custom-call(f32[4,16,16,128]{3,2,1,0:T(8,128)S(1)} %all-to-all-done.2.col_parts_ref, f32[10,16,128]{2,1,0:T(8,128)S(1)} %get-tuple-element.100.first_ref, f32[10,16,128]{2,1,0:T(8,128)S(1)} %collective-permute-done.8.second_ref, ...), custom_call_target="tpu_custom_call" | custom-call | tf_op jit(solution)/shard_map/image/pallas_call | solution.py:516
  76.3 7.3 %all-to-all-start.3 = ((f32[128,1,768]{2,1,0:T(1,128)}), f32[128,1,768]{2,1,0:T(1,128)S(1)}, u32[]{:S(2)}, u32[]{:S(2)}) async-start(f32[128,1,768]{2,1,0:T(1,128)} %get-tuple-element.107), calls=%async_computation.3 | async-start | bytes 786432 | tf_op jit(solution)/shard_map/all_to_all | solution.py:398
  83.5 1.5 %collective-permute-start.11 = (f32[16,1024]{1,0:T(8,128)S(1)}, f32[16,1024]{1,0:T(8,128)S(1)}, u32[]{:S(2)}, u32[]{:S(2)}) collective-permute-start(f32[16,1024]{1,0:T(8,128)S(1)} %get-tuple-element.106), channel_id=1, source_target_pairs={{0,8},{1,9},{2,10},{3,11},{4,12},{5,13},{6,14},{7,15},{8,0},{9,1},... | collective-permute-start | bytes 196616 | tf_op jit(solution)/shard_map/ppermute | solution.py:402
  85.0 4.5 %factor.1 = (f32[48,48]{1,0:T(8,128)S(1)}, f32[32,48]{1,0:T(8,128)S(1)}) custom-call(f32[10,16,128]{2,1,0:T(8,128)S(1)} %get-tuple-element.100.first_ref, f32[10,16,128]{2,1,0:T(8,128)S(1)} %collective-permute-done.8.second_ref, f32[10,16,128]{2,1,0:T(8,128)S(1)} %collective-permute-done.9.third_ref, f32[10,16,128]{2,1,0:T(8,128)S(1)} %collective-permute-done.10.fourth_ref), custom_call_target="tpu_custom_call" | custom-call | tf_op jit(solution)/shard_map/factor/pallas_call | solution.py:522
  89.5 1.0 %orthonormal.1 = f32[48,1024]{1,0:T(8,128)} custom-call(f32[48,48]{1,0:T(8,128)S(1)} %get-tuple-element.104.inverse_ref, f32[2,16,1024]{2,1,0:T(8,128)S(1)} %get-tuple-element.59.basis_ref, f32[16,1024]{1,0:T(8,128)S(1)} %get-tuple-element.97.first_ref.residual_ref), custom_call_target="tpu_custom_call" | custom-call | tf_op jit(solution)/shard_map/orthonormal/pallas_call | solution.py:523
  90.5 0.1 collective-permute-done.11.from_lo_ref
  90.6 1.0 %orthonormal_image.1 = f32[48,1024]{1,0:T(8,128)} custom-call(f32[48,48]{1,0:T(8,128)S(1)} %get-tuple-element.104.inverse_ref, f32[2,16,1024]{2,1,0:T(8,128)S(1)} %get-tuple-element.60.images_ref, f32[16,1024]{1,0:T(8,128)S(1)} %get-tuple-element.105.image_ref, f32[16,1024]{1,0:T(8,128)S(1)} %collective-permute-done.11.from_lo_ref), custom_call_target="tpu_custom_call" | custom-call | tf_op jit(solution)/shard_map/orthonormal_image/pallas_call | solution.py:526
  91.6 4.0 %all-to-all-done.3.received_ref = f32[128,1,768]{2,1,0:T(1,128)S(1)} async-done(((f32[128,1,768]{2,1,0:T(1,128)}), f32[128,1,768]{2,1,0:T(1,128)S(1)}, u32[]{:S(2)}, u32[]{:S(2)}) %all-to-all-start.3) | async-done | bytes 393248 | tf_op jit(solution)/shard_map/all_to_all | solution.py:398
  95.7 1.4 %projected.1 = f32[48,48]{1,0:T(8,128)} custom-call(f32[128,1,768]{2,1,0:T(1,128)S(1)} %all-to-all-done.3.received_ref, f32[48,48]{1,0:T(8,128)S(1)} %get-tuple-element.104.inverse_ref, f32[32,48]{1,0:T(8,128)S(1)} %get-tuple-element.108.early_ref), custom_call_target="tpu_custom_call" | custom-call | tf_op jit(solution)/shard_map/projected/pallas_call | solution.py:531
  (3 shorter events, 0.1 us)
Async XLA Ops:
  2.3 21.0 %all-to-all-start = ((f32[128,1,128]{2,1,0:T(1,128)}), f32[128,1,128]{2,1,0:T(1,128)S(1)}, u32[]{:S(2)}, u32[]{:S(2)}) async-start(f32[128,1,128]{2,1,0:T(1,128)} %bitcast.9), calls=%async_computation | async-start | bytes 131072 | tf_op jit(solution)/shard_map/all_to_all | solution.py:398
  13.8 0.8 copy-start
  14.6 0.8 copy-start.1
  15.4 0.8 copy-start.2
  16.3 0.8 copy-start.3
  24.8 13.0 %all-to-all-start.1 = ((f32[8,10,16,128]{3,2,1,0:T(8,128)}), f32[8,10,16,128]{3,2,1,0:T(8,128)S(1)}, u32[]{:S(2)}, u32[]{:S(2)}) async-start(f32[8,10,16,128]{3,2,1,0:T(8,128)} %get-tuple-element.61), calls=%async_computation.1 | async-start | bytes 1310720 | tf_op jit(solution)/shard_map/all_to_all | solution.py:398
  28.3 4.8 %collective-permute-start = (f32[16,1024]{1,0:T(8,128)S(1)}, f32[16,1024]{1,0:T(8,128)S(1)}, u32[]{:S(2)}, u32[]{:S(2)}) collective-permute-start(f32[16,1024]{1,0:T(8,128)S(1)} %get-tuple-element.97.first_ref.residual_ref), channel_id=1, source_target_pairs={{0,32},{16,48},{32,64},{48,80},{64,96},{80,112},{96,0},{112,16},{1... | collective-permute-start | bytes 196616 | tf_op jit(solution)/shard_map/ppermute | solution.py:407
  28.6 5.5 %collective-permute-start.1 = (f32[16,1024]{1,0:T(8,128)S(1)}, f32[16,1024]{1,0:T(8,128)S(1)}, u32[]{:S(2)}, u32[]{:S(2)}) collective-permute-start(f32[16,1024]{1,0:T(8,128)S(1)} %get-tuple-element.97.first_ref.residual_ref), channel_id=1, source_target_pairs={{0,64},{16,80},{32,96},{48,112},{64,0},{80,16},{96,32},{112,48},{1... | collective-permute-start | bytes 196616 | tf_op jit(solution)/shard_map/ppermute | solution.py:407
  29.9 4.4 %collective-permute-start.2 = (f32[16,1024]{1,0:T(8,128)S(1)}, f32[16,1024]{1,0:T(8,128)S(1)}, u32[]{:S(2)}, u32[]{:S(2)}) collective-permute-start(f32[16,1024]{1,0:T(8,128)S(1)} %get-tuple-element.97.first_ref.residual_ref), channel_id=1, source_target_pairs={{0,96},{16,112},{32,0},{48,16},{64,32},{80,48},{96,64},{112,80},{1... | collective-permute-start | bytes 196616 | tf_op jit(solution)/shard_map/ppermute | solution.py:407
  31.7 0.7 copy-start.4
  32.4 0.7 copy-start.5
  37.8 3.8 %collective-permute-start.3 = (f32[8,10,16,128]{3,2,1,0:T(8,128)S(1)}, f32[8,10,16,128]{3,2,1,0:T(8,128)S(1)}, u32[]{:S(2)}, u32[]{:S(2)}) collective-permute-start(f32[8,10,16,128]{3,2,1,0:T(8,128)S(1)} %all-to-all-done.1.own_ref.range_ref), channel_id=1, source_target_pairs={{0,1},{1,0},{2,3},{3,2},{4,5},{5,4},{6,7},{7,6},{8,9},{9,8},{10,11... | collective-permute-start | bytes 1966088 | tf_op jit(solution)/shard_map/ppermute | solution.py:402
  39.9 9.4 %collective-permute-start.4 = (f32[4,8,16,128]{3,2,1,0:T(8,128)S(1)}, f32[4,8,16,128]{3,2,1,0:T(8,128)S(1)}, u32[]{:S(2)}, u32[]{:S(2)}) collective-permute-start(f32[4,8,16,128]{3,2,1,0:T(8,128)S(1)} %line.1.own_ref), channel_id=1, source_target_pairs={{0,16},{16,0},{32,48},{48,32},{64,80},{80,64},{96,112},{112,96},{1... | collective-permute-start | bytes 786440 | tf_op jit(solution)/shard_map/ppermute | solution.py:402
  49.3 8.9 %collective-permute-start.5 = (f32[34,16,128]{2,1,0:T(8,128)S(1)}, f32[34,16,128]{2,1,0:T(8,128)S(1)}, u32[]{:S(2)}, u32[]{:S(2)}) collective-permute-start(f32[34,16,128]{2,1,0:T(8,128)S(1)} %get-tuple-element.74), channel_id=1, source_target_pairs={{0,16},{16,0},{32,48},{48,32},{64,80},{80,64},{96,112},{112,96},{1... | collective-permute-start | bytes 835592 | tf_op jit(solution)/shard_map/ppermute | solution.py:402
  58.2 3.2 %collective-permute-start.6 = (f32[64,16,128]{2,1,0:T(8,128)S(1)}, f32[64,16,128]{2,1,0:T(8,128)S(1)}, u32[]{:S(2)}, u32[]{:S(2)}) collective-permute-start(f32[64,16,128]{2,1,0:T(8,128)S(1)} %get-tuple-element.80), channel_id=1, source_target_pairs={{0,1},{1,0},{2,3},{3,2},{4,5},{5,4},{6,7},{7,6},{8,9},{9,8},{10,11... | collective-permute-start | bytes 1572872 | tf_op jit(solution)/shard_map/ppermute | solution.py:402
  62.3 12.7 %all-to-all-start.2 = ((f32[4,16,16,128]{3,2,1,0:T(8,128)}), f32[4,16,16,128]{3,2,1,0:T(8,128)S(1)}, u32[]{:S(2)}, u32[]{:S(2)}) async-start(f32[4,16,16,128]{3,2,1,0:T(8,128)} %bitcast.4), calls=%async_computation.2 | async-start | bytes 1048576 | tf_op jit(solution)/shard_map/all_to_all | solution.py:398
  65.8 4.8 %collective-permute-start.7 = (f32[2,16,1024]{2,1,0:T(8,128)S(1)}, f32[2,16,1024]{2,1,0:T(8,128)S(1)}, u32[]{:S(2)}, u32[]{:S(2)}) collective-permute-start(f32[2,16,1024]{2,1,0:T(8,128)S(1)} %get-tuple-element.59.basis_ref), channel_id=1, source_target_pairs={{0,8},{1,9},{2,10},{3,11},{4,12},{5,13},{6,14},{7,15},{8,0},{9,1},... | collective-permute-start | bytes 393224 | tf_op jit(solution)/shard_map/ppermute | solution.py:402
  67.0 3.6 %collective-permute-start.10 = (f32[10,16,128]{2,1,0:T(8,128)S(1)}, f32[10,16,128]{2,1,0:T(8,128)S(1)}, u32[]{:S(2)}, u32[]{:S(2)}) collective-permute-start(f32[10,16,128]{2,1,0:T(8,128)S(1)} %get-tuple-element.91), channel_id=1, source_target_pairs={{0,96},{16,112},{32,0},{48,16},{64,32},{80,48},{96,64},{112,80},{1... | collective-permute-start | bytes 245768 | tf_op jit(solution)/shard_map/ppermute | solution.py:407
  67.3 4.8 %collective-permute-start.8 = (f32[10,16,128]{2,1,0:T(8,128)S(1)}, f32[10,16,128]{2,1,0:T(8,128)S(1)}, u32[]{:S(2)}, u32[]{:S(2)}) collective-permute-start(f32[10,16,128]{2,1,0:T(8,128)S(1)} %get-tuple-element.89), channel_id=1, source_target_pairs={{0,32},{16,48},{32,64},{48,80},{64,96},{80,112},{96,0},{112,16},{1... | collective-permute-start | bytes 245768 | tf_op jit(solution)/shard_map/ppermute | solution.py:407
  68.4 5.6 %collective-permute-start.9 = (f32[10,16,128]{2,1,0:T(8,128)S(1)}, f32[10,16,128]{2,1,0:T(8,128)S(1)}, u32[]{:S(2)}, u32[]{:S(2)}) collective-permute-start(f32[10,16,128]{2,1,0:T(8,128)S(1)} %get-tuple-element.90), channel_id=1, source_target_pairs={{0,64},{16,80},{32,96},{48,112},{64,0},{80,16},{96,32},{112,48},{1... | collective-permute-start | bytes 245768 | tf_op jit(solution)/shard_map/ppermute | solution.py:407
  76.3 19.4 %all-to-all-start.3 = ((f32[128,1,768]{2,1,0:T(1,128)}), f32[128,1,768]{2,1,0:T(1,128)S(1)}, u32[]{:S(2)}, u32[]{:S(2)}) async-start(f32[128,1,768]{2,1,0:T(1,128)} %get-tuple-element.107), calls=%async_computation.3 | async-start | bytes 786432 | tf_op jit(solution)/shard_map/all_to_all | solution.py:398
  83.5 7.1 %collective-permute-start.11 = (f32[16,1024]{1,0:T(8,128)S(1)}, f32[16,1024]{1,0:T(8,128)S(1)}, u32[]{:S(2)}, u32[]{:S(2)}) collective-permute-start(f32[16,1024]{1,0:T(8,128)S(1)} %get-tuple-element.106), channel_id=1, source_target_pairs={{0,8},{1,9},{2,10},{3,11},{4,12},{5,13},{6,14},{7,15},{8,0},{9,1},... | collective-permute-start | bytes 196616 | tf_op jit(solution)/shard_map/ppermute | solution.py:402

commit v10 on v8

--- a/solution.py
+++ b/solution.py
@@ -94,7 +94,9 @@
     cols_out_ref[...] = (other * lines + peer // 2) * blocks + index + other * gap
 
 
-def residual_kernel(sums_ref, basis_ref, images_ref, residual_ref, slots_ref):
+def residual_kernel(
+    sums_ref, basis_ref, images_ref, residual_ref, slots_hbm, piece_ref, extra_ref, sent
+):
     members = basis_ref.shape[1]
     sums = jnp.sum(sums_ref[...], axis=0, keepdims=True)
     lane = lax.broadcasted_iota(jnp.int32, (members, LANES), 1)
@@ -105,11 +107,19 @@
     residual_ref[...] = residual
     blocks = residual.shape[1] // LANES
     for index in range(blocks):
-        for slot in range(slots_ref.shape[0]):
-            slots_ref[slot, index] = block(residual, index)
+        piece_ref[index] = block(residual, index)
+    slots = slots_hbm.shape[0]
+    copies = [
+        pltpu.make_async_copy(piece_ref, slots_hbm.at[slot, pl.ds(0, blocks)], sent.at[slot])
+        for slot in range(slots)
+    ]
+    for copy in copies:
+        copy.start()
     basis = jnp.concatenate([basis_ref[0], residual, basis_ref[1]], axis=0)
-    gram = exact_dot(basis, basis, NT)
-    early = exact_dot(jnp.concatenate([images_ref[0], images_ref[1]], axis=0), basis, NT)
+    rows = jnp.concatenate([basis, images_ref[0], images_ref[1]], axis=0)
+    products = exact_dot(rows, basis, NT)
+    gram = products[: 3 * members]
+    early = products[3 * members :]
     extra = [
         gram[:members],
         gram[members : 2 * members],
@@ -118,8 +128,18 @@
         early[members:],
     ]
     for index, part in enumerate(pack_rows(extra)):
-        for slot in range(slots_ref.shape[0]):
-            slots_ref[slot, blocks + index] = part
+        extra_ref[index] = part
+    extras = extra_ref.shape[0]
+    more = [
+        pltpu.make_async_copy(
+            extra_ref, slots_hbm.at[slot, pl.ds(blocks, extras)], sent.at[slots + slot]
+        )
+        for slot in range(slots)
+    ]
+    for copy in more:
+        copy.start()
+    for copy in copies + more:
+        copy.wait()
 
 
 def line_kernel(first_ref, second_ref, third_ref, fourth_ref, line_ref):
@@ -212,7 +232,9 @@
     basis_ref,
     residual_ref,
     image_ref,
-    slots_ref,
+    slots_hbm,
+    rows_ref,
+    sent,
 ):
     blocks = image_ref.shape[1] // LANES
     for index in range(blocks):
@@ -221,7 +243,16 @@
     basis = jnp.concatenate([basis_ref[0], residual_ref[...], basis_ref[1]], axis=0)
     late = exact_dot(image_ref[...], basis, NT)
     packed = jnp.concatenate([late[row : row + 1] for row in range(late.shape[0])], axis=1)
-    slots_ref[...] = jnp.broadcast_to(packed[None], slots_ref.shape)
+    rows_ref[...] = jnp.broadcast_to(packed[None], rows_ref.shape)
+    some = rows_ref.shape[0]
+    copies = [
+        pltpu.make_async_copy(rows_ref, slots_hbm.at[pl.ds(part * some, some)], sent.at[part])
+        for part in range(slots_hbm.shape[0] // some)
+    ]
+    for copy in copies:
+        copy.start()
+    for copy in copies:
+        copy.wait()
 
 
 def projected_kernel(received_ref, inverse_ref, early_ref, projected_ref):
@@ -369,8 +400,19 @@
     )(count, rows, cols, tiles, own, other)
 
 
-def join_kernel(own_ref, other_ref, out_ref):
-    out_ref[...] = own_ref[...] + other_ref[...]
+def join_kernel(own_ref, other_ref, out_hbm, total_ref, sent):
+    parts = sent.shape[0]
+    size = own_ref.shape[0] // parts
+    copies = []
+    for part in range(parts):
+        place = slice(part * size, (part + 1) * size)
+        total_ref[place] = own_ref[place] + other_ref[place]
+        where = pl.ds(part * size, size)
+        copy = pltpu.make_async_copy(total_ref.at[where], out_hbm.at[where], sent.at[part])
+        copy.start()
+        copies.append(copy)
+    for copy in copies:
+        copy.wait()
 
 
 def exchange(slots, axes, groups=None):
@@ -428,8 +470,21 @@
     )(vectors, previous, hvectors, hprevious)
     sums = exchange(sums, everyone)
     sums, basis, images = lax.optimization_barrier((sums, basis, images))
-    residual, slots = call(
-        residual_kernel, [(members, piece), (chips, blocks + 2, members, LANES)], "residual"
+    residual, slots = pl.pallas_call(
+        residual_kernel,
+        out_shape=[
+            jax.ShapeDtypeStruct((members, piece), f32),
+            jax.ShapeDtypeStruct((chips, blocks + 2, members, LANES), f32),
+        ],
+        in_specs=[vmem_spec] * 3,
+        out_specs=[vmem_spec, hbm_spec],
+        scratch_shapes=[
+            pltpu.VMEM((blocks, members, LANES), f32),
+            pltpu.VMEM((2, members, LANES), f32),
+            pltpu.SemaphoreType.DMA((2 * chips,)),
+        ],
+        compiler_params=params,
+        name="residual",
     )(sums, basis, images)
     pieces = [residual] + [shift_lines(residual, shift) for shift in range(1, lines)]
     (line,) = call(line_kernel, [(lines, blocks, members, LANES)], "line")(*pieces)
@@ -471,20 +526,36 @@
     col_received, own_totals, other_totals = lax.optimization_barrier(
         (col_received, own_totals, other_totals)
     )
+    outs = call(halves_kernel, [(blocks + 2, members, LANES)] * lines, "halves")(
+        col_own, col_received
+    )
+    other_totals, *outs = lax.optimization_barrier((swap(other_totals, "col", 1), *outs))
     (totals,) = pl.pallas_call(
         join_kernel,
         out_shape=[jax.ShapeDtypeStruct(own_totals.shape, f32)],
+        in_specs=[vmem_spec] * 2,
+        out_specs=[hbm_spec],
+        scratch_shapes=[pltpu.VMEM(own_totals.shape, f32), pltpu.SemaphoreType.DMA((4,))],
         compiler_params=pltpu.CompilerParams(vmem_limit_bytes=TILE_VMEM_BYTES),
         name="join",
-    )(own_totals, swap(other_totals, "col", 1))
+    )(own_totals, other_totals)
     col_parts = exchange(totals.reshape(chips, blocks, members, LANES), "col", core_groups)
-    outs = call(halves_kernel, [(blocks + 2, members, LANES)] * lines, "halves")(
-        col_own, col_received
-    )
     row_parts = [outs[0]] + [shift_lines(outs[shift], shift) for shift in range(1, lines)]
     col_parts, *row_parts = lax.optimization_barrier((col_parts, *row_parts))
-    image, slots = call(
-        image_kernel, [(members, piece), (n_row * n_col, 1, members * order)], "image"
+    image, slots = pl.pallas_call(
+        image_kernel,
+        out_shape=[
+            jax.ShapeDtypeStruct((members, piece), f32),
+            jax.ShapeDtypeStruct((n_row * n_col, 1, members * order), f32),
+        ],
+        in_specs=[vmem_spec] * 7,
+        out_specs=[vmem_spec, hbm_spec],
+        scratch_shapes=[
+            pltpu.VMEM((n_col, 1, members * order), f32),
+            pltpu.SemaphoreType.DMA((n_row,)),
+        ],
+        compiler_params=params,
+        name="image",
     )(col_parts, *row_parts, basis, residual)
     late = exchange(slots, everyone)
     image, *row_parts = lax.optimization_barrier((image, *row_parts))

time: 96.7 us -> 96.6 us (level)
  waiting for transfers between devices: 30.8 us -> 28.9 us
  Pallas kernels: 20.8 us -> 22.6 us
    ppermute x4, waiting for transfers between devices: 9.73 us -> 7.8 us  [swap(): lax.ppermute(array, axis, [(i, i ^ distance) for i in range(lax.axis_size...]
    pallas_call x2, Pallas kernels: 7.31 us -> 9.21 us  [tile_call(): pl.pallas_call(functools.partial(tile_kernel, forward=forward), out_shape...]
  transfers between devices with their start and end apart: 14 -> 14, of which waited for: 12 -> 10; matrix products, arithmetic and copies ran while one was open for 0% -> 0% of each run, Pallas kernels for 15% -> 17%
where the time goes in v10:
time: 96.6 us; the launch traced here: 95.9 us
  starting transfers between devices  38.3 us (40%)
  waiting for transfers between devices  28.9 us (30%)
  Pallas kernels  22.6 us (23%)
  local copies, waits for them, and re-layouts  4.71 us (5%)
  between operations  1.42 us (1%)
    all_to_all x4, starting transfers between devices, exchange(): lax.all_to_all(slots, axes, 0, 0, axis_index_groups=groups, tiled=True)  25.7 us
    all_to_all x4, waiting for transfers between devices, exchange(): lax.all_to_all(slots, axes, 0, 0, axis_index_groups=groups, tiled=True)  16.3 us
    pallas_call x2, Pallas kernels, tile_call(): pl.pallas_call(functools.partial(tile_kernel, forward=forward), out_shape...  9.21 us
    ppermute x4, waiting for transfers between devices, swap(): lax.ppermute(array, axis, [(i, i ^ distance) for i in range(lax.axis_size...  7.8 us
    ppermute x6, starting transfers between devices, shift_lines(): lax.ppermute(array, 'row', [(i, (i + 2 * shift) % size) for i in range(si...  6.72 us
    ppermute x4, starting transfers between devices, swap(): lax.ppermute(array, axis, [(i, i ^ distance) for i in range(lax.axis_size...  5.88 us
    ppermute x6, waiting for transfers between devices, shift_lines(): lax.ppermute(array, 'row', [(i, (i + 2 * shift) % size) for i in range(si...  4.78 us
    unnamed x12, local copies, waits for them, and re-layouts  4.71 us
  transfers between devices with their start and end apart: 14, of which 10 were waited for; matrix products, arithmetic and copies ran while one was open for 0% of the time, Pallas kernels for 17%

profile of v10, /device:TPU:1, one launch (start us, length us, event | category | flops | bytes accessed | tf_op | source)
XLA Modules:
  0.0 95.9 jit_solution(2413601350620630496)
XLA Ops:
  0.6 1.6 %stage.1 = f32[128,128]{1,0:T(8,128)} custom-call(f32[16,1024]{1,0:T(8,128)} %vectors_hbm.3, f32[16,1024]{1,0:T(8,128)} %hvectors_hbm.3), custom_call_target="tpu_custom_call" | custom-call | tf_op jit(solution)/shard_map/stage/pallas_call | solution.py:450
  2.3 11.5 %all-to-all-start = ((f32[128,1,128]{2,1,0:T(1,128)}), f32[128,1,128]{2,1,0:T(1,128)S(1)}, u32[]{:S(2)}, u32[]{:S(2)}) async-start(f32[128,1,128]{2,1,0:T(1,128)} %bitcast.9), calls=%async_computation | async-start | bytes 131072 | tf_op jit(solution)/shard_map/all_to_all | solution.py:419
  13.8 0.0 copy-start
  13.8 0.8 copy-done
  14.6 0.0 copy-start.1
  14.6 0.8 copy-done.1
  15.4 0.0 copy-start.2
  15.5 0.8 copy-done.2
  16.3 0.0 copy-start.3
  16.3 0.8 copy-done.3
  17.1 0.3 prepare.1
  17.5 5.8 %all-to-all-done = f32[128,1,128]{2,1,0:T(1,128)S(1)} async-done(((f32[128,1,128]{2,1,0:T(1,128)}), f32[128,1,128]{2,1,0:T(1,128)S(1)}, u32[]{:S(2)}, u32[]{:S(2)}) %all-to-all-start) | async-done | bytes 65568 | tf_op jit(solution)/shard_map/all_to_all | solution.py:419
  23.3 1.4 %residual.1 = (f32[16,1024]{1,0:T(8,128)S(1)}, f32[8,10,16,128]{3,2,1,0:T(8,128)}) custom-call(f32[128,128]{1,0:T(8,128)S(1)} %bitcast.6, f32[2,16,1024]{2,1,0:T(8,128)S(1)} %get-tuple-element.55.basis_ref, f32[2,16,1024]{2,1,0:T(8,128)S(1)} %get-tuple-element.56.images_ref), custom_call_target="tpu_custom_call" | custom-call | tf_op jit(solution)/shard_map/residual/pallas_call | solution.py:473
  24.7 3.6 %all-to-all-start.1 = ((f32[8,10,16,128]{3,2,1,0:T(8,128)}), f32[8,10,16,128]{3,2,1,0:T(8,128)S(1)}, u32[]{:S(2)}, u32[]{:S(2)}) async-start(f32[8,10,16,128]{3,2,1,0:T(8,128)} %get-tuple-element.57), calls=%async_computation.1 | async-start | bytes 1310720 | tf_op jit(solution)/shard_map/all_to_all | solution.py:419
  28.3 0.3 collective-permute-start
  28.5 1.3 %collective-permute-start.1 = (f32[16,1024]{1,0:T(8,128)S(1)}, f32[16,1024]{1,0:T(8,128)S(1)}, u32[]{:S(2)}, u32[]{:S(2)}) collective-permute-start(f32[16,1024]{1,0:T(8,128)S(1)} %get-tuple-element.91.first_ref.residual_ref), channel_id=1, source_target_pairs={{0,64},{16,80},{32,96},{48,112},{64,0},{80,16},{96,32},{112,48},{1... | collective-permute-start | bytes 196616 | tf_op jit(solution)/shard_map/ppermute | solution.py:428
  29.8 1.8 %collective-permute-start.2 = (f32[16,1024]{1,0:T(8,128)S(1)}, f32[16,1024]{1,0:T(8,128)S(1)}, u32[]{:S(2)}, u32[]{:S(2)}) collective-permute-start(f32[16,1024]{1,0:T(8,128)S(1)} %get-tuple-element.91.first_ref.residual_ref), channel_id=1, source_target_pairs={{0,96},{16,112},{32,0},{48,16},{64,32},{80,48},{96,64},{112,80},{1... | collective-permute-start | bytes 196616 | tf_op jit(solution)/shard_map/ppermute | solution.py:428
  31.6 0.0 copy-start.4
  31.6 0.7 copy-done.4
  32.3 0.0 copy-start.5
  32.3 0.7 copy-done.5
  33.0 0.0 collective-permute-done.second_ref
  33.0 1.0 %collective-permute-done.1.third_ref = f32[16,1024]{1,0:T(8,128)S(1)} collective-permute-done((f32[16,1024]{1,0:T(8,128)S(1)}, f32[16,1024]{1,0:T(8,128)S(1)}, u32[]{:S(2)}, u32[]{:S(2)}) %collective-permute-start.1) | collective-permute-done | bytes 65568 | tf_op jit(solution)/shard_map/ppermute | solution.py:428
  34.0 0.2 collective-permute-done.2.fourth_ref
  34.3 3.5 %all-to-all-done.1.own_ref = f32[8,10,16,128]{3,2,1,0:T(8,128)S(1)} async-done(((f32[8,10,16,128]{3,2,1,0:T(8,128)}), f32[8,10,16,128]{3,2,1,0:T(8,128)S(1)}, u32[]{:S(2)}, u32[]{:S(2)}) %all-to-all-start.1) | async-done | bytes 655392 | tf_op jit(solution)/shard_map/all_to_all | solution.py:419
  37.8 2.0 %collective-permute-start.3 = (f32[8,10,16,128]{3,2,1,0:T(8,128)S(1)}, f32[8,10,16,128]{3,2,1,0:T(8,128)S(1)}, u32[]{:S(2)}, u32[]{:S(2)}) collective-permute-start(f32[8,10,16,128]{3,2,1,0:T(8,128)S(1)} %all-to-all-done.1.own_ref), channel_id=1, source_target_pairs={{0,1},{1,0},{2,3},{3,2},{4,5},{5,4},{6,7},{7,6},{8,9},{9,8},{10,11... | collective-permute-start | bytes 1966088 | tf_op jit(solution)/shard_map/ppermute | solution.py:423
  39.8 1.1 %collective-permute-start.4 = (f32[4,8,16,128]{3,2,1,0:T(8,128)S(1)}, f32[4,8,16,128]{3,2,1,0:T(8,128)S(1)}, u32[]{:S(2)}, u32[]{:S(2)}) collective-permute-start(f32[4,8,16,128]{3,2,1,0:T(8,128)S(1)} %line.1.own_ref), channel_id=1, source_target_pairs={{0,16},{16,0},{32,48},{48,32},{64,80},{80,64},{96,112},{112,96},{1... | collective-permute-start | bytes 786440 | tf_op jit(solution)/shard_map/ppermute | solution.py:423
  41.5 0.0 collective-permute-done.3.other_ref
  41.5 3.8 %backward_tiles.1 = (f32[34,16,128]{2,1,0:T(8,128)S(1)}, f32[34,16,128]{2,1,0:T(8,128)S(1)}) custom-call(s32[1,1]{1,0:T(1,128)S(6)} %copy.12.count_ref, s32[1,1,384]{2,1,0:T(1,128)S(1)} %get-tuple-element.63.rows_hbm, s32[1,1,384]{2,1,0:T(1,128)S(1)} %get-tuple-element.64.cols_hbm, bf16[384,128,128]{2,1,0:T(8,128)(2,1)} %bitcast.7, ...), custom_call_target="tpu_custom_call" | custom-call | tf_op jit(solution)/shard_map/backward_tiles/pallas_call | solution.py:384
  45.4 3.9 %collective-permute-done.4.other_ref = f32[4,8,16,128]{3,2,1,0:T(8,128)S(1)} collective-permute-done((f32[4,8,16,128]{3,2,1,0:T(8,128)S(1)}, f32[4,8,16,128]{3,2,1,0:T(8,128)S(1)}, u32[]{:S(2)}, u32[]{:S(2)}) %collective-permute-start.4) | collective-permute-done | bytes 262176 | tf_op jit(solution)/shard_map/ppermute | solution.py:423
  49.2 1.1 %collective-permute-start.5 = (f32[34,16,128]{2,1,0:T(8,128)S(1)}, f32[34,16,128]{2,1,0:T(8,128)S(1)}, u32[]{:S(2)}, u32[]{:S(2)}) collective-permute-start(f32[34,16,128]{2,1,0:T(8,128)S(1)} %get-tuple-element.69), channel_id=1, source_target_pairs={{0,16},{16,0},{32,48},{48,32},{64,80},{80,64},{96,112},{112,96},{1... | collective-permute-start | bytes 835592 | tf_op jit(solution)/shard_map/ppermute | solution.py:423
  50.3 5.4 %forward_tiles.1 = (f32[64,16,128]{2,1,0:T(8,128)S(1)}, f32[64,16,128]{2,1,0:T(8,128)S(1)}) custom-call(s32[1,1]{1,0:T(1,128)S(6)} %copy.12.count_ref, s32[1,1,384]{2,1,0:T(1,128)S(1)} %get-tuple-element.63.rows_hbm, s32[1,1,384]{2,1,0:T(1,128)S(1)} %get-tuple-element.64.cols_hbm, bf16[384,128,128]{2,1,0:T(8,128)(2,1)} %bitcast.8, ...), custom_call_target="tpu_custom_call" | custom-call | tf_op jit(solution)/shard_map/forward_tiles/pallas_call | solution.py:384
  55.7 2.4 %collective-permute-done.5.received_ref = f32[34,16,128]{2,1,0:T(8,128)S(1)} collective-permute-done((f32[34,16,128]{2,1,0:T(8,128)S(1)}, f32[34,16,128]{2,1,0:T(8,128)S(1)}, u32[]{:S(2)}, u32[]{:S(2)}) %collective-permute-start.5) | collective-permute-done | bytes 278560 | tf_op jit(solution)/shard_map/ppermute | solution.py:423
  58.1 1.7 %collective-permute-start.6 = (f32[64,16,128]{2,1,0:T(8,128)S(1)}, f32[64,16,128]{2,1,0:T(8,128)S(1)}, u32[]{:S(2)}, u32[]{:S(2)}) collective-permute-start(f32[64,16,128]{2,1,0:T(8,128)S(1)} %get-tuple-element.74), channel_id=1, source_target_pairs={{0,1},{1,0},{2,3},{3,2},{4,5},{5,4},{6,7},{7,6},{8,9},{9,8},{10,11... | collective-permute-start | bytes 1572872 | tf_op jit(solution)/shard_map/ppermute | solution.py:423
  59.9 1.5 %collective-permute-done.6.other_ref = f32[64,16,128]{2,1,0:T(8,128)S(1)} collective-permute-done((f32[64,16,128]{2,1,0:T(8,128)S(1)}, f32[64,16,128]{2,1,0:T(8,128)S(1)}, u32[]{:S(2)}, u32[]{:S(2)}) %collective-permute-start.6) | collective-permute-done | bytes 524320 | tf_op jit(solution)/shard_map/ppermute | solution.py:423
  61.4 0.9 join.1
  62.2 3.5 %all-to-all-start.2 = ((f32[8,8,16,128]{3,2,1,0:T(8,128)}), f32[8,8,16,128]{3,2,1,0:T(8,128)S(1)}, u32[]{:S(2)}, u32[]{:S(2)}) async-start(f32[8,8,16,128]{3,2,1,0:T(8,128)} %bitcast.4), calls=%async_computation.2 | async-start | bytes 1048576 | tf_op jit(solution)/shard_map/all_to_all | solution.py:419
  65.7 0.3 collective-permute-start.7
  66.0 1.5 %collective-permute-start.8 = (f32[10,16,128]{2,1,0:T(8,128)S(1)}, f32[10,16,128]{2,1,0:T(8,128)S(1)}, u32[]{:S(2)}, u32[]{:S(2)}) collective-permute-start(f32[10,16,128]{2,1,0:T(8,128)S(1)} %get-tuple-element.84), channel_id=1, source_target_pairs={{0,64},{16,80},{32,96},{48,112},{64,0},{80,16},{96,32},{112,48},{1... | collective-permute-start | bytes 245768 | tf_op jit(solution)/shard_map/ppermute | solution.py:428
  67.5 1.6 %collective-permute-start.9 = (f32[10,16,128]{2,1,0:T(8,128)S(1)}, f32[10,16,128]{2,1,0:T(8,128)S(1)}, u32[]{:S(2)}, u32[]{:S(2)}) collective-permute-start(f32[10,16,128]{2,1,0:T(8,128)S(1)} %get-tuple-element.85), channel_id=1, source_target_pairs={{0,96},{16,112},{32,0},{48,16},{64,32},{80,48},{96,64},{112,80},{1... | collective-permute-start | bytes 245768 | tf_op jit(solution)/shard_map/ppermute | solution.py:428
  69.1 3.5 %collective-permute-done.7.second_ref = f32[10,16,128]{2,1,0:T(8,128)S(1)} collective-permute-done((f32[10,16,128]{2,1,0:T(8,128)S(1)}, f32[10,16,128]{2,1,0:T(8,128)S(1)}, u32[]{:S(2)}, u32[]{:S(2)}) %collective-permute-start.7) | collective-permute-done | bytes 81952 | tf_op jit(solution)/shard_map/ppermute | solution.py:428
  72.6 0.0 collective-permute-done.8.third_ref
  72.6 0.0 collective-permute-done.9.fourth_ref
  72.7 1.4 %all-to-all-done.2.col_parts_ref = f32[8,8,16,128]{3,2,1,0:T(8,128)S(1)} async-done(((f32[8,8,16,128]{3,2,1,0:T(8,128)}), f32[8,8,16,128]{3,2,1,0:T(8,128)S(1)}, u32[]{:S(2)}, u32[]{:S(2)}) %all-to-all-start.2) | async-done | bytes 524320 | tf_op jit(solution)/shard_map/all_to_all | solution.py:419
  74.0 1.2 %image.1 = (f32[16,1024]{1,0:T(8,128)S(1)}, f32[128,1,768]{2,1,0:T(1,128)}) custom-call(f32[8,8,16,128]{3,2,1,0:T(8,128)S(1)} %all-to-all-done.2.col_parts_ref, f32[10,16,128]{2,1,0:T(8,128)S(1)} %get-tuple-element.93.first_ref, f32[10,16,128]{2,1,0:T(8,128)S(1)} %collective-permute-done.7.second_ref, f32[10,16,128]{2,1,0:T(8,128)S(1)} %collective-permute-done.8.third_ref, ...), custom_call_target="tpu_custom_call" | custom-call | tf_op jit(solution)/shard_map/image/pallas_call | solution.py:545
  75.3 7.2 %all-to-all-start.3 = ((f32[128,1,768]{2,1,0:T(1,128)}), f32[128,1,768]{2,1,0:T(1,128)S(1)}, u32[]{:S(2)}, u32[]{:S(2)}) async-start(f32[128,1,768]{2,1,0:T(1,128)} %get-tuple-element.99), calls=%async_computation.3 | async-start | bytes 786432 | tf_op jit(solution)/shard_map/all_to_all | solution.py:419
  82.4 4.5 %factor.1 = (f32[48,48]{1,0:T(8,128)S(1)}, f32[32,48]{1,0:T(8,128)S(1)}) custom-call(f32[10,16,128]{2,1,0:T(8,128)S(1)} %get-tuple-element.93.first_ref, f32[10,16,128]{2,1,0:T(8,128)S(1)} %collective-permute-done.7.second_ref, f32[10,16,128]{2,1,0:T(8,128)S(1)} %collective-permute-done.8.third_ref, f32[10,16,128]{2,1,0:T(8,128)S(1)} %collective-permute-done.9.fourth_ref), custom_call_target="tpu_custom_call" | custom-call | tf_op jit(solution)/shard_map/factor/pallas_call | solution.py:562
  86.9 1.0 %orthonormal.1 = f32[48,1024]{1,0:T(8,128)} custom-call(f32[48,48]{1,0:T(8,128)S(1)} %get-tuple-element.97.inverse_ref, f32[2,16,1024]{2,1,0:T(8,128)S(1)} %get-tuple-element.55.basis_ref, f32[16,1024]{1,0:T(8,128)S(1)} %get-tuple-element.91.first_ref.residual_ref), custom_call_target="tpu_custom_call" | custom-call | tf_op jit(solution)/shard_map/orthonormal/pallas_call | solution.py:563
  87.9 1.0 %orthonormal_image.1 = f32[48,1024]{1,0:T(8,128)} custom-call(f32[48,48]{1,0:T(8,128)S(1)} %get-tuple-element.97.inverse_ref, f32[2,16,1024]{2,1,0:T(8,128)S(1)} %get-tuple-element.56.images_ref, f32[16,1024]{1,0:T(8,128)S(1)} %get-tuple-element.98.image_ref), custom_call_target="tpu_custom_call" | custom-call | tf_op jit(solution)/shard_map/orthonormal_image/pallas_call | solution.py:566
  88.9 5.6 %all-to-all-done.3.received_ref = f32[128,1,768]{2,1,0:T(1,128)S(1)} async-done(((f32[128,1,768]{2,1,0:T(1,128)}), f32[128,1,768]{2,1,0:T(1,128)S(1)}, u32[]{:S(2)}, u32[]{:S(2)}) %all-to-all-start.3) | async-done | bytes 393248 | tf_op jit(solution)/shard_map/all_to_all | solution.py:419
  94.5 1.4 %projected.1 = f32[48,48]{1,0:T(8,128)} custom-call(f32[128,1,768]{2,1,0:T(1,128)S(1)} %all-to-all-done.3.received_ref, f32[48,48]{1,0:T(8,128)S(1)} %get-tuple-element.97.inverse_ref, f32[32,48]{1,0:T(8,128)S(1)} %get-tuple-element.100.early_ref), custom_call_target="tpu_custom_call" | custom-call | tf_op jit(solution)/shard_map/projected/pallas_call | solution.py:571
  (3 shorter events, 0.1 us)
Async XLA Ops:
  2.3 21.0 %all-to-all-start = ((f32[128,1,128]{2,1,0:T(1,128)}), f32[128,1,128]{2,1,0:T(1,128)S(1)}, u32[]{:S(2)}, u32[]{:S(2)}) async-start(f32[128,1,128]{2,1,0:T(1,128)} %bitcast.9), calls=%async_computation | async-start | bytes 131072 | tf_op jit(solution)/shard_map/all_to_all | solution.py:419
  13.8 0.8 copy-start
  14.6 0.8 copy-start.1
  15.4 0.8 copy-start.2
  16.3 0.8 copy-start.3
  24.7 13.1 %all-to-all-start.1 = ((f32[8,10,16,128]{3,2,1,0:T(8,128)}), f32[8,10,16,128]{3,2,1,0:T(8,128)S(1)}, u32[]{:S(2)}, u32[]{:S(2)}) async-start(f32[8,10,16,128]{3,2,1,0:T(8,128)} %get-tuple-element.57), calls=%async_computation.1 | async-start | bytes 1310720 | tf_op jit(solution)/shard_map/all_to_all | solution.py:419
  28.3 4.8 %collective-permute-start = (f32[16,1024]{1,0:T(8,128)S(1)}, f32[16,1024]{1,0:T(8,128)S(1)}, u32[]{:S(2)}, u32[]{:S(2)}) collective-permute-start(f32[16,1024]{1,0:T(8,128)S(1)} %get-tuple-element.91.first_ref.residual_ref), channel_id=1, source_target_pairs={{0,32},{16,48},{32,64},{48,80},{64,96},{80,112},{96,0},{112,16},{1... | collective-permute-start | bytes 196616 | tf_op jit(solution)/shard_map/ppermute | solution.py:428
  28.5 5.5 %collective-permute-start.1 = (f32[16,1024]{1,0:T(8,128)S(1)}, f32[16,1024]{1,0:T(8,128)S(1)}, u32[]{:S(2)}, u32[]{:S(2)}) collective-permute-start(f32[16,1024]{1,0:T(8,128)S(1)} %get-tuple-element.91.first_ref.residual_ref), channel_id=1, source_target_pairs={{0,64},{16,80},{32,96},{48,112},{64,0},{80,16},{96,32},{112,48},{1... | collective-permute-start | bytes 196616 | tf_op jit(solution)/shard_map/ppermute | solution.py:428
  29.8 4.4 %collective-permute-start.2 = (f32[16,1024]{1,0:T(8,128)S(1)}, f32[16,1024]{1,0:T(8,128)S(1)}, u32[]{:S(2)}, u32[]{:S(2)}) collective-permute-start(f32[16,1024]{1,0:T(8,128)S(1)} %get-tuple-element.91.first_ref.residual_ref), channel_id=1, source_target_pairs={{0,96},{16,112},{32,0},{48,16},{64,32},{80,48},{96,64},{112,80},{1... | collective-permute-start | bytes 196616 | tf_op jit(solution)/shard_map/ppermute | solution.py:428
  31.6 0.7 copy-start.4
  32.3 0.7 copy-start.5
  37.8 3.8 %collective-permute-start.3 = (f32[8,10,16,128]{3,2,1,0:T(8,128)S(1)}, f32[8,10,16,128]{3,2,1,0:T(8,128)S(1)}, u32[]{:S(2)}, u32[]{:S(2)}) collective-permute-start(f32[8,10,16,128]{3,2,1,0:T(8,128)S(1)} %all-to-all-done.1.own_ref), channel_id=1, source_target_pairs={{0,1},{1,0},{2,3},{3,2},{4,5},{5,4},{6,7},{7,6},{8,9},{9,8},{10,11... | collective-permute-start | bytes 1966088 | tf_op jit(solution)/shard_map/ppermute | solution.py:423
  39.8 9.4 %collective-permute-start.4 = (f32[4,8,16,128]{3,2,1,0:T(8,128)S(1)}, f32[4,8,16,128]{3,2,1,0:T(8,128)S(1)}, u32[]{:S(2)}, u32[]{:S(2)}) collective-permute-start(f32[4,8,16,128]{3,2,1,0:T(8,128)S(1)} %line.1.own_ref), channel_id=1, source_target_pairs={{0,16},{16,0},{32,48},{48,32},{64,80},{80,64},{96,112},{112,96},{1... | collective-permute-start | bytes 786440 | tf_op jit(solution)/shard_map/ppermute | solution.py:423
  49.2 8.9 %collective-permute-start.5 = (f32[34,16,128]{2,1,0:T(8,128)S(1)}, f32[34,16,128]{2,1,0:T(8,128)S(1)}, u32[]{:S(2)}, u32[]{:S(2)}) collective-permute-start(f32[34,16,128]{2,1,0:T(8,128)S(1)} %get-tuple-element.69), channel_id=1, source_target_pairs={{0,16},{16,0},{32,48},{48,32},{64,80},{80,64},{96,112},{112,96},{1... | collective-permute-start | bytes 835592 | tf_op jit(solution)/shard_map/ppermute | solution.py:423
  58.1 3.2 %collective-permute-start.6 = (f32[64,16,128]{2,1,0:T(8,128)S(1)}, f32[64,16,128]{2,1,0:T(8,128)S(1)}, u32[]{:S(2)}, u32[]{:S(2)}) collective-permute-start(f32[64,16,128]{2,1,0:T(8,128)S(1)} %get-tuple-element.74), channel_id=1, source_target_pairs={{0,1},{1,0},{2,3},{3,2},{4,5},{5,4},{6,7},{7,6},{8,9},{9,8},{10,11... | collective-permute-start | bytes 1572872 | tf_op jit(solution)/shard_map/ppermute | solution.py:423
  62.2 11.8 %all-to-all-start.2 = ((f32[8,8,16,128]{3,2,1,0:T(8,128)}), f32[8,8,16,128]{3,2,1,0:T(8,128)S(1)}, u32[]{:S(2)}, u32[]{:S(2)}) async-start(f32[8,8,16,128]{3,2,1,0:T(8,128)} %bitcast.4), calls=%async_computation.2 | async-start | bytes 1048576 | tf_op jit(solution)/shard_map/all_to_all | solution.py:419
  65.7 6.9 %collective-permute-start.7 = (f32[10,16,128]{2,1,0:T(8,128)S(1)}, f32[10,16,128]{2,1,0:T(8,128)S(1)}, u32[]{:S(2)}, u32[]{:S(2)}) collective-permute-start(f32[10,16,128]{2,1,0:T(8,128)S(1)} %get-tuple-element.83), channel_id=1, source_target_pairs={{0,32},{16,48},{32,64},{48,80},{64,96},{80,112},{96,0},{112,16},{1... | collective-permute-start | bytes 245768 | tf_op jit(solution)/shard_map/ppermute | solution.py:428
  66.0 6.6 %collective-permute-start.8 = (f32[10,16,128]{2,1,0:T(8,128)S(1)}, f32[10,16,128]{2,1,0:T(8,128)S(1)}, u32[]{:S(2)}, u32[]{:S(2)}) collective-permute-start(f32[10,16,128]{2,1,0:T(8,128)S(1)} %get-tuple-element.84), channel_id=1, source_target_pairs={{0,64},{16,80},{32,96},{48,112},{64,0},{80,16},{96,32},{112,48},{1... | collective-permute-start | bytes 245768 | tf_op jit(solution)/shard_map/ppermute | solution.py:428
  67.5 5.2 %collective-permute-start.9 = (f32[10,16,128]{2,1,0:T(8,128)S(1)}, f32[10,16,128]{2,1,0:T(8,128)S(1)}, u32[]{:S(2)}, u32[]{:S(2)}) collective-permute-start(f32[10,16,128]{2,1,0:T(8,128)S(1)} %get-tuple-element.85), channel_id=1, source_target_pairs={{0,96},{16,112},{32,0},{48,16},{64,32},{80,48},{96,64},{112,80},{1... | collective-permute-start | bytes 245768 | tf_op jit(solution)/shard_map/ppermute | solution.py:428
  75.3 19.3 %all-to-all-start.3 = ((f32[128,1,768]{2,1,0:T(1,128)}), f32[128,1,768]{2,1,0:T(1,128)S(1)}, u32[]{:S(2)}, u32[]{:S(2)}) async-start(f32[128,1,768]{2,1,0:T(1,128)} %get-tuple-element.99), calls=%async_computation.3 | async-start | bytes 786432 | tf_op jit(solution)/shard_map/all_to_all | solution.py:419

commit v11 on v8

--- a/solution.py
+++ b/solution.py
@@ -108,8 +108,10 @@
         for slot in range(slots_ref.shape[0]):
             slots_ref[slot, index] = block(residual, index)
     basis = jnp.concatenate([basis_ref[0], residual, basis_ref[1]], axis=0)
-    gram = exact_dot(basis, basis, NT)
-    early = exact_dot(jnp.concatenate([images_ref[0], images_ref[1]], axis=0), basis, NT)
+    rows = jnp.concatenate([basis, images_ref[0], images_ref[1]], axis=0)
+    products = exact_dot(rows, basis, NT)
+    gram = products[: 3 * members]
+    early = products[3 * members :]
     extra = [
         gram[:members],
         gram[members : 2 * members],
@@ -471,16 +473,17 @@
     col_received, own_totals, other_totals = lax.optimization_barrier(
         (col_received, own_totals, other_totals)
     )
+    outs = call(halves_kernel, [(blocks + 2, members, LANES)] * lines, "halves")(
+        col_own, col_received
+    )
+    other_totals, *outs = lax.optimization_barrier((swap(other_totals, "col", 1), *outs))
     (totals,) = pl.pallas_call(
         join_kernel,
         out_shape=[jax.ShapeDtypeStruct(own_totals.shape, f32)],
         compiler_params=pltpu.CompilerParams(vmem_limit_bytes=TILE_VMEM_BYTES),
         name="join",
-    )(own_totals, swap(other_totals, "col", 1))
+    )(own_totals, other_totals)
     col_parts = exchange(totals.reshape(chips, blocks, members, LANES), "col", core_groups)
-    outs = call(halves_kernel, [(blocks + 2, members, LANES)] * lines, "halves")(
-        col_own, col_received
-    )
     row_parts = [outs[0]] + [shift_lines(outs[shift], shift) for shift in range(1, lines)]
     col_parts, *row_parts = lax.optimization_barrier((col_parts, *row_parts))
     image, slots = call(

time: 96.7 us -> 97.8 us (1.011)
  waiting for transfers between devices: 30.8 us -> 28.9 us
  Pallas kernels: 20.8 us -> 22.6 us
    ppermute x4, waiting for transfers between devices: 9.73 us -> 7.81 us  [swap(): lax.ppermute(array, axis, [(i, i ^ distance) for i in range(lax.axis_size...]
    pallas_call x2, Pallas kernels: 7.31 us -> 9.2 us  [tile_call(): pl.pallas_call(functools.partial(tile_kernel, forward=forward), out_shape...]
  transfers between devices with their start and end apart: 14 -> 14, of which waited for: 12 -> 10; matrix products, arithmetic and copies ran while one was open for 0% -> 0% of each run, Pallas kernels for 15% -> 17%
where the time goes in v11:
time: 97.8 us; the launch traced here: 96.8 us
  starting transfers between devices  39.2 us (40%)
  waiting for transfers between devices  28.9 us (30%)
  Pallas kernels  22.6 us (23%)
  local copies, waits for them, and re-layouts  4.71 us (5%)
  between operations  1.4 us (1%)
    all_to_all x4, starting transfers between devices, exchange(): lax.all_to_all(slots, axes, 0, 0, axis_index_groups=groups, tiled=True)  26.6 us
    all_to_all x4, waiting for transfers between devices, exchange(): lax.all_to_all(slots, axes, 0, 0, axis_index_groups=groups, tiled=True)  16.3 us
    pallas_call x2, Pallas kernels, tile_call(): pl.pallas_call(functools.partial(tile_kernel, forward=forward), out_shape...  9.2 us
    ppermute x4, waiting for transfers between devices, swap(): lax.ppermute(array, axis, [(i, i ^ distance) for i in range(lax.axis_size...  7.81 us
    ppermute x6, starting transfers between devices, shift_lines(): lax.ppermute(array, 'row', [(i, (i + 2 * shift) % size) for i in range(si...  6.72 us
    ppermute x4, starting transfers between devices, swap(): lax.ppermute(array, axis, [(i, i ^ distance) for i in range(lax.axis_size...  5.87 us
    ppermute x6, waiting for transfers between devices, shift_lines(): lax.ppermute(array, 'row', [(i, (i + 2 * shift) % size) for i in range(si...  4.78 us
    unnamed x12, local copies, waits for them, and re-layouts  4.71 us
  transfers between devices with their start and end apart: 14, of which 10 were waited for; matrix products, arithmetic and copies ran while one was open for 0% of the time, Pallas kernels for 17%

profile of v11, /device:TPU:1, one launch (start us, length us, event | category | flops | bytes accessed | tf_op | source)
XLA Modules:
  0.0 96.8 jit_solution(7181473893667333804)
XLA Ops:
  0.6 1.6 %stage.1 = f32[128,128]{1,0:T(8,128)} custom-call(f32[16,1024]{1,0:T(8,128)} %vectors_hbm.3, f32[16,1024]{1,0:T(8,128)} %hvectors_hbm.3), custom_call_target="tpu_custom_call" | custom-call | tf_op jit(solution)/shard_map/stage/pallas_call | solution.py:410
  2.3 11.5 %all-to-all-start = ((f32[128,1,128]{2,1,0:T(1,128)}), f32[128,1,128]{2,1,0:T(1,128)S(1)}, u32[]{:S(2)}, u32[]{:S(2)}) async-start(f32[128,1,128]{2,1,0:T(1,128)} %bitcast.9), calls=%async_computation | async-start | bytes 131072 | tf_op jit(solution)/shard_map/all_to_all | solution.py:379
  13.8 0.0 copy-start
  13.8 0.8 copy-done
  14.6 0.0 copy-start.1
  14.6 0.8 copy-done.1
  15.4 0.0 copy-start.2
  15.5 0.8 copy-done.2
  16.3 0.0 copy-start.3
  16.3 0.8 copy-done.3
  17.1 0.3 prepare.1
  17.5 5.8 %all-to-all-done = f32[128,1,128]{2,1,0:T(1,128)S(1)} async-done(((f32[128,1,128]{2,1,0:T(1,128)}), f32[128,1,128]{2,1,0:T(1,128)S(1)}, u32[]{:S(2)}, u32[]{:S(2)}) %all-to-all-start) | async-done | bytes 65568 | tf_op jit(solution)/shard_map/all_to_all | solution.py:379
  23.3 1.5 %residual.1 = (f32[16,1024]{1,0:T(8,128)S(1)}, f32[8,10,16,128]{3,2,1,0:T(8,128)}) custom-call(f32[128,128]{1,0:T(8,128)S(1)} %bitcast.6, f32[2,16,1024]{2,1,0:T(8,128)S(1)} %get-tuple-element.55.basis_ref, f32[2,16,1024]{2,1,0:T(8,128)S(1)} %get-tuple-element.56.images_ref), custom_call_target="tpu_custom_call" | custom-call | tf_op jit(solution)/shard_map/residual/pallas_call | solution.py:433
  24.8 3.5 %all-to-all-start.1 = ((f32[8,10,16,128]{3,2,1,0:T(8,128)}), f32[8,10,16,128]{3,2,1,0:T(8,128)S(1)}, u32[]{:S(2)}, u32[]{:S(2)}) async-start(f32[8,10,16,128]{3,2,1,0:T(8,128)} %get-tuple-element.57), calls=%async_computation.1 | async-start | bytes 1310720 | tf_op jit(solution)/shard_map/all_to_all | solution.py:379
  28.3 0.3 collective-permute-start
  28.6 1.3 %collective-permute-start.1 = (f32[16,1024]{1,0:T(8,128)S(1)}, f32[16,1024]{1,0:T(8,128)S(1)}, u32[]{:S(2)}, u32[]{:S(2)}) collective-permute-start(f32[16,1024]{1,0:T(8,128)S(1)} %get-tuple-element.91.first_ref.residual_ref), channel_id=1, source_target_pairs={{0,64},{16,80},{32,96},{48,112},{64,0},{80,16},{96,32},{112,48},{1... | collective-permute-start | bytes 196616 | tf_op jit(solution)/shard_map/ppermute | solution.py:388
  29.9 1.8 %collective-permute-start.2 = (f32[16,1024]{1,0:T(8,128)S(1)}, f32[16,1024]{1,0:T(8,128)S(1)}, u32[]{:S(2)}, u32[]{:S(2)}) collective-permute-start(f32[16,1024]{1,0:T(8,128)S(1)} %get-tuple-element.91.first_ref.residual_ref), channel_id=1, source_target_pairs={{0,96},{16,112},{32,0},{48,16},{64,32},{80,48},{96,64},{112,80},{1... | collective-permute-start | bytes 196616 | tf_op jit(solution)/shard_map/ppermute | solution.py:388
  31.7 0.0 copy-start.4
  31.7 0.7 copy-done.4
  32.4 0.0 copy-start.5
  32.4 0.7 copy-done.5
  33.1 0.0 collective-permute-done.second_ref
  33.1 1.0 %collective-permute-done.1.third_ref = f32[16,1024]{1,0:T(8,128)S(1)} collective-permute-done((f32[16,1024]{1,0:T(8,128)S(1)}, f32[16,1024]{1,0:T(8,128)S(1)}, u32[]{:S(2)}, u32[]{:S(2)}) %collective-permute-start.1) | collective-permute-done | bytes 65568 | tf_op jit(solution)/shard_map/ppermute | solution.py:388
  34.1 0.2 collective-permute-done.2.fourth_ref
  34.3 3.5 %all-to-all-done.1.own_ref = f32[8,10,16,128]{3,2,1,0:T(8,128)S(1)} async-done(((f32[8,10,16,128]{3,2,1,0:T(8,128)}), f32[8,10,16,128]{3,2,1,0:T(8,128)S(1)}, u32[]{:S(2)}, u32[]{:S(2)}) %all-to-all-start.1) | async-done | bytes 655392 | tf_op jit(solution)/shard_map/all_to_all | solution.py:379
  37.8 2.0 %collective-permute-start.3 = (f32[8,10,16,128]{3,2,1,0:T(8,128)S(1)}, f32[8,10,16,128]{3,2,1,0:T(8,128)S(1)}, u32[]{:S(2)}, u32[]{:S(2)}) collective-permute-start(f32[8,10,16,128]{3,2,1,0:T(8,128)S(1)} %all-to-all-done.1.own_ref), channel_id=1, source_target_pairs={{0,1},{1,0},{2,3},{3,2},{4,5},{5,4},{6,7},{7,6},{8,9},{9,8},{10,11... | collective-permute-start | bytes 1966088 | tf_op jit(solution)/shard_map/ppermute | solution.py:383
  39.9 1.1 %collective-permute-start.4 = (f32[4,8,16,128]{3,2,1,0:T(8,128)S(1)}, f32[4,8,16,128]{3,2,1,0:T(8,128)S(1)}, u32[]{:S(2)}, u32[]{:S(2)}) collective-permute-start(f32[4,8,16,128]{3,2,1,0:T(8,128)S(1)} %line.1.own_ref), channel_id=1, source_target_pairs={{0,16},{16,0},{32,48},{48,32},{64,80},{80,64},{96,112},{112,96},{1... | collective-permute-start | bytes 786440 | tf_op jit(solution)/shard_map/ppermute | solution.py:383
  41.6 0.0 collective-permute-done.3.other_ref
  41.6 3.8 %backward_tiles.1 = (f32[34,16,128]{2,1,0:T(8,128)S(1)}, f32[34,16,128]{2,1,0:T(8,128)S(1)}) custom-call(s32[1,1]{1,0:T(1,128)S(6)} %copy.12.count_ref, s32[1,1,384]{2,1,0:T(1,128)S(1)} %get-tuple-element.63.rows_hbm, s32[1,1,384]{2,1,0:T(1,128)S(1)} %get-tuple-element.64.cols_hbm, bf16[384,128,128]{2,1,0:T(8,128)(2,1)} %bitcast.7, ...), custom_call_target="tpu_custom_call" | custom-call | tf_op jit(solution)/shard_map/backward_tiles/pallas_call | solution.py:355
  45.4 3.9 %collective-permute-done.4.other_ref = f32[4,8,16,128]{3,2,1,0:T(8,128)S(1)} collective-permute-done((f32[4,8,16,128]{3,2,1,0:T(8,128)S(1)}, f32[4,8,16,128]{3,2,1,0:T(8,128)S(1)}, u32[]{:S(2)}, u32[]{:S(2)}) %collective-permute-start.4) | collective-permute-done | bytes 262176 | tf_op jit(solution)/shard_map/ppermute | solution.py:383
  49.3 1.1 %collective-permute-start.5 = (f32[34,16,128]{2,1,0:T(8,128)S(1)}, f32[34,16,128]{2,1,0:T(8,128)S(1)}, u32[]{:S(2)}, u32[]{:S(2)}) collective-permute-start(f32[34,16,128]{2,1,0:T(8,128)S(1)} %get-tuple-element.69), channel_id=1, source_target_pairs={{0,16},{16,0},{32,48},{48,32},{64,80},{80,64},{96,112},{112,96},{1... | collective-permute-start | bytes 835592 | tf_op jit(solution)/shard_map/ppermute | solution.py:383
  50.4 5.4 %forward_tiles.1 = (f32[64,16,128]{2,1,0:T(8,128)S(1)}, f32[64,16,128]{2,1,0:T(8,128)S(1)}) custom-call(s32[1,1]{1,0:T(1,128)S(6)} %copy.12.count_ref, s32[1,1,384]{2,1,0:T(1,128)S(1)} %get-tuple-element.63.rows_hbm, s32[1,1,384]{2,1,0:T(1,128)S(1)} %get-tuple-element.64.cols_hbm, bf16[384,128,128]{2,1,0:T(8,128)(2,1)} %bitcast.8, ...), custom_call_target="tpu_custom_call" | custom-call | tf_op jit(solution)/shard_map/forward_tiles/pallas_call | solution.py:355
  55.8 2.4 %collective-permute-done.5.received_ref = f32[34,16,128]{2,1,0:T(8,128)S(1)} collective-permute-done((f32[34,16,128]{2,1,0:T(8,128)S(1)}, f32[34,16,128]{2,1,0:T(8,128)S(1)}, u32[]{:S(2)}, u32[]{:S(2)}) %collective-permute-start.5) | collective-permute-done | bytes 278560 | tf_op jit(solution)/shard_map/ppermute | solution.py:383
  58.2 1.7 %collective-permute-start.6 = (f32[64,16,128]{2,1,0:T(8,128)S(1)}, f32[64,16,128]{2,1,0:T(8,128)S(1)}, u32[]{:S(2)}, u32[]{:S(2)}) collective-permute-start(f32[64,16,128]{2,1,0:T(8,128)S(1)} %get-tuple-element.74), channel_id=1, source_target_pairs={{0,1},{1,0},{2,3},{3,2},{4,5},{5,4},{6,7},{7,6},{8,9},{9,8},{10,11... | collective-permute-start | bytes 1572872 | tf_op jit(solution)/shard_map/ppermute | solution.py:383
  59.9 1.5 %collective-permute-done.6.other_ref = f32[64,16,128]{2,1,0:T(8,128)S(1)} collective-permute-done((f32[64,16,128]{2,1,0:T(8,128)S(1)}, f32[64,16,128]{2,1,0:T(8,128)S(1)}, u32[]{:S(2)}, u32[]{:S(2)}) %collective-permute-start.6) | collective-permute-done | bytes 524320 | tf_op jit(solution)/shard_map/ppermute | solution.py:383
  61.4 0.9 join.1
  62.3 3.5 %all-to-all-start.2 = ((f32[8,8,16,128]{3,2,1,0:T(8,128)}), f32[8,8,16,128]{3,2,1,0:T(8,128)S(1)}, u32[]{:S(2)}, u32[]{:S(2)}) async-start(f32[8,8,16,128]{3,2,1,0:T(8,128)} %bitcast.4), calls=%async_computation.2 | async-start | bytes 1048576 | tf_op jit(solution)/shard_map/all_to_all | solution.py:379
  65.8 0.3 collective-permute-start.7
  66.0 1.5 %collective-permute-start.8 = (f32[10,16,128]{2,1,0:T(8,128)S(1)}, f32[10,16,128]{2,1,0:T(8,128)S(1)}, u32[]{:S(2)}, u32[]{:S(2)}) collective-permute-start(f32[10,16,128]{2,1,0:T(8,128)S(1)} %get-tuple-element.84), channel_id=1, source_target_pairs={{0,64},{16,80},{32,96},{48,112},{64,0},{80,16},{96,32},{112,48},{1... | collective-permute-start | bytes 245768 | tf_op jit(solution)/shard_map/ppermute | solution.py:388
  67.5 1.6 %collective-permute-start.9 = (f32[10,16,128]{2,1,0:T(8,128)S(1)}, f32[10,16,128]{2,1,0:T(8,128)S(1)}, u32[]{:S(2)}, u32[]{:S(2)}) collective-permute-start(f32[10,16,128]{2,1,0:T(8,128)S(1)} %get-tuple-element.85), channel_id=1, source_target_pairs={{0,96},{16,112},{32,0},{48,16},{64,32},{80,48},{96,64},{112,80},{1... | collective-permute-start | bytes 245768 | tf_op jit(solution)/shard_map/ppermute | solution.py:388
  69.1 3.5 %collective-permute-done.7.second_ref = f32[10,16,128]{2,1,0:T(8,128)S(1)} collective-permute-done((f32[10,16,128]{2,1,0:T(8,128)S(1)}, f32[10,16,128]{2,1,0:T(8,128)S(1)}, u32[]{:S(2)}, u32[]{:S(2)}) %collective-permute-start.7) | collective-permute-done | bytes 81952 | tf_op jit(solution)/shard_map/ppermute | solution.py:388
  72.7 0.0 collective-permute-done.8.third_ref
  72.7 0.0 collective-permute-done.9.fourth_ref
  72.7 1.4 %all-to-all-done.2.col_parts_ref = f32[8,8,16,128]{3,2,1,0:T(8,128)S(1)} async-done(((f32[8,8,16,128]{3,2,1,0:T(8,128)}), f32[8,8,16,128]{3,2,1,0:T(8,128)S(1)}, u32[]{:S(2)}, u32[]{:S(2)}) %all-to-all-start.2) | async-done | bytes 524320 | tf_op jit(solution)/shard_map/all_to_all | solution.py:379
  74.1 1.2 %image.1 = (f32[16,1024]{1,0:T(8,128)S(1)}, f32[128,1,768]{2,1,0:T(1,128)}) custom-call(f32[8,8,16,128]{3,2,1,0:T(8,128)S(1)} %all-to-all-done.2.col_parts_ref, f32[10,16,128]{2,1,0:T(8,128)S(1)} %get-tuple-element.93.first_ref, f32[10,16,128]{2,1,0:T(8,128)S(1)} %collective-permute-done.7.second_ref, f32[10,16,128]{2,1,0:T(8,128)S(1)} %collective-permute-done.8.third_ref, ...), custom_call_target="tpu_custom_call" | custom-call | tf_op jit(solution)/shard_map/image/pallas_call | solution.py:489
  75.2 8.1 %all-to-all-start.3 = ((f32[128,1,768]{2,1,0:T(1,128)}), f32[128,1,768]{2,1,0:T(1,128)S(1)}, u32[]{:S(2)}, u32[]{:S(2)}) async-start(f32[128,1,768]{2,1,0:T(1,128)} %get-tuple-element.99), calls=%async_computation.3 | async-start | bytes 786432 | tf_op jit(solution)/shard_map/all_to_all | solution.py:379
  83.4 4.5 %factor.1 = (f32[48,48]{1,0:T(8,128)S(1)}, f32[32,48]{1,0:T(8,128)S(1)}) custom-call(f32[10,16,128]{2,1,0:T(8,128)S(1)} %get-tuple-element.93.first_ref, f32[10,16,128]{2,1,0:T(8,128)S(1)} %collective-permute-done.7.second_ref, f32[10,16,128]{2,1,0:T(8,128)S(1)} %collective-permute-done.8.third_ref, f32[10,16,128]{2,1,0:T(8,128)S(1)} %collective-permute-done.9.fourth_ref), custom_call_target="tpu_custom_call" | custom-call | tf_op jit(solution)/shard_map/factor/pallas_call | solution.py:494
  87.8 1.0 %orthonormal.1 = f32[48,1024]{1,0:T(8,128)} custom-call(f32[48,48]{1,0:T(8,128)S(1)} %get-tuple-element.97.inverse_ref, f32[2,16,1024]{2,1,0:T(8,128)S(1)} %get-tuple-element.55.basis_ref, f32[16,1024]{1,0:T(8,128)S(1)} %get-tuple-element.91.first_ref.residual_ref), custom_call_target="tpu_custom_call" | custom-call | tf_op jit(solution)/shard_map/orthonormal/pallas_call | solution.py:495
  88.9 1.0 %orthonormal_image.1 = f32[48,1024]{1,0:T(8,128)} custom-call(f32[48,48]{1,0:T(8,128)S(1)} %get-tuple-element.97.inverse_ref, f32[2,16,1024]{2,1,0:T(8,128)S(1)} %get-tuple-element.56.images_ref, f32[16,1024]{1,0:T(8,128)S(1)} %get-tuple-element.98.image_ref), custom_call_target="tpu_custom_call" | custom-call | tf_op jit(solution)/shard_map/orthonormal_image/pallas_call | solution.py:498
  89.9 5.6 %all-to-all-done.3.received_ref = f32[128,1,768]{2,1,0:T(1,128)S(1)} async-done(((f32[128,1,768]{2,1,0:T(1,128)}), f32[128,1,768]{2,1,0:T(1,128)S(1)}, u32[]{:S(2)}, u32[]{:S(2)}) %all-to-all-start.3) | async-done | bytes 393248 | tf_op jit(solution)/shard_map/all_to_all | solution.py:379
  95.5 1.4 %projected.1 = f32[48,48]{1,0:T(8,128)} custom-call(f32[128,1,768]{2,1,0:T(1,128)S(1)} %all-to-all-done.3.received_ref, f32[48,48]{1,0:T(8,128)S(1)} %get-tuple-element.97.inverse_ref, f32[32,48]{1,0:T(8,128)S(1)} %get-tuple-element.100.early_ref), custom_call_target="tpu_custom_call" | custom-call | tf_op jit(solution)/shard_map/projected/pallas_call | solution.py:503
  (3 shorter events, 0.1 us)
Async XLA Ops:
  2.3 21.0 %all-to-all-start = ((f32[128,1,128]{2,1,0:T(1,128)}), f32[128,1,128]{2,1,0:T(1,128)S(1)}, u32[]{:S(2)}, u32[]{:S(2)}) async-start(f32[128,1,128]{2,1,0:T(1,128)} %bitcast.9), calls=%async_computation | async-start | bytes 131072 | tf_op jit(solution)/shard_map/all_to_all | solution.py:379
  13.8 0.8 copy-start
  14.6 0.8 copy-start.1
  15.4 0.8 copy-start.2
  16.3 0.8 copy-start.3
  24.8 13.0 %all-to-all-start.1 = ((f32[8,10,16,128]{3,2,1,0:T(8,128)}), f32[8,10,16,128]{3,2,1,0:T(8,128)S(1)}, u32[]{:S(2)}, u32[]{:S(2)}) async-start(f32[8,10,16,128]{3,2,1,0:T(8,128)} %get-tuple-element.57), calls=%async_computation.1 | async-start | bytes 1310720 | tf_op jit(solution)/shard_map/all_to_all | solution.py:379
  28.3 4.8 %collective-permute-start = (f32[16,1024]{1,0:T(8,128)S(1)}, f32[16,1024]{1,0:T(8,128)S(1)}, u32[]{:S(2)}, u32[]{:S(2)}) collective-permute-start(f32[16,1024]{1,0:T(8,128)S(1)} %get-tuple-element.91.first_ref.residual_ref), channel_id=1, source_target_pairs={{0,32},{16,48},{32,64},{48,80},{64,96},{80,112},{96,0},{112,16},{1... | collective-permute-start | bytes 196616 | tf_op jit(solution)/shard_map/ppermute | solution.py:388
  28.6 5.5 %collective-permute-start.1 = (f32[16,1024]{1,0:T(8,128)S(1)}, f32[16,1024]{1,0:T(8,128)S(1)}, u32[]{:S(2)}, u32[]{:S(2)}) collective-permute-start(f32[16,1024]{1,0:T(8,128)S(1)} %get-tuple-element.91.first_ref.residual_ref), channel_id=1, source_target_pairs={{0,64},{16,80},{32,96},{48,112},{64,0},{80,16},{96,32},{112,48},{1... | collective-permute-start | bytes 196616 | tf_op jit(solution)/shard_map/ppermute | solution.py:388
  29.9 4.4 %collective-permute-start.2 = (f32[16,1024]{1,0:T(8,128)S(1)}, f32[16,1024]{1,0:T(8,128)S(1)}, u32[]{:S(2)}, u32[]{:S(2)}) collective-permute-start(f32[16,1024]{1,0:T(8,128)S(1)} %get-tuple-element.91.first_ref.residual_ref), channel_id=1, source_target_pairs={{0,96},{16,112},{32,0},{48,16},{64,32},{80,48},{96,64},{112,80},{1... | collective-permute-start | bytes 196616 | tf_op jit(solution)/shard_map/ppermute | solution.py:388
  31.7 0.7 copy-start.4
  32.4 0.7 copy-start.5
  37.8 3.8 %collective-permute-start.3 = (f32[8,10,16,128]{3,2,1,0:T(8,128)S(1)}, f32[8,10,16,128]{3,2,1,0:T(8,128)S(1)}, u32[]{:S(2)}, u32[]{:S(2)}) collective-permute-start(f32[8,10,16,128]{3,2,1,0:T(8,128)S(1)} %all-to-all-done.1.own_ref), channel_id=1, source_target_pairs={{0,1},{1,0},{2,3},{3,2},{4,5},{5,4},{6,7},{7,6},{8,9},{9,8},{10,11... | collective-permute-start | bytes 1966088 | tf_op jit(solution)/shard_map/ppermute | solution.py:383
  39.9 9.4 %collective-permute-start.4 = (f32[4,8,16,128]{3,2,1,0:T(8,128)S(1)}, f32[4,8,16,128]{3,2,1,0:T(8,128)S(1)}, u32[]{:S(2)}, u32[]{:S(2)}) collective-permute-start(f32[4,8,16,128]{3,2,1,0:T(8,128)S(1)} %line.1.own_ref), channel_id=1, source_target_pairs={{0,16},{16,0},{32,48},{48,32},{64,80},{80,64},{96,112},{112,96},{1... | collective-permute-start | bytes 786440 | tf_op jit(solution)/shard_map/ppermute | solution.py:383
  49.3 8.9 %collective-permute-start.5 = (f32[34,16,128]{2,1,0:T(8,128)S(1)}, f32[34,16,128]{2,1,0:T(8,128)S(1)}, u32[]{:S(2)}, u32[]{:S(2)}) collective-permute-start(f32[34,16,128]{2,1,0:T(8,128)S(1)} %get-tuple-element.69), channel_id=1, source_target_pairs={{0,16},{16,0},{32,48},{48,32},{64,80},{80,64},{96,112},{112,96},{1... | collective-permute-start | bytes 835592 | tf_op jit(solution)/shard_map/ppermute | solution.py:383
  58.2 3.2 %collective-permute-start.6 = (f32[64,16,128]{2,1,0:T(8,128)S(1)}, f32[64,16,128]{2,1,0:T(8,128)S(1)}, u32[]{:S(2)}, u32[]{:S(2)}) collective-permute-start(f32[64,16,128]{2,1,0:T(8,128)S(1)} %get-tuple-element.74), channel_id=1, source_target_pairs={{0,1},{1,0},{2,3},{3,2},{4,5},{5,4},{6,7},{7,6},{8,9},{9,8},{10,11... | collective-permute-start | bytes 1572872 | tf_op jit(solution)/shard_map/ppermute | solution.py:383
  62.3 11.8 %all-to-all-start.2 = ((f32[8,8,16,128]{3,2,1,0:T(8,128)}), f32[8,8,16,128]{3,2,1,0:T(8,128)S(1)}, u32[]{:S(2)}, u32[]{:S(2)}) async-start(f32[8,8,16,128]{3,2,1,0:T(8,128)} %bitcast.4), calls=%async_computation.2 | async-start | bytes 1048576 | tf_op jit(solution)/shard_map/all_to_all | solution.py:379
  65.8 6.9 %collective-permute-start.7 = (f32[10,16,128]{2,1,0:T(8,128)S(1)}, f32[10,16,128]{2,1,0:T(8,128)S(1)}, u32[]{:S(2)}, u32[]{:S(2)}) collective-permute-start(f32[10,16,128]{2,1,0:T(8,128)S(1)} %get-tuple-element.83), channel_id=1, source_target_pairs={{0,32},{16,48},{32,64},{48,80},{64,96},{80,112},{96,0},{112,16},{1... | collective-permute-start | bytes 245768 | tf_op jit(solution)/shard_map/ppermute | solution.py:388
  66.0 6.6 %collective-permute-start.8 = (f32[10,16,128]{2,1,0:T(8,128)S(1)}, f32[10,16,128]{2,1,0:T(8,128)S(1)}, u32[]{:S(2)}, u32[]{:S(2)}) collective-permute-start(f32[10,16,128]{2,1,0:T(8,128)S(1)} %get-tuple-element.84), channel_id=1, source_target_pairs={{0,64},{16,80},{32,96},{48,112},{64,0},{80,16},{96,32},{112,48},{1... | collective-permute-start | bytes 245768 | tf_op jit(solution)/shard_map/ppermute | solution.py:388
  67.5 5.2 %collective-permute-start.9 = (f32[10,16,128]{2,1,0:T(8,128)S(1)}, f32[10,16,128]{2,1,0:T(8,128)S(1)}, u32[]{:S(2)}, u32[]{:S(2)}) collective-permute-start(f32[10,16,128]{2,1,0:T(8,128)S(1)} %get-tuple-element.85), channel_id=1, source_target_pairs={{0,96},{16,112},{32,0},{48,16},{64,32},{80,48},{96,64},{112,80},{1... | collective-permute-start | bytes 245768 | tf_op jit(solution)/shard_map/ppermute | solution.py:388
  75.2 20.2 %all-to-all-start.3 = ((f32[128,1,768]{2,1,0:T(1,128)}), f32[128,1,768]{2,1,0:T(1,128)S(1)}, u32[]{:S(2)}, u32[]{:S(2)}) async-start(f32[128,1,768]{2,1,0:T(1,128)} %get-tuple-element.99), calls=%async_computation.3 | async-start | bytes 786432 | tf_op jit(solution)/shard_map/all_to_all | solution.py:379

commit v12 on v11

--- a/solution.py
+++ b/solution.py
@@ -484,7 +484,8 @@
         name="join",
     )(own_totals, other_totals)
     col_parts = exchange(totals.reshape(chips, blocks, members, LANES), "col", core_groups)
-    row_parts = [outs[0]] + [shift_lines(outs[shift], shift) for shift in range(1, lines)]
+    farthest_first = sorted(range(1, lines), key=lambda shift: -min(shift, lines - shift))
+    row_parts = [outs[0]] + [shift_lines(outs[shift], shift) for shift in farthest_first]
     col_parts, *row_parts = lax.optimization_barrier((col_parts, *row_parts))
     image, slots = call(
         image_kernel, [(members, piece), (n_row * n_col, 1, members * order)], "image"

time: 97.8 us -> 97.6 us (level)
  transfers between devices with their start and end apart: 14 -> 14, of which waited for: 10 -> 11; matrix products, arithmetic and copies ran while one was open for 0% -> 0% of each run, Pallas kernels for 17% -> 17%
where the time goes in v12:
time: 97.6 us; the launch traced here: 95.9 us
  starting transfers between devices  39 us (40%)
  waiting for transfers between devices  28.3 us (29%)
  Pallas kernels  22.6 us (23%)
  local copies, waits for them, and re-layouts  4.71 us (5%)
  between operations  1.4 us (1%)
    all_to_all x4, starting transfers between devices, exchange(): lax.all_to_all(slots, axes, 0, 0, axis_index_groups=groups, tiled=True)  25.7 us
    all_to_all x4, waiting for transfers between devices, exchange(): lax.all_to_all(slots, axes, 0, 0, axis_index_groups=groups, tiled=True)  16 us
    pallas_call x2, Pallas kernels, tile_call(): pl.pallas_call(functools.partial(tile_kernel, forward=forward), out_shape...  9.21 us
    ppermute x4, waiting for transfers between devices, swap(): lax.ppermute(array, axis, [(i, i ^ distance) for i in range(lax.axis_size...  7.8 us
    ppermute x6, starting transfers between devices, shift_lines(): lax.ppermute(array, 'row', [(i, (i + 2 * shift) % size) for i in range(si...  7.34 us
    ppermute x4, starting transfers between devices, swap(): lax.ppermute(array, axis, [(i, i ^ distance) for i in range(lax.axis_size...  5.87 us
    unnamed x12, local copies, waits for them, and re-layouts  4.71 us
    pallas_call x1, Pallas kernels, on_device(): call(factor_kernel, [(order, order), (2 * members, order)], 'factor')  4.48 us
  transfers between devices with their start and end apart: 14, of which 11 were waited for; matrix products, arithmetic and copies ran while one was open for 0% of the time, Pallas kernels for 17%

profile of v12, /device:TPU:1, one launch (start us, length us, event | category | flops | bytes accessed | tf_op | source)
XLA Modules:
  0.0 95.9 jit_solution(11582223711777411768)
XLA Ops:
  0.6 1.6 %stage.1 = f32[128,128]{1,0:T(8,128)} custom-call(f32[16,1024]{1,0:T(8,128)} %vectors_hbm.3, f32[16,1024]{1,0:T(8,128)} %hvectors_hbm.3), custom_call_target="tpu_custom_call" | custom-call | tf_op jit(solution)/shard_map/stage/pallas_call | solution.py:410
  2.3 11.5 %all-to-all-start = ((f32[128,1,128]{2,1,0:T(1,128)}), f32[128,1,128]{2,1,0:T(1,128)S(1)}, u32[]{:S(2)}, u32[]{:S(2)}) async-start(f32[128,1,128]{2,1,0:T(1,128)} %bitcast.9), calls=%async_computation | async-start | bytes 131072 | tf_op jit(solution)/shard_map/all_to_all | solution.py:379
  13.8 0.0 copy-start
  13.8 0.8 copy-done
  14.6 0.0 copy-start.1
  14.6 0.8 copy-done.1
  15.4 0.0 copy-start.2
  15.5 0.8 copy-done.2
  16.3 0.0 copy-start.3
  16.3 0.8 copy-done.3
  17.1 0.3 prepare.1
  17.5 5.8 %all-to-all-done = f32[128,1,128]{2,1,0:T(1,128)S(1)} async-done(((f32[128,1,128]{2,1,0:T(1,128)}), f32[128,1,128]{2,1,0:T(1,128)S(1)}, u32[]{:S(2)}, u32[]{:S(2)}) %all-to-all-start) | async-done | bytes 65568 | tf_op jit(solution)/shard_map/all_to_all | solution.py:379
  23.3 1.5 %residual.1 = (f32[16,1024]{1,0:T(8,128)S(1)}, f32[8,10,16,128]{3,2,1,0:T(8,128)}) custom-call(f32[128,128]{1,0:T(8,128)S(1)} %bitcast.6, f32[2,16,1024]{2,1,0:T(8,128)S(1)} %get-tuple-element.55.basis_ref, f32[2,16,1024]{2,1,0:T(8,128)S(1)} %get-tuple-element.56.images_ref), custom_call_target="tpu_custom_call" | custom-call | tf_op jit(solution)/shard_map/residual/pallas_call | solution.py:433
  24.8 3.5 %all-to-all-start.1 = ((f32[8,10,16,128]{3,2,1,0:T(8,128)}), f32[8,10,16,128]{3,2,1,0:T(8,128)S(1)}, u32[]{:S(2)}, u32[]{:S(2)}) async-start(f32[8,10,16,128]{3,2,1,0:T(8,128)} %get-tuple-element.57), calls=%async_computation.1 | async-start | bytes 1310720 | tf_op jit(solution)/shard_map/all_to_all | solution.py:379
  28.3 0.3 collective-permute-start
  28.6 1.3 %collective-permute-start.1 = (f32[16,1024]{1,0:T(8,128)S(1)}, f32[16,1024]{1,0:T(8,128)S(1)}, u32[]{:S(2)}, u32[]{:S(2)}) collective-permute-start(f32[16,1024]{1,0:T(8,128)S(1)} %get-tuple-element.91.first_ref.residual_ref), channel_id=1, source_target_pairs={{0,64},{16,80},{32,96},{48,112},{64,0},{80,16},{96,32},{112,48},{1... | collective-permute-start | bytes 196616 | tf_op jit(solution)/shard_map/ppermute | solution.py:388
  29.9 1.8 %collective-permute-start.2 = (f32[16,1024]{1,0:T(8,128)S(1)}, f32[16,1024]{1,0:T(8,128)S(1)}, u32[]{:S(2)}, u32[]{:S(2)}) collective-permute-start(f32[16,1024]{1,0:T(8,128)S(1)} %get-tuple-element.91.first_ref.residual_ref), channel_id=1, source_target_pairs={{0,96},{16,112},{32,0},{48,16},{64,32},{80,48},{96,64},{112,80},{1... | collective-permute-start | bytes 196616 | tf_op jit(solution)/shard_map/ppermute | solution.py:388
  31.7 0.0 copy-start.4
  31.7 0.7 copy-done.4
  32.4 0.0 copy-start.5
  32.4 0.7 copy-done.5
  33.1 0.0 collective-permute-done.second_ref
  33.1 1.0 %collective-permute-done.1.third_ref = f32[16,1024]{1,0:T(8,128)S(1)} collective-permute-done((f32[16,1024]{1,0:T(8,128)S(1)}, f32[16,1024]{1,0:T(8,128)S(1)}, u32[]{:S(2)}, u32[]{:S(2)}) %collective-permute-start.1) | collective-permute-done | bytes 65568 | tf_op jit(solution)/shard_map/ppermute | solution.py:388
  34.1 0.2 collective-permute-done.2.fourth_ref
  34.3 3.5 %all-to-all-done.1.own_ref = f32[8,10,16,128]{3,2,1,0:T(8,128)S(1)} async-done(((f32[8,10,16,128]{3,2,1,0:T(8,128)}), f32[8,10,16,128]{3,2,1,0:T(8,128)S(1)}, u32[]{:S(2)}, u32[]{:S(2)}) %all-to-all-start.1) | async-done | bytes 655392 | tf_op jit(solution)/shard_map/all_to_all | solution.py:379
  37.8 2.0 %collective-permute-start.3 = (f32[8,10,16,128]{3,2,1,0:T(8,128)S(1)}, f32[8,10,16,128]{3,2,1,0:T(8,128)S(1)}, u32[]{:S(2)}, u32[]{:S(2)}) collective-permute-start(f32[8,10,16,128]{3,2,1,0:T(8,128)S(1)} %all-to-all-done.1.own_ref), channel_id=1, source_target_pairs={{0,1},{1,0},{2,3},{3,2},{4,5},{5,4},{6,7},{7,6},{8,9},{9,8},{10,11... | collective-permute-start | bytes 1966088 | tf_op jit(solution)/shard_map/ppermute | solution.py:383
  39.9 1.1 %collective-permute-start.4 = (f32[4,8,16,128]{3,2,1,0:T(8,128)S(1)}, f32[4,8,16,128]{3,2,1,0:T(8,128)S(1)}, u32[]{:S(2)}, u32[]{:S(2)}) collective-permute-start(f32[4,8,16,128]{3,2,1,0:T(8,128)S(1)} %line.1.own_ref), channel_id=1, source_target_pairs={{0,16},{16,0},{32,48},{48,32},{64,80},{80,64},{96,112},{112,96},{1... | collective-permute-start | bytes 786440 | tf_op jit(solution)/shard_map/ppermute | solution.py:383
  41.6 0.0 collective-permute-done.3.other_ref
  41.6 3.8 %backward_tiles.1 = (f32[34,16,128]{2,1,0:T(8,128)S(1)}, f32[34,16,128]{2,1,0:T(8,128)S(1)}) custom-call(s32[1,1]{1,0:T(1,128)S(6)} %copy.12.count_ref, s32[1,1,384]{2,1,0:T(1,128)S(1)} %get-tuple-element.63.rows_hbm, s32[1,1,384]{2,1,0:T(1,128)S(1)} %get-tuple-element.64.cols_hbm, bf16[384,128,128]{2,1,0:T(8,128)(2,1)} %bitcast.7, ...), custom_call_target="tpu_custom_call" | custom-call | tf_op jit(solution)/shard_map/backward_tiles/pallas_call | solution.py:355
  45.4 3.9 %collective-permute-done.4.other_ref = f32[4,8,16,128]{3,2,1,0:T(8,128)S(1)} collective-permute-done((f32[4,8,16,128]{3,2,1,0:T(8,128)S(1)}, f32[4,8,16,128]{3,2,1,0:T(8,128)S(1)}, u32[]{:S(2)}, u32[]{:S(2)}) %collective-permute-start.4) | collective-permute-done | bytes 262176 | tf_op jit(solution)/shard_map/ppermute | solution.py:383
  49.3 1.1 %collective-permute-start.5 = (f32[34,16,128]{2,1,0:T(8,128)S(1)}, f32[34,16,128]{2,1,0:T(8,128)S(1)}, u32[]{:S(2)}, u32[]{:S(2)}) collective-permute-start(f32[34,16,128]{2,1,0:T(8,128)S(1)} %get-tuple-element.69), channel_id=1, source_target_pairs={{0,16},{16,0},{32,48},{48,32},{64,80},{80,64},{96,112},{112,96},{1... | collective-permute-start | bytes 835592 | tf_op jit(solution)/shard_map/ppermute | solution.py:383
  50.4 5.4 %forward_tiles.1 = (f32[64,16,128]{2,1,0:T(8,128)S(1)}, f32[64,16,128]{2,1,0:T(8,128)S(1)}) custom-call(s32[1,1]{1,0:T(1,128)S(6)} %copy.12.count_ref, s32[1,1,384]{2,1,0:T(1,128)S(1)} %get-tuple-element.63.rows_hbm, s32[1,1,384]{2,1,0:T(1,128)S(1)} %get-tuple-element.64.cols_hbm, bf16[384,128,128]{2,1,0:T(8,128)(2,1)} %bitcast.8, ...), custom_call_target="tpu_custom_call" | custom-call | tf_op jit(solution)/shard_map/forward_tiles/pallas_call | solution.py:355
  55.8 2.4 %collective-permute-done.5.received_ref = f32[34,16,128]{2,1,0:T(8,128)S(1)} collective-permute-done((f32[34,16,128]{2,1,0:T(8,128)S(1)}, f32[34,16,128]{2,1,0:T(8,128)S(1)}, u32[]{:S(2)}, u32[]{:S(2)}) %collective-permute-start.5) | collective-permute-done | bytes 278560 | tf_op jit(solution)/shard_map/ppermute | solution.py:383
  58.2 1.7 %collective-permute-start.6 = (f32[64,16,128]{2,1,0:T(8,128)S(1)}, f32[64,16,128]{2,1,0:T(8,128)S(1)}, u32[]{:S(2)}, u32[]{:S(2)}) collective-permute-start(f32[64,16,128]{2,1,0:T(8,128)S(1)} %get-tuple-element.74), channel_id=1, source_target_pairs={{0,1},{1,0},{2,3},{3,2},{4,5},{5,4},{6,7},{7,6},{8,9},{9,8},{10,11... | collective-permute-start | bytes 1572872 | tf_op jit(solution)/shard_map/ppermute | solution.py:383
  59.9 1.5 %collective-permute-done.6.other_ref = f32[64,16,128]{2,1,0:T(8,128)S(1)} collective-permute-done((f32[64,16,128]{2,1,0:T(8,128)S(1)}, f32[64,16,128]{2,1,0:T(8,128)S(1)}, u32[]{:S(2)}, u32[]{:S(2)}) %collective-permute-start.6) | collective-permute-done | bytes 524320 | tf_op jit(solution)/shard_map/ppermute | solution.py:383
  61.4 0.9 join.1
  62.3 3.5 %all-to-all-start.2 = ((f32[8,8,16,128]{3,2,1,0:T(8,128)}), f32[8,8,16,128]{3,2,1,0:T(8,128)S(1)}, u32[]{:S(2)}, u32[]{:S(2)}) async-start(f32[8,8,16,128]{3,2,1,0:T(8,128)} %bitcast.4), calls=%async_computation.2 | async-start | bytes 1048576 | tf_op jit(solution)/shard_map/all_to_all | solution.py:379
  65.8 1.3 %collective-permute-start.7 = (f32[10,16,128]{2,1,0:T(8,128)S(1)}, f32[10,16,128]{2,1,0:T(8,128)S(1)}, u32[]{:S(2)}, u32[]{:S(2)}) collective-permute-start(f32[10,16,128]{2,1,0:T(8,128)S(1)} %get-tuple-element.83), channel_id=1, source_target_pairs={{0,64},{16,80},{32,96},{48,112},{64,0},{80,16},{96,32},{112,48},{1... | collective-permute-start | bytes 245768 | tf_op jit(solution)/shard_map/ppermute | solution.py:388
  67.1 0.0 collective-permute-start.8
  67.1 2.7 %collective-permute-start.9 = (f32[10,16,128]{2,1,0:T(8,128)S(1)}, f32[10,16,128]{2,1,0:T(8,128)S(1)}, u32[]{:S(2)}, u32[]{:S(2)}) collective-permute-start(f32[10,16,128]{2,1,0:T(8,128)S(1)} %get-tuple-element.85), channel_id=1, source_target_pairs={{0,96},{16,112},{32,0},{48,16},{64,32},{80,48},{96,64},{112,80},{1... | collective-permute-start | bytes 245768 | tf_op jit(solution)/shard_map/ppermute | solution.py:388
  69.7 1.2 %collective-permute-done.7.second_ref = f32[10,16,128]{2,1,0:T(8,128)S(1)} collective-permute-done((f32[10,16,128]{2,1,0:T(8,128)S(1)}, f32[10,16,128]{2,1,0:T(8,128)S(1)}, u32[]{:S(2)}, u32[]{:S(2)}) %collective-permute-start.7) | collective-permute-done | bytes 81952 | tf_op jit(solution)/shard_map/ppermute | solution.py:388
  71.0 2.0 %collective-permute-done.8.third_ref = f32[10,16,128]{2,1,0:T(8,128)S(1)} collective-permute-done((f32[10,16,128]{2,1,0:T(8,128)S(1)}, f32[10,16,128]{2,1,0:T(8,128)S(1)}, u32[]{:S(2)}, u32[]{:S(2)}) %collective-permute-start.8) | collective-permute-done | bytes 81952 | tf_op jit(solution)/shard_map/ppermute | solution.py:388
  73.0 0.0 collective-permute-done.9.fourth_ref
  73.0 1.1 %all-to-all-done.2.col_parts_ref = f32[8,8,16,128]{3,2,1,0:T(8,128)S(1)} async-done(((f32[8,8,16,128]{3,2,1,0:T(8,128)}), f32[8,8,16,128]{3,2,1,0:T(8,128)S(1)}, u32[]{:S(2)}, u32[]{:S(2)}) %all-to-all-start.2) | async-done | bytes 524320 | tf_op jit(solution)/shard_map/all_to_all | solution.py:379
  74.1 1.2 %image.1 = (f32[16,1024]{1,0:T(8,128)S(1)}, f32[128,1,768]{2,1,0:T(1,128)}) custom-call(f32[8,8,16,128]{3,2,1,0:T(8,128)S(1)} %all-to-all-done.2.col_parts_ref, f32[10,16,128]{2,1,0:T(8,128)S(1)} %get-tuple-element.93.first_ref, f32[10,16,128]{2,1,0:T(8,128)S(1)} %collective-permute-done.7.second_ref, f32[10,16,128]{2,1,0:T(8,128)S(1)} %collective-permute-done.8.third_ref, ...), custom_call_target="tpu_custom_call" | custom-call | tf_op jit(solution)/shard_map/image/pallas_call | solution.py:490
  75.2 7.2 %all-to-all-start.3 = ((f32[128,1,768]{2,1,0:T(1,128)}), f32[128,1,768]{2,1,0:T(1,128)S(1)}, u32[]{:S(2)}, u32[]{:S(2)}) async-start(f32[128,1,768]{2,1,0:T(1,128)} %get-tuple-element.99), calls=%async_computation.3 | async-start | bytes 786432 | tf_op jit(solution)/shard_map/all_to_all | solution.py:379
  82.5 4.5 %factor.1 = (f32[48,48]{1,0:T(8,128)S(1)}, f32[32,48]{1,0:T(8,128)S(1)}) custom-call(f32[10,16,128]{2,1,0:T(8,128)S(1)} %get-tuple-element.93.first_ref, f32[10,16,128]{2,1,0:T(8,128)S(1)} %collective-permute-done.7.second_ref, f32[10,16,128]{2,1,0:T(8,128)S(1)} %collective-permute-done.8.third_ref, f32[10,16,128]{2,1,0:T(8,128)S(1)} %collective-permute-done.9.fourth_ref), custom_call_target="tpu_custom_call" | custom-call | tf_op jit(solution)/shard_map/factor/pallas_call | solution.py:495
  86.9 1.0 %orthonormal.1 = f32[48,1024]{1,0:T(8,128)} custom-call(f32[48,48]{1,0:T(8,128)S(1)} %get-tuple-element.97.inverse_ref, f32[2,16,1024]{2,1,0:T(8,128)S(1)} %get-tuple-element.55.basis_ref, f32[16,1024]{1,0:T(8,128)S(1)} %get-tuple-element.91.first_ref.residual_ref), custom_call_target="tpu_custom_call" | custom-call | tf_op jit(solution)/shard_map/orthonormal/pallas_call | solution.py:496
  88.0 1.0 %orthonormal_image.1 = f32[48,1024]{1,0:T(8,128)} custom-call(f32[48,48]{1,0:T(8,128)S(1)} %get-tuple-element.97.inverse_ref, f32[2,16,1024]{2,1,0:T(8,128)S(1)} %get-tuple-element.56.images_ref, f32[16,1024]{1,0:T(8,128)S(1)} %get-tuple-element.98.image_ref), custom_call_target="tpu_custom_call" | custom-call | tf_op jit(solution)/shard_map/orthonormal_image/pallas_call | solution.py:499
  89.0 5.6 %all-to-all-done.3.received_ref = f32[128,1,768]{2,1,0:T(1,128)S(1)} async-done(((f32[128,1,768]{2,1,0:T(1,128)}), f32[128,1,768]{2,1,0:T(1,128)S(1)}, u32[]{:S(2)}, u32[]{:S(2)}) %all-to-all-start.3) | async-done | bytes 393248 | tf_op jit(solution)/shard_map/all_to_all | solution.py:379
  94.6 1.4 %projected.1 = f32[48,48]{1,0:T(8,128)} custom-call(f32[128,1,768]{2,1,0:T(1,128)S(1)} %all-to-all-done.3.received_ref, f32[48,48]{1,0:T(8,128)S(1)} %get-tuple-element.97.inverse_ref, f32[32,48]{1,0:T(8,128)S(1)} %get-tuple-element.100.early_ref), custom_call_target="tpu_custom_call" | custom-call | tf_op jit(solution)/shard_map/projected/pallas_call | solution.py:504
  (3 shorter events, 0.1 us)
Async XLA Ops:
  2.3 21.0 %all-to-all-start = ((f32[128,1,128]{2,1,0:T(1,128)}), f32[128,1,128]{2,1,0:T(1,128)S(1)}, u32[]{:S(2)}, u32[]{:S(2)}) async-start(f32[128,1,128]{2,1,0:T(1,128)} %bitcast.9), calls=%async_computation | async-start | bytes 131072 | tf_op jit(solution)/shard_map/all_to_all | solution.py:379
  13.8 0.8 copy-start
  14.6 0.8 copy-start.1
  15.4 0.8 copy-start.2
  16.3 0.8 copy-start.3
  24.8 13.0 %all-to-all-start.1 = ((f32[8,10,16,128]{3,2,1,0:T(8,128)}), f32[8,10,16,128]{3,2,1,0:T(8,128)S(1)}, u32[]{:S(2)}, u32[]{:S(2)}) async-start(f32[8,10,16,128]{3,2,1,0:T(8,128)} %get-tuple-element.57), calls=%async_computation.1 | async-start | bytes 1310720 | tf_op jit(solution)/shard_map/all_to_all | solution.py:379
  28.3 4.8 %collective-permute-start = (f32[16,1024]{1,0:T(8,128)S(1)}, f32[16,1024]{1,0:T(8,128)S(1)}, u32[]{:S(2)}, u32[]{:S(2)}) collective-permute-start(f32[16,1024]{1,0:T(8,128)S(1)} %get-tuple-element.91.first_ref.residual_ref), channel_id=1, source_target_pairs={{0,32},{16,48},{32,64},{48,80},{64,96},{80,112},{96,0},{112,16},{1... | collective-permute-start | bytes 196616 | tf_op jit(solution)/shard_map/ppermute | solution.py:388
  28.6 5.5 %collective-permute-start.1 = (f32[16,1024]{1,0:T(8,128)S(1)}, f32[16,1024]{1,0:T(8,128)S(1)}, u32[]{:S(2)}, u32[]{:S(2)}) collective-permute-start(f32[16,1024]{1,0:T(8,128)S(1)} %get-tuple-element.91.first_ref.residual_ref), channel_id=1, source_target_pairs={{0,64},{16,80},{32,96},{48,112},{64,0},{80,16},{96,32},{112,48},{1... | collective-permute-start | bytes 196616 | tf_op jit(solution)/shard_map/ppermute | solution.py:388
  29.9 4.4 %collective-permute-start.2 = (f32[16,1024]{1,0:T(8,128)S(1)}, f32[16,1024]{1,0:T(8,128)S(1)}, u32[]{:S(2)}, u32[]{:S(2)}) collective-permute-start(f32[16,1024]{1,0:T(8,128)S(1)} %get-tuple-element.91.first_ref.residual_ref), channel_id=1, source_target_pairs={{0,96},{16,112},{32,0},{48,16},{64,32},{80,48},{96,64},{112,80},{1... | collective-permute-start | bytes 196616 | tf_op jit(solution)/shard_map/ppermute | solution.py:388
  31.7 0.7 copy-start.4
  32.4 0.7 copy-start.5
  37.8 3.8 %collective-permute-start.3 = (f32[8,10,16,128]{3,2,1,0:T(8,128)S(1)}, f32[8,10,16,128]{3,2,1,0:T(8,128)S(1)}, u32[]{:S(2)}, u32[]{:S(2)}) collective-permute-start(f32[8,10,16,128]{3,2,1,0:T(8,128)S(1)} %all-to-all-done.1.own_ref), channel_id=1, source_target_pairs={{0,1},{1,0},{2,3},{3,2},{4,5},{5,4},{6,7},{7,6},{8,9},{9,8},{10,11... | collective-permute-start | bytes 1966088 | tf_op jit(solution)/shard_map/ppermute | solution.py:383
  39.9 9.4 %collective-permute-start.4 = (f32[4,8,16,128]{3,2,1,0:T(8,128)S(1)}, f32[4,8,16,128]{3,2,1,0:T(8,128)S(1)}, u32[]{:S(2)}, u32[]{:S(2)}) collective-permute-start(f32[4,8,16,128]{3,2,1,0:T(8,128)S(1)} %line.1.own_ref), channel_id=1, source_target_pairs={{0,16},{16,0},{32,48},{48,32},{64,80},{80,64},{96,112},{112,96},{1... | collective-permute-start | bytes 786440 | tf_op jit(solution)/shard_map/ppermute | solution.py:383
  49.3 8.9 %collective-permute-start.5 = (f32[34,16,128]{2,1,0:T(8,128)S(1)}, f32[34,16,128]{2,1,0:T(8,128)S(1)}, u32[]{:S(2)}, u32[]{:S(2)}) collective-permute-start(f32[34,16,128]{2,1,0:T(8,128)S(1)} %get-tuple-element.69), channel_id=1, source_target_pairs={{0,16},{16,0},{32,48},{48,32},{64,80},{80,64},{96,112},{112,96},{1... | collective-permute-start | bytes 835592 | tf_op jit(solution)/shard_map/ppermute | solution.py:383
  58.2 3.2 %collective-permute-start.6 = (f32[64,16,128]{2,1,0:T(8,128)S(1)}, f32[64,16,128]{2,1,0:T(8,128)S(1)}, u32[]{:S(2)}, u32[]{:S(2)}) collective-permute-start(f32[64,16,128]{2,1,0:T(8,128)S(1)} %get-tuple-element.74), channel_id=1, source_target_pairs={{0,1},{1,0},{2,3},{3,2},{4,5},{5,4},{6,7},{7,6},{8,9},{9,8},{10,11... | collective-permute-start | bytes 1572872 | tf_op jit(solution)/shard_map/ppermute | solution.py:383
  62.3 11.8 %all-to-all-start.2 = ((f32[8,8,16,128]{3,2,1,0:T(8,128)}), f32[8,8,16,128]{3,2,1,0:T(8,128)S(1)}, u32[]{:S(2)}, u32[]{:S(2)}) async-start(f32[8,8,16,128]{3,2,1,0:T(8,128)} %bitcast.4), calls=%async_computation.2 | async-start | bytes 1048576 | tf_op jit(solution)/shard_map/all_to_all | solution.py:379
  65.8 5.2 %collective-permute-start.7 = (f32[10,16,128]{2,1,0:T(8,128)S(1)}, f32[10,16,128]{2,1,0:T(8,128)S(1)}, u32[]{:S(2)}, u32[]{:S(2)}) collective-permute-start(f32[10,16,128]{2,1,0:T(8,128)S(1)} %get-tuple-element.83), channel_id=1, source_target_pairs={{0,64},{16,80},{32,96},{48,112},{64,0},{80,16},{96,32},{112,48},{1... | collective-permute-start | bytes 245768 | tf_op jit(solution)/shard_map/ppermute | solution.py:388
  67.1 5.9 %collective-permute-start.8 = (f32[10,16,128]{2,1,0:T(8,128)S(1)}, f32[10,16,128]{2,1,0:T(8,128)S(1)}, u32[]{:S(2)}, u32[]{:S(2)}) collective-permute-start(f32[10,16,128]{2,1,0:T(8,128)S(1)} %get-tuple-element.84), channel_id=1, source_target_pairs={{0,32},{16,48},{32,64},{48,80},{64,96},{80,112},{96,0},{112,16},{1... | collective-permute-start | bytes 245768 | tf_op jit(solution)/shard_map/ppermute | solution.py:388
  67.1 5.9 %collective-permute-start.9 = (f32[10,16,128]{2,1,0:T(8,128)S(1)}, f32[10,16,128]{2,1,0:T(8,128)S(1)}, u32[]{:S(2)}, u32[]{:S(2)}) collective-permute-start(f32[10,16,128]{2,1,0:T(8,128)S(1)} %get-tuple-element.85), channel_id=1, source_target_pairs={{0,96},{16,112},{32,0},{48,16},{64,32},{80,48},{96,64},{112,80},{1... | collective-permute-start | bytes 245768 | tf_op jit(solution)/shard_map/ppermute | solution.py:388
  75.2 19.3 %all-to-all-start.3 = ((f32[128,1,768]{2,1,0:T(1,128)}), f32[128,1,768]{2,1,0:T(1,128)S(1)}, u32[]{:S(2)}, u32[]{:S(2)}) async-start(f32[128,1,768]{2,1,0:T(1,128)} %get-tuple-element.99), calls=%async_computation.3 | async-start | bytes 786432 | tf_op jit(solution)/shard_map/all_to_all | solution.py:379
